TPU v7x, 512 devices: a whole 4x8x8 slice. The times are simulated.
512 devices in a mesh: wide: 64 (over y_hi, z, core), narrow: 8 (over x, y_lo).
Axes of the slice: x: 4, y: 8 (y_hi: 4, y_lo: 2; y = y_hi * 2 + y_lo), z: 8, core: 2. Of those that a mesh axis runs over, the one named last changes fastest.
Arguments:
- images: bfloat16 [8192, 72, 256], P('wide'), may hold values from -512 to 512
- defocus: float32 [8192], P('wide'), may hold values from 1 to 3
- class_index: int32 [8192], P('wide'), may hold values from 0 to 191
- rotation_index: int32 [8192], P('wide'), may hold values from 0 to 71
- owner_map: int32 [192], replicated, may hold values from 0 to 63, as said below
- roster: int32 [8, 3], replicated, may hold values from 0 to 63, as said below
- ref_store: bfloat16 [64, 8, 8, 72, 256], P('wide', 'narrow'), may hold values from -0.25 to 0.25
Outputs:
- new_references: bfloat16 [64, 8, 4, 72, 256], P('wide', 'narrow')
- log_evidence: float32 [8192], P('wide')
Inputs may be any that keep to these rules, and one draw needn't show every extreme that they name: Each row of roster names 3 different indices. `owner_map`: in each group of 24 consecutive classes, no index is named more than 4 times, and one index is named exactly 4 times.
All inputs are finite; a program needn't handle non-finite values.
Results may differ from a plain program's by a relative error of at most 0.0038.
The roundings to bfloat16 on the way count: a program that leaves them out, or rounds other values in their place, can miss the bound.
Values may be sent and summed in bfloat16 or wider, within the bound.
No kernel may reach another device: no remote copies, remote signals or barrier semaphores. Data moves between devices by JAX's collectives and lax.ppermute only.
A program may use at most 128 MiB of HBM per device.

v0:
```python
import math

import jax
import jax.numpy as jnp
from jax import lax
from jax.sharding import Mesh
from jax.sharding import PartitionSpec as P

CYCLES = 128
ANGLES = 72
STEPS = 3
OWN_MAX = 4
CLS_GRP = 24
SIGMA_ROT = 8
WIDE = ("wide_0", "wide_1", "wide_2")


TAU = 1.0
CONTRAST = 0.1
TOP_PRECISION = lax.Precision.HIGHEST


def from_root(x, axis, root):
    return lax.dynamic_index_in_dim(lax.all_gather(x, axis), root, 0, keepdims=False)


def gathered_once(x, axis):
    leaves = jax.tree.leaves(x)
    order = sorted(range(len(leaves)), key=lambda k: -leaves[k].size)
    width = (1, *leaves[order[0]].shape)[-1]
    lines = [
        jnp.pad(leaves[k].reshape(-1), (0, -leaves[k].size % width)).reshape(-1, width)
        for k in order
    ]
    both, at, found = (lax.all_gather(jnp.concatenate(lines), axis), 0, {})
    for k, line in zip(order, lines):
        section = both[:, at : at + len(line)].reshape(len(both), -1)
        found[k] = section[:, : leaves[k].size].reshape(-1, *leaves[k].shape)
        at += len(line)
    numbers = iter(range(len(leaves)))
    return jax.tree.map(lambda _: found[next(numbers)], x)


def combined_all(x, axis, combine):
    everything = gathered_once(x, axis)
    leading = jax.tree.map(lambda part: part[0], everything)

    def lap(k, so_far):
        return combine(so_far, jax.tree.map(lambda part: part[k], everything))

    return lax.fori_loop(1, lax.axis_size(axis), lap, leading)


def cut_along(x, dim, peers):
    lengths = x.shape
    tiles = x.reshape(*lengths[:dim], peers, lengths[dim] // peers, *lengths[dim + 1 :])
    return jnp.moveaxis(tiles, dim, 0)


def sent_and_summed(x, axis, dim):
    tiles = cut_along(x, dim, lax.axis_size(axis))
    arrived = lax.all_to_all(tiles, axis, split_axis=0, concat_axis=0, tiled=True)
    return arrived.sum(axis=0)


def joined_along(tiles, dim):
    lengths = list(tiles.shape[1:])
    lengths[dim] *= tiles.shape[0]
    return jnp.moveaxis(tiles, 0, dim).reshape(lengths)


def exchange_in_order(tiles, axes, order):
    inside = tiles.shape[1:]
    result = tiles.reshape(*(lax.axis_size(a) for a in axes), *inside)
    for k in order:
        result = lax.all_to_all(result, axes[k], k, k, tiled=True)
    return result.reshape(-1, *inside)


def exchange_by_chip(x, groups, order, split_dim, concat_dim):
    peers = lax.axis_size(groups[0]) * lax.axis_size(groups[1])
    tiles = cut_along(x, split_dim, peers)
    return joined_along(exchange_in_order(tiles, groups, order), concat_dim)


def angle_tables(length):
    counting = jnp.arange(length, dtype=jnp.int32)
    products = counting[:, None] * counting[None, :] % length
    phase_angle = products.astype(jnp.float32) * (2.0 * math.pi / length)
    return (jnp.cos(phase_angle), jnp.sin(phase_angle))


def contrast(defocus_rows):
    cycle_freq = (jnp.arange(CYCLES, dtype=jnp.float32) + 1.0) / CYCLES
    phase_angle = 8.0 * math.pi * defocus_rows[:, None] * cycle_freq[None, :] ** 2
    return -jnp.sin(phase_angle) - CONTRAST * jnp.cos(phase_angle)


def spectrum(polar, cosines_low, sines_low):
    cos_part = jnp.einsum("ma,naj->nmj", cosines_low, polar, preferred_element_type=jnp.float32)
    sin_part = jnp.einsum("ma,naj->nmj", sines_low, polar, preferred_element_type=jnp.float32)
    real_part = cos_part[..., :CYCLES] + sin_part[..., CYCLES:]
    imag_part = cos_part[..., CYCLES:] - sin_part[..., :CYCLES]
    return jnp.concatenate([real_part, imag_part], axis=-1).astype(jnp.bfloat16)


def rotation_prior(rotation_rows):
    counting = jnp.arange(ANGLES, dtype=jnp.int32)
    distance = jnp.abs(counting[None, :] - rotation_rows[:, None])
    distance = jnp.minimum(distance, ANGLES - distance).astype(jnp.float32)
    return -0.5 * (distance / SIGMA_ROT) ** 2


def polar_image(harmonic, cosine_table, sine_table):
    real_part = harmonic[..., :CYCLES]
    imag_part = harmonic[..., CYCLES:]
    polar_real = (
        jnp.einsum("cmk,ma->cak", real_part, cosine_table, precision=TOP_PRECISION)
        - jnp.einsum("cmk,ma->cak", imag_part, sine_table, precision=TOP_PRECISION)
    ) / ANGLES
    polar_imag = (
        jnp.einsum("cmk,ma->cak", imag_part, cosine_table, precision=TOP_PRECISION)
        + jnp.einsum("cmk,ma->cak", real_part, sine_table, precision=TOP_PRECISION)
    ) / ANGLES
    return jnp.concatenate([polar_real, polar_imag], axis=-1)


def combine(earlier, later):
    joined = jnp.maximum(earlier[0], later[0])
    return (
        joined,
        earlier[1] * jnp.exp(earlier[0] - joined) + later[1] * jnp.exp(later[0] - joined),
    )


def per_device(images, defocus, class_index, rotation_index, owner_map, roster, ref_store):
    class_group = lax.axis_index("narrow")
    wide_count = lax.axis_size(WIDE)
    particles = images.shape[0]
    feature_len = ANGLES * 2 * CYCLES
    cosine_table, sine_table = angle_tables(ANGLES)
    cosines_low = cosine_table.astype(jnp.bfloat16)
    sines_low = sine_table.astype(jnp.bfloat16)
    contrast_rows = contrast(defocus)
    contrast_sq = contrast_rows * contrast_rows
    doubled = jnp.concatenate([contrast_rows, contrast_rows], axis=-1)
    weighted = (images.astype(jnp.float32) * doubled[:, None, :]).astype(jnp.bfloat16)
    spectra = spectrum(weighted, cosines_low, sines_low)
    prior_rows = rotation_prior(rotation_index)
    owner_plan = lax.dynamic_index_in_dim(roster, class_group, 0, keepdims=False)
    leading_class = class_group * CLS_GRP

    def fetch_block(block_step):
        return from_root(ref_store[0, 0], WIDE, owner_plan[block_step])

    carried = (
        jnp.full((particles,), -jnp.inf, jnp.float32),
        jnp.zeros((particles,), jnp.float32),
        jnp.zeros((particles, ANGLES), jnp.float32),
    )
    blocks = [fetch_block(block_step) for block_step in range(STEPS)]
    refs = jnp.concatenate(blocks, axis=0)
    running_max, running_sum, own_scores = carried
    ref_spec = spectrum(refs, cosines_low, sines_low)
    ref_swap = jnp.concatenate([-ref_spec[..., CYCLES:], ref_spec[..., :CYCLES]], axis=-1)
    real_correlation = jnp.einsum(
        "pmj,cmj->pcm", spectra, ref_spec, preferred_element_type=jnp.float32
    )
    imaginary_correlation = jnp.einsum(
        "pmj,cmj->pcm", spectra, ref_swap, preferred_element_type=jnp.float32
    )
    turned_images = jnp.einsum(
        "exj,ji->exi", real_correlation, cosine_table, precision=TOP_PRECISION
    ) - jnp.einsum("exj,ji->exi", imaginary_correlation, sine_table, precision=TOP_PRECISION)
    power = jnp.sum(jnp.square(ref_spec.astype(jnp.float32)), axis=1)
    power = power[:, :CYCLES] + power[:, CYCLES:]
    energy = jnp.dot(contrast_sq, power.T, precision=TOP_PRECISION)
    scores = (turned_images - 0.5 * energy[:, :, None]) / ANGLES + prior_rows[:, None, :]
    class_ids = leading_class + jnp.arange(refs.shape[0], dtype=jnp.int32)
    matches = (class_index[:, None] == class_ids[None, :]).astype(jnp.float32)
    own_scores = jnp.einsum("pj,pjr->pr", matches, scores, precision=TOP_PRECISION)
    block_max = jnp.max(scores, axis=(1, 2))
    running_sum = running_sum * jnp.exp(running_max - block_max) + jnp.sum(
        jnp.exp(scores - block_max[:, None, None]), axis=(1, 2)
    )
    carried = (block_max, running_sum, own_scores)
    running_max, running_sum, own_scores = carried
    joined_max, joined_sum = combined_all((running_max, running_sum), "narrow", combine)
    log_evidence = joined_max + jnp.log(joined_sum)
    weight = jax.nn.softmax(own_scores, axis=-1)
    h_real = jnp.dot(weight, cosine_table, precision=TOP_PRECISION)
    h_imag = jnp.dot(weight, sine_table, precision=TOP_PRECISION)
    spectra_wide = spectra.astype(jnp.float32)
    x_real = spectra_wide[..., :CYCLES]
    x_imag = spectra_wide[..., CYCLES:]
    a_real = x_real * h_real[:, :, None] - x_imag * h_imag[:, :, None]
    a_imag = x_real * h_imag[:, :, None] + x_imag * h_real[:, :, None]
    aligned = jnp.concatenate([a_real, a_imag], axis=-1).astype(jnp.bfloat16)
    group_ids = leading_class + jnp.arange(CLS_GRP, dtype=jnp.int32)
    members = class_index[None, :] == group_ids[:, None]
    numer_part = jnp.dot(
        members.astype(jnp.bfloat16),
        aligned.reshape(particles, feature_len),
        preferred_element_type=jnp.float32,
    )
    denom_part = jnp.dot(members.astype(jnp.float32), contrast_sq, precision=TOP_PRECISION)
    owners = lax.dynamic_slice_in_dim(owner_map, leading_class, CLS_GRP)
    matches = (owners[None, :] == jnp.arange(wide_count, dtype=jnp.int32)[:, None]).astype(
        jnp.int32
    )
    ranking = jnp.cumsum(matches, axis=1) - 1
    slot_range = jnp.arange(OWN_MAX, dtype=jnp.int32)
    slot_pick = (
        (matches[:, None, :] == 1) & (ranking[:, None, :] == slot_range[None, :, None])
    ).astype(jnp.float32)
    numer_share, denom_share = (
        sent_and_summed(numer_part, WIDE, 1),
        sent_and_summed(denom_part, WIDE, 1),
    )
    send_numer = jnp.einsum("wsc,cf->wsf", slot_pick, numer_share, precision=TOP_PRECISION)
    send_denom = jnp.einsum("wsc,ck->wsk", slot_pick, denom_share, precision=TOP_PRECISION)
    numer_got, denom_got = (
        exchange_by_chip(send_numer, (("wide_0", "wide_1"), "wide_2"), (1, 0), 0, 2),
        exchange_by_chip(send_denom, (("wide_0", "wide_1"), "wide_2"), (1, 0), 0, 2),
    )
    numerator = numer_got[0]
    denominator = denom_got[0]
    doubled_den = jnp.concatenate([denominator, denominator], axis=-1)
    harmonic = numerator.reshape(OWN_MAX, ANGLES, 2 * CYCLES) / (doubled_den[:, None, :] + TAU)
    polar = polar_image(harmonic, cosine_table, sine_table)
    new_references = polar.astype(jnp.bfloat16).reshape(1, 1, OWN_MAX, ANGLES, 2 * CYCLES)
    return (new_references, log_evidence)


def solution(mesh):
    split = Mesh(
        mesh.devices.reshape(4, 8, 2, mesh.shape["narrow"]),
        ("wide_0", "wide_1", "wide_2", "narrow"),
    )
    placed = (
        P(WIDE, None, None),
        P(WIDE),
        P(WIDE),
        P(WIDE),
        P(),
        P(),
        P(WIDE, "narrow", None, None, None),
    )
    return jax.shard_map(
        per_device,
        mesh=split,
        in_specs=placed,
        out_specs=(P(WIDE, "narrow", None, None, None), P(WIDE)),
        check_vma=False,
    )
```

profile of v0, /device:TPU:1, one launch (start us, length us, event | category | flops | bytes accessed | tf_op | source)
XLA Modules:
  0.0 313.4 jit_solution(1256460655724264599)
XLA Ops:
  7.2 0.7 all-gather.5.cloned.1.call-update
  7.9 0.7 multiply_multiply_fusion
  8.6 1.8 fusion.46
  10.4 17.6 %all-to-all-start.3 = ((f32[64,24,2]{1,2,0:T(2,128)}), f32[64,24,2]{1,2,0:T(2,128)S(1)}, u32[]{:S(2)}, u32[]{:S(2)}) async-start(f32[64,24,2]{1,2,0:T(2,128)} %bitcast.32), calls=%async_computation.3 | async-start | bytes 131072 | tf_op jit(solution)/shard_map/all_to_all | solution.py:62
  28.1 0.8 dynamic_slice.37
  28.9 0.4 reduce_window_sum.11
  29.4 0.3 fusion.44
  29.7 0.8 fusion.58
  30.6 1.0 compare_convert_fusion
  31.5 4.2 %fusion.11 = f32[128,72,256]{2,1,0:T(8,128)S(1)} fusion(bf16[128,72,256]{2,1,0:T(8,128)(2,1)} %param.9, f32[128,256]{1,0:T(8,128)S(1)} %pad_maximum_fusion.8), kind=kOutput, calls=%fused_computation.22 | convolution fusion | flops 346868352 | bytes 14286848 | tf_op jit(solution)/shard_map/ma,naj->nmj/dot_general | solution.py:101
  35.7 1.6 fusion.10
  37.3 1.3 fusion.3
  38.6 5.9 %pad_maximum_fusion = (bf16[128,72,256]{2,1,0:T(8,128)(2,1)}, f32[128,72,256]{2,1,0:T(8,128)}) fusion(bf16[128,72,128]{2,1,0:T(8,128)(2,1)S(1)} %get-tuple-element.157, bf16[128,72,128]{2,1,0:T(8,128)(2,1)S(1)} %get-tuple-element.156), kind=kLoop, calls=%fused_computation.11 | loop fusion | flops 11796480 | bytes 18874368 | tf_op jit(solution)/shard_map/concatenate | solution.py:104
  44.5 0.6 fusion.170
  51.6 3.7 %all_to_all.30 = f32[2,1,256]{2,1,0:T(1,128)S(1)} all-to-all(f32[2,1,256]{2,1,0:T(1,128)S(1)} %reshape.245), channel_id=1, replica_groups=mesh['wide_0'=4,'wide_1'=8,'wide_2'=2,'narrow'=8] {'wide_2'}, dimensions={0} | all-to-all | bytes 4096 | tf_op jit(solution)/shard_map/all_to_all | solution.py:76
  55.3 0.5 broadcast.138
  55.8 0.7 reduce.2
  56.5 0.7 copy.102
  57.3 12.0 %all-to-all-start.5 = ((f32[32,2,1,4,2]{3,4,2,1,0:T(2,128)}), f32[32,2,1,4,2]{3,4,2,1,0:T(2,128)S(1)}, u32[]{:S(2)}, u32[]{:S(2)}) async-start(f32[32,2,1,4,2]{3,4,2,1,0:T(2,128)} %copy.102), calls=%async_computation.5 | async-start | bytes 131072 | tf_op jit(solution)/shard_map/all_to_all | solution.py:76
  69.3 98.5 %all-gather.5.cloned.1.call-done = bf16[64,1,8,72,256]{4,3,2,1,0:T(8,128)(2,1)} async-done(((bf16[1,1,8,72,256]{4,3,2,1,0:T(8,128)(2,1)}), bf16[64,1,8,72,256]{4,3,2,1,0:T(8,128)(2,1)}) %all-gather.5.cloned.1.call-update) | async-done | bytes 18874384 | tf_op jit(solution)/shard_map/all_gather | solution.py:24
  167.8 1.2 dynamic-slice_bitcast_fusion.2
  169.1 0.6 convolution_bitcast_fusion.1
  169.6 0.6 convolution_bitcast_fusion.2
  170.7 0.5 convolution_multiply_fusion
  171.6 1.3 fusion.12
  172.9 1.4 fusion.15
  174.3 1.1 fusion.31
  175.4 1.3 fusion.171
  177.0 0.4 fusion.78
  177.4 0.4 fusion.72
  177.8 6.5 %subtract_convert_fusion = (bf16[128,72,128]{2,1,0:T(8,128)(2,1)S(1)}, bf16[128,72,128]{2,1,0:T(8,128)(2,1)S(1)}) fusion(f32[128,72,256]{2,1,0:T(8,128)} %get-tuple-element.161, f32[128,72]{1,0:T(8,128)S(1)} %fusion.78, f32[128,72]{1,0:T(8,128)S(1)} %fusion.72), kind=kLoop, calls=%fused_computation.14 | loop fusion | flops 9437184 | bytes 14229504 | tf_op jit(solution)/shard_map/convert.6
  184.3 2.7 pad_maximum_fusion.1
  187.0 7.1 %copy.125 = bf16[128,72,256]{0,2,1:T(8,128)(2,1)} copy(bf16[128,72,256]{2,1,0:T(8,128)(2,1)} %pad_maximum_fusion.1) | data formatting | bytes 9437184 | tf_op jit(solution)/shard_map/convert_element_type | solution.py:198
  194.1 5.7 %convolution_bitcast_fusion = f32[64,24,288]{2,1,0:T(8,128)} fusion(bf16[64,288,128]{2,1,0:T(8,128)(2,1)} %bitcast.133, s32[128]{0:T(128)S(1)} %copy-done.2, s32[24]{0:T(128)S(1)} %iota_add_fusion), kind=kOutput, calls=%fused_computation.24 | convolution fusion | flops 113249280 | bytes 6488672 | tf_op jit(solution)/shard_map/dot_general | solution.py:201
  199.8 7.8 %all-to-all-start = ((f32[64,24,288]{2,1,0:T(8,128)}), f32[64,24,288]{2,1,0:T(8,128)S(1)}, u32[]{:S(2)}, u32[]{:S(2)}) async-start(f32[64,24,288]{2,1,0:T(8,128)} %convolution_bitcast_fusion), calls=%async_computation | async-start | bytes 4718592 | tf_op jit(solution)/shard_map/all_to_all | solution.py:62
  207.8 60.8 %all-gather.2 = f32[8,2,128]{2,1,0:T(2,128)S(1)} all-gather(f32[1,2,128]{2,1,0:T(2,128)S(1)} %maximum_bitcast_fusion), channel_id=3, replica_groups=mesh['wide_0'=4,'wide_1'=8,'wide_2'=2,'narrow'=8] {'narrow'}, dimensions={0}, use_global_device_ids=true | all-gather | bytes 9216 | tf_op jit(solution)/shard_map/all_gather | solution.py:35
  268.9 0.4 convolution_bitcast_fusion.3
  269.3 6.9 %all_to_all.31 = f32[32,2,1,4,288]{4,0,3,2,1:T(8,128)S(1)} all-to-all(f32[32,2,1,4,288]{4,0,3,2,1:T(8,128)S(1)} %convolution_bitcast_fusion.3), channel_id=1, replica_groups=mesh['wide_0'=4,'wide_1'=8,'wide_2'=2,'narrow'=8] {'wide_2'}, dimensions={1} | all-to-all | bytes 589824 | tf_op jit(solution)/shard_map/all_to_all | solution.py:76
  276.1 1.0 copy.98
  277.1 12.0 %all-to-all-start.2 = ((f32[32,2,1,4,288]{4,3,1,2,0:T(4,128)}), f32[32,2,1,4,288]{4,3,1,2,0:T(4,128)S(1)}, u32[]{:S(2)}, u32[]{:S(2)}) async-start(f32[32,2,1,4,288]{4,3,1,2,0:T(4,128)} %copy.98), calls=%async_computation.2 | async-start | bytes 786432 | tf_op jit(solution)/shard_map/all_to_all | solution.py:76
  289.5 0.5 log_add_fusion
  290.0 13.7 %all-to-all-done.2 = f32[32,2,1,4,288]{4,3,1,2,0:T(4,128)S(1)} async-done(((f32[32,2,1,4,288]{4,3,1,2,0:T(4,128)}), f32[32,2,1,4,288]{4,3,1,2,0:T(4,128)S(1)}, u32[]{:S(2)}, u32[]{:S(2)}) %all-to-all-start.2) | async-done | bytes 294944 | tf_op jit(solution)/shard_map/all_to_all | solution.py:76
  303.7 0.3 reshape_squeeze_reshape.3
  304.1 0.4 fusion.34
  304.5 0.4 fusion.38
  305.0 0.4 fusion.26
  305.4 0.4 fusion.25
  305.9 0.7 pad_maximum_fusion.7
  (59 shorter events, 2.9 us)
Async XLA Ops:
  7.2 22.1 %copy-start = (s32[8,3]{0,1:T(4,128)S(1)}, s32[8,3]{0,1:T(4,128)}, u32[]{:S(2)}) copy-start(s32[8,3]{0,1:T(4,128)} %param.14) | copy-start | bytes 292
  7.2 160.7 %all-gather.5.cloned.1.call-start = ((), (), s32[]{:S(2)}) async-start(), calls=%async_computation.6 | async-start | bytes 19169280 | tf_op jit(solution)/shard_map/all_gather | solution.py:24
  10.4 40.8 %all-to-all-start.3 = ((f32[64,24,2]{1,2,0:T(2,128)}), f32[64,24,2]{1,2,0:T(2,128)S(1)}, u32[]{:S(2)}, u32[]{:S(2)}) async-start(f32[64,24,2]{1,2,0:T(2,128)} %bitcast.32), calls=%async_computation.3 | async-start | bytes 131072 | tf_op jit(solution)/shard_map/all_to_all | solution.py:62
  29.7 6.0 %slice-start.2 = ((s8[4718592]{0:T(1024)(128)(4,1)}), s8[4194304]{0:T(1024)(128)(4,1)S(1)}, s32[]{:S(2)}) async-start(s8[4718592]{0:T(1024)(128)(4,1)} %bitcast.131), calls=%async_computation.9 | async-start | bytes 8388608
  31.5 4.2 %slice-start.3 = ((s8[4718592]{0:T(1024)(128)(4,1)}), s8[524288]{0:T(1024)(128)(4,1)S(1)}, s32[]{:S(2)}) async-start(s8[4718592]{0:T(1024)(128)(4,1)} %bitcast.131), calls=%async_computation.10 | async-start | bytes 1048576
  57.3 142.5 %all-to-all-start.5 = ((f32[32,2,1,4,2]{3,4,2,1,0:T(2,128)}), f32[32,2,1,4,2]{3,4,2,1,0:T(2,128)S(1)}, u32[]{:S(2)}, u32[]{:S(2)}) async-start(f32[32,2,1,4,2]{3,4,2,1,0:T(2,128)} %copy.102), calls=%async_computation.5 | async-start | bytes 131072 | tf_op jit(solution)/shard_map/all_to_all | solution.py:76
  169.0 2.3 slice-start
  170.2 1.4 slice-start.1
  187.0 7.1 %copy-start.2 = (s32[128]{0:T(128)S(1)}, s32[128]{0:T(128)}, u32[]{:S(2)}) copy-start(s32[128]{0:T(128)} %param.11) | copy-start | bytes 1540
  199.8 68.9 %all-to-all-start = ((f32[64,24,288]{2,1,0:T(8,128)}), f32[64,24,288]{2,1,0:T(8,128)S(1)}, u32[]{:S(2)}, u32[]{:S(2)}) async-start(f32[64,24,288]{2,1,0:T(8,128)} %convolution_bitcast_fusion), calls=%async_computation | async-start | bytes 4718592 | tf_op jit(solution)/shard_map/all_to_all | solution.py:62
  207.6 98.9 %copy-start.1 = (s32[8,3]{0,1:T(4,128)S(1)}, s32[8,3]{0,1:T(4,128)}, u32[]{:S(2)}) copy-start(s32[8,3]{0,1:T(4,128)} %param.14) | copy-start | bytes 292
  277.1 26.6 %all-to-all-start.2 = ((f32[32,2,1,4,288]{4,3,1,2,0:T(4,128)}), f32[32,2,1,4,288]{4,3,1,2,0:T(4,128)S(1)}, u32[]{:S(2)}, u32[]{:S(2)}) async-start(f32[32,2,1,4,288]{4,3,1,2,0:T(4,128)} %copy.98), calls=%async_computation.2 | async-start | bytes 786432 | tf_op jit(solution)/shard_map/all_to_all | solution.py:76
Sparse Core Ops, SparseCore 0:
  11.3 156.4 all-gather.4
where the time goes:
time: 316 us; the launch traced here: 313 us
  waiting for transfers between devices  113 us (36%)
  blocking collectives  71.4 us (23%)
  starting transfers between devices  49.6 us (16%)
  other arithmetic  23 us (7%)
  matrix products  23 us (7%)
  between operations  20.3 us (6%)
  local copies, waits for them, and re-layouts  13 us (4%)
    all_gather x1, waiting for transfers between devices, from_root(): lax.all_gather(x, axis)  98.5 us
    all_gather x1, blocking collectives, gathered_once(): both, at, found = (lax.all_gather(jnp.concatenate(lines), axis), 0, {})  60.8 us
    all_to_all x2, starting transfers between devices, sent_and_summed(): lax.all_to_all(tiles, axis, split_axis=0, concat_axis=0, tiled=True)  25.5 us
    all_to_all x2, starting transfers between devices, exchange_in_order(): result = lax.all_to_all(result, axes[k], k, k, tiled=True)  24.1 us
    all_to_all x2, waiting for transfers between devices, exchange_in_order(): result = lax.all_to_all(result, axes[k], k, k, tiled=True)  13.7 us
    all_to_all x2, blocking collectives, exchange_in_order(): result = lax.all_to_all(result, axes[k], k, k, tiled=True)  10.6 us
    another operation x2, other arithmetic  7.79 us
    convert_element_type x1, local copies, waits for them, and re-layouts, per_device(): aligned = jnp.concatenate([a_real, a_imag], axis=-1).astype(jnp.bfloat16)  7.07 us
  transfers between devices with their start and end apart: 5, of which 2 were waited for; matrix products, arithmetic and copies ran while one was open for 17% of the time, Pallas kernels for 0%

commit v1 on v0

v1 whole, which is shorter than its diff:
```python
import math

import jax
import jax.numpy as jnp
from jax import lax
from jax.sharding import Mesh
from jax.sharding import PartitionSpec as P

CYCLES = 128
ANGLES = 72
STEPS = 3
BLOCK = 8
OWN_MAX = 4
CLS_GRP = 24
SIGMA_ROT = 8
ROWS = 9
WIDE = ("wide_0", "wide_1", "wide_2")


TAU = 1.0
CONTRAST = 0.1
TOP_PRECISION = lax.Precision.HIGHEST


def spread(x, axis):
    copies = jnp.broadcast_to(x[None], (lax.axis_size(axis), *x.shape))
    return lax.all_to_all(copies, axis, 0, 0, tiled=True)


def swapped(x):
    return lax.ppermute(x, "wide_2", [(0, 1), (1, 0)])


def angle_tables(length):
    counting = jnp.arange(length, dtype=jnp.int32)
    products = counting[:, None] * counting[None, :] % length
    phase_angle = products.astype(jnp.float32) * (2.0 * math.pi / length)
    return (jnp.cos(phase_angle), jnp.sin(phase_angle))


def contrast(defocus_rows):
    cycle_freq = (jnp.arange(CYCLES, dtype=jnp.float32) + 1.0) / CYCLES
    phase_angle = 8.0 * math.pi * defocus_rows[:, None] * cycle_freq[None, :] ** 2
    return -jnp.sin(phase_angle) - CONTRAST * jnp.cos(phase_angle)


def spectrum(polar, cosines_low, sines_low):
    cos_part = jnp.einsum("ma,naj->nmj", cosines_low, polar, preferred_element_type=jnp.float32)
    sin_part = jnp.einsum("ma,naj->nmj", sines_low, polar, preferred_element_type=jnp.float32)
    real_part = cos_part[..., :CYCLES] + sin_part[..., CYCLES:]
    imag_part = cos_part[..., CYCLES:] - sin_part[..., :CYCLES]
    return jnp.concatenate([real_part, imag_part], axis=-1).astype(jnp.bfloat16)


def rotation_prior(rotation_rows):
    counting = jnp.arange(ANGLES, dtype=jnp.int32)
    distance = jnp.abs(counting[None, :] - rotation_rows[:, None])
    distance = jnp.minimum(distance, ANGLES - distance).astype(jnp.float32)
    return -0.5 * (distance / SIGMA_ROT) ** 2


def fetch(blocks, holders):
    halves = blocks.reshape(BLOCK, ANGLES, 2, CYCLES).transpose(0, 2, 1, 3)
    halves = halves.reshape(BLOCK * 2, ANGLES, CYCLES)
    sliced = lax.all_to_all(halves, ("wide_1", "wide_2"), 0, 0, tiled=True)
    inner, outer = holders % 16, holders // 16
    picked = jnp.stack(
        [lax.dynamic_index_in_dim(sliced, inner[s], 0, keepdims=False) for s in range(STEPS)]
    )
    planes = spread(picked, "wide_0")
    picked = jnp.stack(
        [lax.dynamic_index_in_dim(planes[:, s], outer[s], 0, keepdims=False) for s in range(STEPS)]
    )
    mine = spread(picked, "wide_1").reshape(CLS_GRP, ANGLES, CYCLES)
    other = swapped(mine)
    first = lax.axis_index("wide_2") == 0
    return jnp.concatenate(
        [jnp.where(first, mine, other), jnp.where(first, other, mine)], axis=-1
    )


def per_device(images, defocus, class_index, rotation_index, owner_map, roster, ref_store):
    class_group = lax.axis_index("narrow")
    z_index = lax.axis_index("wide_1")
    core = lax.axis_index("wide_2")
    wide_count = lax.axis_size(WIDE)
    cosine_table, sine_table = angle_tables(ANGLES)
    cosines_low = cosine_table.astype(jnp.bfloat16)
    sines_low = sine_table.astype(jnp.bfloat16)
    leading_class = class_group * CLS_GRP
    arrival = jnp.arange(CLS_GRP, dtype=jnp.int32)
    within = arrival % STEPS * BLOCK + arrival // STEPS
    class_ids = leading_class + within
    holders = lax.dynamic_index_in_dim(roster, class_group, 0, keepdims=False)

    contrast_rows = contrast(defocus)
    contrast_sq = contrast_rows * contrast_rows
    doubled = jnp.concatenate([contrast_rows, contrast_rows], axis=-1)
    weighted = (images.astype(jnp.float32) * doubled[:, None, :]).astype(jnp.bfloat16)
    spectra = spectrum(weighted, cosines_low, sines_low)
    turned = spectra.transpose(1, 0, 2)
    prior_rows = rotation_prior(rotation_index)

    refs = fetch(ref_store[0, 0], holders)
    ref_spec = spectrum(refs, cosines_low, sines_low)
    ref_swap = jnp.concatenate([-ref_spec[..., CYCLES:], ref_spec[..., :CYCLES]], axis=-1)
    real_correlation = jnp.einsum(
        "mpj,cmj->pcm", turned, ref_spec, preferred_element_type=jnp.float32
    )
    imaginary_correlation = jnp.einsum(
        "mpj,cmj->pcm", turned, ref_swap, preferred_element_type=jnp.float32
    )
    turned_images = jnp.einsum(
        "exj,ji->exi", real_correlation, cosine_table, precision=TOP_PRECISION
    ) - jnp.einsum("exj,ji->exi", imaginary_correlation, sine_table, precision=TOP_PRECISION)
    power = jnp.sum(jnp.square(ref_spec.astype(jnp.float32)), axis=1)
    power = power[:, :CYCLES] + power[:, CYCLES:]
    energy = jnp.dot(contrast_sq, power.T, precision=TOP_PRECISION)
    scores = (turned_images - 0.5 * energy[:, :, None]) / ANGLES + prior_rows[:, None, :]
    members = class_index[:, None] == class_ids[None, :]
    own_scores = jnp.einsum(
        "pj,pjr->pr", members.astype(jnp.float32), scores, precision=TOP_PRECISION
    )
    block_max = jnp.max(scores, axis=(1, 2))
    block_sum = jnp.sum(jnp.exp(scores - block_max[:, None, None]), axis=(1, 2))

    weight = jax.nn.softmax(own_scores, axis=-1)
    h_real = jnp.einsum("pr,rm->mp", weight, cosine_table, precision=TOP_PRECISION)
    h_imag = jnp.einsum("pr,rm->mp", weight, sine_table, precision=TOP_PRECISION)
    x_real = turned[..., :CYCLES].astype(jnp.float32)
    x_imag = turned[..., CYCLES:].astype(jnp.float32)
    a_real = x_real * h_real[:, :, None] - x_imag * h_imag[:, :, None]
    a_imag = x_real * h_imag[:, :, None] + x_imag * h_real[:, :, None]
    chosen = members.astype(jnp.bfloat16)
    numer_real = jnp.einsum(
        "pc,mpk->mck", chosen, a_real.astype(jnp.bfloat16), preferred_element_type=jnp.float32
    )
    numer_imag = jnp.einsum(
        "pc,mpk->mck", chosen, a_imag.astype(jnp.bfloat16), preferred_element_type=jnp.float32
    )
    denom = jnp.einsum(
        "pc,pk->ck", members.astype(jnp.float32), contrast_sq, precision=TOP_PRECISION
    )

    denom = denom + swapped(denom)
    numer = jnp.where(core == 0, numer_real, numer_imag) + swapped(
        jnp.where(core == 0, numer_imag, numer_real)
    )
    high = denom.astype(jnp.bfloat16)
    low = (denom - high.astype(jnp.float32)).astype(jnp.bfloat16)
    extra = jnp.concatenate([high[None], low[None], jnp.zeros((6, CLS_GRP, CYCLES), jnp.bfloat16)])
    share = jnp.concatenate(
        [numer.astype(jnp.bfloat16).reshape(8, ROWS, CLS_GRP, CYCLES), extra[:, None]], axis=1
    )
    share = share.reshape(8, (ROWS + 1) * CLS_GRP, CYCLES)
    share = lax.all_to_all(share, "wide_1", 0, 0, tiled=True)
    share = share.astype(jnp.float32).sum(axis=0).reshape(ROWS + 1, CLS_GRP, CYCLES)
    owners = lax.dynamic_slice_in_dim(owner_map, leading_class, CLS_GRP)
    owners = owners.reshape(STEPS, BLOCK).T.reshape(CLS_GRP)
    same = owners[:, None] == owners[None, :]
    ranking = jnp.sum(same & (within[None, :] < within[:, None]), axis=1)
    place = owners * OWN_MAX + ranking
    pick = place[None, :] == jnp.arange(wide_count * OWN_MAX, dtype=jnp.int32)[:, None]
    numer_share = share[:ROWS].astype(jnp.bfloat16)
    denom_high = share[ROWS:].astype(jnp.bfloat16)
    denom_low = (share[ROWS:] - denom_high.astype(jnp.float32)).astype(jnp.bfloat16)
    share = jnp.concatenate([numer_share, jnp.where(core == 0, denom_high, denom_low)])
    sent = jnp.einsum(
        "wsc,tck->wtsk",
        pick.reshape(wide_count, OWN_MAX, CLS_GRP).astype(jnp.bfloat16),
        share,
        preferred_element_type=jnp.float32,
    ).astype(jnp.bfloat16)
    sent = sent.reshape(wide_count, (ROWS + 1) * OWN_MAX, CYCLES)
    got = lax.all_to_all(sent, WIDE, 0, 0, tiled=True)
    got = got.reshape(4, 8, 2, ROWS + 1, OWN_MAX, CYCLES).astype(jnp.float32).sum(axis=0)
    denominator = got[0, 0, ROWS] + got[0, 1, ROWS] + got[1, 0, ROWS]
    scale = 1.0 / (denominator + TAU) / ANGLES
    real_part = got[:, 0, :ROWS].reshape(ANGLES, OWN_MAX, CYCLES) * scale
    imag_part = got[:, 1, :ROWS].reshape(ANGLES, OWN_MAX, CYCLES) * scale
    mixed = lambda x, table: jnp.einsum("mck,ma->cak", x, table, precision=TOP_PRECISION)
    polar = jnp.concatenate(
        [
            mixed(real_part, cosine_table) - mixed(imag_part, sine_table),
            mixed(imag_part, cosine_table) + mixed(real_part, sine_table),
        ],
        axis=-1,
    )
    new_references = polar.astype(jnp.bfloat16).reshape(1, 1, OWN_MAX, ANGLES, 2 * CYCLES)

    pairs = spread(jnp.stack([block_max, block_sum]), "narrow")
    joined = jnp.max(pairs[:, 0], axis=0)
    log_evidence = joined + jnp.log(jnp.sum(pairs[:, 1] * jnp.exp(pairs[:, 0] - joined), axis=0))
    return (new_references, log_evidence)


def solution(mesh):
    split = Mesh(
        mesh.devices.reshape(4, 8, 2, mesh.shape["narrow"]),
        ("wide_0", "wide_1", "wide_2", "narrow"),
    )
    placed = (
        P(WIDE, None, None),
        P(WIDE),
        P(WIDE),
        P(WIDE),
        P(),
        P(),
        P(WIDE, "narrow", None, None, None),
    )
    return jax.shard_map(
        per_device,
        mesh=split,
        in_specs=placed,
        out_specs=(P(WIDE, "narrow", None, None, None), P(WIDE)),
        check_vma=False,
    )
```

time: 316 us -> 167 us (0.53)
  blocking collectives: 71.4 us -> 0 us
  waiting for transfers between devices: 113 us -> 49.6 us
  between operations: 20.3 us -> 12.1 us
  local copies, waits for them, and re-layouts: 13 us -> 6.57 us
  matrix products: 23 us -> 26.2 us
    all_gather x1 -> x0, waiting for transfers between devices: 98.5 us -> none  [from_root(): lax.all_gather(x, axis)]
    all_gather x1 -> x0, blocking collectives: 60.8 us -> none  [gathered_once(): both, at, found = (lax.all_gather(jnp.concatenate(lines), axis), 0, {})]
    all_to_all x4 -> x6, waiting for transfers between devices: 13.7 us -> 48.8 us  [the longest x1 21.3 us: per_device(): got = lax.all_to_all(sent, WIDE, 0, 0, tiled=True)]
    all_to_all x2 -> x0, blocking collectives: 10.6 us -> none  [exchange_in_order(): result = lax.all_to_all(result, axes[k], k, k, tiled=True)]
    concatenate x3 -> x2, other arithmetic: 9.3 us -> 1.5 us  [the longest x1 0.82 us: per_device(): jnp.concatenate([numer.astype(jnp.bfloat16).reshape(8, ROWS, CLS_GRP, CYC...]
    all_to_all x4 -> x6, starting transfers between devices: 49.6 us -> 42.2 us  [the longest x3 17.5 us: spread(): return lax.all_to_all(copies, axis, 0, 0, tiled=True)]
    convert_element_type x1 -> x0, local copies, waits for them, and re-layouts: 7.07 us -> none  [per_device(): aligned = jnp.concatenate([a_real, a_imag], axis=-1).astype(jnp.bfloat16)]
    ppermute x0 -> x3, starting transfers between devices: none -> 7 us  [swapped(): return lax.ppermute(x, 'wide_2', [(0, 1), (1, 0)])]
  transfers between devices with their start and end apart: 5 -> 9, of which waited for: 2 -> 5; matrix products, arithmetic and copies ran while one was open for 17% -> 19% of each run, Pallas kernels for 0% -> 0%
where the time goes in v1:
time: 167 us; the launch traced here: 166 us
  waiting for transfers between devices  49.6 us (30%)
  starting transfers between devices  49.2 us (29%)
  matrix products  26.2 us (16%)
  other arithmetic  22.4 us (13%)
  between operations  12.1 us (7%)
  local copies, waits for them, and re-layouts  6.57 us (4%)
    all_to_all x1, waiting for transfers between devices, per_device(): got = lax.all_to_all(sent, WIDE, 0, 0, tiled=True)  21.3 us
    all_to_all x3, starting transfers between devices, spread(): return lax.all_to_all(copies, axis, 0, 0, tiled=True)  17.5 us
    all_to_all x1, waiting for transfers between devices, per_device(): share = lax.all_to_all(share, 'wide_1', 0, 0, tiled=True)  16.7 us
    all_to_all x1, starting transfers between devices, fetch(): sliced = lax.all_to_all(halves, ('wide_1', 'wide_2'), 0, 0, tiled=True)  11.8 us
    all_to_all x3, waiting for transfers between devices, spread(): return lax.all_to_all(copies, axis, 0, 0, tiled=True)  10.9 us
    all_to_all x1, starting transfers between devices, per_device(): got = lax.all_to_all(sent, WIDE, 0, 0, tiled=True)  9.37 us
    another operation x1, other arithmetic  8.4 us
    dot_general x2, matrix products, spectrum(): jnp.einsum('ma,naj->nmj', cosines_low, polar, preferred_element_type=jnp....  8.14 us
  transfers between devices with their start and end apart: 9, of which 5 were waited for; matrix products, arithmetic and copies ran while one was open for 19% of the time, Pallas kernels for 0%

profile of v1, /device:TPU:1, one launch (start us, length us, event | category | flops | bytes accessed | tf_op | source)
XLA Modules:
  0.0 166.1 jit_solution(6668365160231316690)
XLA Ops:
  0.6 1.0 reshape_squeeze.9
  1.7 0.8 copy.107
  2.4 11.8 %all-to-all-start = ((bf16[16,72,128]{2,1,0:T(8,128)(2,1)}), bf16[16,72,128]{2,1,0:T(8,128)(2,1)S(1)}, u32[]{:S(2)}, u32[]{:S(2)}) async-start(bf16[16,72,128]{2,1,0:T(8,128)(2,1)} %bitcast.7), calls=%async_computation | async-start | bytes 589824 | tf_op jit(solution)/shard_map/all_to_all | solution.py:65
  14.5 0.6 fusion.183
  18.7 0.7 multiply_multiply_fusion
  19.4 0.3 fusion.46
  21.5 7.5 %fusion.13 = f32[128,72,256]{2,1,0:T(8,128)} fusion(bf16[128,72,256]{2,1,0:T(8,128)(2,1)} %param.7, f32[128,256]{1,0:T(8,128)S(1)} %pad_maximum_fusion.7), kind=kOutput, calls=%fused_computation.21 | convolution fusion | flops 346868352 | bytes 14286848 | tf_op jit(solution)/shard_map/ma,naj->nmj/dot_general | solution.py:49
  29.1 0.7 broadcast_in_dim.14
  29.8 6.8 %all-to-all-start.1 = ((bf16[4,3,72,128]{3,2,1,0:T(8,128)(2,1)}), bf16[4,3,72,128]{3,2,1,0:T(8,128)(2,1)S(1)}, u32[]{:S(2)}, u32[]{:S(2)}) async-start(bf16[4,3,72,128]{3,2,1,0:T(8,128)(2,1)} %broadcast_in_dim.14), calls=%async_computation.1 | async-start | bytes 442368 | tf_op jit(solution)/shard_map/all_to_all | solution.py:27
  36.7 7.6 %fusion.12 = f32[128,72,256]{2,1,0:T(8,128)} fusion(bf16[128,72,256]{2,1,0:T(8,128)(2,1)} %param.7, f32[128,256]{1,0:T(8,128)S(1)} %pad_maximum_fusion.7), kind=kOutput, calls=%fused_computation.20 | convolution fusion | flops 346868352 | bytes 14286848 | tf_op jit(solution)/shard_map/ma,naj->nmj/dot_general | solution.py:48
  50.0 0.8 broadcast_in_dim.15
  50.8 6.5 %all-to-all-start.2 = ((bf16[8,3,72,128]{3,2,1,0:T(8,128)(2,1)}), bf16[8,3,72,128]{3,2,1,0:T(8,128)(2,1)S(1)}, u32[]{:S(2)}, u32[]{:S(2)}) async-start(bf16[8,3,72,128]{3,2,1,0:T(8,128)(2,1)} %broadcast_in_dim.15), calls=%async_computation.2 | async-start | bytes 884736 | tf_op jit(solution)/shard_map/all_to_all | solution.py:27
  57.4 8.4 %fusion.5 = (bf16[128,72,128]{2,1,0:T(8,128)(2,1)S(1)}, bf16[128,72,128]{2,1,0:T(8,128)(2,1)}) fusion(f32[128,72,256]{2,1,0:T(8,128)} %fusion.13, f32[128,72,256]{2,1,0:T(8,128)} %fusion.12), kind=kLoop, calls=%fused_computation.12 | loop fusion | flops 4718592 | bytes 23592960 | tf_op jit(solution)/shard_map/convert.10
  65.8 7.7 %all-to-all-done.2 = bf16[8,3,72,128]{3,2,1,0:T(8,128)(2,1)S(1)} async-done(((bf16[8,3,72,128]{3,2,1,0:T(8,128)(2,1)}), bf16[8,3,72,128]{3,2,1,0:T(8,128)(2,1)S(1)}, u32[]{:S(2)}, u32[]{:S(2)}) %all-to-all-start.2) | async-done | bytes 442400 | tf_op jit(solution)/shard_map/all_to_all | solution.py:27
  73.4 2.7 %collective-permute-start = (bf16[24,72,128]{2,1,0:T(8,128)(2,1)S(1)}, bf16[24,72,128]{2,1,0:T(8,128)(2,1)S(1)}, u32[]{:S(2)}, u32[]{:S(2)}) collective-permute-start(bf16[24,72,128]{2,1,0:T(8,128)(2,1)S(1)} %bitcast.123), channel_id=1, source_target_pairs={{0,8},{8,0},{1,9},{9,1},{2,10},{10,2},{3,11},{11,3},{4,12},{12,4},... | collective-permute-start | bytes 1327112 | tf_op jit(solution)/shard_map/ppermute | solution.py:31
  76.2 2.6 %maximum_bitcast_fusion = bf16[72,128,256]{2,0,1:T(8,128)(2,1)S(1)} fusion(bf16[128,72,128]{2,1,0:T(8,128)(2,1)} %get-tuple-element.7, bf16[128,72,128]{2,1,0:T(8,128)(2,1)S(1)} %get-tuple-element.6), kind=kLoop, calls=%fused_computation.13 | loop fusion | flops 9437184 | bytes 9437184 | tf_op jit(solution)/shard_map/transpose | solution.py:101
  78.9 0.6 convolution_bitcast_fusion
  79.5 0.6 convolution_bitcast_fusion.1
  80.5 0.5 convolution_multiply_fusion
  81.2 1.3 fusion.18
  82.5 1.1 fusion.36
  83.7 1.3 fusion.21
  85.0 1.3 fusion.185
  86.7 0.4 fusion.79
  87.0 0.4 fusion.73
  87.4 6.2 %fusion.1 = (bf16[72,128,128]{2,0,1:T(8,128)(2,1)S(1)}, bf16[72,128,128]{2,0,1:T(8,128)(2,1)S(1)}) fusion(f32[72,128]{0,1:T(8,128)S(1)} %fusion.79, f32[72,128]{0,1:T(8,128)S(1)} %fusion.73, bf16[72,128,256]{2,0,1:T(8,128)(2,1)} %copy-done.1), kind=kLoop, calls=%fused_computation.6 | loop fusion | flops 11796480 | bytes 9510912 | tf_op jit(solution)/shard_map/convert_element_type | solution.py:136
  93.7 0.5 fusion.14
  94.2 0.5 fusion.16
  94.7 1.9 %collective-permute-start.1 = (f32[72,24,128]{2,1,0:T(8,128)S(1)}, f32[72,24,128]{2,1,0:T(8,128)S(1)}, u32[]{:S(2)}, u32[]{:S(2)}) collective-permute-start(f32[72,24,128]{2,1,0:T(8,128)S(1)} %select_bitcast_fusion), channel_id=1, source_target_pairs={{0,8},{8,0},{1,9},{9,1},{2,10},{10,2},{3,11},{11,3},{4,12},{12,4},... | collective-permute-start | bytes 2654216 | tf_op jit(solution)/shard_map/ppermute | solution.py:31
  96.7 0.4 fusion.48
  97.1 2.4 %collective-permute-start.2 = (f32[24,128]{1,0:T(8,128)S(1)}, f32[24,128]{1,0:T(8,128)S(1)}, u32[]{:S(2)}, u32[]{:S(2)}) collective-permute-start(f32[24,128]{1,0:T(8,128)S(1)} %fusion.48), channel_id=1, source_target_pairs={{0,8},{8,0},{1,9},{9,1},{2,10},{10,2},{3,11},{11,3},{4,12},{12,4},... | collective-permute-start | bytes 36872 | tf_op jit(solution)/shard_map/ppermute | solution.py:31
  99.6 0.7 collective-permute-done.2
  100.6 0.8 pad_maximum_fusion.5
  101.4 3.5 %all-to-all-start.3 = ((bf16[8,240,128]{2,1,0:T(8,128)(2,1)}), bf16[8,240,128]{2,1,0:T(8,128)(2,1)S(1)}, u32[]{:S(2)}, u32[]{:S(2)}) async-start(bf16[8,240,128]{2,1,0:T(8,128)(2,1)} %bitcast.32), calls=%async_computation.3 | async-start | bytes 983040 | tf_op jit(solution)/shard_map/all_to_all | solution.py:156
  105.4 16.7 %all-to-all-done.3 = bf16[8,240,128]{2,1,0:T(8,128)(2,1)S(1)} async-done(((bf16[8,240,128]{2,1,0:T(8,128)(2,1)}), bf16[8,240,128]{2,1,0:T(8,128)(2,1)S(1)}, u32[]{:S(2)}, u32[]{:S(2)}) %all-to-all-start.3) | async-done | bytes 491552 | tf_op jit(solution)/shard_map/all_to_all | solution.py:156
  122.1 0.6 broadcast_in_dim.20
  122.7 4.1 %all-to-all-start.5 = ((f32[8,2,128]{2,1,0:T(2,128)}), f32[8,2,128]{2,1,0:T(2,128)S(1)}, u32[]{:S(2)}, u32[]{:S(2)}) async-start(f32[8,2,128]{2,1,0:T(2,128)} %broadcast_in_dim.20), calls=%async_computation.5 | async-start | bytes 16384 | tf_op jit(solution)/shard_map/all_to_all | solution.py:27
  126.9 0.4 convolution_convert_fusion
  127.4 1.3 copy.121
  128.7 3.2 %all-to-all-done.5 = f32[8,2,128]{2,1,0:T(2,128)S(1)} async-done(((f32[8,2,128]{2,1,0:T(2,128)}), f32[8,2,128]{2,1,0:T(2,128)S(1)}, u32[]{:S(2)}, u32[]{:S(2)}) %all-to-all-start.5) | async-done | bytes 8224 | tf_op jit(solution)/shard_map/all_to_all | solution.py:27
  131.9 9.4 %all-to-all-start.4 = ((bf16[64,40,128]{2,1,0:T(8,128)(2,1)}), bf16[64,40,128]{2,1,0:T(8,128)(2,1)S(1)}, u32[]{:S(2)}, u32[]{:S(2)}) async-start(bf16[64,40,128]{2,1,0:T(8,128)(2,1)} %copy.121), calls=%async_computation.4 | async-start | bytes 1310720 | tf_op jit(solution)/shard_map/all_to_all | solution.py:175
  141.3 0.5 log_add_fusion
  141.9 21.3 %all-to-all-done.4 = bf16[64,40,128]{2,1,0:T(8,128)(2,1)S(1)} async-done(((bf16[64,40,128]{2,1,0:T(8,128)(2,1)}), bf16[64,40,128]{2,1,0:T(8,128)(2,1)S(1)}, u32[]{:S(2)}, u32[]{:S(2)}) %all-to-all-start.4) | async-done | bytes 655392 | tf_op jit(solution)/shard_map/all_to_all | solution.py:175
  163.6 0.4 fusion.39
  164.0 0.4 fusion.43
  164.5 0.4 fusion.29
  164.9 0.4 fusion.30
  165.4 0.7 pad_maximum_fusion.6
  (60 shorter events, 3.0 us)
Async XLA Ops:
  0.6 13.6 %copy-start = (s32[8,3]{0,1:T(4,128)S(1)}, s32[8,3]{0,1:T(4,128)}, u32[]{:S(2)}) copy-start(s32[8,3]{0,1:T(4,128)} %param.12) | copy-start | bytes 292
  2.4 26.6 %all-to-all-start = ((bf16[16,72,128]{2,1,0:T(8,128)(2,1)}), bf16[16,72,128]{2,1,0:T(8,128)(2,1)S(1)}, u32[]{:S(2)}, u32[]{:S(2)}) async-start(bf16[16,72,128]{2,1,0:T(8,128)(2,1)} %bitcast.7), calls=%async_computation | async-start | bytes 589824 | tf_op jit(solution)/shard_map/all_to_all | solution.py:65
  29.8 20.0 %all-to-all-start.1 = ((bf16[4,3,72,128]{3,2,1,0:T(8,128)(2,1)}), bf16[4,3,72,128]{3,2,1,0:T(8,128)(2,1)S(1)}, u32[]{:S(2)}, u32[]{:S(2)}) async-start(bf16[4,3,72,128]{3,2,1,0:T(8,128)(2,1)} %broadcast_in_dim.14), calls=%async_computation.1 | async-start | bytes 442368 | tf_op jit(solution)/shard_map/all_to_all | solution.py:27
  36.7 20.7 %copy-start.3 = (s32[128]{0:T(128)S(1)}, s32[128]{0:T(128)}, u32[]{:S(2)}) copy-start(s32[128]{0:T(128)} %param.10) | copy-start | bytes 1540
  50.8 22.6 %all-to-all-start.2 = ((bf16[8,3,72,128]{3,2,1,0:T(8,128)(2,1)}), bf16[8,3,72,128]{3,2,1,0:T(8,128)(2,1)S(1)}, u32[]{:S(2)}, u32[]{:S(2)}) async-start(bf16[8,3,72,128]{3,2,1,0:T(8,128)(2,1)} %broadcast_in_dim.15), calls=%async_computation.2 | async-start | bytes 884736 | tf_op jit(solution)/shard_map/all_to_all | solution.py:27
  57.3 18.7 %copy-start.2 = (s32[128]{0:T(128)S(1)}, s32[128]{0:T(128)}, u32[]{:S(2)}) copy-start(s32[128]{0:T(128)} %param.9) | copy-start | bytes 1540
  73.4 5.4 %collective-permute-start = (bf16[24,72,128]{2,1,0:T(8,128)(2,1)S(1)}, bf16[24,72,128]{2,1,0:T(8,128)(2,1)S(1)}, u32[]{:S(2)}, u32[]{:S(2)}) collective-permute-start(bf16[24,72,128]{2,1,0:T(8,128)(2,1)S(1)} %bitcast.123), channel_id=1, source_target_pairs={{0,8},{8,0},{1,9},{9,1},{2,10},{10,2},{3,11},{11,3},{4,12},{12,4},... | collective-permute-start | bytes 1327112 | tf_op jit(solution)/shard_map/ppermute | solution.py:31
  78.8 4.9 %copy-start.1 = (bf16[72,128,256]{2,0,1:T(8,128)(2,1)}, bf16[72,128,256]{2,0,1:T(8,128)(2,1)S(1)}, u32[]{:S(2)}) copy-start(bf16[72,128,256]{2,0,1:T(8,128)(2,1)S(1)} %maximum_bitcast_fusion) | copy-start | bytes 14155780
  94.6 10.3 %copy-start.4 = (s32[192]{0:T(256)S(1)}, s32[192]{0:T(256)}, u32[]{:S(2)}) copy-start(s32[192]{0:T(256)} %param.11) | copy-start | bytes 2308
  94.7 5.7 %collective-permute-start.1 = (f32[72,24,128]{2,1,0:T(8,128)S(1)}, f32[72,24,128]{2,1,0:T(8,128)S(1)}, u32[]{:S(2)}, u32[]{:S(2)}) collective-permute-start(f32[72,24,128]{2,1,0:T(8,128)S(1)} %select_bitcast_fusion), channel_id=1, source_target_pairs={{0,8},{8,0},{1,9},{9,1},{2,10},{10,2},{3,11},{11,3},{4,12},{12,4},... | collective-permute-start | bytes 2654216 | tf_op jit(solution)/shard_map/ppermute | solution.py:31
  97.1 3.2 %collective-permute-start.2 = (f32[24,128]{1,0:T(8,128)S(1)}, f32[24,128]{1,0:T(8,128)S(1)}, u32[]{:S(2)}, u32[]{:S(2)}) collective-permute-start(f32[24,128]{1,0:T(8,128)S(1)} %fusion.48), channel_id=1, source_target_pairs={{0,8},{8,0},{1,9},{9,1},{2,10},{10,2},{3,11},{11,3},{4,12},{12,4},... | collective-permute-start | bytes 36872 | tf_op jit(solution)/shard_map/ppermute | solution.py:31
  101.4 20.7 %all-to-all-start.3 = ((bf16[8,240,128]{2,1,0:T(8,128)(2,1)}), bf16[8,240,128]{2,1,0:T(8,128)(2,1)S(1)}, u32[]{:S(2)}, u32[]{:S(2)}) async-start(bf16[8,240,128]{2,1,0:T(8,128)(2,1)} %bitcast.32), calls=%async_computation.3 | async-start | bytes 983040 | tf_op jit(solution)/shard_map/all_to_all | solution.py:156
  122.7 9.2 %all-to-all-start.5 = ((f32[8,2,128]{2,1,0:T(2,128)}), f32[8,2,128]{2,1,0:T(2,128)S(1)}, u32[]{:S(2)}, u32[]{:S(2)}) async-start(f32[8,2,128]{2,1,0:T(2,128)} %broadcast_in_dim.20), calls=%async_computation.5 | async-start | bytes 16384 | tf_op jit(solution)/shard_map/all_to_all | solution.py:27
  131.9 31.2 %all-to-all-start.4 = ((bf16[64,40,128]{2,1,0:T(8,128)(2,1)}), bf16[64,40,128]{2,1,0:T(8,128)(2,1)S(1)}, u32[]{:S(2)}, u32[]{:S(2)}) async-start(bf16[64,40,128]{2,1,0:T(8,128)(2,1)} %copy.121), calls=%async_computation.4 | async-start | bytes 1310720 | tf_op jit(solution)/shard_map/all_to_all | solution.py:175

commit v2 on v1

v2 whole, which is shorter than its diff:
```python
import math

import jax
import jax.numpy as jnp
from jax import lax
from jax.experimental import pallas as pl
from jax.experimental.pallas import tpu as pltpu
from jax.sharding import Mesh
from jax.sharding import PartitionSpec as P

CYCLES = 128
ANGLES = 72
STEPS = 3
BLOCK = 8
OWN_MAX = 4
CLS_GRP = 24
SIGMA_ROT = 8
ROWS = 9
WIDE = ("wide_0", "wide_1", "wide_2")


TAU = 1.0
CONTRAST = 0.1
TOP_PRECISION = lax.Precision.HIGHEST


def swapped(x):
    return lax.ppermute(x, "wide_2", [(0, 1), (1, 0)])


def angle_tables(length):
    counting = jnp.arange(length, dtype=jnp.int32)
    products = counting[:, None] * counting[None, :] % length
    phase_angle = products.astype(jnp.float32) * (2.0 * math.pi / length)
    return (jnp.cos(phase_angle), jnp.sin(phase_angle))


def contrast(defocus_rows):
    cycle_freq = (jnp.arange(CYCLES, dtype=jnp.float32) + 1.0) / CYCLES
    phase_angle = 8.0 * math.pi * defocus_rows[:, None] * cycle_freq[None, :] ** 2
    return -jnp.sin(phase_angle) - CONTRAST * jnp.cos(phase_angle)


def spectrum_of(polar, table):
    both = jnp.dot(table, polar, preferred_element_type=jnp.float32)
    cos_part, sin_part = both[:ANGLES], both[ANGLES:]
    real_part = cos_part[:, :CYCLES] + sin_part[:, CYCLES:]
    imag_part = cos_part[:, CYCLES:] - sin_part[:, :CYCLES]
    return real_part, imag_part


def spectra_kernel(table_ref, contrast_ref, image_ref, out_ref, held_real, held_imag):
    table = table_ref[...]
    count = image_ref.shape[0]
    for row in range(count):
        factor = contrast_ref[row : row + 1, :]
        factor = jnp.concatenate([factor, factor], axis=-1)
        weighted = (image_ref[row].astype(jnp.float32) * factor).astype(jnp.bfloat16)
        rows = pl.ds(row, ANGLES, stride=count)
        held_real[rows, :], held_imag[rows, :] = spectrum_of(weighted, table)
    shape = (ANGLES, count, CYCLES)
    out_ref[:, :, :CYCLES] = held_real[...].reshape(shape).astype(jnp.bfloat16)
    out_ref[:, :, CYCLES:] = held_imag[...].reshape(shape).astype(jnp.bfloat16)


def image_spectra(images, contrast_rows, table):
    particles = images.shape[0]
    count = 16
    return pl.pallas_call(
        spectra_kernel,
        grid=(particles // count,),
        in_specs=[
            pl.BlockSpec((2 * ANGLES, ANGLES), lambda i: (0, 0)),
            pl.BlockSpec((count, CYCLES), lambda i: (i, 0)),
            pl.BlockSpec((count, ANGLES, 2 * CYCLES), lambda i: (i, 0, 0)),
        ],
        out_specs=pl.BlockSpec((ANGLES, count, 2 * CYCLES), lambda i: (0, i, 0)),
        out_shape=jax.ShapeDtypeStruct((ANGLES, particles, 2 * CYCLES), jnp.bfloat16),
        scratch_shapes=[pltpu.VMEM((ANGLES * count, CYCLES), jnp.float32)] * 2,
        cost_estimate=pl.CostEstimate(
            flops=particles * 4 * ANGLES * ANGLES * 2 * CYCLES,
            bytes_accessed=4 * particles * ANGLES * 2 * CYCLES,
            transcendentals=0,
        ),
    )(table, contrast_rows, images)


def pick_kernel(index_ref, source_ref, out_ref):
    for step in range(STEPS):
        at = index_ref[step]
        value = source_ref[at, step if source_ref.shape[1] == STEPS else 0]
        for copy in range(out_ref.shape[0]):
            out_ref[copy, step] = value


def pick(source, index, copies):
    return pl.pallas_call(
        pick_kernel,
        in_specs=[
            pl.BlockSpec(memory_space=pltpu.SMEM),
            pl.BlockSpec(memory_space=pltpu.VMEM),
        ],
        out_specs=pl.BlockSpec(memory_space=pltpu.VMEM),
        out_shape=jax.ShapeDtypeStruct((copies, STEPS, ANGLES, CYCLES), jnp.bfloat16),
    )(index, source)


def score_kernel(
    core_ref,
    mine_ref,
    other_ref,
    spectra_ref,
    low_ref,
    turn_ref,
    back_ref,
    square_ref,
    prior_ref,
    member_ref,
    keep_ref,
    send_ref,
    top_ref,
    sum_ref,
    ref_real,
    ref_imag,
    corr,
    scores,
    power,
):
    particles = spectra_ref.shape[1]
    first = core_ref[0] == 0
    table = low_ref[...]
    for c in range(CLS_GRP):
        mine, other = mine_ref[c], other_ref[c]
        polar = jnp.concatenate(
            [jnp.where(first, mine, other), jnp.where(first, other, mine)], axis=-1
        )
        real, imag = (
            part.astype(jnp.bfloat16).astype(jnp.float32) for part in spectrum_of(polar, table)
        )
        rows = pl.ds(c, ANGLES, stride=CLS_GRP)
        ref_real[rows, :], ref_imag[rows, :] = real, imag
        power[c : c + 1, :] = jnp.sum(real * real + imag * imag, axis=0, keepdims=True)
    square = square_ref[...]
    across = (((1,), (1,)), ((), ()))
    energy = 0.5 * lax.dot_general(
        power[...], square, across, precision=TOP_PRECISION, preferred_element_type=jnp.float32
    )
    for m in range(ANGLES):
        rows = slice(m * CLS_GRP, (m + 1) * CLS_GRP)
        real, imag = ref_real[rows, :], ref_imag[rows, :]
        both = jnp.concatenate(
            [jnp.concatenate([real, -imag], axis=0), jnp.concatenate([imag, real], axis=0)],
            axis=-1,
        ).astype(jnp.bfloat16)
        corr[m * 2 * CLS_GRP : (m + 1) * 2 * CLS_GRP, :] = lax.dot_general(
            both, spectra_ref[m], across, preferred_element_type=jnp.float32
        )
    turn, prior = turn_ref[...], prior_ref[...]
    best = jnp.full((ANGLES, particles), -jnp.inf, jnp.float32)
    own = jnp.zeros((ANGLES, particles), jnp.float32)
    for c in range(0, CLS_GRP, 2):
        pair = [
            jnp.concatenate(
                [
                    corr[pl.ds(k, ANGLES, stride=2 * CLS_GRP), :],
                    corr[pl.ds(CLS_GRP + k, ANGLES, stride=2 * CLS_GRP), :],
                ],
                axis=0,
            )
            for k in (c, c + 1)
        ]
        rotated = jnp.dot(
            turn,
            jnp.concatenate(pair, axis=-1),
            precision=TOP_PRECISION,
            preferred_element_type=jnp.float32,
        )
        for k in range(2):
            value = rotated[:, k * particles : (k + 1) * particles]
            value = (value - energy[c + k : c + k + 1, :]) * (1.0 / ANGLES) + prior
            scores[c + k] = value
            best = jnp.maximum(best, value)
            own = own + jnp.where(member_ref[c + k : c + k + 1, :] > 0, value, 0.0)
    top = jnp.max(best, axis=0, keepdims=True)
    total = jnp.zeros((ANGLES, particles), jnp.float32)
    for c in range(CLS_GRP):
        total = total + jnp.exp(scores[c] - top)
    top_ref[...] = top
    sum_ref[...] = jnp.sum(total, axis=0, keepdims=True)
    weight = jnp.exp(own - jnp.max(own, axis=0, keepdims=True))
    weight = weight / jnp.sum(weight, axis=0, keepdims=True)
    turned_back = jnp.dot(
        back_ref[...], weight, precision=TOP_PRECISION, preferred_element_type=jnp.float32
    )
    h_real = turned_back[:particles].T
    h_imag = turned_back[particles:].T
    member = member_ref[...]
    chosen = member.astype(jnp.bfloat16)
    for m in range(ANGLES):
        x_real = spectra_ref[m, :, :CYCLES].astype(jnp.float32)
        x_imag = spectra_ref[m, :, CYCLES:].astype(jnp.float32)
        hr, hi = h_real[:, m : m + 1], h_imag[:, m : m + 1]
        aligned = jnp.concatenate(
            [x_real * hr - x_imag * hi, x_real * hi + x_imag * hr], axis=-1
        ).astype(jnp.bfloat16)
        sums = jnp.dot(chosen, aligned, preferred_element_type=jnp.float32)
        real_sum, imag_sum = sums[:, :CYCLES], sums[:, CYCLES:]
        keep_ref[m] = jnp.where(first, real_sum, imag_sum)
        send_ref[m] = jnp.where(first, imag_sum, real_sum)
    denom = jnp.dot(
        member, square, precision=TOP_PRECISION, preferred_element_type=jnp.float32
    )
    keep_ref[ANGLES] = denom
    send_ref[ANGLES] = denom


def score(core, mine, other, spectra, low_table, turn, back, square, prior, member):
    particles = spectra.shape[1]
    sums = jax.ShapeDtypeStruct((ANGLES + 1, CLS_GRP, CYCLES), jnp.float32)
    row = jax.ShapeDtypeStruct((1, particles), jnp.float32)
    vmem = pl.BlockSpec(memory_space=pltpu.VMEM)
    return pl.pallas_call(
        score_kernel,
        in_specs=[pl.BlockSpec(memory_space=pltpu.SMEM)] + [vmem] * 9,
        out_specs=(vmem, vmem, vmem, vmem),
        out_shape=(sums, sums, row, row),
        scratch_shapes=[
            pltpu.VMEM((ANGLES * CLS_GRP, CYCLES), jnp.float32),
            pltpu.VMEM((ANGLES * CLS_GRP, CYCLES), jnp.float32),
            pltpu.VMEM((ANGLES * 2 * CLS_GRP, particles), jnp.float32),
            pltpu.VMEM((CLS_GRP, ANGLES, particles), jnp.float32),
            pltpu.VMEM((CLS_GRP, CYCLES), jnp.float32),
        ],
        compiler_params=pltpu.CompilerParams(vmem_limit_bytes=40 * 1024 * 1024),
    )(core, mine, other, spectra, low_table, turn, back, square, prior, member)


def pack_kernel(keep_ref, got_ref, out_ref):
    denom = keep_ref[ANGLES] + got_ref[ANGLES]
    high = denom.astype(jnp.bfloat16)
    low = (denom - high.astype(jnp.float32)).astype(jnp.bfloat16)
    for z in range(out_ref.shape[0]):
        at = pl.ds(z * ROWS, ROWS)
        out_ref[z, :ROWS] = (keep_ref[at] + got_ref[at]).astype(jnp.bfloat16)
        out_ref[z, ROWS] = high if z == 0 else low


def pack(keep, got):
    vmem = pl.BlockSpec(memory_space=pltpu.VMEM)
    return pl.pallas_call(
        pack_kernel,
        in_specs=[vmem, vmem],
        out_specs=vmem,
        out_shape=jax.ShapeDtypeStruct((8, ROWS + 1, CLS_GRP, CYCLES), jnp.bfloat16),
    )(keep, got)


def rotation_prior(rotation_rows):
    counting = jnp.arange(ANGLES, dtype=jnp.int32)
    distance = jnp.abs(counting[None, :] - rotation_rows[:, None])
    distance = jnp.minimum(distance, ANGLES - distance).astype(jnp.float32)
    return -0.5 * (distance / SIGMA_ROT) ** 2


def fetch(blocks, holders):
    halves = jnp.stack([blocks[..., :CYCLES], blocks[..., CYCLES:]], axis=1)
    halves = halves.reshape(BLOCK * 2, ANGLES, CYCLES)
    sliced = lax.all_to_all(halves, ("wide_1", "wide_2"), 0, 0, tiled=True)
    picked = pick(sliced[:, None], holders % 16, 4)
    planes = lax.all_to_all(picked, "wide_0", 0, 0, tiled=True)
    picked = pick(planes, holders // 16, 8)
    return lax.all_to_all(picked, "wide_1", 0, 0, tiled=True).reshape(CLS_GRP, ANGLES, CYCLES)


def joined_evidence(top, total):
    for bit in (1, 2, 4):
        pair = jnp.concatenate([top, total])
        got = lax.ppermute(pair, "narrow", [(k, k ^ bit) for k in range(8)])
        joined = jnp.maximum(top, got[:1])
        total = total * jnp.exp(top - joined) + got[1:] * jnp.exp(got[:1] - joined)
        top = joined
    return (top + jnp.log(total)).reshape(-1)


def per_device(images, defocus, class_index, rotation_index, owner_map, roster, ref_store):
    class_group = lax.axis_index("narrow")
    z_index = lax.axis_index("wide_1")
    core = lax.axis_index("wide_2")
    wide_count = lax.axis_size(WIDE)
    cosine_table, sine_table = angle_tables(ANGLES)
    cosines_low = cosine_table.astype(jnp.bfloat16)
    sines_low = sine_table.astype(jnp.bfloat16)
    leading_class = class_group * CLS_GRP
    arrival = jnp.arange(CLS_GRP, dtype=jnp.int32)
    within = arrival % STEPS * BLOCK + arrival // STEPS
    class_ids = leading_class + within
    holders = lax.dynamic_index_in_dim(roster, class_group, 0, keepdims=False)

    low_table = jnp.concatenate([cosines_low, sines_low])
    turn = jnp.concatenate([cosine_table, -sine_table], axis=-1)
    filled = ((0, CYCLES - ANGLES), (0, 0))
    back = jnp.concatenate([jnp.pad(cosine_table, filled), jnp.pad(sine_table, filled)])
    contrast_rows = contrast(defocus)
    square = contrast_rows * contrast_rows
    prior = rotation_prior(rotation_index).T
    member = (class_index[None, :] == class_ids[:, None]).astype(jnp.float32)
    spectra = image_spectra(images, contrast_rows, low_table)

    mine = fetch(ref_store[0, 0], holders)
    other = swapped(mine)
    keep, send, top, total = score(
        core.reshape(1), mine, other, spectra, low_table, turn, back, square, prior, member
    )
    share = pack(keep, swapped(send)).reshape(8, (ROWS + 1) * CLS_GRP, CYCLES)
    share = lax.all_to_all(share, "wide_1", 0, 0, tiled=True)
    share = share.astype(jnp.float32).sum(axis=0).reshape(ROWS + 1, CLS_GRP, CYCLES)
    owners = lax.dynamic_slice_in_dim(owner_map, leading_class, CLS_GRP)
    owners = owners.reshape(STEPS, BLOCK).T.reshape(CLS_GRP)
    same = owners[:, None] == owners[None, :]
    ranking = jnp.sum(same & (within[None, :] < within[:, None]), axis=1)
    place = owners * OWN_MAX + ranking
    pick = place[None, :] == jnp.arange(wide_count * OWN_MAX, dtype=jnp.int32)[:, None]
    numer_share = share[:ROWS].astype(jnp.bfloat16)
    denom_high = share[ROWS:].astype(jnp.bfloat16)
    denom_low = (share[ROWS:] - denom_high.astype(jnp.float32)).astype(jnp.bfloat16)
    share = jnp.concatenate([numer_share, jnp.where(core == 0, denom_high, denom_low)])
    sent = jnp.einsum(
        "wsc,tck->wtsk",
        pick.reshape(wide_count, OWN_MAX, CLS_GRP).astype(jnp.bfloat16),
        share,
        preferred_element_type=jnp.float32,
    ).astype(jnp.bfloat16)
    sent = sent.reshape(wide_count, (ROWS + 1) * OWN_MAX, CYCLES)
    got = lax.all_to_all(sent, WIDE, 0, 0, tiled=True)
    got = got.reshape(4, 8, 2, ROWS + 1, OWN_MAX, CYCLES).astype(jnp.float32).sum(axis=0)
    denominator = got[0, 0, ROWS] + got[0, 1, ROWS] + got[1, 0, ROWS]
    scale = 1.0 / (denominator + TAU) / ANGLES
    real_part = got[:, 0, :ROWS].reshape(ANGLES, OWN_MAX, CYCLES) * scale
    imag_part = got[:, 1, :ROWS].reshape(ANGLES, OWN_MAX, CYCLES) * scale
    mixed = lambda x, table: jnp.einsum("mck,ma->cak", x, table, precision=TOP_PRECISION)
    polar = jnp.concatenate(
        [
            mixed(real_part, cosine_table) - mixed(imag_part, sine_table),
            mixed(imag_part, cosine_table) + mixed(real_part, sine_table),
        ],
        axis=-1,
    )
    new_references = polar.astype(jnp.bfloat16).reshape(1, 1, OWN_MAX, ANGLES, 2 * CYCLES)

    top, total, _ = lax.optimization_barrier((top, total, sent))
    log_evidence = joined_evidence(top, total)
    return (new_references, log_evidence)


def solution(mesh):
    split = Mesh(
        mesh.devices.reshape(4, 8, 2, mesh.shape["narrow"]),
        ("wide_0", "wide_1", "wide_2", "narrow"),
    )
    placed = (
        P(WIDE, None, None),
        P(WIDE),
        P(WIDE),
        P(WIDE),
        P(),
        P(),
        P(WIDE, "narrow", None, None, None),
    )
    return jax.shard_map(
        per_device,
        mesh=split,
        in_specs=placed,
        out_specs=(P(WIDE, "narrow", None, None, None), P(WIDE)),
        check_vma=False,
    )
```

time: 167 us -> 149 us (0.89)
  the two profiles are of different devices: /device:TPU:1 before, /device:TPU:42 now
where the time goes in v2:
time: 149 us; the launch traced here: 148 us
  waiting for transfers between devices  59.1 us (40%)
  starting transfers between devices  47.5 us (32%)
  Pallas kernels  23.7 us (16%)
  local copies, waits for them, and re-layouts  9.23 us (6%)
  other arithmetic  5.51 us (4%)
  matrix products  2.32 us (2%)
    ppermute x3, waiting for transfers between devices, joined_evidence(): got = lax.ppermute(pair, 'narrow', [(k, k ^ bit) for k in range(8)])  18.9 us
    all_to_all x1, waiting for transfers between devices, per_device(): share = lax.all_to_all(share, 'wide_1', 0, 0, tiled=True)  16.6 us
    all_to_all x1, waiting for transfers between devices, fetch(): sliced = lax.all_to_all(halves, ('wide_1', 'wide_2'), 0, 0, tiled=True)  11 us
    all_to_all x1, starting transfers between devices, fetch(): sliced = lax.all_to_all(halves, ('wide_1', 'wide_2'), 0, 0, tiled=True)  10.4 us
    pallas_call x1, Pallas kernels, image_spectra(): pl.pallas_call(spectra_kernel, grid=(particles // count,), in_specs=[pl.B...  9.87 us
    all_to_all x1, starting transfers between devices, per_device(): got = lax.all_to_all(sent, WIDE, 0, 0, tiled=True)  9.85 us
    ppermute x3, starting transfers between devices, joined_evidence(): got = lax.ppermute(pair, 'narrow', [(k, k ^ bit) for k in range(8)])  8.93 us
    pallas_call x1, Pallas kernels, score(): pl.pallas_call(score_kernel, in_specs=[pl.BlockSpec(memory_space=pltpu.SM...  8.04 us
  transfers between devices with their start and end apart: 10, of which 9 were waited for; matrix products, arithmetic and copies ran while one was open for 3% of the time, Pallas kernels for 7%

profile of v2, /device:TPU:42, one launch (start us, length us, event | category | flops | bytes accessed | tf_op | source)
XLA Modules:
  0.0 148.2 jit_solution(11726997388674136211)
XLA Ops:
  0.6 1.0 slice_bitcast_fusion.1
  1.7 0.7 copy.41
  2.4 10.4 %all-to-all-start = ((bf16[16,72,128]{2,1,0:T(8,128)(2,1)}), bf16[16,72,128]{2,1,0:T(8,128)(2,1)S(1)}, u32[]{:S(2)}, u32[]{:S(2)}) async-start(bf16[16,72,128]{2,1,0:T(8,128)(2,1)} %bitcast.5), calls=%async_computation | async-start | bytes 589824 | tf_op jit(solution)/shard_map/all_to_all | solution.py:268
  12.9 0.2 dynamic-slice_reduce_fusion
  13.1 0.6 and_select_fusion.2
  13.6 11.0 %all-to-all-done = bf16[16,72,128]{2,1,0:T(8,128)(2,1)S(1)} async-done(((bf16[16,72,128]{2,1,0:T(8,128)(2,1)}), bf16[16,72,128]{2,1,0:T(8,128)(2,1)S(1)}, u32[]{:S(2)}, u32[]{:S(2)}) %all-to-all-start) | async-done | bytes 294944 | tf_op jit(solution)/shard_map/all_to_all | solution.py:268
  24.6 0.7 copy-done.4
  25.3 1.7 %shard_map.86 = bf16[4,3,72,128]{3,2,1,0:T(8,128)(2,1)} custom-call(s32[3]{0:T(128)} %get-tuple-element.29.index_ref, bf16[16,1,72,128]{3,2,1,0:T(8,128)(2,1)} %bitcast.66), custom_call_target="tpu_custom_call" | custom-call | tf_op jit(solution)/shard_map/pallas_call | solution.py:97
  27.0 7.2 %all-to-all-start.1 = ((bf16[4,3,72,128]{3,2,1,0:T(8,128)(2,1)}), bf16[4,3,72,128]{3,2,1,0:T(8,128)(2,1)S(1)}, u32[]{:S(2)}, u32[]{:S(2)}) async-start(bf16[4,3,72,128]{3,2,1,0:T(8,128)(2,1)} %shard_map.86), calls=%async_computation.1 | async-start | bytes 442368 | tf_op jit(solution)/shard_map/all_to_all | solution.py:270
  34.2 0.7 multiply_multiply_fusion
  34.9 1.0 fusion.34
  35.9 5.2 %all-to-all-done.1.source_ref = bf16[4,3,72,128]{3,2,1,0:T(8,128)(2,1)S(1)} async-done(((bf16[4,3,72,128]{3,2,1,0:T(8,128)(2,1)}), bf16[4,3,72,128]{3,2,1,0:T(8,128)(2,1)S(1)}, u32[]{:S(2)}, u32[]{:S(2)}) %all-to-all-start.1) | async-done | bytes 221216 | tf_op jit(solution)/shard_map/all_to_all | solution.py:270
  41.0 0.7 copy-done.6
  41.7 1.8 %shard_map.87 = bf16[8,3,72,128]{3,2,1,0:T(8,128)(2,1)} custom-call(s32[3]{0:T(128)} %get-tuple-element.30.index_ref, bf16[4,3,72,128]{3,2,1,0:T(8,128)(2,1)} %copy-done.6), custom_call_target="tpu_custom_call" | custom-call | tf_op jit(solution)/shard_map/pallas_call | solution.py:97
  43.5 3.5 %all-to-all-start.2 = ((bf16[8,3,72,128]{3,2,1,0:T(8,128)(2,1)}), bf16[8,3,72,128]{3,2,1,0:T(8,128)(2,1)S(1)}, u32[]{:S(2)}, u32[]{:S(2)}) async-start(bf16[8,3,72,128]{3,2,1,0:T(8,128)(2,1)} %shard_map.87), calls=%async_computation.2 | async-start | bytes 884736 | tf_op jit(solution)/shard_map/all_to_all | solution.py:272
  47.0 0.2 fusion.38
  47.1 0.6 pad_maximum_fusion.3.table_ref.low_ref
  47.8 9.9 %shard_map.88.spectra_ref = bf16[72,128,256]{2,1,0:T(8,128)(2,1)} custom-call(bf16[144,72]{1,0:T(8,128)(2,1)} %pad_maximum_fusion.3.table_ref.low_ref, f32[128,128]{1,0:T(8,128)} %get-tuple-element.28.contrast_ref, bf16[128,72,256]{2,1,0:T(8,128)(2,1)} %image_ref.1), custom_call_target="tpu_custom_call" | custom-call | flops 679477248 | bytes 9437184 | tf_op jit(solution)/shard_map/pallas_call | solution.py:69
  57.8 0.2 fusion.30
  58.1 3.5 %all-to-all-done.2 = bf16[8,3,72,128]{3,2,1,0:T(8,128)(2,1)S(1)} async-done(((bf16[8,3,72,128]{3,2,1,0:T(8,128)(2,1)}), bf16[8,3,72,128]{3,2,1,0:T(8,128)(2,1)S(1)}, u32[]{:S(2)}, u32[]{:S(2)}) %all-to-all-start.2) | async-done | bytes 442400 | tf_op jit(solution)/shard_map/all_to_all | solution.py:272
  61.6 1.9 %collective-permute-start = (bf16[24,72,128]{2,1,0:T(8,128)(2,1)S(1)}, bf16[24,72,128]{2,1,0:T(8,128)(2,1)S(1)}, u32[]{:S(2)}, u32[]{:S(2)}) collective-permute-start(bf16[24,72,128]{2,1,0:T(8,128)(2,1)S(1)} %bitcast.61), channel_id=1, source_target_pairs={{0,8},{8,0},{1,9},{9,1},{2,10},{10,2},{3,11},{11,3},{4,12},{12,4},... | collective-permute-start | bytes 1327112 | tf_op jit(solution)/shard_map/ppermute | solution.py:28
  63.6 1.6 %collective-permute-done.other_ref = bf16[24,72,128]{2,1,0:T(8,128)(2,1)S(1)} collective-permute-done((bf16[24,72,128]{2,1,0:T(8,128)(2,1)S(1)}, bf16[24,72,128]{2,1,0:T(8,128)(2,1)S(1)}, u32[]{:S(2)}, u32[]{:S(2)}) %collective-permute-start) | collective-permute-done | bytes 442400 | tf_op jit(solution)/shard_map/ppermute | solution.py:28
  65.3 2.3 %copy-done.1 = bf16[72,128,256]{2,1,0:T(8,128)(2,1)S(1)} copy-done((bf16[72,128,256]{2,1,0:T(8,128)(2,1)S(1)}, bf16[72,128,256]{2,1,0:T(8,128)(2,1)}, u32[]{:S(2)}) %copy-start.1) | copy-done | bytes 4718616
  67.6 8.0 %shard_map.89 = (f32[73,24,128]{2,1,0:T(8,128)S(1)}, f32[73,24,128]{2,1,0:T(8,128)S(1)}, f32[1,128]{1,0:T(1,128)S(1)}, f32[1,128]{1,0:T(1,128)S(1)}) custom-call(s32[1]{0:T(128)} %bitcast.1.core_ref, bf16[24,72,128]{2,1,0:T(8,128)(2,1)S(1)} %bitcast.62, bf16[24,72,128]{2,1,0:T(8,128)(2,1)S(1)} %collective-permute-done.other_ref, ...), custom_call_target="tpu_custom_call" | custom-call | tf_op jit(solution)/shard_map/pallas_call | solution.py:222
  75.7 0.9 copy-done.2
  76.6 2.0 %collective-permute-start.1 = (f32[73,24,128]{2,1,0:T(8,128)S(1)}, f32[73,24,128]{2,1,0:T(8,128)S(1)}, u32[]{:S(2)}, u32[]{:S(2)}) collective-permute-start(f32[73,24,128]{2,1,0:T(8,128)S(1)} %get-tuple-element.9), channel_id=1, source_target_pairs={{0,8},{8,0},{1,9},{9,1},{2,10},{10,2},{3,11},{11,3},{4,12},{12,4},... | collective-permute-start | bytes 2691080 | tf_op jit(solution)/shard_map/ppermute | solution.py:28
  78.6 2.3 %collective-permute-done.1.got_ref = f32[73,24,128]{2,1,0:T(8,128)S(1)} collective-permute-done((f32[73,24,128]{2,1,0:T(8,128)S(1)}, f32[73,24,128]{2,1,0:T(8,128)S(1)}, u32[]{:S(2)}, u32[]{:S(2)}) %collective-permute-start.1) | collective-permute-done | bytes 897056 | tf_op jit(solution)/shard_map/ppermute | solution.py:28
  80.9 1.0 copy-done.5
  81.9 2.3 %shard_map.90 = bf16[8,10,24,128]{3,2,1,0:T(8,128)(2,1)} custom-call(f32[73,24,128]{2,1,0:T(8,128)} %copy-done.2, f32[73,24,128]{2,1,0:T(8,128)} %copy-done.5), custom_call_target="tpu_custom_call" | custom-call | tf_op jit(solution)/shard_map/pallas_call | solution.py:250
  84.2 3.7 %all-to-all-start.3 = ((bf16[8,240,128]{2,1,0:T(8,128)(2,1)}), bf16[8,240,128]{2,1,0:T(8,128)(2,1)S(1)}, u32[]{:S(2)}, u32[]{:S(2)}) async-start(bf16[8,240,128]{2,1,0:T(8,128)(2,1)} %bitcast.65), calls=%async_computation.3 | async-start | bytes 983040 | tf_op jit(solution)/shard_map/all_to_all | solution.py:315
  88.2 0.2 convert_reduce_fusion.2
  88.4 16.6 %all-to-all-done.3 = bf16[8,240,128]{2,1,0:T(8,128)(2,1)S(1)} async-done(((bf16[8,240,128]{2,1,0:T(8,128)(2,1)}), bf16[8,240,128]{2,1,0:T(8,128)(2,1)S(1)}, u32[]{:S(2)}, u32[]{:S(2)}) %all-to-all-start.3) | async-done | bytes 491552 | tf_op jit(solution)/shard_map/all_to_all | solution.py:315
  105.1 0.4 convolution_convert_fusion
  105.5 1.3 copy.43
  106.8 9.9 %all-to-all-start.4 = ((bf16[64,40,128]{2,1,0:T(8,128)(2,1)}), bf16[64,40,128]{2,1,0:T(8,128)(2,1)S(1)}, u32[]{:S(2)}, u32[]{:S(2)}) async-start(bf16[64,40,128]{2,1,0:T(8,128)(2,1)} %copy.43), calls=%async_computation.4 | async-start | bytes 1310720 | tf_op jit(solution)/shard_map/all_to_all | solution.py:334
  116.7 2.5 %collective-permute-start.2 = (f32[2,128]{1,0:T(2,128)S(1)}, f32[2,128]{1,0:T(2,128)S(1)}, u32[]{:S(2)}, u32[]{:S(2)}) collective-permute-start(f32[2,128]{1,0:T(2,128)S(1)} %pad_maximum_fusion.4), channel_id=1, source_target_pairs={{0,1},{1,0},{2,3},{3,2},{4,5},{5,4},{6,7},{7,6},{8,9},{9,8},{10,11... | collective-permute-start | bytes 3080 | tf_op jit(solution)/shard_map/ppermute | solution.py:278
  119.2 13.0 %collective-permute-done.2 = f32[2,128]{1,0:T(2,128)S(1)} collective-permute-done((f32[2,128]{1,0:T(2,128)S(1)}, f32[2,128]{1,0:T(2,128)S(1)}, u32[]{:S(2)}, u32[]{:S(2)}) %collective-permute-start.2) | collective-permute-done | bytes 1056 | tf_op jit(solution)/shard_map/ppermute | solution.py:278
  132.1 2.4 %collective-permute-start.3 = (f32[2,128]{1,0:T(2,128)S(1)}, f32[2,128]{1,0:T(2,128)S(1)}, u32[]{:S(2)}, u32[]{:S(2)}) collective-permute-start(f32[2,128]{1,0:T(2,128)S(1)} %pad_maximum_fusion.5), channel_id=1, source_target_pairs={{0,2},{1,3},{2,0},{3,1},{4,6},{5,7},{6,4},{7,5},{8,10},{9,11},{10,... | collective-permute-start | bytes 3080 | tf_op jit(solution)/shard_map/ppermute | solution.py:278
  134.6 3.0 %collective-permute-done.3 = f32[2,128]{1,0:T(2,128)S(1)} collective-permute-done((f32[2,128]{1,0:T(2,128)S(1)}, f32[2,128]{1,0:T(2,128)S(1)}, u32[]{:S(2)}, u32[]{:S(2)}) %collective-permute-start.3) | collective-permute-done | bytes 1056 | tf_op jit(solution)/shard_map/ppermute | solution.py:278
  137.6 4.0 %collective-permute-start.4 = (f32[2,128]{1,0:T(2,128)S(1)}, f32[2,128]{1,0:T(2,128)S(1)}, u32[]{:S(2)}, u32[]{:S(2)}) collective-permute-start(f32[2,128]{1,0:T(2,128)S(1)} %pad_maximum_fusion.6), channel_id=1, source_target_pairs={{0,4},{1,5},{2,6},{3,7},{4,0},{5,1},{6,2},{7,3},{8,12},{9,13},{10,... | collective-permute-start | bytes 3080 | tf_op jit(solution)/shard_map/ppermute | solution.py:278
  141.7 2.9 %collective-permute-done.4 = f32[2,128]{1,0:T(2,128)S(1)} collective-permute-done((f32[2,128]{1,0:T(2,128)S(1)}, f32[2,128]{1,0:T(2,128)S(1)}, u32[]{:S(2)}, u32[]{:S(2)}) %collective-permute-start.4) | collective-permute-done | bytes 1056 | tf_op jit(solution)/shard_map/ppermute | solution.py:278
  144.6 0.5 add_bitcast_fusion
  145.1 0.3 convert_reduce_fusion
  145.6 0.5 fusion.8
  146.1 0.5 fusion.4
  146.6 0.5 fusion.3
  147.0 0.5 fusion.2
  147.5 0.7 pad_maximum_fusion.1
  (42 shorter events, 1.0 us)
Async XLA Ops:
  0.6 12.2 %copy-start = (s32[8,3]{0,1:T(4,128)S(1)}, s32[8,3]{0,1:T(4,128)}, u32[]{:S(2)}) copy-start(s32[8,3]{0,1:T(4,128)} %param.12) | copy-start | bytes 292
  2.4 22.2 %all-to-all-start = ((bf16[16,72,128]{2,1,0:T(8,128)(2,1)}), bf16[16,72,128]{2,1,0:T(8,128)(2,1)S(1)}, u32[]{:S(2)}, u32[]{:S(2)}) async-start(bf16[16,72,128]{2,1,0:T(8,128)(2,1)} %bitcast.5), calls=%async_computation | async-start | bytes 589824 | tf_op jit(solution)/shard_map/all_to_all | solution.py:268
  24.6 0.7 copy-start.4
  27.0 14.0 %all-to-all-start.1 = ((bf16[4,3,72,128]{3,2,1,0:T(8,128)(2,1)}), bf16[4,3,72,128]{3,2,1,0:T(8,128)(2,1)S(1)}, u32[]{:S(2)}, u32[]{:S(2)}) async-start(bf16[4,3,72,128]{3,2,1,0:T(8,128)(2,1)} %shard_map.86), calls=%async_computation.1 | async-start | bytes 442368 | tf_op jit(solution)/shard_map/all_to_all | solution.py:270
  41.0 0.7 copy-start.6
  43.5 18.1 %all-to-all-start.2 = ((bf16[8,3,72,128]{3,2,1,0:T(8,128)(2,1)}), bf16[8,3,72,128]{3,2,1,0:T(8,128)(2,1)S(1)}, u32[]{:S(2)}, u32[]{:S(2)}) async-start(bf16[8,3,72,128]{3,2,1,0:T(8,128)(2,1)} %shard_map.87), calls=%async_computation.2 | async-start | bytes 884736 | tf_op jit(solution)/shard_map/all_to_all | solution.py:272
  47.8 15.8 %copy-start.8 = (s32[128]{0:T(128)S(1)}, s32[128]{0:T(128)}, u32[]{:S(2)}) copy-start(s32[128]{0:T(128)} %param.9) | copy-start | bytes 1540
  47.8 15.8 %copy-start.7 = (s32[128]{0:T(128)S(1)}, s32[128]{0:T(128)}, u32[]{:S(2)}) copy-start(s32[128]{0:T(128)} %param.10) | copy-start | bytes 1540
  47.8 17.5 %copy-start.3 = (bf16[144,72]{1,0:T(8,128)(2,1)S(1)}, bf16[144,72]{1,0:T(8,128)(2,1)}, u32[]{:S(2)}) copy-start(bf16[144,72]{1,0:T(8,128)(2,1)} %pad_maximum_fusion.3.table_ref.low_ref) | copy-start | bytes 62212
  58.1 29.8 %copy-start.9 = (s32[192]{0:T(256)S(1)}, s32[192]{0:T(256)}, u32[]{:S(2)}) copy-start(s32[192]{0:T(256)} %param.11) | copy-start | bytes 2308
  61.6 3.7 %collective-permute-start = (bf16[24,72,128]{2,1,0:T(8,128)(2,1)S(1)}, bf16[24,72,128]{2,1,0:T(8,128)(2,1)S(1)}, u32[]{:S(2)}, u32[]{:S(2)}) collective-permute-start(bf16[24,72,128]{2,1,0:T(8,128)(2,1)S(1)} %bitcast.61), channel_id=1, source_target_pairs={{0,8},{8,0},{1,9},{9,1},{2,10},{10,2},{3,11},{11,3},{4,12},{12,4},... | collective-permute-start | bytes 1327112 | tf_op jit(solution)/shard_map/ppermute | solution.py:28
  65.3 2.3 %copy-start.1 = (bf16[72,128,256]{2,1,0:T(8,128)(2,1)S(1)}, bf16[72,128,256]{2,1,0:T(8,128)(2,1)}, u32[]{:S(2)}) copy-start(bf16[72,128,256]{2,1,0:T(8,128)(2,1)} %shard_map.88.spectra_ref) | copy-start | bytes 14155780
  75.7 0.9 copy-start.2
  76.6 4.3 %collective-permute-start.1 = (f32[73,24,128]{2,1,0:T(8,128)S(1)}, f32[73,24,128]{2,1,0:T(8,128)S(1)}, u32[]{:S(2)}, u32[]{:S(2)}) collective-permute-start(f32[73,24,128]{2,1,0:T(8,128)S(1)} %get-tuple-element.9), channel_id=1, source_target_pairs={{0,8},{8,0},{1,9},{9,1},{2,10},{10,2},{3,11},{11,3},{4,12},{12,4},... | collective-permute-start | bytes 2691080 | tf_op jit(solution)/shard_map/ppermute | solution.py:28
  80.9 1.0 copy-start.5
  84.2 20.8 %all-to-all-start.3 = ((bf16[8,240,128]{2,1,0:T(8,128)(2,1)}), bf16[8,240,128]{2,1,0:T(8,128)(2,1)S(1)}, u32[]{:S(2)}, u32[]{:S(2)}) async-start(bf16[8,240,128]{2,1,0:T(8,128)(2,1)} %bitcast.65), calls=%async_computation.3 | async-start | bytes 983040 | tf_op jit(solution)/shard_map/all_to_all | solution.py:315
  106.8 38.3 %all-to-all-start.4 = ((bf16[64,40,128]{2,1,0:T(8,128)(2,1)}), bf16[64,40,128]{2,1,0:T(8,128)(2,1)S(1)}, u32[]{:S(2)}, u32[]{:S(2)}) async-start(bf16[64,40,128]{2,1,0:T(8,128)(2,1)} %copy.43), calls=%async_computation.4 | async-start | bytes 1310720 | tf_op jit(solution)/shard_map/all_to_all | solution.py:334
  116.7 15.4 %collective-permute-start.2 = (f32[2,128]{1,0:T(2,128)S(1)}, f32[2,128]{1,0:T(2,128)S(1)}, u32[]{:S(2)}, u32[]{:S(2)}) collective-permute-start(f32[2,128]{1,0:T(2,128)S(1)} %pad_maximum_fusion.4), channel_id=1, source_target_pairs={{0,1},{1,0},{2,3},{3,2},{4,5},{5,4},{6,7},{7,6},{8,9},{9,8},{10,11... | collective-permute-start | bytes 3080 | tf_op jit(solution)/shard_map/ppermute | solution.py:278
  132.1 5.5 %collective-permute-start.3 = (f32[2,128]{1,0:T(2,128)S(1)}, f32[2,128]{1,0:T(2,128)S(1)}, u32[]{:S(2)}, u32[]{:S(2)}) collective-permute-start(f32[2,128]{1,0:T(2,128)S(1)} %pad_maximum_fusion.5), channel_id=1, source_target_pairs={{0,2},{1,3},{2,0},{3,1},{4,6},{5,7},{6,4},{7,5},{8,10},{9,11},{10,... | collective-permute-start | bytes 3080 | tf_op jit(solution)/shard_map/ppermute | solution.py:278
  137.6 7.0 %collective-permute-start.4 = (f32[2,128]{1,0:T(2,128)S(1)}, f32[2,128]{1,0:T(2,128)S(1)}, u32[]{:S(2)}, u32[]{:S(2)}) collective-permute-start(f32[2,128]{1,0:T(2,128)S(1)} %pad_maximum_fusion.6), channel_id=1, source_target_pairs={{0,4},{1,5},{2,6},{3,7},{4,0},{5,1},{6,2},{7,3},{8,12},{9,13},{10,... | collective-permute-start | bytes 3080 | tf_op jit(solution)/shard_map/ppermute | solution.py:278

commit v3 on v2

--- a/solution.py
+++ b/solution.py
@@ -77,6 +77,7 @@
         out_specs=pl.BlockSpec((ANGLES, count, 2 * CYCLES), lambda i: (0, i, 0)),
         out_shape=jax.ShapeDtypeStruct((ANGLES, particles, 2 * CYCLES), jnp.bfloat16),
         scratch_shapes=[pltpu.VMEM((ANGLES * count, CYCLES), jnp.float32)] * 2,
+        compiler_params=pltpu.CompilerParams(vmem_limit_bytes=8 * 1024 * 1024),
         cost_estimate=pl.CostEstimate(
             flops=particles * 4 * ANGLES * ANGLES * 2 * CYCLES,
             bytes_accessed=4 * particles * ANGLES * 2 * CYCLES,
@@ -102,6 +103,7 @@
         ],
         out_specs=pl.BlockSpec(memory_space=pltpu.VMEM),
         out_shape=jax.ShapeDtypeStruct((copies, STEPS, ANGLES, CYCLES), jnp.bfloat16),
+        compiler_params=pltpu.CompilerParams(vmem_limit_bytes=2 * 1024 * 1024),
     )(index, source)
 
 
@@ -109,7 +111,7 @@
     core_ref,
     mine_ref,
     other_ref,
-    spectra_ref,
+    source_ref,
     low_ref,
     turn_ref,
     back_ref,
@@ -125,8 +127,12 @@
     corr,
     scores,
     power,
+    spectra_ref,
+    sem,
 ):
     particles = spectra_ref.shape[1]
+    arriving = pltpu.make_async_copy(source_ref, spectra_ref, sem)
+    arriving.start()
     first = core_ref[0] == 0
     table = low_ref[...]
     for c in range(CLS_GRP):
@@ -145,6 +151,7 @@
     energy = 0.5 * lax.dot_general(
         power[...], square, across, precision=TOP_PRECISION, preferred_element_type=jnp.float32
     )
+    arriving.wait()
     for m in range(ANGLES):
         rows = slice(m * CLS_GRP, (m + 1) * CLS_GRP)
         real, imag = ref_real[rows, :], ref_imag[rows, :]
@@ -221,7 +228,9 @@
     vmem = pl.BlockSpec(memory_space=pltpu.VMEM)
     return pl.pallas_call(
         score_kernel,
-        in_specs=[pl.BlockSpec(memory_space=pltpu.SMEM)] + [vmem] * 9,
+        in_specs=[pl.BlockSpec(memory_space=pltpu.SMEM), vmem, vmem]
+        + [pl.BlockSpec(memory_space=pltpu.HBM)]
+        + [vmem] * 6,
         out_specs=(vmem, vmem, vmem, vmem),
         out_shape=(sums, sums, row, row),
         scratch_shapes=[
@@ -230,8 +239,10 @@
             pltpu.VMEM((ANGLES * 2 * CLS_GRP, particles), jnp.float32),
             pltpu.VMEM((CLS_GRP, ANGLES, particles), jnp.float32),
             pltpu.VMEM((CLS_GRP, CYCLES), jnp.float32),
+            pltpu.VMEM((ANGLES, particles, 2 * CYCLES), jnp.bfloat16),
+            pltpu.SemaphoreType.DMA,
         ],
-        compiler_params=pltpu.CompilerParams(vmem_limit_bytes=40 * 1024 * 1024),
+        compiler_params=pltpu.CompilerParams(vmem_limit_bytes=20 * 1024 * 1024),
     )(core, mine, other, spectra, low_table, turn, back, square, prior, member)
 
 
@@ -252,6 +263,7 @@
         in_specs=[vmem, vmem],
         out_specs=vmem,
         out_shape=jax.ShapeDtypeStruct((8, ROWS + 1, CLS_GRP, CYCLES), jnp.bfloat16),
+        compiler_params=pltpu.CompilerParams(vmem_limit_bytes=4 * 1024 * 1024),
     )(keep, got)
 
 
@@ -262,9 +274,114 @@
     return -0.5 * (distance / SIGMA_ROT) ** 2
 
 
+def halve_kernel(blocks_ref, out_ref, sems):
+    copies = [
+        pltpu.make_async_copy(
+            blocks_ref.at[:, :, half * CYCLES : (half + 1) * CYCLES], out_ref.at[:, half], sems.at[half]
+        )
+        for half in range(2)
+    ]
+    for copy in copies:
+        copy.start()
+    for copy in copies:
+        copy.wait()
+
+
+def halve(blocks):
+    return pl.pallas_call(
+        halve_kernel,
+        in_specs=[pl.BlockSpec(memory_space=pltpu.HBM)],
+        out_specs=pl.BlockSpec(memory_space=pltpu.HBM),
+        out_shape=jax.ShapeDtypeStruct((BLOCK, 2, ANGLES, CYCLES), jnp.bfloat16),
+        scratch_shapes=[pltpu.SemaphoreType.DMA((2,))],
+        compiler_params=pltpu.CompilerParams(vmem_limit_bytes=1024 * 1024),
+    )(blocks)
+
+
+def route_kernel(core_ref, place_ref, got_ref, out_ref):
+    total = got_ref[0].astype(jnp.float32)
+    for z in range(1, got_ref.shape[0]):
+        total = total + got_ref[z].astype(jnp.float32)
+    denom = total[ROWS * CLS_GRP :]
+    high = denom.astype(jnp.bfloat16).astype(jnp.float32)
+    denom = jnp.where(core_ref[0] == 0, high, denom - high)
+    share = jnp.concatenate([total[: ROWS * CLS_GRP], denom], axis=0).astype(jnp.bfloat16)
+    rows, columns = (ROWS + 1) * OWN_MAX, (ROWS + 1) * CLS_GRP
+    place = place_ref[...]
+    line = lax.broadcasted_iota(jnp.int32, (rows, columns), 0)
+    line = (line // OWN_MAX) * 1024 + line % OWN_MAX - place
+    for owner in range(0, 64, 8):
+        chosen = jnp.concatenate(
+            [jnp.where(line == -OWN_MAX * (owner + k), 1.0, 0.0) for k in range(8)], axis=0
+        ).astype(jnp.bfloat16)
+        out_ref[owner * rows : (owner + 8) * rows, :] = jnp.dot(
+            chosen, share, preferred_element_type=jnp.float32
+        ).astype(jnp.bfloat16)
+
+
+def route(core, place, got):
+    vmem = pl.BlockSpec(memory_space=pltpu.VMEM)
+    return pl.pallas_call(
+        route_kernel,
+        in_specs=[pl.BlockSpec(memory_space=pltpu.SMEM), vmem, vmem],
+        out_specs=vmem,
+        out_shape=jax.ShapeDtypeStruct((64 * (ROWS + 1) * OWN_MAX, CYCLES), jnp.bfloat16),
+        compiler_params=pltpu.CompilerParams(vmem_limit_bytes=6 * 1024 * 1024),
+    )(core, place, got)
+
+
+def finish_kernel(table_ref, got_ref, out_ref, held):
+    total = got_ref[0].astype(jnp.float32)
+    for plane in range(1, got_ref.shape[0]):
+        total = total + got_ref[plane].astype(jnp.float32)
+    held[...] = total
+    rows = (ROWS + 1) * OWN_MAX
+    at = ROWS * OWN_MAX
+    denom = total[at : at + OWN_MAX] + total[rows + at : rows + at + OWN_MAX]
+    denom = denom + total[2 * rows + at : 2 * rows + at + OWN_MAX]
+    scale = (1.0 / ANGLES) / (denom + TAU)
+    for slot in range(0, OWN_MAX, 2):
+        pair = [
+            held[pl.ds(k, 16 * (ROWS + 1), stride=OWN_MAX), :] * scale[k : k + 1]
+            for k in (slot, slot + 1)
+        ]
+        polar = jnp.dot(
+            table_ref[...],
+            jnp.concatenate(pair, axis=-1),
+            precision=TOP_PRECISION,
+            preferred_element_type=jnp.float32,
+        ).astype(jnp.bfloat16)
+        for k in range(2):
+            columns = slice(k * CYCLES, (k + 1) * CYCLES)
+            out_ref[slot + k, :, :CYCLES] = polar[:ANGLES, columns]
+            out_ref[slot + k, :, CYCLES:] = polar[ANGLES:, columns]
+
+
+def finish(table, got):
+    vmem = pl.BlockSpec(memory_space=pltpu.VMEM)
+    return pl.pallas_call(
+        finish_kernel,
+        in_specs=[vmem, vmem],
+        out_specs=vmem,
+        out_shape=jax.ShapeDtypeStruct((OWN_MAX, ANGLES, 2 * CYCLES), jnp.bfloat16),
+        scratch_shapes=[pltpu.VMEM((16 * (ROWS + 1) * OWN_MAX, CYCLES), jnp.float32)],
+        compiler_params=pltpu.CompilerParams(vmem_limit_bytes=6 * 1024 * 1024),
+    )(table, got)
+
+
+def finish_table(cosine_table, sine_table):
+    def laid(table):
+        table = table.reshape(ANGLES, 8, 1, ROWS)
+        return jnp.pad(table, ((0, 0), (0, 0), (0, 0), (0, 1)))
+
+    cosine, sine = laid(cosine_table), laid(sine_table)
+    real = jnp.concatenate([cosine, -sine], axis=2).reshape(ANGLES, 16 * (ROWS + 1))
+    imag = jnp.concatenate([sine, cosine], axis=2).reshape(ANGLES, 16 * (ROWS + 1))
+    return jnp.concatenate([real, imag])
+
+
 def fetch(blocks, holders):
-    halves = jnp.stack([blocks[..., :CYCLES], blocks[..., CYCLES:]], axis=1)
-    halves = halves.reshape(BLOCK * 2, ANGLES, CYCLES)
+    halves = halve(blocks).reshape(BLOCK * 2, ANGLES, CYCLES)
     sliced = lax.all_to_all(halves, ("wide_1", "wide_2"), 0, 0, tiled=True)
     picked = pick(sliced[:, None], holders % 16, 4)
     planes = lax.all_to_all(picked, "wide_0", 0, 0, tiled=True)
@@ -284,9 +401,7 @@
 
 def per_device(images, defocus, class_index, rotation_index, owner_map, roster, ref_store):
     class_group = lax.axis_index("narrow")
-    z_index = lax.axis_index("wide_1")
     core = lax.axis_index("wide_2")
-    wide_count = lax.axis_size(WIDE)
     cosine_table, sine_table = angle_tables(ANGLES)
     cosines_low = cosine_table.astype(jnp.bfloat16)
     sines_low = sine_table.astype(jnp.bfloat16)
@@ -311,44 +426,23 @@
     keep, send, top, total = score(
         core.reshape(1), mine, other, spectra, low_table, turn, back, square, prior, member
     )
-    share = pack(keep, swapped(send)).reshape(8, (ROWS + 1) * CLS_GRP, CYCLES)
-    share = lax.all_to_all(share, "wide_1", 0, 0, tiled=True)
-    share = share.astype(jnp.float32).sum(axis=0).reshape(ROWS + 1, CLS_GRP, CYCLES)
     owners = lax.dynamic_slice_in_dim(owner_map, leading_class, CLS_GRP)
     owners = owners.reshape(STEPS, BLOCK).T.reshape(CLS_GRP)
     same = owners[:, None] == owners[None, :]
     ranking = jnp.sum(same & (within[None, :] < within[:, None]), axis=1)
     place = owners * OWN_MAX + ranking
-    pick = place[None, :] == jnp.arange(wide_count * OWN_MAX, dtype=jnp.int32)[:, None]
-    numer_share = share[:ROWS].astype(jnp.bfloat16)
-    denom_high = share[ROWS:].astype(jnp.bfloat16)
-    denom_low = (share[ROWS:] - denom_high.astype(jnp.float32)).astype(jnp.bfloat16)
-    share = jnp.concatenate([numer_share, jnp.where(core == 0, denom_high, denom_low)])
-    sent = jnp.einsum(
-        "wsc,tck->wtsk",
-        pick.reshape(wide_count, OWN_MAX, CLS_GRP).astype(jnp.bfloat16),
-        share,
-        preferred_element_type=jnp.float32,
-    ).astype(jnp.bfloat16)
-    sent = sent.reshape(wide_count, (ROWS + 1) * OWN_MAX, CYCLES)
+    place = jnp.arange(ROWS + 1, dtype=jnp.int32)[:, None] * 1024 + place[None, :]
+    place = place.reshape(1, (ROWS + 1) * CLS_GRP)
+    table = finish_table(cosine_table, sine_table)
+    share = pack(keep, swapped(send)).reshape(8, (ROWS + 1) * CLS_GRP, CYCLES)
+    top, total, share = lax.optimization_barrier((top, total, share))
+    share = lax.all_to_all(share, "wide_1", 0, 0, tiled=True)
+    log_evidence = joined_evidence(top, total)
+    share, log_evidence = lax.optimization_barrier((share, log_evidence))
+    sent = route(core.reshape(1), place, share).reshape(64, (ROWS + 1) * OWN_MAX, CYCLES)
     got = lax.all_to_all(sent, WIDE, 0, 0, tiled=True)
-    got = got.reshape(4, 8, 2, ROWS + 1, OWN_MAX, CYCLES).astype(jnp.float32).sum(axis=0)
-    denominator = got[0, 0, ROWS] + got[0, 1, ROWS] + got[1, 0, ROWS]
-    scale = 1.0 / (denominator + TAU) / ANGLES
-    real_part = got[:, 0, :ROWS].reshape(ANGLES, OWN_MAX, CYCLES) * scale
-    imag_part = got[:, 1, :ROWS].reshape(ANGLES, OWN_MAX, CYCLES) * scale
-    mixed = lambda x, table: jnp.einsum("mck,ma->cak", x, table, precision=TOP_PRECISION)
-    polar = jnp.concatenate(
-        [
-            mixed(real_part, cosine_table) - mixed(imag_part, sine_table),
-            mixed(imag_part, cosine_table) + mixed(real_part, sine_table),
-        ],
-        axis=-1,
-    )
-    new_references = polar.astype(jnp.bfloat16).reshape(1, 1, OWN_MAX, ANGLES, 2 * CYCLES)
-
-    top, total, _ = lax.optimization_barrier((top, total, sent))
-    log_evidence = joined_evidence(top, total)
+    got = got.reshape(4, 16 * (ROWS + 1) * OWN_MAX, CYCLES)
+    new_references = finish(table, got).reshape(1, 1, OWN_MAX, ANGLES, 2 * CYCLES)
     return (new_references, log_evidence)
 
 

time: 149 us -> 139 us (0.933)
  the two profiles are of different devices: /device:TPU:42 before, /device:TPU:1 now
where the time goes in v3:
time: 139 us; the launch traced here: 138 us
  waiting for transfers between devices  56.4 us (41%)
  starting transfers between devices  47.2 us (34%)
  Pallas kernels  22.2 us (16%)
  local copies, waits for them, and re-layouts  8.58 us (6%)
  other arithmetic  2.97 us (2%)
    all_to_all x1, waiting for transfers between devices, per_device(): got = lax.all_to_all(sent, WIDE, 0, 0, tiled=True)  21 us
    all_to_all x1, waiting for transfers between devices, fetch(): sliced = lax.all_to_all(halves, ('wide_1', 'wide_2'), 0, 0, tiled=True)  12.2 us
    all_to_all x1, starting transfers between devices, fetch(): sliced = lax.all_to_all(halves, ('wide_1', 'wide_2'), 0, 0, tiled=True)  11.8 us
    ppermute x3, starting transfers between devices, joined_evidence(): got = lax.ppermute(pair, 'narrow', [(k, k ^ bit) for k in range(8)])  10.9 us
    pallas_call x1, Pallas kernels, score(): pl.pallas_call(score_kernel, in_specs=[pl.BlockSpec(memory_space=pltpu.SM...  8.83 us
    all_to_all x1, waiting for transfers between devices, fetch(): planes = lax.all_to_all(picked, 'wide_0', 0, 0, tiled=True)  8.23 us
    unnamed x16, local copies, waits for them, and re-layouts  7.79 us
    all_to_all x1, starting transfers between devices, fetch(): planes = lax.all_to_all(picked, 'wide_0', 0, 0, tiled=True)  6.81 us
  transfers between devices with their start and end apart: 10, of which 9 were waited for; matrix products, arithmetic and copies ran while one was open for 3% of the time, Pallas kernels for 5%

profile of v3, /device:TPU:1, one launch (start us, length us, event | category | flops | bytes accessed | tf_op | source)
XLA Modules:
  0.0 138.3 jit_solution(14624824388030489551)
XLA Ops:
  0.7 1.0 copy-done.4
  1.6 0.7 shard_map.86
  2.4 11.8 %all-to-all-start = ((bf16[16,72,128]{2,1,0:T(8,128)(2,1)}), bf16[16,72,128]{2,1,0:T(8,128)(2,1)S(1)}, u32[]{:S(2)}, u32[]{:S(2)}) async-start(bf16[16,72,128]{2,1,0:T(8,128)(2,1)} %bitcast.3), calls=%async_computation | async-start | bytes 589824 | tf_op jit(solution)/shard_map/all_to_all | solution.py:385
  14.2 0.2 dynamic-slice_reduce_fusion
  14.4 12.2 %all-to-all-done = bf16[16,72,128]{2,1,0:T(8,128)(2,1)S(1)} async-done(((bf16[16,72,128]{2,1,0:T(8,128)(2,1)}), bf16[16,72,128]{2,1,0:T(8,128)(2,1)S(1)}, u32[]{:S(2)}, u32[]{:S(2)}) %all-to-all-start) | async-done | bytes 294944 | tf_op jit(solution)/shard_map/all_to_all | solution.py:385
  26.6 1.3 shard_map.87
  27.8 6.8 %all-to-all-start.1 = ((bf16[4,3,72,128]{3,2,1,0:T(8,128)(2,1)}), bf16[4,3,72,128]{3,2,1,0:T(8,128)(2,1)S(1)}, u32[]{:S(2)}, u32[]{:S(2)}) async-start(bf16[4,3,72,128]{3,2,1,0:T(8,128)(2,1)} %shard_map.87), calls=%async_computation.1 | async-start | bytes 442368 | tf_op jit(solution)/shard_map/all_to_all | solution.py:387
  34.6 0.7 multiply_multiply_fusion
  35.3 0.3 fusion.21
  35.6 8.2 %all-to-all-done.1.source_ref = bf16[4,3,72,128]{3,2,1,0:T(8,128)(2,1)S(1)} async-done(((bf16[4,3,72,128]{3,2,1,0:T(8,128)(2,1)}), bf16[4,3,72,128]{3,2,1,0:T(8,128)(2,1)S(1)}, u32[]{:S(2)}, u32[]{:S(2)}) %all-to-all-start.1) | async-done | bytes 221216 | tf_op jit(solution)/shard_map/all_to_all | solution.py:387
  43.9 1.4 shard_map.88
  45.2 3.5 %all-to-all-start.2 = ((bf16[8,3,72,128]{3,2,1,0:T(8,128)(2,1)}), bf16[8,3,72,128]{3,2,1,0:T(8,128)(2,1)S(1)}, u32[]{:S(2)}, u32[]{:S(2)}) async-start(bf16[8,3,72,128]{3,2,1,0:T(8,128)(2,1)} %shard_map.88), calls=%async_computation.2 | async-start | bytes 884736 | tf_op jit(solution)/shard_map/all_to_all | solution.py:389
  48.7 0.2 fusion.23
  48.9 2.3 %copy-done.3 = bf16[128,72,256]{2,1,0:T(8,128)(2,1)S(1)} copy-done((bf16[128,72,256]{2,1,0:T(8,128)(2,1)S(1)}, bf16[128,72,256]{2,1,0:T(8,128)(2,1)}, u32[]{:S(2)}) %copy-start.3) | copy-done | bytes 4718616
  51.3 6.6 %shard_map.89.source_ref = bf16[72,128,256]{2,1,0:T(8,128)(2,1)S(1)} custom-call(bf16[144,72]{1,0:T(8,128)(2,1)S(1)} %pad_maximum_fusion.4.table_ref.low_ref, f32[128,128]{1,0:T(8,128)S(1)} %get-tuple-element.31.contrast_ref, bf16[128,72,256]{2,1,0:T(8,128)(2,1)S(1)} %copy-done.3), custom_call_target="tpu_custom_call" | custom-call | flops 679477248 | bytes 9437184 | tf_op jit(solution)/shard_map/pallas_call | solution.py:69
  57.9 2.1 %copy-done.1 = bf16[72,128,256]{2,1,0:T(8,128)(2,1)} copy-done((bf16[72,128,256]{2,1,0:T(8,128)(2,1)}, bf16[72,128,256]{2,1,0:T(8,128)(2,1)S(1)}, u32[]{:S(2)}) %copy-start.1) | copy-done | bytes 4718616
  60.0 0.2 fusion.18
  60.2 0.2 fusion.19
  60.4 0.1 pad_maximum_fusion.3.turn_ref
  60.5 3.6 %all-to-all-done.2 = bf16[8,3,72,128]{3,2,1,0:T(8,128)(2,1)S(1)} async-done(((bf16[8,3,72,128]{3,2,1,0:T(8,128)(2,1)}), bf16[8,3,72,128]{3,2,1,0:T(8,128)(2,1)S(1)}, u32[]{:S(2)}, u32[]{:S(2)}) %all-to-all-start.2) | async-done | bytes 442400 | tf_op jit(solution)/shard_map/all_to_all | solution.py:389
  64.1 3.1 %collective-permute-start = (bf16[24,72,128]{2,1,0:T(8,128)(2,1)S(1)}, bf16[24,72,128]{2,1,0:T(8,128)(2,1)S(1)}, u32[]{:S(2)}, u32[]{:S(2)}) collective-permute-start(bf16[24,72,128]{2,1,0:T(8,128)(2,1)S(1)} %bitcast.17), channel_id=1, source_target_pairs={{0,8},{8,0},{1,9},{9,1},{2,10},{10,2},{3,11},{11,3},{4,12},{12,4},... | collective-permute-start | bytes 1327112 | tf_op jit(solution)/shard_map/ppermute | solution.py:28
  67.3 1.3 collective-permute-done.other_ref
  68.6 2.3 %copy-done.2 = bf16[72,128,256]{2,1,0:T(8,128)(2,1)S(1)} copy-done((bf16[72,128,256]{2,1,0:T(8,128)(2,1)S(1)}, bf16[72,128,256]{2,1,0:T(8,128)(2,1)}, u32[]{:S(2)}) %copy-start.2) | copy-done | bytes 4718616
  71.0 8.8 %shard_map.90 = (f32[73,24,128]{2,1,0:T(8,128)S(1)}, f32[73,24,128]{2,1,0:T(8,128)S(1)}, f32[1,128]{1,0:T(1,128)S(1)}, f32[1,128]{1,0:T(1,128)S(1)}) custom-call(s32[1]{0:T(128)} %bitcast.core_ref, bf16[24,72,128]{2,1,0:T(8,128)(2,1)S(1)} %bitcast.18, bf16[24,72,128]{2,1,0:T(8,128)(2,1)S(1)} %collective-permute-done.other_ref, ...), custom_call_target="tpu_custom_call" | custom-call | tf_op jit(solution)/shard_map/pallas_call | solution.py:229
  79.8 2.3 %collective-permute-start.1 = (f32[73,24,128]{2,1,0:T(8,128)S(1)}, f32[73,24,128]{2,1,0:T(8,128)S(1)}, u32[]{:S(2)}, u32[]{:S(2)}) collective-permute-start(f32[73,24,128]{2,1,0:T(8,128)S(1)} %get-tuple-element.14), channel_id=1, source_target_pairs={{0,8},{8,0},{1,9},{9,1},{2,10},{10,2},{3,11},{11,3},{4,12},{12,4},... | collective-permute-start | bytes 2691080 | tf_op jit(solution)/shard_map/ppermute | solution.py:28
  82.1 0.1 dynamic_slice.7
  82.2 0.1 reshape.194
  82.3 0.1 copy.15
  82.3 0.1 reshape.195
  82.4 0.2 convert_reduce_fusion
  82.6 1.5 %collective-permute-done.1.got_ref = f32[73,24,128]{2,1,0:T(8,128)S(1)} collective-permute-done((f32[73,24,128]{2,1,0:T(8,128)S(1)}, f32[73,24,128]{2,1,0:T(8,128)S(1)}, u32[]{:S(2)}, u32[]{:S(2)}) %collective-permute-start.1) | collective-permute-done | bytes 897056 | tf_op jit(solution)/shard_map/ppermute | solution.py:28
  84.1 0.9 shard_map.91
  85.0 3.1 %collective-permute-start.2 = (f32[2,128]{1,0:T(2,128)S(1)}, f32[2,128]{1,0:T(2,128)S(1)}, u32[]{:S(2)}, u32[]{:S(2)}) collective-permute-start(f32[2,128]{1,0:T(2,128)S(1)} %pad_maximum_fusion.5), channel_id=1, source_target_pairs={{0,1},{1,0},{2,3},{3,2},{4,5},{5,4},{6,7},{7,6},{8,9},{9,8},{10,11... | collective-permute-start | bytes 3080 | tf_op jit(solution)/shard_map/ppermute | solution.py:395
  88.1 3.5 %all-to-all-start.3 = ((bf16[8,240,128]{2,1,0:T(8,128)(2,1)}), bf16[8,240,128]{2,1,0:T(8,128)(2,1)S(1)}, u32[]{:S(2)}, u32[]{:S(2)}) async-start(bf16[8,240,128]{2,1,0:T(8,128)(2,1)} %bitcast.6), calls=%async_computation.3 | async-start | bytes 983040 | tf_op jit(solution)/shard_map/all_to_all | solution.py:439
  91.7 3.1 %collective-permute-start.3 = (f32[2,128]{1,0:T(2,128)S(1)}, f32[2,128]{1,0:T(2,128)S(1)}, u32[]{:S(2)}, u32[]{:S(2)}) collective-permute-start(f32[2,128]{1,0:T(2,128)S(1)} %pad_maximum_fusion.6), channel_id=1, source_target_pairs={{0,2},{1,3},{2,0},{3,1},{4,6},{5,7},{6,4},{7,5},{8,10},{9,11},{10,... | collective-permute-start | bytes 3080 | tf_op jit(solution)/shard_map/ppermute | solution.py:395
  94.8 1.5 %collective-permute-done.3 = f32[2,128]{1,0:T(2,128)S(1)} collective-permute-done((f32[2,128]{1,0:T(2,128)S(1)}, f32[2,128]{1,0:T(2,128)S(1)}, u32[]{:S(2)}, u32[]{:S(2)}) %collective-permute-start.3) | collective-permute-done | bytes 1056 | tf_op jit(solution)/shard_map/ppermute | solution.py:395
  96.3 4.7 %collective-permute-start.4 = (f32[2,128]{1,0:T(2,128)S(1)}, f32[2,128]{1,0:T(2,128)S(1)}, u32[]{:S(2)}, u32[]{:S(2)}) collective-permute-start(f32[2,128]{1,0:T(2,128)S(1)} %pad_maximum_fusion.7), channel_id=1, source_target_pairs={{0,4},{1,5},{2,6},{3,7},{4,0},{5,1},{6,2},{7,3},{8,12},{9,13},{10,... | collective-permute-start | bytes 3080 | tf_op jit(solution)/shard_map/ppermute | solution.py:395
  101.0 0.1 add.177.place_ref
  101.1 1.3 collective-permute-done.4
  102.4 0.5 add_bitcast_fusion
  103.0 5.8 %all-to-all-done.3.got_ref = bf16[8,240,128]{2,1,0:T(8,128)(2,1)S(1)} async-done(((bf16[8,240,128]{2,1,0:T(8,128)(2,1)}), bf16[8,240,128]{2,1,0:T(8,128)(2,1)S(1)}, u32[]{:S(2)}, u32[]{:S(2)}) %all-to-all-start.3) | async-done | bytes 491552 | tf_op jit(solution)/shard_map/all_to_all | solution.py:439
  108.8 1.4 %shard_map.92 = bf16[2560,128]{1,0:T(8,128)(2,1)} custom-call(s32[1]{0:T(128)} %bitcast.core_ref, s32[1,240]{1,0:T(1,128)S(1)} %add.177.place_ref, bf16[8,240,128]{2,1,0:T(8,128)(2,1)S(1)} %all-to-all-done.3.got_ref), custom_call_target="tpu_custom_call" | custom-call | tf_op jit(solution)/shard_map/pallas_call | solution.py:324
  110.2 5.3 %all-to-all-start.4 = ((bf16[64,40,128]{2,1,0:T(8,128)(2,1)}), bf16[64,40,128]{2,1,0:T(8,128)(2,1)S(1)}, u32[]{:S(2)}, u32[]{:S(2)}) async-start(bf16[64,40,128]{2,1,0:T(8,128)(2,1)} %bitcast.8), calls=%async_computation.4 | async-start | bytes 1310720 | tf_op jit(solution)/shard_map/all_to_all | solution.py:443
  115.5 0.3 fusion.7
  115.9 0.1 copy.13
  116.0 0.1 copy.14
  116.1 21.0 %all-to-all-done.4 = bf16[64,40,128]{2,1,0:T(8,128)(2,1)S(1)} async-done(((bf16[64,40,128]{2,1,0:T(8,128)(2,1)}), bf16[64,40,128]{2,1,0:T(8,128)(2,1)S(1)}, u32[]{:S(2)}, u32[]{:S(2)}) %all-to-all-start.4) | async-done | bytes 655392 | tf_op jit(solution)/shard_map/all_to_all | solution.py:443
  137.1 1.2 shard_map.93
  (35 shorter events, 0.4 us)
Async XLA Ops:
  0.6 13.6 %copy-start = (s32[8,3]{0,1:T(4,128)S(1)}, s32[8,3]{0,1:T(4,128)}, u32[]{:S(2)}) copy-start(s32[8,3]{0,1:T(4,128)} %param.12) | copy-start | bytes 292
  0.6 1.0 copy-start.4
  2.4 24.2 %all-to-all-start = ((bf16[16,72,128]{2,1,0:T(8,128)(2,1)}), bf16[16,72,128]{2,1,0:T(8,128)(2,1)S(1)}, u32[]{:S(2)}, u32[]{:S(2)}) async-start(bf16[16,72,128]{2,1,0:T(8,128)(2,1)} %bitcast.3), calls=%async_computation | async-start | bytes 589824 | tf_op jit(solution)/shard_map/all_to_all | solution.py:385
  27.8 16.0 %all-to-all-start.1 = ((bf16[4,3,72,128]{3,2,1,0:T(8,128)(2,1)}), bf16[4,3,72,128]{3,2,1,0:T(8,128)(2,1)S(1)}, u32[]{:S(2)}, u32[]{:S(2)}) async-start(bf16[4,3,72,128]{3,2,1,0:T(8,128)(2,1)} %shard_map.87), calls=%async_computation.1 | async-start | bytes 442368 | tf_op jit(solution)/shard_map/all_to_all | solution.py:387
  45.2 18.9 %all-to-all-start.2 = ((bf16[8,3,72,128]{3,2,1,0:T(8,128)(2,1)}), bf16[8,3,72,128]{3,2,1,0:T(8,128)(2,1)S(1)}, u32[]{:S(2)}, u32[]{:S(2)}) async-start(bf16[8,3,72,128]{3,2,1,0:T(8,128)(2,1)} %shard_map.88), calls=%async_computation.2 | async-start | bytes 884736 | tf_op jit(solution)/shard_map/all_to_all | solution.py:389
  48.9 2.3 %copy-start.3 = (bf16[128,72,256]{2,1,0:T(8,128)(2,1)S(1)}, bf16[128,72,256]{2,1,0:T(8,128)(2,1)}, u32[]{:S(2)}) copy-start(bf16[128,72,256]{2,1,0:T(8,128)(2,1)} %image_ref.1) | copy-start | bytes 14155780
  51.2 16.0 %copy-start.6 = (s32[128]{0:T(128)S(1)}, s32[128]{0:T(128)}, u32[]{:S(2)}) copy-start(s32[128]{0:T(128)} %param.9) | copy-start | bytes 1540
  51.3 16.1 %copy-start.5 = (s32[128]{0:T(128)S(1)}, s32[128]{0:T(128)}, u32[]{:S(2)}) copy-start(s32[128]{0:T(128)} %param.10) | copy-start | bytes 1540
  57.9 2.2 %copy-start.1 = (bf16[72,128,256]{2,1,0:T(8,128)(2,1)}, bf16[72,128,256]{2,1,0:T(8,128)(2,1)S(1)}, u32[]{:S(2)}) copy-start(bf16[72,128,256]{2,1,0:T(8,128)(2,1)S(1)} %shard_map.89.source_ref) | copy-start | bytes 14155780
  60.0 22.1 %copy-start.7 = (s32[192]{0:T(256)S(1)}, s32[192]{0:T(256)}, u32[]{:S(2)}) copy-start(s32[192]{0:T(256)} %param.11) | copy-start | bytes 2308
  64.1 4.5 %collective-permute-start = (bf16[24,72,128]{2,1,0:T(8,128)(2,1)S(1)}, bf16[24,72,128]{2,1,0:T(8,128)(2,1)S(1)}, u32[]{:S(2)}, u32[]{:S(2)}) collective-permute-start(bf16[24,72,128]{2,1,0:T(8,128)(2,1)S(1)} %bitcast.17), channel_id=1, source_target_pairs={{0,8},{8,0},{1,9},{9,1},{2,10},{10,2},{3,11},{11,3},{4,12},{12,4},... | collective-permute-start | bytes 1327112 | tf_op jit(solution)/shard_map/ppermute | solution.py:28
  68.6 2.3 %copy-start.2 = (bf16[72,128,256]{2,1,0:T(8,128)(2,1)S(1)}, bf16[72,128,256]{2,1,0:T(8,128)(2,1)}, u32[]{:S(2)}) copy-start(bf16[72,128,256]{2,1,0:T(8,128)(2,1)} %copy-done.1) | copy-start | bytes 14155780
  79.8 4.3 %collective-permute-start.1 = (f32[73,24,128]{2,1,0:T(8,128)S(1)}, f32[73,24,128]{2,1,0:T(8,128)S(1)}, u32[]{:S(2)}, u32[]{:S(2)}) collective-permute-start(f32[73,24,128]{2,1,0:T(8,128)S(1)} %get-tuple-element.14), channel_id=1, source_target_pairs={{0,8},{8,0},{1,9},{9,1},{2,10},{10,2},{3,11},{11,3},{4,12},{12,4},... | collective-permute-start | bytes 2691080 | tf_op jit(solution)/shard_map/ppermute | solution.py:28
  85.0 6.6 %collective-permute-start.2 = (f32[2,128]{1,0:T(2,128)S(1)}, f32[2,128]{1,0:T(2,128)S(1)}, u32[]{:S(2)}, u32[]{:S(2)}) collective-permute-start(f32[2,128]{1,0:T(2,128)S(1)} %pad_maximum_fusion.5), channel_id=1, source_target_pairs={{0,1},{1,0},{2,3},{3,2},{4,5},{5,4},{6,7},{7,6},{8,9},{9,8},{10,11... | collective-permute-start | bytes 3080 | tf_op jit(solution)/shard_map/ppermute | solution.py:395
  88.1 20.7 %all-to-all-start.3 = ((bf16[8,240,128]{2,1,0:T(8,128)(2,1)}), bf16[8,240,128]{2,1,0:T(8,128)(2,1)S(1)}, u32[]{:S(2)}, u32[]{:S(2)}) async-start(bf16[8,240,128]{2,1,0:T(8,128)(2,1)} %bitcast.6), calls=%async_computation.3 | async-start | bytes 983040 | tf_op jit(solution)/shard_map/all_to_all | solution.py:439
  91.7 4.6 %collective-permute-start.3 = (f32[2,128]{1,0:T(2,128)S(1)}, f32[2,128]{1,0:T(2,128)S(1)}, u32[]{:S(2)}, u32[]{:S(2)}) collective-permute-start(f32[2,128]{1,0:T(2,128)S(1)} %pad_maximum_fusion.6), channel_id=1, source_target_pairs={{0,2},{1,3},{2,0},{3,1},{4,6},{5,7},{6,4},{7,5},{8,10},{9,11},{10,... | collective-permute-start | bytes 3080 | tf_op jit(solution)/shard_map/ppermute | solution.py:395
  96.3 6.1 %collective-permute-start.4 = (f32[2,128]{1,0:T(2,128)S(1)}, f32[2,128]{1,0:T(2,128)S(1)}, u32[]{:S(2)}, u32[]{:S(2)}) collective-permute-start(f32[2,128]{1,0:T(2,128)S(1)} %pad_maximum_fusion.7), channel_id=1, source_target_pairs={{0,4},{1,5},{2,6},{3,7},{4,0},{5,1},{6,2},{7,3},{8,12},{9,13},{10,... | collective-permute-start | bytes 3080 | tf_op jit(solution)/shard_map/ppermute | solution.py:395
  110.2 26.9 %all-to-all-start.4 = ((bf16[64,40,128]{2,1,0:T(8,128)(2,1)}), bf16[64,40,128]{2,1,0:T(8,128)(2,1)S(1)}, u32[]{:S(2)}, u32[]{:S(2)}) async-start(bf16[64,40,128]{2,1,0:T(8,128)(2,1)} %bitcast.8), calls=%async_computation.4 | async-start | bytes 1310720 | tf_op jit(solution)/shard_map/all_to_all | solution.py:443

commit v4 on v3

--- a/solution.py
+++ b/solution.py
@@ -63,21 +63,22 @@
     out_ref[:, :, CYCLES:] = held_imag[...].reshape(shape).astype(jnp.bfloat16)
 
 
-def image_spectra(images, contrast_rows, table):
-    particles = images.shape[0]
+def image_spectra(images, half, contrast_rows, table):
+    particles = contrast_rows.shape[0]
     count = 16
+    skipped = half * particles // count
     return pl.pallas_call(
         spectra_kernel,
         grid=(particles // count,),
         in_specs=[
             pl.BlockSpec((2 * ANGLES, ANGLES), lambda i: (0, 0)),
             pl.BlockSpec((count, CYCLES), lambda i: (i, 0)),
-            pl.BlockSpec((count, ANGLES, 2 * CYCLES), lambda i: (i, 0, 0)),
+            pl.BlockSpec((count, ANGLES, 2 * CYCLES), lambda i: (i + skipped, 0, 0)),
         ],
         out_specs=pl.BlockSpec((ANGLES, count, 2 * CYCLES), lambda i: (0, i, 0)),
         out_shape=jax.ShapeDtypeStruct((ANGLES, particles, 2 * CYCLES), jnp.bfloat16),
         scratch_shapes=[pltpu.VMEM((ANGLES * count, CYCLES), jnp.float32)] * 2,
-        compiler_params=pltpu.CompilerParams(vmem_limit_bytes=8 * 1024 * 1024),
+        compiler_params=pltpu.CompilerParams(vmem_limit_bytes=56 * 1024 * 1024),
         cost_estimate=pl.CostEstimate(
             flops=particles * 4 * ANGLES * ANGLES * 2 * CYCLES,
             bytes_accessed=4 * particles * ANGLES * 2 * CYCLES,
@@ -111,7 +112,8 @@
     core_ref,
     mine_ref,
     other_ref,
-    source_ref,
+    early_ref,
+    late_ref,
     low_ref,
     turn_ref,
     back_ref,
@@ -131,8 +133,14 @@
     sem,
 ):
     particles = spectra_ref.shape[1]
-    arriving = pltpu.make_async_copy(source_ref, spectra_ref, sem)
-    arriving.start()
+    arriving = [
+        pltpu.make_async_copy(
+            source, spectra_ref.at[:, pl.ds(k * particles // 2, particles // 2)], sem.at[k]
+        )
+        for k, source in enumerate((early_ref, late_ref))
+    ]
+    for copy in arriving:
+        copy.start()
     first = core_ref[0] == 0
     table = low_ref[...]
     for c in range(CLS_GRP):
@@ -151,7 +159,8 @@
     energy = 0.5 * lax.dot_general(
         power[...], square, across, precision=TOP_PRECISION, preferred_element_type=jnp.float32
     )
-    arriving.wait()
+    for copy in arriving:
+        copy.wait()
     for m in range(ANGLES):
         rows = slice(m * CLS_GRP, (m + 1) * CLS_GRP)
         real, imag = ref_real[rows, :], ref_imag[rows, :]
@@ -221,15 +230,15 @@
     send_ref[ANGLES] = denom
 
 
-def score(core, mine, other, spectra, low_table, turn, back, square, prior, member):
-    particles = spectra.shape[1]
+def score(core, mine, other, early, late, low_table, turn, back, square, prior, member):
+    particles = 2 * early.shape[1]
     sums = jax.ShapeDtypeStruct((ANGLES + 1, CLS_GRP, CYCLES), jnp.float32)
     row = jax.ShapeDtypeStruct((1, particles), jnp.float32)
     vmem = pl.BlockSpec(memory_space=pltpu.VMEM)
     return pl.pallas_call(
         score_kernel,
         in_specs=[pl.BlockSpec(memory_space=pltpu.SMEM), vmem, vmem]
-        + [pl.BlockSpec(memory_space=pltpu.HBM)]
+        + [pl.BlockSpec(memory_space=pltpu.HBM)] * 2
         + [vmem] * 6,
         out_specs=(vmem, vmem, vmem, vmem),
         out_shape=(sums, sums, row, row),
@@ -240,10 +249,10 @@
             pltpu.VMEM((CLS_GRP, ANGLES, particles), jnp.float32),
             pltpu.VMEM((CLS_GRP, CYCLES), jnp.float32),
             pltpu.VMEM((ANGLES, particles, 2 * CYCLES), jnp.bfloat16),
-            pltpu.SemaphoreType.DMA,
+            pltpu.SemaphoreType.DMA((2,)),
         ],
-        compiler_params=pltpu.CompilerParams(vmem_limit_bytes=20 * 1024 * 1024),
-    )(core, mine, other, spectra, low_table, turn, back, square, prior, member)
+        compiler_params=pltpu.CompilerParams(vmem_limit_bytes=50 * 1024 * 1024),
+    )(core, mine, other, early, late, low_table, turn, back, square, prior, member)
 
 
 def pack_kernel(keep_ref, got_ref, out_ref):
@@ -294,7 +303,7 @@
         out_specs=pl.BlockSpec(memory_space=pltpu.HBM),
         out_shape=jax.ShapeDtypeStruct((BLOCK, 2, ANGLES, CYCLES), jnp.bfloat16),
         scratch_shapes=[pltpu.SemaphoreType.DMA((2,))],
-        compiler_params=pltpu.CompilerParams(vmem_limit_bytes=1024 * 1024),
+        compiler_params=pltpu.CompilerParams(vmem_limit_bytes=62 * 1024 * 1024),
     )(blocks)
 
 
@@ -380,23 +389,26 @@
     return jnp.concatenate([real, imag])
 
 
-def fetch(blocks, holders):
+def fetch(blocks, holders, images, contrast_rows, table):
+    half = contrast_rows.shape[0] // 2
     halves = halve(blocks).reshape(BLOCK * 2, ANGLES, CYCLES)
     sliced = lax.all_to_all(halves, ("wide_1", "wide_2"), 0, 0, tiled=True)
+    early = image_spectra(images, 0, contrast_rows[:half], table)
+    sliced, early, later = lax.optimization_barrier((sliced, early, contrast_rows[half:]))
     picked = pick(sliced[:, None], holders % 16, 4)
     planes = lax.all_to_all(picked, "wide_0", 0, 0, tiled=True)
+    late = image_spectra(images, 1, later, table)
+    planes, late = lax.optimization_barrier((planes, late))
     picked = pick(planes, holders // 16, 8)
-    return lax.all_to_all(picked, "wide_1", 0, 0, tiled=True).reshape(CLS_GRP, ANGLES, CYCLES)
-
-
-def joined_evidence(top, total):
-    for bit in (1, 2, 4):
-        pair = jnp.concatenate([top, total])
-        got = lax.ppermute(pair, "narrow", [(k, k ^ bit) for k in range(8)])
-        joined = jnp.maximum(top, got[:1])
-        total = total * jnp.exp(top - joined) + got[1:] * jnp.exp(got[:1] - joined)
-        top = joined
-    return (top + jnp.log(total)).reshape(-1)
+    mine = lax.all_to_all(picked, "wide_1", 0, 0, tiled=True).reshape(CLS_GRP, ANGLES, CYCLES)
+    return mine, early, late
+
+
+def exchanged_evidence(top, total, bit):
+    pair = jnp.concatenate([top, total])
+    got = lax.ppermute(pair, "narrow", [(k, k ^ bit) for k in range(8)])
+    joined = jnp.maximum(top, got[:1])
+    return joined, total * jnp.exp(top - joined) + got[1:] * jnp.exp(got[:1] - joined)
 
 
 def per_device(images, defocus, class_index, rotation_index, owner_map, roster, ref_store):
@@ -419,12 +431,10 @@
     square = contrast_rows * contrast_rows
     prior = rotation_prior(rotation_index).T
     member = (class_index[None, :] == class_ids[:, None]).astype(jnp.float32)
-    spectra = image_spectra(images, contrast_rows, low_table)
-
-    mine = fetch(ref_store[0, 0], holders)
+    mine, early, late = fetch(ref_store[0, 0], holders, images, contrast_rows, low_table)
     other = swapped(mine)
     keep, send, top, total = score(
-        core.reshape(1), mine, other, spectra, low_table, turn, back, square, prior, member
+        core.reshape(1), mine, other, early, late, low_table, turn, back, square, prior, member
     )
     owners = lax.dynamic_slice_in_dim(owner_map, leading_class, CLS_GRP)
     owners = owners.reshape(STEPS, BLOCK).T.reshape(CLS_GRP)
@@ -437,11 +447,15 @@
     share = pack(keep, swapped(send)).reshape(8, (ROWS + 1) * CLS_GRP, CYCLES)
     top, total, share = lax.optimization_barrier((top, total, share))
     share = lax.all_to_all(share, "wide_1", 0, 0, tiled=True)
-    log_evidence = joined_evidence(top, total)
-    share, log_evidence = lax.optimization_barrier((share, log_evidence))
+    top, total = exchanged_evidence(top, total, 1)
+    share, top, total = lax.optimization_barrier((share, top, total))
     sent = route(core.reshape(1), place, share).reshape(64, (ROWS + 1) * OWN_MAX, CYCLES)
+    top, total, sent = lax.optimization_barrier((top, total, sent))
     got = lax.all_to_all(sent, WIDE, 0, 0, tiled=True)
     got = got.reshape(4, 16 * (ROWS + 1) * OWN_MAX, CYCLES)
+    top, total = exchanged_evidence(top, total, 2)
+    top, total = exchanged_evidence(top, total, 4)
+    log_evidence = (top + jnp.log(total)).reshape(-1)
     new_references = finish(table, got).reshape(1, 1, OWN_MAX, ANGLES, 2 * CYCLES)
     return (new_references, log_evidence)
 

time: 139 us -> 148 us (1.065)
  the two profiles are of different devices: /device:TPU:1 before, /device:TPU:77 now
where the time goes in v4:
time: 148 us; the launch traced here: 147 us
  waiting for transfers between devices  54.1 us (37%)
  starting transfers between devices  49.3 us (33%)
  Pallas kernels  37.8 us (26%)
  other arithmetic  3.58 us (2%)
    all_to_all x1, waiting for transfers between devices, per_device(): got = lax.all_to_all(sent, WIDE, 0, 0, tiled=True)  16.6 us
    all_to_all x1, waiting for transfers between devices, fetch(): lax.all_to_all(picked, 'wide_1', 0, 0, tiled=True)  11.3 us
    pallas_call x2, Pallas kernels, image_spectra(): pl.pallas_call(spectra_kernel, grid=(particles // count,), in_specs=[pl.B...  11.2 us
    all_to_all x1, waiting for transfers between devices, per_device(): share = lax.all_to_all(share, 'wide_1', 0, 0, tiled=True)  10.5 us
    pallas_call x1, Pallas kernels, score(): pl.pallas_call(score_kernel, in_specs=[pl.BlockSpec(memory_space=pltpu.SM...  10.5 us
    all_to_all x1, starting transfers between devices, fetch(): sliced = lax.all_to_all(halves, ('wide_1', 'wide_2'), 0, 0, tiled=True)  10.3 us
    pallas_call x1, Pallas kernels, halve(): pl.pallas_call(halve_kernel, in_specs=[pl.BlockSpec(memory_space=pltpu.HB...  10.1 us
    ppermute x2, starting transfers between devices, swapped(): return lax.ppermute(x, 'wide_2', [(0, 1), (1, 0)])  8.01 us
  transfers between devices with their start and end apart: 10, of which 10 were waited for; matrix products, arithmetic and copies ran while one was open for 3% of the time, Pallas kernels for 8%

profile of v4, /device:TPU:77, one launch (start us, length us, event | category | flops | bytes accessed | tf_op | source)
XLA Modules:
  0.0 147.1 jit_solution(18053978552848961797)
XLA Ops:
  0.6 10.1 %shard_map.86 = bf16[8,2,72,128]{3,2,1,0:T(8,128)(2,1)} custom-call(bf16[8,72,256]{2,1,0:T(8,128)(2,1)} %bitcast.21), custom_call_target="tpu_custom_call" | custom-call | tf_op jit(solution)/shard_map/pallas_call | solution.py:300
  10.7 10.3 %all-to-all-start = ((bf16[16,72,128]{2,1,0:T(8,128)(2,1)}), bf16[16,72,128]{2,1,0:T(8,128)(2,1)S(1)}, u32[]{:S(2)}, u32[]{:S(2)}) async-start(bf16[16,72,128]{2,1,0:T(8,128)(2,1)} %bitcast.20), calls=%async_computation | async-start | bytes 589824 | tf_op jit(solution)/shard_map/all_to_all | solution.py:395
  21.0 0.2 fusion.23
  21.2 0.7 multiply_multiply_fusion
  21.9 0.3 fusion.21
  22.2 0.2 dynamic-slice_reduce_fusion
  22.4 0.6 pad_maximum_fusion.4.table_ref.low_ref
  23.0 0.6 fusion.29
  23.7 5.6 %shard_map.87.early_ref = bf16[72,64,256]{2,1,0:T(8,128)(2,1)} custom-call(bf16[144,72]{1,0:T(8,128)(2,1)} %pad_maximum_fusion.4.table_ref.low_ref, f32[64,128]{1,0:T(8,128)} %get-tuple-element.41.contrast_ref, bf16[128,72,256]{2,1,0:T(8,128)(2,1)} %image_ref.3), custom_call_target="tpu_custom_call" | custom-call | flops 339738624 | bytes 4718592 | tf_op jit(solution)/shard_map/pallas_call | solution.py:70
  29.2 2.2 %all-to-all-done = bf16[16,72,128]{2,1,0:T(8,128)(2,1)S(1)} async-done(((bf16[16,72,128]{2,1,0:T(8,128)(2,1)}), bf16[16,72,128]{2,1,0:T(8,128)(2,1)S(1)}, u32[]{:S(2)}, u32[]{:S(2)}) %all-to-all-start) | async-done | bytes 294944 | tf_op jit(solution)/shard_map/all_to_all | solution.py:395
  31.4 1.3 shard_map.88
  32.7 5.9 %all-to-all-start.1 = ((bf16[4,3,72,128]{3,2,1,0:T(8,128)(2,1)}), bf16[4,3,72,128]{3,2,1,0:T(8,128)(2,1)S(1)}, u32[]{:S(2)}, u32[]{:S(2)}) async-start(bf16[4,3,72,128]{3,2,1,0:T(8,128)(2,1)} %shard_map.88), calls=%async_computation.1 | async-start | bytes 442368 | tf_op jit(solution)/shard_map/all_to_all | solution.py:399
  38.6 5.6 %shard_map.89.late_ref = bf16[72,64,256]{2,1,0:T(8,128)(2,1)} custom-call(bf16[144,72]{1,0:T(8,128)(2,1)} %pad_maximum_fusion.4.table_ref.low_ref, f32[64,128]{1,0:T(8,128)} %get-tuple-element.21.contrast_ref, bf16[128,72,256]{2,1,0:T(8,128)(2,1)} %image_ref.3), custom_call_target="tpu_custom_call" | custom-call | flops 339738624 | bytes 4718592 | tf_op jit(solution)/shard_map/pallas_call | solution.py:70
  44.3 3.0 %all-to-all-done.1.source_ref = bf16[4,3,72,128]{3,2,1,0:T(8,128)(2,1)S(1)} async-done(((bf16[4,3,72,128]{3,2,1,0:T(8,128)(2,1)}), bf16[4,3,72,128]{3,2,1,0:T(8,128)(2,1)S(1)}, u32[]{:S(2)}, u32[]{:S(2)}) %all-to-all-start.1) | async-done | bytes 221216 | tf_op jit(solution)/shard_map/all_to_all | solution.py:399
  47.3 1.4 shard_map.90
  48.7 6.7 %all-to-all-start.2 = ((bf16[8,3,72,128]{3,2,1,0:T(8,128)(2,1)}), bf16[8,3,72,128]{3,2,1,0:T(8,128)(2,1)S(1)}, u32[]{:S(2)}, u32[]{:S(2)}) async-start(bf16[8,3,72,128]{3,2,1,0:T(8,128)(2,1)} %shard_map.90), calls=%async_computation.2 | async-start | bytes 884736 | tf_op jit(solution)/shard_map/all_to_all | solution.py:403
  55.4 0.2 fusion.18
  55.6 0.2 fusion.19
  55.7 0.1 pad_maximum_fusion.3.turn_ref
  55.8 11.3 %all-to-all-done.2 = bf16[8,3,72,128]{3,2,1,0:T(8,128)(2,1)S(1)} async-done(((bf16[8,3,72,128]{3,2,1,0:T(8,128)(2,1)}), bf16[8,3,72,128]{3,2,1,0:T(8,128)(2,1)S(1)}, u32[]{:S(2)}, u32[]{:S(2)}) %all-to-all-start.2) | async-done | bytes 442400 | tf_op jit(solution)/shard_map/all_to_all | solution.py:403
  67.1 5.7 %collective-permute-start = (bf16[24,72,128]{2,1,0:T(8,128)(2,1)S(1)}, bf16[24,72,128]{2,1,0:T(8,128)(2,1)S(1)}, u32[]{:S(2)}, u32[]{:S(2)}) collective-permute-start(bf16[24,72,128]{2,1,0:T(8,128)(2,1)S(1)} %bitcast.17), channel_id=1, source_target_pairs={{0,8},{8,0},{1,9},{9,1},{2,10},{10,2},{3,11},{11,3},{4,12},{12,4},... | collective-permute-start | bytes 1327112 | tf_op jit(solution)/shard_map/ppermute | solution.py:28
  72.9 1.3 collective-permute-done.other_ref
  74.2 10.5 %shard_map.91 = (f32[73,24,128]{2,1,0:T(8,128)S(1)}, f32[73,24,128]{2,1,0:T(8,128)S(1)}, f32[1,128]{1,0:T(1,128)S(1)}, f32[1,128]{1,0:T(1,128)S(1)}) custom-call(s32[1]{0:T(128)} %bitcast.core_ref, bf16[24,72,128]{2,1,0:T(8,128)(2,1)S(1)} %bitcast.18, bf16[24,72,128]{2,1,0:T(8,128)(2,1)S(1)} %collective-permute-done.other_ref, ...), custom_call_target="tpu_custom_call" | custom-call | tf_op jit(solution)/shard_map/pallas_call | solution.py:238
  84.8 2.3 %collective-permute-start.1 = (f32[73,24,128]{2,1,0:T(8,128)S(1)}, f32[73,24,128]{2,1,0:T(8,128)S(1)}, u32[]{:S(2)}, u32[]{:S(2)}) collective-permute-start(f32[73,24,128]{2,1,0:T(8,128)S(1)} %get-tuple-element.28), channel_id=1, source_target_pairs={{0,8},{8,0},{1,9},{9,1},{2,10},{10,2},{3,11},{11,3},{4,12},{12,4},... | collective-permute-start | bytes 2691080 | tf_op jit(solution)/shard_map/ppermute | solution.py:28
  87.1 0.1 dynamic_slice.8
  87.1 0.1 reshape.197
  87.2 0.1 copy.15
  87.3 0.1 reshape.198
  87.4 0.2 convert_reduce_fusion
  87.6 1.5 %collective-permute-done.1.got_ref = f32[73,24,128]{2,1,0:T(8,128)S(1)} collective-permute-done((f32[73,24,128]{2,1,0:T(8,128)S(1)}, f32[73,24,128]{2,1,0:T(8,128)S(1)}, u32[]{:S(2)}, u32[]{:S(2)}) %collective-permute-start.1) | collective-permute-done | bytes 897056 | tf_op jit(solution)/shard_map/ppermute | solution.py:28
  89.1 0.9 shard_map.92
  90.0 4.6 %all-to-all-start.3 = ((bf16[8,240,128]{2,1,0:T(8,128)(2,1)}), bf16[8,240,128]{2,1,0:T(8,128)(2,1)S(1)}, u32[]{:S(2)}, u32[]{:S(2)}) async-start(bf16[8,240,128]{2,1,0:T(8,128)(2,1)} %bitcast.5), calls=%async_computation.3 | async-start | bytes 983040 | tf_op jit(solution)/shard_map/all_to_all | solution.py:449
  94.6 2.2 %collective-permute-start.2 = (f32[2,128]{1,0:T(2,128)S(1)}, f32[2,128]{1,0:T(2,128)S(1)}, u32[]{:S(2)}, u32[]{:S(2)}) collective-permute-start(f32[2,128]{1,0:T(2,128)S(1)} %pad_maximum_fusion.5), channel_id=1, source_target_pairs={{0,1},{1,0},{2,3},{3,2},{4,5},{5,4},{6,7},{7,6},{8,9},{9,8},{10,11... | collective-permute-start | bytes 3080 | tf_op jit(solution)/shard_map/ppermute | solution.py:409
  96.8 0.1 add.185.place_ref
  96.9 2.3 %collective-permute-done.2 = f32[2,128]{1,0:T(2,128)S(1)} collective-permute-done((f32[2,128]{1,0:T(2,128)S(1)}, f32[2,128]{1,0:T(2,128)S(1)}, u32[]{:S(2)}, u32[]{:S(2)}) %collective-permute-start.2) | collective-permute-done | bytes 1056 | tf_op jit(solution)/shard_map/ppermute | solution.py:409
  99.2 10.5 %all-to-all-done.3.got_ref = bf16[8,240,128]{2,1,0:T(8,128)(2,1)S(1)} async-done(((bf16[8,240,128]{2,1,0:T(8,128)(2,1)}), bf16[8,240,128]{2,1,0:T(8,128)(2,1)S(1)}, u32[]{:S(2)}, u32[]{:S(2)}) %all-to-all-start.3) | async-done | bytes 491552 | tf_op jit(solution)/shard_map/all_to_all | solution.py:449
  109.7 1.4 shard_map.93
  111.1 6.6 %all-to-all-start.4 = ((bf16[64,40,128]{2,1,0:T(8,128)(2,1)}), bf16[64,40,128]{2,1,0:T(8,128)(2,1)S(1)}, u32[]{:S(2)}, u32[]{:S(2)}) async-start(bf16[64,40,128]{2,1,0:T(8,128)(2,1)} %bitcast.7), calls=%async_computation.4 | async-start | bytes 1310720 | tf_op jit(solution)/shard_map/all_to_all | solution.py:454
  117.7 0.3 fusion.7
  118.1 2.8 %collective-permute-start.3 = (f32[2,128]{1,0:T(2,128)S(1)}, f32[2,128]{1,0:T(2,128)S(1)}, u32[]{:S(2)}, u32[]{:S(2)}) collective-permute-start(f32[2,128]{1,0:T(2,128)S(1)} %pad_maximum_fusion.6), channel_id=1, source_target_pairs={{0,2},{1,3},{2,0},{3,1},{4,6},{5,7},{6,4},{7,5},{8,10},{9,11},{10,... | collective-permute-start | bytes 3080 | tf_op jit(solution)/shard_map/ppermute | solution.py:409
  121.0 0.1 copy.13
  121.1 0.1 copy.14
  121.2 1.5 %collective-permute-done.3 = f32[2,128]{1,0:T(2,128)S(1)} collective-permute-done((f32[2,128]{1,0:T(2,128)S(1)}, f32[2,128]{1,0:T(2,128)S(1)}, u32[]{:S(2)}, u32[]{:S(2)}) %collective-permute-start.3) | collective-permute-done | bytes 1056 | tf_op jit(solution)/shard_map/ppermute | solution.py:409
  122.8 2.1 %collective-permute-start.4 = (f32[2,128]{1,0:T(2,128)S(1)}, f32[2,128]{1,0:T(2,128)S(1)}, u32[]{:S(2)}, u32[]{:S(2)}) collective-permute-start(f32[2,128]{1,0:T(2,128)S(1)} %pad_maximum_fusion.7), channel_id=1, source_target_pairs={{0,4},{1,5},{2,6},{3,7},{4,0},{5,1},{6,2},{7,3},{8,12},{9,13},{10,... | collective-permute-start | bytes 3080 | tf_op jit(solution)/shard_map/ppermute | solution.py:409
  124.9 3.9 %collective-permute-done.4 = f32[2,128]{1,0:T(2,128)S(1)} collective-permute-done((f32[2,128]{1,0:T(2,128)S(1)}, f32[2,128]{1,0:T(2,128)S(1)}, u32[]{:S(2)}, u32[]{:S(2)}) %collective-permute-start.4) | collective-permute-done | bytes 1056 | tf_op jit(solution)/shard_map/ppermute | solution.py:409
  128.9 0.5 add_bitcast_fusion
  129.4 16.6 %all-to-all-done.4 = bf16[64,40,128]{2,1,0:T(8,128)(2,1)S(1)} async-done(((bf16[64,40,128]{2,1,0:T(8,128)(2,1)}), bf16[64,40,128]{2,1,0:T(8,128)(2,1)S(1)}, u32[]{:S(2)}, u32[]{:S(2)}) %all-to-all-start.4) | async-done | bytes 655392 | tf_op jit(solution)/shard_map/all_to_all | solution.py:454
  146.0 1.2 shard_map.94
  (31 shorter events, 0.4 us)
Async XLA Ops:
  0.6 21.6 %copy-start = (s32[8,3]{0,1:T(4,128)S(1)}, s32[8,3]{0,1:T(4,128)}, u32[]{:S(2)}) copy-start(s32[8,3]{0,1:T(4,128)} %param.12) | copy-start | bytes 292
  10.7 20.7 %all-to-all-start = ((bf16[16,72,128]{2,1,0:T(8,128)(2,1)}), bf16[16,72,128]{2,1,0:T(8,128)(2,1)S(1)}, u32[]{:S(2)}, u32[]{:S(2)}) async-start(bf16[16,72,128]{2,1,0:T(8,128)(2,1)} %bitcast.20), calls=%async_computation | async-start | bytes 589824 | tf_op jit(solution)/shard_map/all_to_all | solution.py:395
  32.7 14.6 %all-to-all-start.1 = ((bf16[4,3,72,128]{3,2,1,0:T(8,128)(2,1)}), bf16[4,3,72,128]{3,2,1,0:T(8,128)(2,1)S(1)}, u32[]{:S(2)}, u32[]{:S(2)}) async-start(bf16[4,3,72,128]{3,2,1,0:T(8,128)(2,1)} %shard_map.88), calls=%async_computation.1 | async-start | bytes 442368 | tf_op jit(solution)/shard_map/all_to_all | solution.py:399
  38.6 34.2 %copy-start.3 = (s32[128]{0:T(128)S(1)}, s32[128]{0:T(128)}, u32[]{:S(2)}) copy-start(s32[128]{0:T(128)} %param.9) | copy-start | bytes 1540
  38.6 34.3 %copy-start.2 = (s32[128]{0:T(128)S(1)}, s32[128]{0:T(128)}, u32[]{:S(2)}) copy-start(s32[128]{0:T(128)} %param.10) | copy-start | bytes 1540
  38.6 35.6 %copy-start.1 = (bf16[144,72]{1,0:T(8,128)(2,1)S(1)}, bf16[144,72]{1,0:T(8,128)(2,1)}, u32[]{:S(2)}) copy-start(bf16[144,72]{1,0:T(8,128)(2,1)} %pad_maximum_fusion.4.table_ref.low_ref) | copy-start | bytes 62212
  48.7 18.5 %all-to-all-start.2 = ((bf16[8,3,72,128]{3,2,1,0:T(8,128)(2,1)}), bf16[8,3,72,128]{3,2,1,0:T(8,128)(2,1)S(1)}, u32[]{:S(2)}, u32[]{:S(2)}) async-start(bf16[8,3,72,128]{3,2,1,0:T(8,128)(2,1)} %shard_map.90), calls=%async_computation.2 | async-start | bytes 884736 | tf_op jit(solution)/shard_map/all_to_all | solution.py:403
  67.1 7.1 %collective-permute-start = (bf16[24,72,128]{2,1,0:T(8,128)(2,1)S(1)}, bf16[24,72,128]{2,1,0:T(8,128)(2,1)S(1)}, u32[]{:S(2)}, u32[]{:S(2)}) collective-permute-start(bf16[24,72,128]{2,1,0:T(8,128)(2,1)S(1)} %bitcast.17), channel_id=1, source_target_pairs={{0,8},{8,0},{1,9},{9,1},{2,10},{10,2},{3,11},{11,3},{4,12},{12,4},... | collective-permute-start | bytes 1327112 | tf_op jit(solution)/shard_map/ppermute | solution.py:28
  74.2 12.8 %copy-start.4 = (s32[192]{0:T(256)S(1)}, s32[192]{0:T(256)}, u32[]{:S(2)}) copy-start(s32[192]{0:T(256)} %param.11) | copy-start | bytes 2308
  84.8 4.3 %collective-permute-start.1 = (f32[73,24,128]{2,1,0:T(8,128)S(1)}, f32[73,24,128]{2,1,0:T(8,128)S(1)}, u32[]{:S(2)}, u32[]{:S(2)}) collective-permute-start(f32[73,24,128]{2,1,0:T(8,128)S(1)} %get-tuple-element.28), channel_id=1, source_target_pairs={{0,8},{8,0},{1,9},{9,1},{2,10},{10,2},{3,11},{11,3},{4,12},{12,4},... | collective-permute-start | bytes 2691080 | tf_op jit(solution)/shard_map/ppermute | solution.py:28
  90.0 19.7 %all-to-all-start.3 = ((bf16[8,240,128]{2,1,0:T(8,128)(2,1)}), bf16[8,240,128]{2,1,0:T(8,128)(2,1)S(1)}, u32[]{:S(2)}, u32[]{:S(2)}) async-start(bf16[8,240,128]{2,1,0:T(8,128)(2,1)} %bitcast.5), calls=%async_computation.3 | async-start | bytes 983040 | tf_op jit(solution)/shard_map/all_to_all | solution.py:449
  94.6 4.6 %collective-permute-start.2 = (f32[2,128]{1,0:T(2,128)S(1)}, f32[2,128]{1,0:T(2,128)S(1)}, u32[]{:S(2)}, u32[]{:S(2)}) collective-permute-start(f32[2,128]{1,0:T(2,128)S(1)} %pad_maximum_fusion.5), channel_id=1, source_target_pairs={{0,1},{1,0},{2,3},{3,2},{4,5},{5,4},{6,7},{7,6},{8,9},{9,8},{10,11... | collective-permute-start | bytes 3080 | tf_op jit(solution)/shard_map/ppermute | solution.py:409
  111.1 34.9 %all-to-all-start.4 = ((bf16[64,40,128]{2,1,0:T(8,128)(2,1)}), bf16[64,40,128]{2,1,0:T(8,128)(2,1)S(1)}, u32[]{:S(2)}, u32[]{:S(2)}) async-start(bf16[64,40,128]{2,1,0:T(8,128)(2,1)} %bitcast.7), calls=%async_computation.4 | async-start | bytes 1310720 | tf_op jit(solution)/shard_map/all_to_all | solution.py:454
  118.1 4.6 %collective-permute-start.3 = (f32[2,128]{1,0:T(2,128)S(1)}, f32[2,128]{1,0:T(2,128)S(1)}, u32[]{:S(2)}, u32[]{:S(2)}) collective-permute-start(f32[2,128]{1,0:T(2,128)S(1)} %pad_maximum_fusion.6), channel_id=1, source_target_pairs={{0,2},{1,3},{2,0},{3,1},{4,6},{5,7},{6,4},{7,5},{8,10},{9,11},{10,... | collective-permute-start | bytes 3080 | tf_op jit(solution)/shard_map/ppermute | solution.py:409
  122.8 6.1 %collective-permute-start.4 = (f32[2,128]{1,0:T(2,128)S(1)}, f32[2,128]{1,0:T(2,128)S(1)}, u32[]{:S(2)}, u32[]{:S(2)}) collective-permute-start(f32[2,128]{1,0:T(2,128)S(1)} %pad_maximum_fusion.7), channel_id=1, source_target_pairs={{0,4},{1,5},{2,6},{3,7},{4,0},{5,1},{6,2},{7,3},{8,12},{9,13},{10,... | collective-permute-start | bytes 3080 | tf_op jit(solution)/shard_map/ppermute | solution.py:409

commit v5 on v4

--- a/solution.py
+++ b/solution.py
@@ -16,6 +16,8 @@
 CLS_GRP = 24
 SIGMA_ROT = 8
 ROWS = 9
+EVIDENCE_ROWS = 256
+CHUNKS = 4
 WIDE = ("wide_0", "wide_1", "wide_2")
 
 
@@ -122,8 +124,7 @@
     member_ref,
     keep_ref,
     send_ref,
-    top_ref,
-    sum_ref,
+    evidence_ref,
     ref_real,
     ref_imag,
     corr,
@@ -133,10 +134,14 @@
     sem,
 ):
     particles = spectra_ref.shape[1]
+    depth, half = ANGLES // CHUNKS, particles // 2
     arriving = [
         pltpu.make_async_copy(
-            source, spectra_ref.at[:, pl.ds(k * particles // 2, particles // 2)], sem.at[k]
-        )
+            source.at[pl.ds(n * depth, depth)],
+            spectra_ref.at[pl.ds(n * depth, depth), pl.ds(k * half, half)],
+            sem.at[n, k],
+        )
+        for n in range(CHUNKS)
         for k, source in enumerate((early_ref, late_ref))
     ]
     for copy in arriving:
@@ -159,9 +164,10 @@
     energy = 0.5 * lax.dot_general(
         power[...], square, across, precision=TOP_PRECISION, preferred_element_type=jnp.float32
     )
-    for copy in arriving:
-        copy.wait()
     for m in range(ANGLES):
+        if m % depth == 0:
+            for copy in arriving[m // depth * 2 : m // depth * 2 + 2]:
+                copy.wait()
         rows = slice(m * CLS_GRP, (m + 1) * CLS_GRP)
         real, imag = ref_real[rows, :], ref_imag[rows, :]
         both = jnp.concatenate(
@@ -201,8 +207,9 @@
     total = jnp.zeros((ANGLES, particles), jnp.float32)
     for c in range(CLS_GRP):
         total = total + jnp.exp(scores[c] - top)
-    top_ref[...] = top
-    sum_ref[...] = jnp.sum(total, axis=0, keepdims=True)
+    evidence_ref[...] = jnp.zeros_like(evidence_ref)
+    evidence_ref[0:1, :] = top
+    evidence_ref[1:2, :] = jnp.sum(total, axis=0, keepdims=True)
     weight = jnp.exp(own - jnp.max(own, axis=0, keepdims=True))
     weight = weight / jnp.sum(weight, axis=0, keepdims=True)
     turned_back = jnp.dot(
@@ -233,15 +240,15 @@
 def score(core, mine, other, early, late, low_table, turn, back, square, prior, member):
     particles = 2 * early.shape[1]
     sums = jax.ShapeDtypeStruct((ANGLES + 1, CLS_GRP, CYCLES), jnp.float32)
-    row = jax.ShapeDtypeStruct((1, particles), jnp.float32)
+    evidence = jax.ShapeDtypeStruct((EVIDENCE_ROWS, particles), jnp.float32)
     vmem = pl.BlockSpec(memory_space=pltpu.VMEM)
     return pl.pallas_call(
         score_kernel,
         in_specs=[pl.BlockSpec(memory_space=pltpu.SMEM), vmem, vmem]
         + [pl.BlockSpec(memory_space=pltpu.HBM)] * 2
         + [vmem] * 6,
-        out_specs=(vmem, vmem, vmem, vmem),
-        out_shape=(sums, sums, row, row),
+        out_specs=(vmem, vmem, vmem),
+        out_shape=(sums, sums, evidence),
         scratch_shapes=[
             pltpu.VMEM((ANGLES * CLS_GRP, CYCLES), jnp.float32),
             pltpu.VMEM((ANGLES * CLS_GRP, CYCLES), jnp.float32),
@@ -249,7 +256,7 @@
             pltpu.VMEM((CLS_GRP, ANGLES, particles), jnp.float32),
             pltpu.VMEM((CLS_GRP, CYCLES), jnp.float32),
             pltpu.VMEM((ANGLES, particles, 2 * CYCLES), jnp.bfloat16),
-            pltpu.SemaphoreType.DMA((2,)),
+            pltpu.SemaphoreType.DMA((CHUNKS, 2)),
         ],
         compiler_params=pltpu.CompilerParams(vmem_limit_bytes=50 * 1024 * 1024),
     )(core, mine, other, early, late, low_table, turn, back, square, prior, member)
@@ -299,11 +306,11 @@
 def halve(blocks):
     return pl.pallas_call(
         halve_kernel,
-        in_specs=[pl.BlockSpec(memory_space=pltpu.HBM)],
-        out_specs=pl.BlockSpec(memory_space=pltpu.HBM),
+        in_specs=[pl.BlockSpec(memory_space=pl.ANY)],
+        out_specs=pl.BlockSpec(memory_space=pl.ANY),
         out_shape=jax.ShapeDtypeStruct((BLOCK, 2, ANGLES, CYCLES), jnp.bfloat16),
         scratch_shapes=[pltpu.SemaphoreType.DMA((2,))],
-        compiler_params=pltpu.CompilerParams(vmem_limit_bytes=62 * 1024 * 1024),
+        compiler_params=pltpu.CompilerParams(vmem_limit_bytes=1024 * 1024),
     )(blocks)
 
 
@@ -404,11 +411,9 @@
     return mine, early, late
 
 
-def exchanged_evidence(top, total, bit):
-    pair = jnp.concatenate([top, total])
-    got = lax.ppermute(pair, "narrow", [(k, k ^ bit) for k in range(8)])
-    joined = jnp.maximum(top, got[:1])
-    return joined, total * jnp.exp(top - joined) + got[1:] * jnp.exp(got[:1] - joined)
+def joined_evidence(blocks):
+    top = jnp.max(blocks[:, 0], axis=0)
+    return top + jnp.log(jnp.sum(blocks[:, 1] * jnp.exp(blocks[:, 0] - top), axis=0))
 
 
 def per_device(images, defocus, class_index, rotation_index, owner_map, roster, ref_store):
@@ -433,7 +438,7 @@
     member = (class_index[None, :] == class_ids[:, None]).astype(jnp.float32)
     mine, early, late = fetch(ref_store[0, 0], holders, images, contrast_rows, low_table)
     other = swapped(mine)
-    keep, send, top, total = score(
+    keep, send, evidence = score(
         core.reshape(1), mine, other, early, late, low_table, turn, back, square, prior, member
     )
     owners = lax.dynamic_slice_in_dim(owner_map, leading_class, CLS_GRP)
@@ -445,17 +450,12 @@
     place = place.reshape(1, (ROWS + 1) * CLS_GRP)
     table = finish_table(cosine_table, sine_table)
     share = pack(keep, swapped(send)).reshape(8, (ROWS + 1) * CLS_GRP, CYCLES)
-    top, total, share = lax.optimization_barrier((top, total, share))
     share = lax.all_to_all(share, "wide_1", 0, 0, tiled=True)
-    top, total = exchanged_evidence(top, total, 1)
-    share, top, total = lax.optimization_barrier((share, top, total))
+    evidence = lax.all_gather(evidence, "narrow")
     sent = route(core.reshape(1), place, share).reshape(64, (ROWS + 1) * OWN_MAX, CYCLES)
-    top, total, sent = lax.optimization_barrier((top, total, sent))
     got = lax.all_to_all(sent, WIDE, 0, 0, tiled=True)
+    log_evidence = joined_evidence(evidence[:, :2])
     got = got.reshape(4, 16 * (ROWS + 1) * OWN_MAX, CYCLES)
-    top, total = exchanged_evidence(top, total, 2)
-    top, total = exchanged_evidence(top, total, 4)
-    log_evidence = (top + jnp.log(total)).reshape(-1)
     new_references = finish(table, got).reshape(1, 1, OWN_MAX, ANGLES, 2 * CYCLES)
     return (new_references, log_evidence)
 

time: 148 us -> 151 us (1.020)
  the two profiles are of different devices: /device:TPU:77 before, /device:TPU:1 now
where the time goes in v5:
time: 151 us; the launch traced here: 150 us
  waiting for transfers between devices  65.1 us (43%)
  starting transfers between devices  35.6 us (24%)
  Pallas kernels  27.9 us (18%)
  between operations  14.3 us (9%)
  other arithmetic  3.57 us (2%)
  local copies, waits for them, and re-layouts  3.26 us (2%)
    all_to_all x1, waiting for transfers between devices, per_device(): got = lax.all_to_all(sent, WIDE, 0, 0, tiled=True)  19.4 us
    all_to_all x1, waiting for transfers between devices, per_device(): share = lax.all_to_all(share, 'wide_1', 0, 0, tiled=True)  16.5 us
    all_to_all x1, waiting for transfers between devices, fetch(): lax.all_to_all(picked, 'wide_1', 0, 0, tiled=True)  14.9 us
    all_to_all x1, starting transfers between devices, fetch(): sliced = lax.all_to_all(halves, ('wide_1', 'wide_2'), 0, 0, tiled=True)  11.8 us
    pallas_call x2, Pallas kernels, image_spectra(): pl.pallas_call(spectra_kernel, grid=(particles // count,), in_specs=[pl.B...  11.2 us
    pallas_call x1, Pallas kernels, score(): pl.pallas_call(score_kernel, in_specs=[pl.BlockSpec(memory_space=pltpu.SM...  9.81 us
    all_to_all x1, starting transfers between devices, fetch(): planes = lax.all_to_all(picked, 'wide_0', 0, 0, tiled=True)  6.81 us
    ppermute x2, starting transfers between devices, swapped(): return lax.ppermute(x, 'wide_2', [(0, 1), (1, 0)])  5.4 us
  transfers between devices with their start and end apart: 8, of which 8 were waited for; matrix products, arithmetic and copies ran while one was open for 4% of the time, Pallas kernels for 9%

profile of v5, /device:TPU:1, one launch (start us, length us, event | category | flops | bytes accessed | tf_op | source)
XLA Modules:
  0.0 149.7 jit_solution(15076826047808995643)
XLA Ops:
  7.2 1.0 copy-done.2
  8.1 0.7 shard_map.86
  8.9 11.8 %all-to-all-start = ((bf16[16,72,128]{2,1,0:T(8,128)(2,1)}), bf16[16,72,128]{2,1,0:T(8,128)(2,1)S(1)}, u32[]{:S(2)}, u32[]{:S(2)}) async-start(bf16[16,72,128]{2,1,0:T(8,128)(2,1)} %bitcast.3), calls=%async_computation | async-start | bytes 589824 | tf_op jit(solution)/shard_map/all_to_all | solution.py:402
  20.7 0.2 fusion.23
  20.9 0.7 multiply_multiply_fusion
  21.6 0.3 fusion.21
  21.9 0.2 dynamic-slice_reduce_fusion
  22.1 0.6 pad_maximum_fusion.4.table_ref.low_ref
  22.7 0.6 fusion.28
  23.4 5.6 %shard_map.87.early_ref = bf16[72,64,256]{2,1,0:T(8,128)(2,1)} custom-call(bf16[144,72]{1,0:T(8,128)(2,1)} %pad_maximum_fusion.4.table_ref.low_ref, f32[64,128]{1,0:T(8,128)} %get-tuple-element.21.contrast_ref, bf16[128,72,256]{2,1,0:T(8,128)(2,1)} %image_ref.3), custom_call_target="tpu_custom_call" | custom-call | flops 339738624 | bytes 4718592 | tf_op jit(solution)/shard_map/pallas_call | solution.py:72
  29.0 4.1 %all-to-all-done = bf16[16,72,128]{2,1,0:T(8,128)(2,1)S(1)} async-done(((bf16[16,72,128]{2,1,0:T(8,128)(2,1)}), bf16[16,72,128]{2,1,0:T(8,128)(2,1)S(1)}, u32[]{:S(2)}, u32[]{:S(2)}) %all-to-all-start) | async-done | bytes 294944 | tf_op jit(solution)/shard_map/all_to_all | solution.py:402
  33.1 1.3 shard_map.88
  34.4 6.8 %all-to-all-start.1 = ((bf16[4,3,72,128]{3,2,1,0:T(8,128)(2,1)}), bf16[4,3,72,128]{3,2,1,0:T(8,128)(2,1)S(1)}, u32[]{:S(2)}, u32[]{:S(2)}) async-start(bf16[4,3,72,128]{3,2,1,0:T(8,128)(2,1)} %shard_map.88), calls=%async_computation.1 | async-start | bytes 442368 | tf_op jit(solution)/shard_map/all_to_all | solution.py:406
  41.2 5.6 %shard_map.89.late_ref = bf16[72,64,256]{2,1,0:T(8,128)(2,1)} custom-call(bf16[144,72]{1,0:T(8,128)(2,1)} %pad_maximum_fusion.4.table_ref.low_ref, f32[64,128]{1,0:T(8,128)} %get-tuple-element.11.contrast_ref, bf16[128,72,256]{2,1,0:T(8,128)(2,1)} %image_ref.3), custom_call_target="tpu_custom_call" | custom-call | flops 339738624 | bytes 4718592 | tf_op jit(solution)/shard_map/pallas_call | solution.py:72
  46.8 3.6 %all-to-all-done.1.source_ref = bf16[4,3,72,128]{3,2,1,0:T(8,128)(2,1)S(1)} async-done(((bf16[4,3,72,128]{3,2,1,0:T(8,128)(2,1)}), bf16[4,3,72,128]{3,2,1,0:T(8,128)(2,1)S(1)}, u32[]{:S(2)}, u32[]{:S(2)}) %all-to-all-start.1) | async-done | bytes 221216 | tf_op jit(solution)/shard_map/all_to_all | solution.py:406
  50.4 1.4 shard_map.90
  51.8 3.5 %all-to-all-start.2 = ((bf16[8,3,72,128]{3,2,1,0:T(8,128)(2,1)}), bf16[8,3,72,128]{3,2,1,0:T(8,128)(2,1)S(1)}, u32[]{:S(2)}, u32[]{:S(2)}) async-start(bf16[8,3,72,128]{3,2,1,0:T(8,128)(2,1)} %shard_map.90), calls=%async_computation.2 | async-start | bytes 884736 | tf_op jit(solution)/shard_map/all_to_all | solution.py:410
  55.3 0.0 all-gather.3.cloned.1.call-start
  55.3 0.2 fusion.18
  55.5 0.2 fusion.19
  55.7 0.1 pad_maximum_fusion.3.turn_ref
  55.8 14.9 %all-to-all-done.2 = bf16[8,3,72,128]{3,2,1,0:T(8,128)(2,1)S(1)} async-done(((bf16[8,3,72,128]{3,2,1,0:T(8,128)(2,1)}), bf16[8,3,72,128]{3,2,1,0:T(8,128)(2,1)S(1)}, u32[]{:S(2)}, u32[]{:S(2)}) %all-to-all-start.2) | async-done | bytes 442400 | tf_op jit(solution)/shard_map/all_to_all | solution.py:410
  70.6 3.1 %collective-permute-start = (bf16[24,72,128]{2,1,0:T(8,128)(2,1)S(1)}, bf16[24,72,128]{2,1,0:T(8,128)(2,1)S(1)}, u32[]{:S(2)}, u32[]{:S(2)}) collective-permute-start(bf16[24,72,128]{2,1,0:T(8,128)(2,1)S(1)} %bitcast.20), channel_id=1, source_target_pairs={{0,8},{8,0},{1,9},{9,1},{2,10},{10,2},{3,11},{11,3},{4,12},{12,4},... | collective-permute-start | bytes 1327112 | tf_op jit(solution)/shard_map/ppermute | solution.py:30
  73.8 0.1 compare_convert_fusion.member_ref
  73.9 1.3 collective-permute-done.other_ref
  75.2 9.8 %shard_map.91 = (f32[73,24,128]{2,1,0:T(8,128)S(1)}, f32[73,24,128]{2,1,0:T(8,128)S(1)}, f32[256,128]{1,0:T(8,128)}) custom-call(s32[1]{0:T(128)} %bitcast.core_ref, bf16[24,72,128]{2,1,0:T(8,128)(2,1)S(1)} %bitcast.21, bf16[24,72,128]{2,1,0:T(8,128)(2,1)S(1)} %collective-permute-done.other_ref, bf16[72,64,256]{2,1,0:T(8,128)(2,1)} %shard_map.87.early_ref, ...), custom_call_target="tpu_custom_call" | custom-call | tf_op jit(solution)/shard_map/pallas_call | solution.py:245
  85.0 2.3 %collective-permute-start.1 = (f32[73,24,128]{2,1,0:T(8,128)S(1)}, f32[73,24,128]{2,1,0:T(8,128)S(1)}, u32[]{:S(2)}, u32[]{:S(2)}) collective-permute-start(f32[73,24,128]{2,1,0:T(8,128)S(1)} %get-tuple-element.16), channel_id=1, source_target_pairs={{0,8},{8,0},{1,9},{9,1},{2,10},{10,2},{3,11},{11,3},{4,12},{12,4},... | collective-permute-start | bytes 2691080 | tf_op jit(solution)/shard_map/ppermute | solution.py:30
  87.3 2.0 %collective-permute-done.1.got_ref = f32[73,24,128]{2,1,0:T(8,128)S(1)} collective-permute-done((f32[73,24,128]{2,1,0:T(8,128)S(1)}, f32[73,24,128]{2,1,0:T(8,128)S(1)}, u32[]{:S(2)}, u32[]{:S(2)}) %collective-permute-start.1) | collective-permute-done | bytes 897056 | tf_op jit(solution)/shard_map/ppermute | solution.py:30
  89.3 0.9 shard_map.92
  90.2 3.5 %all-to-all-start.3 = ((bf16[8,240,128]{2,1,0:T(8,128)(2,1)}), bf16[8,240,128]{2,1,0:T(8,128)(2,1)S(1)}, u32[]{:S(2)}, u32[]{:S(2)}) async-start(bf16[8,240,128]{2,1,0:T(8,128)(2,1)} %bitcast.6), calls=%async_computation.3 | async-start | bytes 983040 | tf_op jit(solution)/shard_map/all_to_all | solution.py:453
  93.7 0.1 dynamic_slice.7
  93.8 0.1 reshape.192
  93.9 0.1 copy.17
  94.0 0.1 reshape.193
  94.1 0.2 convert_reduce_fusion
  94.3 0.1 broadcast_add_fusion
  94.4 0.1 add.168.place_ref
  94.5 16.5 %all-to-all-done.3.got_ref = bf16[8,240,128]{2,1,0:T(8,128)(2,1)S(1)} async-done(((bf16[8,240,128]{2,1,0:T(8,128)(2,1)}), bf16[8,240,128]{2,1,0:T(8,128)(2,1)S(1)}, u32[]{:S(2)}, u32[]{:S(2)}) %all-to-all-start.3) | async-done | bytes 491552 | tf_op jit(solution)/shard_map/all_to_all | solution.py:453
  110.9 1.4 shard_map.93
  112.3 4.5 %all-to-all-start.4 = ((bf16[64,40,128]{2,1,0:T(8,128)(2,1)}), bf16[64,40,128]{2,1,0:T(8,128)(2,1)S(1)}, u32[]{:S(2)}, u32[]{:S(2)}) async-start(bf16[64,40,128]{2,1,0:T(8,128)(2,1)} %bitcast.7), calls=%async_computation.4 | async-start | bytes 1310720 | tf_op jit(solution)/shard_map/all_to_all | solution.py:456
  116.9 0.3 fusion.7
  117.3 0.1 copy.15
  117.4 0.1 copy.16
  117.5 3.4 %all-gather.3.cloned.1.call-done = f32[2048,128]{1,0:T(8,128)} async-done(((f32[256,128]{1,0:T(8,128)}), f32[2048,128]{1,0:T(8,128)}) %all-gather.3.cloned.1.call-update) | async-done | bytes 1048592 | tf_op jit(solution)/shard_map/all_gather | solution.py:454
  120.9 0.8 fusion.27
  121.8 0.5 log_add_fusion
  122.3 19.4 %all-to-all-done.4 = bf16[64,40,128]{2,1,0:T(8,128)(2,1)S(1)} async-done(((bf16[64,40,128]{2,1,0:T(8,128)(2,1)}), bf16[64,40,128]{2,1,0:T(8,128)(2,1)S(1)}, u32[]{:S(2)}, u32[]{:S(2)}) %all-to-all-start.4) | async-done | bytes 655392 | tf_op jit(solution)/shard_map/all_to_all | solution.py:456
  141.7 1.2 shard_map.94
  (28 shorter events, 0.3 us)
Async XLA Ops:
  7.2 14.7 %copy-start = (s32[8,3]{0,1:T(4,128)S(1)}, s32[8,3]{0,1:T(4,128)}, u32[]{:S(2)}) copy-start(s32[8,3]{0,1:T(4,128)} %param.12) | copy-start | bytes 292
  7.2 1.0 copy-start.2
  8.9 24.2 %all-to-all-start = ((bf16[16,72,128]{2,1,0:T(8,128)(2,1)}), bf16[16,72,128]{2,1,0:T(8,128)(2,1)S(1)}, u32[]{:S(2)}, u32[]{:S(2)}) async-start(bf16[16,72,128]{2,1,0:T(8,128)(2,1)} %bitcast.3), calls=%async_computation | async-start | bytes 589824 | tf_op jit(solution)/shard_map/all_to_all | solution.py:402
  34.4 16.0 %all-to-all-start.1 = ((bf16[4,3,72,128]{3,2,1,0:T(8,128)(2,1)}), bf16[4,3,72,128]{3,2,1,0:T(8,128)(2,1)S(1)}, u32[]{:S(2)}, u32[]{:S(2)}) async-start(bf16[4,3,72,128]{3,2,1,0:T(8,128)(2,1)} %shard_map.88), calls=%async_computation.1 | async-start | bytes 442368 | tf_op jit(solution)/shard_map/all_to_all | solution.py:406
  41.2 32.6 %copy-start.4 = (s32[128]{0:T(128)S(1)}, s32[128]{0:T(128)}, u32[]{:S(2)}) copy-start(s32[128]{0:T(128)} %param.9) | copy-start | bytes 1540
  41.2 32.7 %copy-start.3 = (s32[128]{0:T(128)S(1)}, s32[128]{0:T(128)}, u32[]{:S(2)}) copy-start(s32[128]{0:T(128)} %param.10) | copy-start | bytes 1540
  41.2 34.0 %copy-start.1 = (bf16[144,72]{1,0:T(8,128)(2,1)S(1)}, bf16[144,72]{1,0:T(8,128)(2,1)}, u32[]{:S(2)}) copy-start(bf16[144,72]{1,0:T(8,128)(2,1)} %pad_maximum_fusion.4.table_ref.low_ref) | copy-start | bytes 62212
  51.8 18.9 %all-to-all-start.2 = ((bf16[8,3,72,128]{3,2,1,0:T(8,128)(2,1)}), bf16[8,3,72,128]{3,2,1,0:T(8,128)(2,1)S(1)}, u32[]{:S(2)}, u32[]{:S(2)}) async-start(bf16[8,3,72,128]{3,2,1,0:T(8,128)(2,1)} %shard_map.90), calls=%async_computation.2 | async-start | bytes 884736 | tf_op jit(solution)/shard_map/all_to_all | solution.py:410
  55.3 65.6 %all-gather.3.cloned.1.call-start = ((), (), s32[]{:S(2)}) async-start(), calls=%async_computation.5 | async-start | bytes 1179648 | tf_op jit(solution)/shard_map/all_gather | solution.py:454
  70.6 4.5 %collective-permute-start = (bf16[24,72,128]{2,1,0:T(8,128)(2,1)S(1)}, bf16[24,72,128]{2,1,0:T(8,128)(2,1)S(1)}, u32[]{:S(2)}, u32[]{:S(2)}) collective-permute-start(bf16[24,72,128]{2,1,0:T(8,128)(2,1)S(1)} %bitcast.20), channel_id=1, source_target_pairs={{0,8},{8,0},{1,9},{9,1},{2,10},{10,2},{3,11},{11,3},{4,12},{12,4},... | collective-permute-start | bytes 1327112 | tf_op jit(solution)/shard_map/ppermute | solution.py:30
  85.0 8.7 %copy-start.5 = (s32[192]{0:T(256)S(1)}, s32[192]{0:T(256)}, u32[]{:S(2)}) copy-start(s32[192]{0:T(256)} %param.11) | copy-start | bytes 2308
  85.0 4.3 %collective-permute-start.1 = (f32[73,24,128]{2,1,0:T(8,128)S(1)}, f32[73,24,128]{2,1,0:T(8,128)S(1)}, u32[]{:S(2)}, u32[]{:S(2)}) collective-permute-start(f32[73,24,128]{2,1,0:T(8,128)S(1)} %get-tuple-element.16), channel_id=1, source_target_pairs={{0,8},{8,0},{1,9},{9,1},{2,10},{10,2},{3,11},{11,3},{4,12},{12,4},... | collective-permute-start | bytes 2691080 | tf_op jit(solution)/shard_map/ppermute | solution.py:30
  90.2 20.7 %all-to-all-start.3 = ((bf16[8,240,128]{2,1,0:T(8,128)(2,1)}), bf16[8,240,128]{2,1,0:T(8,128)(2,1)S(1)}, u32[]{:S(2)}, u32[]{:S(2)}) async-start(bf16[8,240,128]{2,1,0:T(8,128)(2,1)} %bitcast.6), calls=%async_computation.3 | async-start | bytes 983040 | tf_op jit(solution)/shard_map/all_to_all | solution.py:453
  112.3 29.4 %all-to-all-start.4 = ((bf16[64,40,128]{2,1,0:T(8,128)(2,1)}), bf16[64,40,128]{2,1,0:T(8,128)(2,1)S(1)}, u32[]{:S(2)}, u32[]{:S(2)}) async-start(bf16[64,40,128]{2,1,0:T(8,128)(2,1)} %bitcast.7), calls=%async_computation.4 | async-start | bytes 1310720 | tf_op jit(solution)/shard_map/all_to_all | solution.py:456
Sparse Core Ops, SparseCore 0:
  87.4 33.3 all-gather.2

commit v6 on v5

--- a/solution.py
+++ b/solution.py
@@ -16,7 +16,6 @@
 CLS_GRP = 24
 SIGMA_ROT = 8
 ROWS = 9
-EVIDENCE_ROWS = 256
 CHUNKS = 4
 WIDE = ("wide_0", "wide_1", "wide_2")
 
@@ -207,7 +206,6 @@
     total = jnp.zeros((ANGLES, particles), jnp.float32)
     for c in range(CLS_GRP):
         total = total + jnp.exp(scores[c] - top)
-    evidence_ref[...] = jnp.zeros_like(evidence_ref)
     evidence_ref[0:1, :] = top
     evidence_ref[1:2, :] = jnp.sum(total, axis=0, keepdims=True)
     weight = jnp.exp(own - jnp.max(own, axis=0, keepdims=True))
@@ -240,7 +238,7 @@
 def score(core, mine, other, early, late, low_table, turn, back, square, prior, member):
     particles = 2 * early.shape[1]
     sums = jax.ShapeDtypeStruct((ANGLES + 1, CLS_GRP, CYCLES), jnp.float32)
-    evidence = jax.ShapeDtypeStruct((EVIDENCE_ROWS, particles), jnp.float32)
+    evidence = jax.ShapeDtypeStruct((2, particles), jnp.float32)
     vmem = pl.BlockSpec(memory_space=pltpu.VMEM)
     return pl.pallas_call(
         score_kernel,
@@ -396,7 +394,7 @@
     return jnp.concatenate([real, imag])
 
 
-def fetch(blocks, holders, images, contrast_rows, table):
+def fetch(blocks, holders, images, contrast_rows, table, small):
     half = contrast_rows.shape[0] // 2
     halves = halve(blocks).reshape(BLOCK * 2, ANGLES, CYCLES)
     sliced = lax.all_to_all(halves, ("wide_1", "wide_2"), 0, 0, tiled=True)
@@ -405,15 +403,17 @@
     picked = pick(sliced[:, None], holders % 16, 4)
     planes = lax.all_to_all(picked, "wide_0", 0, 0, tiled=True)
     late = image_spectra(images, 1, later, table)
-    planes, late = lax.optimization_barrier((planes, late))
+    planes, late, small = lax.optimization_barrier((planes, late, small))
     picked = pick(planes, holders // 16, 8)
     mine = lax.all_to_all(picked, "wide_1", 0, 0, tiled=True).reshape(CLS_GRP, ANGLES, CYCLES)
-    return mine, early, late
-
-
-def joined_evidence(blocks):
-    top = jnp.max(blocks[:, 0], axis=0)
-    return top + jnp.log(jnp.sum(blocks[:, 1] * jnp.exp(blocks[:, 0] - top), axis=0))
+    return mine, early, late, small
+
+
+def exchanged_evidence(pair, bit):
+    got = lax.ppermute(pair, "narrow", [(k, k ^ bit) for k in range(8)])
+    top = jnp.maximum(pair[:1], got[:1])
+    total = pair[1:] * jnp.exp(pair[:1] - top) + got[1:] * jnp.exp(got[:1] - top)
+    return jnp.concatenate([top, total])
 
 
 def per_device(images, defocus, class_index, rotation_index, owner_map, roster, ref_store):
@@ -436,11 +436,6 @@
     square = contrast_rows * contrast_rows
     prior = rotation_prior(rotation_index).T
     member = (class_index[None, :] == class_ids[:, None]).astype(jnp.float32)
-    mine, early, late = fetch(ref_store[0, 0], holders, images, contrast_rows, low_table)
-    other = swapped(mine)
-    keep, send, evidence = score(
-        core.reshape(1), mine, other, early, late, low_table, turn, back, square, prior, member
-    )
     owners = lax.dynamic_slice_in_dim(owner_map, leading_class, CLS_GRP)
     owners = owners.reshape(STEPS, BLOCK).T.reshape(CLS_GRP)
     same = owners[:, None] == owners[None, :]
@@ -449,12 +444,24 @@
     place = jnp.arange(ROWS + 1, dtype=jnp.int32)[:, None] * 1024 + place[None, :]
     place = place.reshape(1, (ROWS + 1) * CLS_GRP)
     table = finish_table(cosine_table, sine_table)
-    share = pack(keep, swapped(send)).reshape(8, (ROWS + 1) * CLS_GRP, CYCLES)
+    small = (turn, back, square, prior, member, place, table)
+
+    mine, early, late, small = fetch(
+        ref_store[0, 0], holders, images, contrast_rows, low_table, small
+    )
+    turn, back, square, prior, member, place, table = small
+    other = swapped(mine)
+    keep, send, evidence = score(
+        core.reshape(1), mine, other, early, late, low_table, turn, back, square, prior, member
+    )
+    got, evidence = lax.optimization_barrier((swapped(send), exchanged_evidence(evidence, 1)))
+    share = pack(keep, got).reshape(8, (ROWS + 1) * CLS_GRP, CYCLES)
     share = lax.all_to_all(share, "wide_1", 0, 0, tiled=True)
-    evidence = lax.all_gather(evidence, "narrow")
     sent = route(core.reshape(1), place, share).reshape(64, (ROWS + 1) * OWN_MAX, CYCLES)
+    sent, evidence = lax.optimization_barrier((sent, evidence))
     got = lax.all_to_all(sent, WIDE, 0, 0, tiled=True)
-    log_evidence = joined_evidence(evidence[:, :2])
+    evidence = exchanged_evidence(exchanged_evidence(evidence, 2), 4)
+    log_evidence = evidence[0] + jnp.log(evidence[1])
     got = got.reshape(4, 16 * (ROWS + 1) * OWN_MAX, CYCLES)
     new_references = finish(table, got).reshape(1, 1, OWN_MAX, ANGLES, 2 * CYCLES)
     return (new_references, log_evidence)

time: 151 us -> 135 us (0.89)
  waiting for transfers between devices: 65.1 us -> 21.7 us
  blocking collectives: 0 us -> 32.9 us
  between operations: 14.3 us -> 0.94 us
  starting transfers between devices: 35.6 us -> 45.8 us
  Pallas kernels: 27.9 us -> 26.3 us
    all_to_all x0 -> x2, blocking collectives: none -> 32.9 us  [the longest x1 17.2 us: per_device(): share = lax.all_to_all(share, 'wide_1', 0, 0, tiled=True)]
    all_to_all x2 -> x0, waiting for transfers between devices: 31.3 us -> none  [the longest x1 16.5 us: per_device(): share = lax.all_to_all(share, 'wide_1', 0, 0, tiled=True)]
    ppermute x0 -> x3, starting transfers between devices: none -> 10.2 us  [exchanged_evidence(): got = lax.ppermute(pair, 'narrow', [(k, k ^ bit) for k in range(8)])]
    all_to_all x1, waiting for transfers between devices: 19.4 us -> 10.4 us  [per_device(): got = lax.all_to_all(sent, WIDE, 0, 0, tiled=True)]
    all_to_all x2 -> x0, starting transfers between devices: 6.95 us -> none  [the longest x1 3.48 us: per_device(): share = lax.all_to_all(share, 'wide_1', 0, 0, tiled=True)]
    ppermute x0 -> x3, waiting for transfers between devices: none -> 4.82 us  [exchanged_evidence(): got = lax.ppermute(pair, 'narrow', [(k, k ^ bit) for k in range(8)])]
    all_to_all x1, starting transfers between devices: 4.55 us -> 8.07 us  [per_device(): got = lax.all_to_all(sent, WIDE, 0, 0, tiled=True)]
    ppermute x2, starting transfers between devices: 5.4 us -> 8.87 us  [swapped(): return lax.ppermute(x, 'wide_2', [(0, 1), (1, 0)])]
  transfers between devices with their start and end apart: 8 -> 8, of which waited for: 8 -> 7; matrix products, arithmetic and copies ran while one was open for 4% -> 4% of each run, Pallas kernels for 9% -> 8%
where the time goes in v6:
time: 135 us; the launch traced here: 134 us
  starting transfers between devices  45.8 us (34%)
  blocking collectives  32.9 us (24%)
  Pallas kernels  26.3 us (19%)
  waiting for transfers between devices  21.7 us (16%)
  other arithmetic  3.58 us (3%)
  local copies, waits for them, and re-layouts  3.1 us (2%)
    all_to_all x1, blocking collectives, per_device(): share = lax.all_to_all(share, 'wide_1', 0, 0, tiled=True)  17.2 us
    all_to_all x1, blocking collectives, fetch(): lax.all_to_all(picked, 'wide_1', 0, 0, tiled=True)  15.6 us
    all_to_all x1, starting transfers between devices, fetch(): sliced = lax.all_to_all(halves, ('wide_1', 'wide_2'), 0, 0, tiled=True)  11.8 us
    pallas_call x2, Pallas kernels, image_spectra(): pl.pallas_call(spectra_kernel, grid=(particles // count,), in_specs=[pl.B...  11.2 us
    all_to_all x1, waiting for transfers between devices, per_device(): got = lax.all_to_all(sent, WIDE, 0, 0, tiled=True)  10.4 us
    ppermute x3, starting transfers between devices, exchanged_evidence(): got = lax.ppermute(pair, 'narrow', [(k, k ^ bit) for k in range(8)])  10.2 us
    pallas_call x1, Pallas kernels, score(): pl.pallas_call(score_kernel, in_specs=[pl.BlockSpec(memory_space=pltpu.SM...  9.79 us
    ppermute x2, starting transfers between devices, swapped(): return lax.ppermute(x, 'wide_2', [(0, 1), (1, 0)])  8.87 us
  transfers between devices with their start and end apart: 8, of which 7 were waited for; matrix products, arithmetic and copies ran while one was open for 4% of the time, Pallas kernels for 8%

profile of v6, /device:TPU:1, one launch (start us, length us, event | category | flops | bytes accessed | tf_op | source)
XLA Modules:
  0.0 134.2 jit_solution(11084411417537316408)
XLA Ops:
  0.7 1.0 copy-done.2
  1.6 0.7 shard_map.86
  2.4 11.8 %all-to-all-start = ((bf16[16,72,128]{2,1,0:T(8,128)(2,1)}), bf16[16,72,128]{2,1,0:T(8,128)(2,1)S(1)}, u32[]{:S(2)}, u32[]{:S(2)}) async-start(bf16[16,72,128]{2,1,0:T(8,128)(2,1)} %bitcast.1), calls=%async_computation | async-start | bytes 589824 | tf_op jit(solution)/shard_map/all_to_all | solution.py:400
  14.2 0.2 fusion.18
  14.4 0.2 fusion.23
  14.6 0.2 fusion.19
  14.8 0.7 multiply_multiply_fusion
  15.4 0.8 dynamic_slice.8
  16.2 0.1 reshape.191
  16.3 0.1 copy.13
  16.3 0.1 reshape.192
  16.4 0.2 convert_reduce_fusion
  16.6 0.1 broadcast_add_fusion
  16.7 0.1 add.186.place_ref
  16.8 0.3 fusion.7
  17.2 0.1 copy.14
  17.3 0.1 copy.15
  17.4 0.3 fusion.21
  17.7 0.6 fusion.29
  18.4 0.2 dynamic-slice_reduce_fusion
  18.6 0.6 pad_maximum_fusion.4.table_ref.low_ref
  19.3 5.6 %shard_map.87.early_ref = bf16[72,64,256]{2,1,0:T(8,128)(2,1)} custom-call(bf16[144,72]{1,0:T(8,128)(2,1)} %pad_maximum_fusion.4.table_ref.low_ref, f32[64,128]{1,0:T(8,128)} %get-tuple-element.49.contrast_ref, bf16[128,72,256]{2,1,0:T(8,128)(2,1)} %image_ref.3), custom_call_target="tpu_custom_call" | custom-call | flops 339738624 | bytes 4718592 | tf_op jit(solution)/shard_map/pallas_call | solution.py:71
  24.9 0.1 compare_convert_fusion.member_ref
  25.0 1.6 %all-to-all-done = bf16[16,72,128]{2,1,0:T(8,128)(2,1)S(1)} async-done(((bf16[16,72,128]{2,1,0:T(8,128)(2,1)}), bf16[16,72,128]{2,1,0:T(8,128)(2,1)S(1)}, u32[]{:S(2)}, u32[]{:S(2)}) %all-to-all-start) | async-done | bytes 294944 | tf_op jit(solution)/shard_map/all_to_all | solution.py:400
  26.6 1.3 shard_map.88
  27.8 6.8 %all-to-all-start.1 = ((bf16[4,3,72,128]{3,2,1,0:T(8,128)(2,1)}), bf16[4,3,72,128]{3,2,1,0:T(8,128)(2,1)S(1)}, u32[]{:S(2)}, u32[]{:S(2)}) async-start(bf16[4,3,72,128]{3,2,1,0:T(8,128)(2,1)} %shard_map.88), calls=%async_computation.1 | async-start | bytes 442368 | tf_op jit(solution)/shard_map/all_to_all | solution.py:404
  34.7 0.1 pad_maximum_fusion.3.turn_ref
  34.8 5.6 %shard_map.89.late_ref = bf16[72,64,256]{2,1,0:T(8,128)(2,1)} custom-call(bf16[144,72]{1,0:T(8,128)(2,1)} %pad_maximum_fusion.4.table_ref.low_ref, f32[64,128]{1,0:T(8,128)} %get-tuple-element.22.contrast_ref, bf16[128,72,256]{2,1,0:T(8,128)(2,1)} %image_ref.3), custom_call_target="tpu_custom_call" | custom-call | flops 339738624 | bytes 4718592 | tf_op jit(solution)/shard_map/pallas_call | solution.py:71
  40.4 3.5 %all-to-all-done.1.source_ref = bf16[4,3,72,128]{3,2,1,0:T(8,128)(2,1)S(1)} async-done(((bf16[4,3,72,128]{3,2,1,0:T(8,128)(2,1)}), bf16[4,3,72,128]{3,2,1,0:T(8,128)(2,1)S(1)}, u32[]{:S(2)}, u32[]{:S(2)}) %all-to-all-start.1) | async-done | bytes 221216 | tf_op jit(solution)/shard_map/all_to_all | solution.py:404
  43.9 0.6 shard_map.90
  44.5 15.6 %all_to_all.25 = bf16[8,3,72,128]{3,2,1,0:T(8,128)(2,1)S(1)} all-to-all(bf16[8,3,72,128]{3,2,1,0:T(8,128)(2,1)S(1)} %shard_map.90), channel_id=1, replica_groups=mesh['wide_0'=4,'wide_1'=8,'wide_2'=2,'narrow'=8] {'wide_1'}, dimensions={0} | all-to-all | bytes 884736 | tf_op jit(solution)/shard_map/all_to_all | solution.py:408
  60.1 6.6 %collective-permute-start = (bf16[24,72,128]{2,1,0:T(8,128)(2,1)S(1)}, bf16[24,72,128]{2,1,0:T(8,128)(2,1)S(1)}, u32[]{:S(2)}, u32[]{:S(2)}) collective-permute-start(bf16[24,72,128]{2,1,0:T(8,128)(2,1)S(1)} %bitcast.18), channel_id=1, source_target_pairs={{0,8},{8,0},{1,9},{9,1},{2,10},{10,2},{3,11},{11,3},{4,12},{12,4},... | collective-permute-start | bytes 1327112 | tf_op jit(solution)/shard_map/ppermute | solution.py:29
  66.7 1.4 %collective-permute-done.other_ref = bf16[24,72,128]{2,1,0:T(8,128)(2,1)S(1)} collective-permute-done((bf16[24,72,128]{2,1,0:T(8,128)(2,1)S(1)}, bf16[24,72,128]{2,1,0:T(8,128)(2,1)S(1)}, u32[]{:S(2)}, u32[]{:S(2)}) %collective-permute-start) | collective-permute-done | bytes 442400 | tf_op jit(solution)/shard_map/ppermute | solution.py:29
  68.1 9.8 %shard_map.91 = (f32[73,24,128]{2,1,0:T(8,128)S(1)}, f32[73,24,128]{2,1,0:T(8,128)S(1)}, f32[2,128]{1,0:T(2,128)S(1)}) custom-call(s32[1]{0:T(128)} %bitcast.4.core_ref, bf16[24,72,128]{2,1,0:T(8,128)(2,1)S(1)} %bitcast.19, bf16[24,72,128]{2,1,0:T(8,128)(2,1)S(1)} %collective-permute-done.other_ref, bf16[72,64,256]{2,1,0:T(8,128)(2,1)} %shard_map.87.early_ref, ...), custom_call_target="tpu_custom_call" | custom-call | tf_op jit(solution)/shard_map/pallas_call | solution.py:243
  77.9 2.3 %collective-permute-start.1 = (f32[73,24,128]{2,1,0:T(8,128)S(1)}, f32[73,24,128]{2,1,0:T(8,128)S(1)}, u32[]{:S(2)}, u32[]{:S(2)}) collective-permute-start(f32[73,24,128]{2,1,0:T(8,128)S(1)} %get-tuple-element.34), channel_id=1, source_target_pairs={{0,8},{8,0},{1,9},{9,1},{2,10},{10,2},{3,11},{11,3},{4,12},{12,4},... | collective-permute-start | bytes 2691080 | tf_op jit(solution)/shard_map/ppermute | solution.py:29
  80.2 2.4 %collective-permute-start.2 = (f32[2,128]{1,0:T(2,128)S(1)}, f32[2,128]{1,0:T(2,128)S(1)}, u32[]{:S(2)}, u32[]{:S(2)}) collective-permute-start(f32[2,128]{1,0:T(2,128)S(1)} %get-tuple-element.35), channel_id=1, source_target_pairs={{0,1},{1,0},{2,3},{3,2},{4,5},{5,4},{6,7},{7,6},{8,9},{9,8},{10,11... | collective-permute-start | bytes 3080 | tf_op jit(solution)/shard_map/ppermute | solution.py:413
  82.6 1.9 %collective-permute-done.2 = f32[2,128]{1,0:T(2,128)S(1)} collective-permute-done((f32[2,128]{1,0:T(2,128)S(1)}, f32[2,128]{1,0:T(2,128)S(1)}, u32[]{:S(2)}, u32[]{:S(2)}) %collective-permute-start.2) | collective-permute-done | bytes 1056 | tf_op jit(solution)/shard_map/ppermute | solution.py:413
  84.5 0.1 shard_map.92
  84.6 17.2 %all_to_all.26.got_ref = bf16[8,240,128]{2,1,0:T(8,128)(2,1)S(1)} all-to-all(bf16[8,240,128]{2,1,0:T(8,128)(2,1)S(1)} %bitcast.17), channel_id=1, replica_groups=mesh['wide_0'=4,'wide_1'=8,'wide_2'=2,'narrow'=8] {'wide_1'}, dimensions={0} | all-to-all | bytes 983040 | tf_op jit(solution)/shard_map/all_to_all | solution.py:459
  101.9 1.4 %shard_map.93 = bf16[2560,128]{1,0:T(8,128)(2,1)} custom-call(s32[1]{0:T(128)} %bitcast.4.core_ref, s32[1,240]{1,0:T(1,128)S(1)} %add.186.place_ref, bf16[8,240,128]{2,1,0:T(8,128)(2,1)S(1)} %all_to_all.26.got_ref), custom_call_target="tpu_custom_call" | custom-call | tf_op jit(solution)/shard_map/pallas_call | solution.py:338
  103.3 8.1 %all-to-all-start.4 = ((bf16[64,40,128]{2,1,0:T(8,128)(2,1)}), bf16[64,40,128]{2,1,0:T(8,128)(2,1)S(1)}, u32[]{:S(2)}, u32[]{:S(2)}) async-start(bf16[64,40,128]{2,1,0:T(8,128)(2,1)} %bitcast.7), calls=%async_computation.4 | async-start | bytes 1310720 | tf_op jit(solution)/shard_map/all_to_all | solution.py:462
  111.4 3.1 %collective-permute-start.3 = (f32[2,128]{1,0:T(2,128)S(1)}, f32[2,128]{1,0:T(2,128)S(1)}, u32[]{:S(2)}, u32[]{:S(2)}) collective-permute-start(f32[2,128]{1,0:T(2,128)S(1)} %pad_maximum_fusion.5), channel_id=1, source_target_pairs={{0,2},{1,3},{2,0},{3,1},{4,6},{5,7},{6,4},{7,5},{8,10},{9,11},{10,... | collective-permute-start | bytes 3080 | tf_op jit(solution)/shard_map/ppermute | solution.py:413
  114.5 1.5 %collective-permute-done.3 = f32[2,128]{1,0:T(2,128)S(1)} collective-permute-done((f32[2,128]{1,0:T(2,128)S(1)}, f32[2,128]{1,0:T(2,128)S(1)}, u32[]{:S(2)}, u32[]{:S(2)}) %collective-permute-start.3) | collective-permute-done | bytes 1056 | tf_op jit(solution)/shard_map/ppermute | solution.py:413
  116.0 4.6 %collective-permute-start.4 = (f32[2,128]{1,0:T(2,128)S(1)}, f32[2,128]{1,0:T(2,128)S(1)}, u32[]{:S(2)}, u32[]{:S(2)}) collective-permute-start(f32[2,128]{1,0:T(2,128)S(1)} %pad_maximum_fusion.6), channel_id=1, source_target_pairs={{0,4},{1,5},{2,6},{3,7},{4,0},{5,1},{6,2},{7,3},{8,12},{9,13},{10,... | collective-permute-start | bytes 3080 | tf_op jit(solution)/shard_map/ppermute | solution.py:413
  120.7 1.5 %collective-permute-done.4 = f32[2,128]{1,0:T(2,128)S(1)} collective-permute-done((f32[2,128]{1,0:T(2,128)S(1)}, f32[2,128]{1,0:T(2,128)S(1)}, u32[]{:S(2)}, u32[]{:S(2)}) %collective-permute-start.4) | collective-permute-done | bytes 1056 | tf_op jit(solution)/shard_map/ppermute | solution.py:413
  122.1 0.5 add_bitcast_fusion
  122.6 10.4 %all-to-all-done.4 = bf16[64,40,128]{2,1,0:T(8,128)(2,1)S(1)} async-done(((bf16[64,40,128]{2,1,0:T(8,128)(2,1)}), bf16[64,40,128]{2,1,0:T(8,128)(2,1)S(1)}, u32[]{:S(2)}, u32[]{:S(2)}) %all-to-all-start.4) | async-done | bytes 655392 | tf_op jit(solution)/shard_map/all_to_all | solution.py:462
  133.0 1.2 shard_map.94
  (28 shorter events, 0.2 us)
Async XLA Ops:
  0.6 17.8 %copy-start = (s32[8,3]{0,1:T(4,128)S(1)}, s32[8,3]{0,1:T(4,128)}, u32[]{:S(2)}) copy-start(s32[8,3]{0,1:T(4,128)} %param.12) | copy-start | bytes 292
  0.6 1.0 copy-start.2
  2.4 24.2 %all-to-all-start = ((bf16[16,72,128]{2,1,0:T(8,128)(2,1)}), bf16[16,72,128]{2,1,0:T(8,128)(2,1)S(1)}, u32[]{:S(2)}, u32[]{:S(2)}) async-start(bf16[16,72,128]{2,1,0:T(8,128)(2,1)} %bitcast.1), calls=%async_computation | async-start | bytes 589824 | tf_op jit(solution)/shard_map/all_to_all | solution.py:400
  19.2 5.6 %copy-start.4 = (s32[128]{0:T(128)S(1)}, s32[128]{0:T(128)}, u32[]{:S(2)}) copy-start(s32[128]{0:T(128)} %param.9) | copy-start | bytes 1540
  19.2 15.5 %copy-start.3 = (s32[128]{0:T(128)S(1)}, s32[128]{0:T(128)}, u32[]{:S(2)}) copy-start(s32[128]{0:T(128)} %param.10) | copy-start | bytes 1540
  27.8 16.0 %all-to-all-start.1 = ((bf16[4,3,72,128]{3,2,1,0:T(8,128)(2,1)}), bf16[4,3,72,128]{3,2,1,0:T(8,128)(2,1)S(1)}, u32[]{:S(2)}, u32[]{:S(2)}) async-start(bf16[4,3,72,128]{3,2,1,0:T(8,128)(2,1)} %shard_map.88), calls=%async_computation.1 | async-start | bytes 442368 | tf_op jit(solution)/shard_map/all_to_all | solution.py:404
  34.8 33.3 %copy-start.1 = (bf16[144,72]{1,0:T(8,128)(2,1)S(1)}, bf16[144,72]{1,0:T(8,128)(2,1)}, u32[]{:S(2)}) copy-start(bf16[144,72]{1,0:T(8,128)(2,1)} %pad_maximum_fusion.4.table_ref.low_ref) | copy-start | bytes 62212
  60.1 8.0 %collective-permute-start = (bf16[24,72,128]{2,1,0:T(8,128)(2,1)S(1)}, bf16[24,72,128]{2,1,0:T(8,128)(2,1)S(1)}, u32[]{:S(2)}, u32[]{:S(2)}) collective-permute-start(bf16[24,72,128]{2,1,0:T(8,128)(2,1)S(1)} %bitcast.18), channel_id=1, source_target_pairs={{0,8},{8,0},{1,9},{9,1},{2,10},{10,2},{3,11},{11,3},{4,12},{12,4},... | collective-permute-start | bytes 1327112 | tf_op jit(solution)/shard_map/ppermute | solution.py:29
  77.9 6.6 %collective-permute-start.1 = (f32[73,24,128]{2,1,0:T(8,128)S(1)}, f32[73,24,128]{2,1,0:T(8,128)S(1)}, u32[]{:S(2)}, u32[]{:S(2)}) collective-permute-start(f32[73,24,128]{2,1,0:T(8,128)S(1)} %get-tuple-element.34), channel_id=1, source_target_pairs={{0,8},{8,0},{1,9},{9,1},{2,10},{10,2},{3,11},{11,3},{4,12},{12,4},... | collective-permute-start | bytes 2691080 | tf_op jit(solution)/shard_map/ppermute | solution.py:29
  80.2 4.3 %collective-permute-start.2 = (f32[2,128]{1,0:T(2,128)S(1)}, f32[2,128]{1,0:T(2,128)S(1)}, u32[]{:S(2)}, u32[]{:S(2)}) collective-permute-start(f32[2,128]{1,0:T(2,128)S(1)} %get-tuple-element.35), channel_id=1, source_target_pairs={{0,1},{1,0},{2,3},{3,2},{4,5},{5,4},{6,7},{7,6},{8,9},{9,8},{10,11... | collective-permute-start | bytes 3080 | tf_op jit(solution)/shard_map/ppermute | solution.py:413
  103.3 29.7 %all-to-all-start.4 = ((bf16[64,40,128]{2,1,0:T(8,128)(2,1)}), bf16[64,40,128]{2,1,0:T(8,128)(2,1)S(1)}, u32[]{:S(2)}, u32[]{:S(2)}) async-start(bf16[64,40,128]{2,1,0:T(8,128)(2,1)} %bitcast.7), calls=%async_computation.4 | async-start | bytes 1310720 | tf_op jit(solution)/shard_map/all_to_all | solution.py:462
  111.4 4.6 %collective-permute-start.3 = (f32[2,128]{1,0:T(2,128)S(1)}, f32[2,128]{1,0:T(2,128)S(1)}, u32[]{:S(2)}, u32[]{:S(2)}) collective-permute-start(f32[2,128]{1,0:T(2,128)S(1)} %pad_maximum_fusion.5), channel_id=1, source_target_pairs={{0,2},{1,3},{2,0},{3,1},{4,6},{5,7},{6,4},{7,5},{8,10},{9,11},{10,... | collective-permute-start | bytes 3080 | tf_op jit(solution)/shard_map/ppermute | solution.py:413
  116.0 6.1 %collective-permute-start.4 = (f32[2,128]{1,0:T(2,128)S(1)}, f32[2,128]{1,0:T(2,128)S(1)}, u32[]{:S(2)}, u32[]{:S(2)}) collective-permute-start(f32[2,128]{1,0:T(2,128)S(1)} %pad_maximum_fusion.6), channel_id=1, source_target_pairs={{0,4},{1,5},{2,6},{3,7},{4,0},{5,1},{6,2},{7,3},{8,12},{9,13},{10,... | collective-permute-start | bytes 3080 | tf_op jit(solution)/shard_map/ppermute | solution.py:413

commit v7 on v6

--- a/solution.py
+++ b/solution.py
@@ -2,6 +2,7 @@
 
 import jax
 import jax.numpy as jnp
+import numpy as np
 from jax import lax
 from jax.experimental import pallas as pl
 from jax.experimental.pallas import tpu as pltpu
@@ -30,10 +31,10 @@
 
 
 def angle_tables(length):
-    counting = jnp.arange(length, dtype=jnp.int32)
+    counting = np.arange(length)
     products = counting[:, None] * counting[None, :] % length
-    phase_angle = products.astype(jnp.float32) * (2.0 * math.pi / length)
-    return (jnp.cos(phase_angle), jnp.sin(phase_angle))
+    phase_angle = products.astype(np.float64) * (2.0 * math.pi / length)
+    return (np.cos(phase_angle).astype(np.float32), np.sin(phase_angle).astype(np.float32))
 
 
 def contrast(defocus_rows):
@@ -288,27 +289,20 @@
     return -0.5 * (distance / SIGMA_ROT) ** 2
 
 
-def halve_kernel(blocks_ref, out_ref, sems):
-    copies = [
-        pltpu.make_async_copy(
-            blocks_ref.at[:, :, half * CYCLES : (half + 1) * CYCLES], out_ref.at[:, half], sems.at[half]
-        )
-        for half in range(2)
-    ]
-    for copy in copies:
-        copy.start()
-    for copy in copies:
-        copy.wait()
+def halve_kernel(blocks_ref, out_ref):
+    for half in range(2):
+        out_ref[:, half] = blocks_ref[:, :, half * CYCLES : (half + 1) * CYCLES]
 
 
 def halve(blocks):
+    count = 4
     return pl.pallas_call(
         halve_kernel,
-        in_specs=[pl.BlockSpec(memory_space=pl.ANY)],
-        out_specs=pl.BlockSpec(memory_space=pl.ANY),
+        grid=(BLOCK // count,),
+        in_specs=[pl.BlockSpec((count, ANGLES, 2 * CYCLES), lambda i: (i, 0, 0))],
+        out_specs=pl.BlockSpec((count, 2, ANGLES, CYCLES), lambda i: (i, 0, 0, 0)),
         out_shape=jax.ShapeDtypeStruct((BLOCK, 2, ANGLES, CYCLES), jnp.bfloat16),
-        scratch_shapes=[pltpu.SemaphoreType.DMA((2,))],
-        compiler_params=pltpu.CompilerParams(vmem_limit_bytes=1024 * 1024),
+        compiler_params=pltpu.CompilerParams(vmem_limit_bytes=60 * 1024 * 1024),
     )(blocks)
 
 
@@ -386,12 +380,12 @@
 def finish_table(cosine_table, sine_table):
     def laid(table):
         table = table.reshape(ANGLES, 8, 1, ROWS)
-        return jnp.pad(table, ((0, 0), (0, 0), (0, 0), (0, 1)))
+        return np.pad(table, ((0, 0), (0, 0), (0, 0), (0, 1)))
 
     cosine, sine = laid(cosine_table), laid(sine_table)
-    real = jnp.concatenate([cosine, -sine], axis=2).reshape(ANGLES, 16 * (ROWS + 1))
-    imag = jnp.concatenate([sine, cosine], axis=2).reshape(ANGLES, 16 * (ROWS + 1))
-    return jnp.concatenate([real, imag])
+    real = np.concatenate([cosine, -sine], axis=2).reshape(ANGLES, 16 * (ROWS + 1))
+    imag = np.concatenate([sine, cosine], axis=2).reshape(ANGLES, 16 * (ROWS + 1))
+    return np.concatenate([real, imag])
 
 
 def fetch(blocks, holders, images, contrast_rows, table, small):
@@ -420,23 +414,22 @@
     class_group = lax.axis_index("narrow")
     core = lax.axis_index("wide_2")
     cosine_table, sine_table = angle_tables(ANGLES)
-    cosines_low = cosine_table.astype(jnp.bfloat16)
-    sines_low = sine_table.astype(jnp.bfloat16)
     leading_class = class_group * CLS_GRP
     arrival = jnp.arange(CLS_GRP, dtype=jnp.int32)
     within = arrival % STEPS * BLOCK + arrival // STEPS
     class_ids = leading_class + within
-    holders = lax.dynamic_index_in_dim(roster, class_group, 0, keepdims=False)
-
-    low_table = jnp.concatenate([cosines_low, sines_low])
-    turn = jnp.concatenate([cosine_table, -sine_table], axis=-1)
+    mine_group = jnp.arange(8, dtype=jnp.int32)[:, None] == class_group
+    holders = jnp.sum(jnp.where(mine_group, roster, 0), axis=0)
+
+    low_table = np.concatenate([cosine_table, sine_table]).astype(jnp.bfloat16)
+    turn = np.concatenate([cosine_table, -sine_table], axis=-1)
     filled = ((0, CYCLES - ANGLES), (0, 0))
-    back = jnp.concatenate([jnp.pad(cosine_table, filled), jnp.pad(sine_table, filled)])
+    back = np.concatenate([np.pad(cosine_table, filled), np.pad(sine_table, filled)])
     contrast_rows = contrast(defocus)
     square = contrast_rows * contrast_rows
     prior = rotation_prior(rotation_index).T
     member = (class_index[None, :] == class_ids[:, None]).astype(jnp.float32)
-    owners = lax.dynamic_slice_in_dim(owner_map, leading_class, CLS_GRP)
+    owners = jnp.sum(jnp.where(mine_group, owner_map.reshape(8, CLS_GRP), 0), axis=0)
     owners = owners.reshape(STEPS, BLOCK).T.reshape(CLS_GRP)
     same = owners[:, None] == owners[None, :]
     ranking = jnp.sum(same & (within[None, :] < within[:, None]), axis=1)
@@ -444,23 +437,23 @@
     place = jnp.arange(ROWS + 1, dtype=jnp.int32)[:, None] * 1024 + place[None, :]
     place = place.reshape(1, (ROWS + 1) * CLS_GRP)
     table = finish_table(cosine_table, sine_table)
-    small = (turn, back, square, prior, member, place, table)
+    small = (square, prior, member, place)
 
     mine, early, late, small = fetch(
         ref_store[0, 0], holders, images, contrast_rows, low_table, small
     )
-    turn, back, square, prior, member, place, table = small
+    square, prior, member, place = small
     other = swapped(mine)
     keep, send, evidence = score(
         core.reshape(1), mine, other, early, late, low_table, turn, back, square, prior, member
     )
-    got, evidence = lax.optimization_barrier((swapped(send), exchanged_evidence(evidence, 1)))
-    share = pack(keep, got).reshape(8, (ROWS + 1) * CLS_GRP, CYCLES)
+    share = pack(keep, swapped(send)).reshape(8, (ROWS + 1) * CLS_GRP, CYCLES)
     share = lax.all_to_all(share, "wide_1", 0, 0, tiled=True)
     sent = route(core.reshape(1), place, share).reshape(64, (ROWS + 1) * OWN_MAX, CYCLES)
     sent, evidence = lax.optimization_barrier((sent, evidence))
     got = lax.all_to_all(sent, WIDE, 0, 0, tiled=True)
-    evidence = exchanged_evidence(exchanged_evidence(evidence, 2), 4)
+    for bit in (2, 4, 1):
+        evidence = exchanged_evidence(evidence, bit)
     log_evidence = evidence[0] + jnp.log(evidence[1])
     got = got.reshape(4, 16 * (ROWS + 1) * OWN_MAX, CYCLES)
     new_references = finish(table, got).reshape(1, 1, OWN_MAX, ANGLES, 2 * CYCLES)

time: 135 us -> 132 us (0.978)
  starting transfers between devices: 45.8 us -> 43.2 us
  local copies, waits for them, and re-layouts: 3.1 us -> 1.75 us
    all_to_all x1, waiting for transfers between devices: 10.4 us -> 5.64 us  [per_device(): got = lax.all_to_all(sent, WIDE, 0, 0, tiled=True)]
    all_to_all x1, blocking collectives: 17.2 us -> 19.7 us  [per_device(): share = lax.all_to_all(share, 'wide_1', 0, 0, tiled=True)]
    all_to_all x1, starting transfers between devices: 8.07 us -> 5.72 us  [per_device(): got = lax.all_to_all(sent, WIDE, 0, 0, tiled=True)]
    ppermute x2, waiting for transfers between devices: 1.4 us -> 3.44 us  [swapped(): return lax.ppermute(x, 'wide_2', [(0, 1), (1, 0)])]
  transfers between devices with their start and end apart: 8 -> 8, of which waited for: 7 -> 8; matrix products, arithmetic and copies ran while one was open for 4% -> 3% of each run, Pallas kernels for 8% -> 9%
where the time goes in v7:
time: 132 us; the launch traced here: 131 us
  starting transfers between devices  43.2 us (33%)
  blocking collectives  34.2 us (26%)
  Pallas kernels  27.2 us (21%)
  waiting for transfers between devices  20.7 us (16%)
  other arithmetic  2.85 us (2%)
  local copies, waits for them, and re-layouts  1.75 us (1%)
    all_to_all x1, blocking collectives, per_device(): share = lax.all_to_all(share, 'wide_1', 0, 0, tiled=True)  19.7 us
    all_to_all x1, blocking collectives, fetch(): lax.all_to_all(picked, 'wide_1', 0, 0, tiled=True)  14.5 us
    all_to_all x1, starting transfers between devices, fetch(): sliced = lax.all_to_all(halves, ('wide_1', 'wide_2'), 0, 0, tiled=True)  11.8 us
    pallas_call x2, Pallas kernels, image_spectra(): pl.pallas_call(spectra_kernel, grid=(particles // count,), in_specs=[pl.B...  11.2 us
    ppermute x3, starting transfers between devices, exchanged_evidence(): got = lax.ppermute(pair, 'narrow', [(k, k ^ bit) for k in range(8)])  10.1 us
    pallas_call x1, Pallas kernels, score(): pl.pallas_call(score_kernel, in_specs=[pl.BlockSpec(memory_space=pltpu.SM...  9.8 us
    ppermute x2, starting transfers between devices, swapped(): return lax.ppermute(x, 'wide_2', [(0, 1), (1, 0)])  8.75 us
    all_to_all x1, starting transfers between devices, fetch(): planes = lax.all_to_all(picked, 'wide_0', 0, 0, tiled=True)  6.81 us
  transfers between devices with their start and end apart: 8, of which 8 were waited for; matrix products, arithmetic and copies ran while one was open for 3% of the time, Pallas kernels for 9%

profile of v7, /device:TPU:1, one launch (start us, length us, event | category | flops | bytes accessed | tf_op | source)
XLA Modules:
  0.0 130.7 jit_solution(3147141835516509337)
XLA Ops:
  0.6 1.7 %shard_map.122 = bf16[8,2,72,128]{3,2,1,0:T(8,128)(2,1)} custom-call(bf16[8,72,256]{2,1,0:T(8,128)(2,1)} %bitcast.18), custom_call_target="tpu_custom_call" | custom-call | tf_op jit(solution)/shard_map/pallas_call | solution.py:299
  2.3 11.8 %all-to-all-start = ((bf16[16,72,128]{2,1,0:T(8,128)(2,1)}), bf16[16,72,128]{2,1,0:T(8,128)(2,1)S(1)}, u32[]{:S(2)}, u32[]{:S(2)}) async-start(bf16[16,72,128]{2,1,0:T(8,128)(2,1)} %bitcast.17), calls=%async_computation | async-start | bytes 589824 | tf_op jit(solution)/shard_map/all_to_all | solution.py:394
  14.2 0.8 select_reduce_fusion.1
  15.0 0.7 multiply_multiply_fusion
  15.7 0.8 reshape.134
  16.4 0.1 select_reduce_fusion
  16.5 0.1 reshape.135
  16.6 0.1 copy.15
  16.7 0.1 reshape.136
  16.8 0.3 fusion.7
  17.1 0.6 fusion.12
  17.7 0.2 convert_reduce_fusion
  17.9 0.0 copy-start.4
  17.9 5.6 %shard_map.123.early_ref = bf16[72,64,256]{2,1,0:T(8,128)(2,1)} custom-call(bf16[144,72]{1,0:T(8,128)(2,1)} %constant.86.clone.table_ref.low_ref, f32[64,128]{1,0:T(8,128)} %get-tuple-element.35.contrast_ref, bf16[128,72,256]{2,1,0:T(8,128)(2,1)} %image_ref.3), custom_call_target="tpu_custom_call" | custom-call | flops 339738624 | bytes 4718592 | tf_op jit(solution)/shard_map/pallas_call | solution.py:72
  23.5 0.0 copy-done.5
  23.5 0.1 compare_convert_fusion.member_ref
  23.6 2.9 %all-to-all-done = bf16[16,72,128]{2,1,0:T(8,128)(2,1)S(1)} async-done(((bf16[16,72,128]{2,1,0:T(8,128)(2,1)}), bf16[16,72,128]{2,1,0:T(8,128)(2,1)S(1)}, u32[]{:S(2)}, u32[]{:S(2)}) %all-to-all-start) | async-done | bytes 294944 | tf_op jit(solution)/shard_map/all_to_all | solution.py:394
  26.5 1.3 shard_map.124
  27.8 6.8 %all-to-all-start.1 = ((bf16[4,3,72,128]{3,2,1,0:T(8,128)(2,1)}), bf16[4,3,72,128]{3,2,1,0:T(8,128)(2,1)S(1)}, u32[]{:S(2)}, u32[]{:S(2)}) async-start(bf16[4,3,72,128]{3,2,1,0:T(8,128)(2,1)} %shard_map.124), calls=%async_computation.1 | async-start | bytes 442368 | tf_op jit(solution)/shard_map/all_to_all | solution.py:398
  34.6 0.1 broadcast_add_fusion
  34.7 0.1 add.130.place_ref
  34.8 0.0 copy-done.4
  34.8 0.0 copy-start
  34.8 0.0 copy-start.2
  34.8 0.0 copy-start.3
  34.8 5.6 %shard_map.125.late_ref = bf16[72,64,256]{2,1,0:T(8,128)(2,1)} custom-call(bf16[144,72]{1,0:T(8,128)(2,1)} %constant.86.clone.table_ref.low_ref, f32[64,128]{1,0:T(8,128)} %get-tuple-element.17.contrast_ref, bf16[128,72,256]{2,1,0:T(8,128)(2,1)} %image_ref.3), custom_call_target="tpu_custom_call" | custom-call | flops 339738624 | bytes 4718592 | tf_op jit(solution)/shard_map/pallas_call | solution.py:72
  40.5 3.4 %all-to-all-done.1.source_ref = bf16[4,3,72,128]{3,2,1,0:T(8,128)(2,1)S(1)} async-done(((bf16[4,3,72,128]{3,2,1,0:T(8,128)(2,1)}), bf16[4,3,72,128]{3,2,1,0:T(8,128)(2,1)S(1)}, u32[]{:S(2)}, u32[]{:S(2)}) %all-to-all-start.1) | async-done | bytes 221216 | tf_op jit(solution)/shard_map/all_to_all | solution.py:398
  43.8 0.6 shard_map.126
  44.4 14.5 %all_to_all.25 = bf16[8,3,72,128]{3,2,1,0:T(8,128)(2,1)S(1)} all-to-all(bf16[8,3,72,128]{3,2,1,0:T(8,128)(2,1)S(1)} %shard_map.126), channel_id=1, replica_groups=mesh['wide_0'=4,'wide_1'=8,'wide_2'=2,'narrow'=8] {'wide_1'}, dimensions={0} | all-to-all | bytes 884736 | tf_op jit(solution)/shard_map/all_to_all | solution.py:402
  59.0 6.5 %collective-permute-start = (bf16[24,72,128]{2,1,0:T(8,128)(2,1)S(1)}, bf16[24,72,128]{2,1,0:T(8,128)(2,1)S(1)}, u32[]{:S(2)}, u32[]{:S(2)}) collective-permute-start(bf16[24,72,128]{2,1,0:T(8,128)(2,1)S(1)} %bitcast.14), channel_id=1, source_target_pairs={{0,8},{8,0},{1,9},{9,1},{2,10},{10,2},{3,11},{11,3},{4,12},{12,4},... | collective-permute-start | bytes 1327112 | tf_op jit(solution)/shard_map/ppermute | solution.py:30
  65.4 1.4 %collective-permute-done.other_ref = bf16[24,72,128]{2,1,0:T(8,128)(2,1)S(1)} collective-permute-done((bf16[24,72,128]{2,1,0:T(8,128)(2,1)S(1)}, bf16[24,72,128]{2,1,0:T(8,128)(2,1)S(1)}, u32[]{:S(2)}, u32[]{:S(2)}) %collective-permute-start) | collective-permute-done | bytes 442400 | tf_op jit(solution)/shard_map/ppermute | solution.py:30
  66.8 0.0 copy-done
  66.8 9.8 %shard_map.127 = (f32[73,24,128]{2,1,0:T(8,128)S(1)}, f32[73,24,128]{2,1,0:T(8,128)S(1)}, f32[2,128]{1,0:T(2,128)S(1)}) custom-call(s32[1]{0:T(128)} %bitcast.core_ref, bf16[24,72,128]{2,1,0:T(8,128)(2,1)S(1)} %bitcast.15, bf16[24,72,128]{2,1,0:T(8,128)(2,1)S(1)} %collective-permute-done.other_ref, bf16[72,64,256]{2,1,0:T(8,128)(2,1)} %shard_map.123.early_ref, ...), custom_call_target="tpu_custom_call" | custom-call | tf_op jit(solution)/shard_map/pallas_call | solution.py:244
  76.6 2.3 %collective-permute-start.1 = (f32[73,24,128]{2,1,0:T(8,128)S(1)}, f32[73,24,128]{2,1,0:T(8,128)S(1)}, u32[]{:S(2)}, u32[]{:S(2)}) collective-permute-start(f32[73,24,128]{2,1,0:T(8,128)S(1)} %get-tuple-element.26), channel_id=1, source_target_pairs={{0,8},{8,0},{1,9},{9,1},{2,10},{10,2},{3,11},{11,3},{4,12},{12,4},... | collective-permute-start | bytes 2691080 | tf_op jit(solution)/shard_map/ppermute | solution.py:30
  78.9 2.0 %collective-permute-done.1.got_ref = f32[73,24,128]{2,1,0:T(8,128)S(1)} collective-permute-done((f32[73,24,128]{2,1,0:T(8,128)S(1)}, f32[73,24,128]{2,1,0:T(8,128)S(1)}, u32[]{:S(2)}, u32[]{:S(2)}) %collective-permute-start.1) | collective-permute-done | bytes 897056 | tf_op jit(solution)/shard_map/ppermute | solution.py:30
  81.0 0.1 shard_map.128
  81.1 19.7 %all_to_all.26.got_ref = bf16[8,240,128]{2,1,0:T(8,128)(2,1)S(1)} all-to-all(bf16[8,240,128]{2,1,0:T(8,128)(2,1)S(1)} %bitcast.13), channel_id=1, replica_groups=mesh['wide_0'=4,'wide_1'=8,'wide_2'=2,'narrow'=8] {'wide_1'}, dimensions={0} | all-to-all | bytes 983040 | tf_op jit(solution)/shard_map/all_to_all | solution.py:451
  100.7 1.4 %shard_map.129 = bf16[2560,128]{1,0:T(8,128)(2,1)} custom-call(s32[1]{0:T(128)} %bitcast.core_ref, s32[1,240]{1,0:T(1,128)S(1)} %add.130.place_ref, bf16[8,240,128]{2,1,0:T(8,128)(2,1)S(1)} %all_to_all.26.got_ref), custom_call_target="tpu_custom_call" | custom-call | tf_op jit(solution)/shard_map/pallas_call | solution.py:332
  102.1 5.7 %all-to-all-start.4 = ((bf16[64,40,128]{2,1,0:T(8,128)(2,1)}), bf16[64,40,128]{2,1,0:T(8,128)(2,1)S(1)}, u32[]{:S(2)}, u32[]{:S(2)}) async-start(bf16[64,40,128]{2,1,0:T(8,128)(2,1)} %bitcast.7), calls=%async_computation.4 | async-start | bytes 1310720 | tf_op jit(solution)/shard_map/all_to_all | solution.py:454
  107.9 3.1 %collective-permute-start.2 = (f32[2,128]{1,0:T(2,128)S(1)}, f32[2,128]{1,0:T(2,128)S(1)}, u32[]{:S(2)}, u32[]{:S(2)}) collective-permute-start(f32[2,128]{1,0:T(2,128)S(1)} %get-tuple-element.29), channel_id=1, source_target_pairs={{0,2},{1,3},{2,0},{3,1},{4,6},{5,7},{6,4},{7,5},{8,10},{9,11},{10,... | collective-permute-start | bytes 3080 | tf_op jit(solution)/shard_map/ppermute | solution.py:407
  111.0 1.5 %collective-permute-done.2 = f32[2,128]{1,0:T(2,128)S(1)} collective-permute-done((f32[2,128]{1,0:T(2,128)S(1)}, f32[2,128]{1,0:T(2,128)S(1)}, u32[]{:S(2)}, u32[]{:S(2)}) %collective-permute-start.2) | collective-permute-done | bytes 1056 | tf_op jit(solution)/shard_map/ppermute | solution.py:407
  112.5 4.6 %collective-permute-start.3 = (f32[2,128]{1,0:T(2,128)S(1)}, f32[2,128]{1,0:T(2,128)S(1)}, u32[]{:S(2)}, u32[]{:S(2)}) collective-permute-start(f32[2,128]{1,0:T(2,128)S(1)} %pad_maximum_fusion), channel_id=1, source_target_pairs={{0,4},{1,5},{2,6},{3,7},{4,0},{5,1},{6,2},{7,3},{8,12},{9,13},{10,... | collective-permute-start | bytes 3080 | tf_op jit(solution)/shard_map/ppermute | solution.py:407
  117.2 1.5 %collective-permute-done.3 = f32[2,128]{1,0:T(2,128)S(1)} collective-permute-done((f32[2,128]{1,0:T(2,128)S(1)}, f32[2,128]{1,0:T(2,128)S(1)}, u32[]{:S(2)}, u32[]{:S(2)}) %collective-permute-start.3) | collective-permute-done | bytes 1056 | tf_op jit(solution)/shard_map/ppermute | solution.py:407
  118.6 2.3 %collective-permute-start.4 = (f32[2,128]{1,0:T(2,128)S(1)}, f32[2,128]{1,0:T(2,128)S(1)}, u32[]{:S(2)}, u32[]{:S(2)}) collective-permute-start(f32[2,128]{1,0:T(2,128)S(1)} %pad_maximum_fusion.1), channel_id=1, source_target_pairs={{0,1},{1,0},{2,3},{3,2},{4,5},{5,4},{6,7},{7,6},{8,9},{9,8},{10,11... | collective-permute-start | bytes 3080 | tf_op jit(solution)/shard_map/ppermute | solution.py:407
  120.9 2.4 %collective-permute-done.4 = f32[2,128]{1,0:T(2,128)S(1)} collective-permute-done((f32[2,128]{1,0:T(2,128)S(1)}, f32[2,128]{1,0:T(2,128)S(1)}, u32[]{:S(2)}, u32[]{:S(2)}) %collective-permute-start.4) | collective-permute-done | bytes 1056 | tf_op jit(solution)/shard_map/ppermute | solution.py:407
  123.3 0.5 add_bitcast_fusion
  123.9 5.6 %all-to-all-done.4 = bf16[64,40,128]{2,1,0:T(8,128)(2,1)S(1)} async-done(((bf16[64,40,128]{2,1,0:T(8,128)(2,1)}), bf16[64,40,128]{2,1,0:T(8,128)(2,1)S(1)}, u32[]{:S(2)}, u32[]{:S(2)}) %all-to-all-start.4) | async-done | bytes 655392 | tf_op jit(solution)/shard_map/all_to_all | solution.py:454
  129.5 1.2 shard_map.130
  (16 shorter events, 0.1 us)
Async XLA Ops:
  2.3 24.2 %all-to-all-start = ((bf16[16,72,128]{2,1,0:T(8,128)(2,1)}), bf16[16,72,128]{2,1,0:T(8,128)(2,1)S(1)}, u32[]{:S(2)}, u32[]{:S(2)}) async-start(bf16[16,72,128]{2,1,0:T(8,128)(2,1)} %bitcast.17), calls=%async_computation | async-start | bytes 589824 | tf_op jit(solution)/shard_map/all_to_all | solution.py:394
  17.9 5.6 %copy-start.5 = (s32[128]{0:T(128)S(1)}, s32[128]{0:T(128)}, u32[]{:S(2)}) copy-start(s32[128]{0:T(128)} %param.13) | copy-start | bytes 1540
  17.9 16.9 %copy-start.4 = (s32[128]{0:T(128)S(1)}, s32[128]{0:T(128)}, u32[]{:S(2)}) copy-start(s32[128]{0:T(128)} %param.14) | copy-start | bytes 1540
  27.8 16.0 %all-to-all-start.1 = ((bf16[4,3,72,128]{3,2,1,0:T(8,128)(2,1)}), bf16[4,3,72,128]{3,2,1,0:T(8,128)(2,1)S(1)}, u32[]{:S(2)}, u32[]{:S(2)}) async-start(bf16[4,3,72,128]{3,2,1,0:T(8,128)(2,1)} %shard_map.124), calls=%async_computation.1 | async-start | bytes 442368 | tf_op jit(solution)/shard_map/all_to_all | solution.py:398
  34.8 32.0 %copy-start = (bf16[144,72]{1,0:T(8,128)(2,1)S(1)}, bf16[144,72]{1,0:T(8,128)(2,1)}, u32[]{:S(2)}) copy-start(bf16[144,72]{1,0:T(8,128)(2,1)} %constant.86.clone.table_ref.low_ref) | copy-start | bytes 62212
  34.8 32.0 %copy-start.2 = (f32[256,72]{1,0:T(8,128)S(1)}, f32[256,72]{1,0:T(8,128)}, u32[]{:S(2)}) copy-start(f32[256,72]{1,0:T(8,128)} %constant.88.clone.back_ref) | copy-start | bytes 221188
  34.8 32.0 %copy-start.3 = (f32[72,144]{1,0:T(8,128)S(1)}, f32[72,144]{1,0:T(8,128)}, u32[]{:S(2)}) copy-start(f32[72,144]{1,0:T(8,128)} %constant.87.clone.turn_ref) | copy-start | bytes 124420
  59.0 7.9 %collective-permute-start = (bf16[24,72,128]{2,1,0:T(8,128)(2,1)S(1)}, bf16[24,72,128]{2,1,0:T(8,128)(2,1)S(1)}, u32[]{:S(2)}, u32[]{:S(2)}) collective-permute-start(bf16[24,72,128]{2,1,0:T(8,128)(2,1)S(1)} %bitcast.14), channel_id=1, source_target_pairs={{0,8},{8,0},{1,9},{9,1},{2,10},{10,2},{3,11},{11,3},{4,12},{12,4},... | collective-permute-start | bytes 1327112 | tf_op jit(solution)/shard_map/ppermute | solution.py:30
  76.6 4.3 %collective-permute-start.1 = (f32[73,24,128]{2,1,0:T(8,128)S(1)}, f32[73,24,128]{2,1,0:T(8,128)S(1)}, u32[]{:S(2)}, u32[]{:S(2)}) collective-permute-start(f32[73,24,128]{2,1,0:T(8,128)S(1)} %get-tuple-element.26), channel_id=1, source_target_pairs={{0,8},{8,0},{1,9},{9,1},{2,10},{10,2},{3,11},{11,3},{4,12},{12,4},... | collective-permute-start | bytes 2691080 | tf_op jit(solution)/shard_map/ppermute | solution.py:30
  81.0 48.5 %copy-start.1 = (f32[144,160]{1,0:T(8,128)S(1)}, f32[144,160]{1,0:T(8,128)}, u32[]{:S(2)}) copy-start(f32[144,160]{1,0:T(8,128)} %constant.89.clone.table_ref) | copy-start | bytes 276484
  102.1 27.4 %all-to-all-start.4 = ((bf16[64,40,128]{2,1,0:T(8,128)(2,1)}), bf16[64,40,128]{2,1,0:T(8,128)(2,1)S(1)}, u32[]{:S(2)}, u32[]{:S(2)}) async-start(bf16[64,40,128]{2,1,0:T(8,128)(2,1)} %bitcast.7), calls=%async_computation.4 | async-start | bytes 1310720 | tf_op jit(solution)/shard_map/all_to_all | solution.py:454
  107.9 4.6 %collective-permute-start.2 = (f32[2,128]{1,0:T(2,128)S(1)}, f32[2,128]{1,0:T(2,128)S(1)}, u32[]{:S(2)}, u32[]{:S(2)}) collective-permute-start(f32[2,128]{1,0:T(2,128)S(1)} %get-tuple-element.29), channel_id=1, source_target_pairs={{0,2},{1,3},{2,0},{3,1},{4,6},{5,7},{6,4},{7,5},{8,10},{9,11},{10,... | collective-permute-start | bytes 3080 | tf_op jit(solution)/shard_map/ppermute | solution.py:407
  112.5 6.1 %collective-permute-start.3 = (f32[2,128]{1,0:T(2,128)S(1)}, f32[2,128]{1,0:T(2,128)S(1)}, u32[]{:S(2)}, u32[]{:S(2)}) collective-permute-start(f32[2,128]{1,0:T(2,128)S(1)} %pad_maximum_fusion), channel_id=1, source_target_pairs={{0,4},{1,5},{2,6},{3,7},{4,0},{5,1},{6,2},{7,3},{8,12},{9,13},{10,... | collective-permute-start | bytes 3080 | tf_op jit(solution)/shard_map/ppermute | solution.py:407
  118.6 4.7 %collective-permute-start.4 = (f32[2,128]{1,0:T(2,128)S(1)}, f32[2,128]{1,0:T(2,128)S(1)}, u32[]{:S(2)}, u32[]{:S(2)}) collective-permute-start(f32[2,128]{1,0:T(2,128)S(1)} %pad_maximum_fusion.1), channel_id=1, source_target_pairs={{0,1},{1,0},{2,3},{3,2},{4,5},{5,4},{6,7},{7,6},{8,9},{9,8},{10,11... | collective-permute-start | bytes 3080 | tf_op jit(solution)/shard_map/ppermute | solution.py:407

commit v8 on v7

--- a/solution.py
+++ b/solution.py
@@ -30,11 +30,17 @@
     return lax.ppermute(x, "wide_2", [(0, 1), (1, 0)])
 
 
+def stepped(classes):
+    length = lax.axis_size("wide_1")
+    got = lax.ppermute(classes, "wide_1", [(k, (k + 1) % length) for k in range(length)])
+    return got[:, :1] >> 8
+
+
 def angle_tables(length):
     counting = np.arange(length)
     products = counting[:, None] * counting[None, :] % length
-    phase_angle = products.astype(np.float64) * (2.0 * math.pi / length)
-    return (np.cos(phase_angle).astype(np.float32), np.sin(phase_angle).astype(np.float32))
+    phase_angle = products.astype(np.float32) * np.float32(2.0 * math.pi / length)
+    return (np.cos(phase_angle), np.sin(phase_angle))
 
 
 def contrast(defocus_rows):
@@ -388,19 +394,21 @@
     return np.concatenate([real, imag])
 
 
-def fetch(blocks, holders, images, contrast_rows, table, small):
+def fetch(blocks, holders, images, contrast_rows, table, classes, small):
     half = contrast_rows.shape[0] // 2
     halves = halve(blocks).reshape(BLOCK * 2, ANGLES, CYCLES)
     sliced = lax.all_to_all(halves, ("wide_1", "wide_2"), 0, 0, tiled=True)
     early = image_spectra(images, 0, contrast_rows[:half], table)
-    sliced, early, later = lax.optimization_barrier((sliced, early, contrast_rows[half:]))
+    sliced, early, later, classes, small = lax.optimization_barrier(
+        (sliced, early, contrast_rows[half:], classes, small)
+    )
     picked = pick(sliced[:, None], holders % 16, 4)
     planes = lax.all_to_all(picked, "wide_0", 0, 0, tiled=True)
     late = image_spectra(images, 1, later, table)
-    planes, late, small = lax.optimization_barrier((planes, late, small))
+    planes, late, step = lax.optimization_barrier((planes, late, stepped(classes)))
     picked = pick(planes, holders // 16, 8)
     mine = lax.all_to_all(picked, "wide_1", 0, 0, tiled=True).reshape(CLS_GRP, ANGLES, CYCLES)
-    return mine, early, late, small
+    return mine, early, late, (*small, step)
 
 
 def exchanged_evidence(pair, bit):
@@ -435,14 +443,14 @@
     ranking = jnp.sum(same & (within[None, :] < within[:, None]), axis=1)
     place = owners * OWN_MAX + ranking
     place = jnp.arange(ROWS + 1, dtype=jnp.int32)[:, None] * 1024 + place[None, :]
-    place = place.reshape(1, (ROWS + 1) * CLS_GRP)
+    small = (square, prior, member, place.reshape(1, (ROWS + 1) * CLS_GRP))
+    classes = class_index[None, :]
     table = finish_table(cosine_table, sine_table)
-    small = (square, prior, member, place)
-
     mine, early, late, small = fetch(
-        ref_store[0, 0], holders, images, contrast_rows, low_table, small
-    )
-    square, prior, member, place = small
+        ref_store[0, 0], holders, images, contrast_rows, low_table, classes, small
+    )
+    square, prior, member, place, step = small
+    mine, place = lax.optimization_barrier((mine, place + step))
     other = swapped(mine)
     keep, send, evidence = score(
         core.reshape(1), mine, other, early, late, low_table, turn, back, square, prior, member

time: 132 us -> 135 us (1.023)
  blocking collectives: 34.2 us -> 19.7 us
  waiting for transfers between devices: 20.7 us -> 31.7 us
  starting transfers between devices: 43.2 us -> 49.2 us
    all_to_all x1 -> x0, blocking collectives: 14.5 us -> none  [fetch(): lax.all_to_all(picked, 'wide_1', 0, 0, tiled=True)]
    all_to_all x0 -> x1, waiting for transfers between devices: none -> 13.1 us  [fetch(): lax.all_to_all(picked, 'wide_1', 0, 0, tiled=True)]
    all_to_all x0 -> x1, starting transfers between devices: none -> 3.47 us  [fetch(): lax.all_to_all(picked, 'wide_1', 0, 0, tiled=True)]
    ppermute x0 -> x1, starting transfers between devices: none -> 2.05 us  [stepped(): lax.ppermute(classes, 'wide_1', [(k, (k + 1) % length) for k in range(len...]
    all_to_all x1, waiting for transfers between devices: 3.35 us -> 1.49 us  [fetch(): planes = lax.all_to_all(picked, 'wide_0', 0, 0, tiled=True)]
    all_to_all x1, starting transfers between devices: 5.72 us -> 7.23 us  [per_device(): got = lax.all_to_all(sent, WIDE, 0, 0, tiled=True)]
  transfers between devices with their start and end apart: 8 -> 10, of which waited for: 8 -> 9; matrix products, arithmetic and copies ran while one was open for 3% -> 3% of each run, Pallas kernels for 9% -> 8%
where the time goes in v8:
time: 135 us; the launch traced here: 134 us
  starting transfers between devices  49.2 us (36%)
  waiting for transfers between devices  31.7 us (23%)
  Pallas kernels  28 us (21%)
  blocking collectives  19.7 us (15%)
  other arithmetic  2.85 us (2%)
  local copies, waits for them, and re-layouts  1.74 us (1%)
    all_to_all x1, blocking collectives, per_device(): share = lax.all_to_all(share, 'wide_1', 0, 0, tiled=True)  19.7 us
    all_to_all x1, waiting for transfers between devices, fetch(): lax.all_to_all(picked, 'wide_1', 0, 0, tiled=True)  13.1 us
    all_to_all x1, starting transfers between devices, fetch(): sliced = lax.all_to_all(halves, ('wide_1', 'wide_2'), 0, 0, tiled=True)  11.8 us
    pallas_call x2, Pallas kernels, image_spectra(): pl.pallas_call(spectra_kernel, grid=(particles // count,), in_specs=[pl.B...  11.2 us
    ppermute x3, starting transfers between devices, exchanged_evidence(): got = lax.ppermute(pair, 'narrow', [(k, k ^ bit) for k in range(8)])  10.1 us
    pallas_call x1, Pallas kernels, score(): pl.pallas_call(score_kernel, in_specs=[pl.BlockSpec(memory_space=pltpu.SM...  9.79 us
    ppermute x2, starting transfers between devices, swapped(): return lax.ppermute(x, 'wide_2', [(0, 1), (1, 0)])  7.71 us
    all_to_all x1, starting transfers between devices, per_device(): got = lax.all_to_all(sent, WIDE, 0, 0, tiled=True)  7.23 us
  transfers between devices with their start and end apart: 10, of which 9 were waited for; matrix products, arithmetic and copies ran while one was open for 3% of the time, Pallas kernels for 8%

profile of v8, /device:TPU:1, one launch (start us, length us, event | category | flops | bytes accessed | tf_op | source)
XLA Modules:
  0.0 133.9 jit_solution(7518031667136536658)
XLA Ops:
  0.6 1.7 %shard_map.122 = bf16[8,2,72,128]{3,2,1,0:T(8,128)(2,1)} custom-call(bf16[8,72,256]{2,1,0:T(8,128)(2,1)} %bitcast.21), custom_call_target="tpu_custom_call" | custom-call | tf_op jit(solution)/shard_map/pallas_call | solution.py:305
  2.3 11.8 %all-to-all-start = ((bf16[16,72,128]{2,1,0:T(8,128)(2,1)}), bf16[16,72,128]{2,1,0:T(8,128)(2,1)S(1)}, u32[]{:S(2)}, u32[]{:S(2)}) async-start(bf16[16,72,128]{2,1,0:T(8,128)(2,1)} %bitcast.20), calls=%async_computation | async-start | bytes 589824 | tf_op jit(solution)/shard_map/all_to_all | solution.py:400
  14.2 0.8 select_reduce_fusion.1
  15.0 0.7 multiply_multiply_fusion
  15.7 0.8 reshape.136
  16.4 0.1 select_reduce_fusion
  16.5 0.1 reshape.137
  16.6 0.1 copy.15
  16.7 0.1 reshape.138
  16.8 0.2 convert_reduce_fusion
  16.9 0.1 broadcast_add_fusion
  17.0 0.1 add.140
  17.1 0.3 fusion.7
  17.4 0.6 fusion.12
  18.1 5.6 %shard_map.123.early_ref = bf16[72,64,256]{2,1,0:T(8,128)(2,1)} custom-call(bf16[144,72]{1,0:T(8,128)(2,1)} %constant.88.clone.table_ref.low_ref, f32[64,128]{1,0:T(8,128)} %get-tuple-element.43.contrast_ref, bf16[128,72,256]{2,1,0:T(8,128)(2,1)} %image_ref.3), custom_call_target="tpu_custom_call" | custom-call | flops 339738624 | bytes 4718592 | tf_op jit(solution)/shard_map/pallas_call | solution.py:78
  23.7 0.0 copy-done.5
  23.7 0.1 compare_convert_fusion.member_ref
  23.8 0.0 copy-done.4
  23.8 2.7 %all-to-all-done = bf16[16,72,128]{2,1,0:T(8,128)(2,1)S(1)} async-done(((bf16[16,72,128]{2,1,0:T(8,128)(2,1)}), bf16[16,72,128]{2,1,0:T(8,128)(2,1)S(1)}, u32[]{:S(2)}, u32[]{:S(2)}) %all-to-all-start) | async-done | bytes 294944 | tf_op jit(solution)/shard_map/all_to_all | solution.py:400
  26.5 1.3 shard_map.124
  27.8 6.8 %all-to-all-start.1 = ((bf16[4,3,72,128]{3,2,1,0:T(8,128)(2,1)}), bf16[4,3,72,128]{3,2,1,0:T(8,128)(2,1)S(1)}, u32[]{:S(2)}, u32[]{:S(2)}) async-start(bf16[4,3,72,128]{3,2,1,0:T(8,128)(2,1)} %shard_map.124), calls=%async_computation.1 | async-start | bytes 442368 | tf_op jit(solution)/shard_map/all_to_all | solution.py:406
  34.6 2.1 %collective-permute-start = (s32[1,128]{1,0:T(1,128)S(1)}, s32[1,128]{1,0:T(1,128)S(1)}, u32[]{:S(2)}, u32[]{:S(2)}) collective-permute-start(s32[1,128]{1,0:T(1,128)S(1)} %bitcast.24), channel_id=1, source_target_pairs={{0,16},{16,32},{32,48},{48,64},{64,80},{80,96},{96,112},{112,0},{1... | collective-permute-start | bytes 1544 | tf_op jit(solution)/shard_map/ppermute | solution.py:35
  36.7 5.6 %shard_map.125.late_ref = bf16[72,64,256]{2,1,0:T(8,128)(2,1)} custom-call(bf16[144,72]{1,0:T(8,128)(2,1)} %constant.88.clone.table_ref.low_ref, f32[64,128]{1,0:T(8,128)} %get-tuple-element.21.contrast_ref, bf16[128,72,256]{2,1,0:T(8,128)(2,1)} %image_ref.3), custom_call_target="tpu_custom_call" | custom-call | flops 339738624 | bytes 4718592 | tf_op jit(solution)/shard_map/pallas_call | solution.py:78
  42.3 0.0 collective-permute-done
  42.3 1.5 %all-to-all-done.1.source_ref = bf16[4,3,72,128]{3,2,1,0:T(8,128)(2,1)S(1)} async-done(((bf16[4,3,72,128]{3,2,1,0:T(8,128)(2,1)}), bf16[4,3,72,128]{3,2,1,0:T(8,128)(2,1)S(1)}, u32[]{:S(2)}, u32[]{:S(2)}) %all-to-all-start.1) | async-done | bytes 221216 | tf_op jit(solution)/shard_map/all_to_all | solution.py:406
  43.8 1.4 %shard_map.126 = bf16[8,3,72,128]{3,2,1,0:T(8,128)(2,1)} custom-call(s32[3]{0:T(128)S(1)} %get-tuple-element.47.index_ref, bf16[4,3,72,128]{3,2,1,0:T(8,128)(2,1)S(1)} %all-to-all-done.1.source_ref), custom_call_target="tpu_custom_call" | custom-call | tf_op jit(solution)/shard_map/pallas_call | solution.py:107
  45.2 3.5 %all-to-all-start.2 = ((bf16[8,3,72,128]{3,2,1,0:T(8,128)(2,1)}), bf16[8,3,72,128]{3,2,1,0:T(8,128)(2,1)S(1)}, u32[]{:S(2)}, u32[]{:S(2)}) async-start(bf16[8,3,72,128]{3,2,1,0:T(8,128)(2,1)} %shard_map.126), calls=%async_computation.2 | async-start | bytes 884736 | tf_op jit(solution)/shard_map/all_to_all | solution.py:410
  48.7 13.1 %all-to-all-done.2 = bf16[8,3,72,128]{3,2,1,0:T(8,128)(2,1)S(1)} async-done(((bf16[8,3,72,128]{3,2,1,0:T(8,128)(2,1)}), bf16[8,3,72,128]{3,2,1,0:T(8,128)(2,1)S(1)}, u32[]{:S(2)}, u32[]{:S(2)}) %all-to-all-start.2) | async-done | bytes 442400 | tf_op jit(solution)/shard_map/all_to_all | solution.py:410
  61.7 5.4 %collective-permute-start.1 = (bf16[24,72,128]{2,1,0:T(8,128)(2,1)S(1)}, bf16[24,72,128]{2,1,0:T(8,128)(2,1)S(1)}, u32[]{:S(2)}, u32[]{:S(2)}) collective-permute-start(bf16[24,72,128]{2,1,0:T(8,128)(2,1)S(1)} %bitcast.17), channel_id=1, source_target_pairs={{0,8},{8,0},{1,9},{9,1},{2,10},{10,2},{3,11},{11,3},{4,12},{12,4},... | collective-permute-start | bytes 1327112 | tf_op jit(solution)/shard_map/ppermute | solution.py:30
  67.2 1.4 %collective-permute-done.1.other_ref = bf16[24,72,128]{2,1,0:T(8,128)(2,1)S(1)} collective-permute-done((bf16[24,72,128]{2,1,0:T(8,128)(2,1)S(1)}, bf16[24,72,128]{2,1,0:T(8,128)(2,1)S(1)}, u32[]{:S(2)}, u32[]{:S(2)}) %collective-permute-start.1) | collective-permute-done | bytes 442400 | tf_op jit(solution)/shard_map/ppermute | solution.py:30
  68.6 0.0 copy-done
  68.6 0.0 copy-done.2
  68.6 9.8 %shard_map.127 = (f32[73,24,128]{2,1,0:T(8,128)S(1)}, f32[73,24,128]{2,1,0:T(8,128)S(1)}, f32[2,128]{1,0:T(2,128)S(1)}) custom-call(s32[1]{0:T(128)} %bitcast.core_ref, bf16[24,72,128]{2,1,0:T(8,128)(2,1)S(1)} %bitcast.18, bf16[24,72,128]{2,1,0:T(8,128)(2,1)S(1)} %collective-permute-done.1.other_ref, bf16[72,64,256]{2,1,0:T(8,128)(2,1)} %shard_map.123.early_ref, ...), custom_call_target="tpu_custom_call" | custom-call | tf_op jit(solution)/shard_map/pallas_call | solution.py:250
  78.4 2.3 %collective-permute-start.2 = (f32[73,24,128]{2,1,0:T(8,128)S(1)}, f32[73,24,128]{2,1,0:T(8,128)S(1)}, u32[]{:S(2)}, u32[]{:S(2)}) collective-permute-start(f32[73,24,128]{2,1,0:T(8,128)S(1)} %get-tuple-element.34), channel_id=1, source_target_pairs={{0,8},{8,0},{1,9},{9,1},{2,10},{10,2},{3,11},{11,3},{4,12},{12,4},... | collective-permute-start | bytes 2691080 | tf_op jit(solution)/shard_map/ppermute | solution.py:30
  80.7 2.0 %collective-permute-done.2.got_ref = f32[73,24,128]{2,1,0:T(8,128)S(1)} collective-permute-done((f32[73,24,128]{2,1,0:T(8,128)S(1)}, f32[73,24,128]{2,1,0:T(8,128)S(1)}, u32[]{:S(2)}, u32[]{:S(2)}) %collective-permute-start.2) | collective-permute-done | bytes 897056 | tf_op jit(solution)/shard_map/ppermute | solution.py:30
  82.7 0.1 shard_map.128
  82.8 19.7 %all_to_all.25.got_ref = bf16[8,240,128]{2,1,0:T(8,128)(2,1)S(1)} all-to-all(bf16[8,240,128]{2,1,0:T(8,128)(2,1)S(1)} %bitcast.16), channel_id=1, replica_groups=mesh['wide_0'=4,'wide_1'=8,'wide_2'=2,'narrow'=8] {'wide_1'}, dimensions={0} | all-to-all | bytes 983040 | tf_op jit(solution)/shard_map/all_to_all | solution.py:459
  102.5 1.4 %shard_map.129 = bf16[2560,128]{1,0:T(8,128)(2,1)} custom-call(s32[1]{0:T(128)} %bitcast.core_ref, s32[1,240]{1,0:T(1,128)S(1)} %broadcast_add_fusion.1.place_ref, bf16[8,240,128]{2,1,0:T(8,128)(2,1)S(1)} %all_to_all.25.got_ref), custom_call_target="tpu_custom_call" | custom-call | tf_op jit(solution)/shard_map/pallas_call | solution.py:338
  103.8 7.2 %all-to-all-start.4 = ((bf16[64,40,128]{2,1,0:T(8,128)(2,1)}), bf16[64,40,128]{2,1,0:T(8,128)(2,1)S(1)}, u32[]{:S(2)}, u32[]{:S(2)}) async-start(bf16[64,40,128]{2,1,0:T(8,128)(2,1)} %bitcast.9), calls=%async_computation.4 | async-start | bytes 1310720 | tf_op jit(solution)/shard_map/all_to_all | solution.py:462
  111.1 3.1 %collective-permute-start.3 = (f32[2,128]{1,0:T(2,128)S(1)}, f32[2,128]{1,0:T(2,128)S(1)}, u32[]{:S(2)}, u32[]{:S(2)}) collective-permute-start(f32[2,128]{1,0:T(2,128)S(1)} %get-tuple-element.37), channel_id=1, source_target_pairs={{0,2},{1,3},{2,0},{3,1},{4,6},{5,7},{6,4},{7,5},{8,10},{9,11},{10,... | collective-permute-start | bytes 3080 | tf_op jit(solution)/shard_map/ppermute | solution.py:415
  114.2 1.5 %collective-permute-done.3 = f32[2,128]{1,0:T(2,128)S(1)} collective-permute-done((f32[2,128]{1,0:T(2,128)S(1)}, f32[2,128]{1,0:T(2,128)S(1)}, u32[]{:S(2)}, u32[]{:S(2)}) %collective-permute-start.3) | collective-permute-done | bytes 1056 | tf_op jit(solution)/shard_map/ppermute | solution.py:415
  115.7 4.6 %collective-permute-start.4 = (f32[2,128]{1,0:T(2,128)S(1)}, f32[2,128]{1,0:T(2,128)S(1)}, u32[]{:S(2)}, u32[]{:S(2)}) collective-permute-start(f32[2,128]{1,0:T(2,128)S(1)} %pad_maximum_fusion), channel_id=1, source_target_pairs={{0,4},{1,5},{2,6},{3,7},{4,0},{5,1},{6,2},{7,3},{8,12},{9,13},{10,... | collective-permute-start | bytes 3080 | tf_op jit(solution)/shard_map/ppermute | solution.py:415
  120.4 1.5 %collective-permute-done.4 = f32[2,128]{1,0:T(2,128)S(1)} collective-permute-done((f32[2,128]{1,0:T(2,128)S(1)}, f32[2,128]{1,0:T(2,128)S(1)}, u32[]{:S(2)}, u32[]{:S(2)}) %collective-permute-start.4) | collective-permute-done | bytes 1056 | tf_op jit(solution)/shard_map/ppermute | solution.py:415
  121.9 2.3 %collective-permute-start.5 = (f32[2,128]{1,0:T(2,128)S(1)}, f32[2,128]{1,0:T(2,128)S(1)}, u32[]{:S(2)}, u32[]{:S(2)}) collective-permute-start(f32[2,128]{1,0:T(2,128)S(1)} %pad_maximum_fusion.1), channel_id=1, source_target_pairs={{0,1},{1,0},{2,3},{3,2},{4,5},{5,4},{6,7},{7,6},{8,9},{9,8},{10,11... | collective-permute-start | bytes 3080 | tf_op jit(solution)/shard_map/ppermute | solution.py:415
  124.2 2.4 %collective-permute-done.5 = f32[2,128]{1,0:T(2,128)S(1)} collective-permute-done((f32[2,128]{1,0:T(2,128)S(1)}, f32[2,128]{1,0:T(2,128)S(1)}, u32[]{:S(2)}, u32[]{:S(2)}) %collective-permute-start.5) | collective-permute-done | bytes 1056 | tf_op jit(solution)/shard_map/ppermute | solution.py:415
  126.6 0.5 add_bitcast_fusion
  127.1 5.6 %all-to-all-done.4 = bf16[64,40,128]{2,1,0:T(8,128)(2,1)S(1)} async-done(((bf16[64,40,128]{2,1,0:T(8,128)(2,1)}), bf16[64,40,128]{2,1,0:T(8,128)(2,1)S(1)}, u32[]{:S(2)}, u32[]{:S(2)}) %all-to-all-start.4) | async-done | bytes 655392 | tf_op jit(solution)/shard_map/all_to_all | solution.py:462
  132.7 1.2 shard_map.130
  (20 shorter events, 0.1 us)
Async XLA Ops:
  2.3 24.2 %all-to-all-start = ((bf16[16,72,128]{2,1,0:T(8,128)(2,1)}), bf16[16,72,128]{2,1,0:T(8,128)(2,1)S(1)}, u32[]{:S(2)}, u32[]{:S(2)}) async-start(bf16[16,72,128]{2,1,0:T(8,128)(2,1)} %bitcast.20), calls=%async_computation | async-start | bytes 589824 | tf_op jit(solution)/shard_map/all_to_all | solution.py:400
  18.1 5.6 %copy-start.5 = (s32[128]{0:T(128)S(1)}, s32[128]{0:T(128)}, u32[]{:S(2)}) copy-start(s32[128]{0:T(128)} %param.13) | copy-start | bytes 1540
  18.1 5.7 %copy-start.4 = (s32[128]{0:T(128)S(1)}, s32[128]{0:T(128)}, u32[]{:S(2)}) copy-start(s32[128]{0:T(128)} %param.14) | copy-start | bytes 1540
  27.8 16.0 %all-to-all-start.1 = ((bf16[4,3,72,128]{3,2,1,0:T(8,128)(2,1)}), bf16[4,3,72,128]{3,2,1,0:T(8,128)(2,1)S(1)}, u32[]{:S(2)}, u32[]{:S(2)}) async-start(bf16[4,3,72,128]{3,2,1,0:T(8,128)(2,1)} %shard_map.124), calls=%async_computation.1 | async-start | bytes 442368 | tf_op jit(solution)/shard_map/all_to_all | solution.py:406
  34.6 34.0 %copy-start = (bf16[144,72]{1,0:T(8,128)(2,1)S(1)}, bf16[144,72]{1,0:T(8,128)(2,1)}, u32[]{:S(2)}) copy-start(bf16[144,72]{1,0:T(8,128)(2,1)} %constant.88.clone.table_ref.low_ref) | copy-start | bytes 62212
  34.6 34.0 %copy-start.2 = (f32[256,72]{1,0:T(8,128)S(1)}, f32[256,72]{1,0:T(8,128)}, u32[]{:S(2)}) copy-start(f32[256,72]{1,0:T(8,128)} %constant.90.clone.back_ref) | copy-start | bytes 221188
  34.6 34.0 %copy-start.3 = (f32[72,144]{1,0:T(8,128)S(1)}, f32[72,144]{1,0:T(8,128)}, u32[]{:S(2)}) copy-start(f32[72,144]{1,0:T(8,128)} %constant.89.clone.turn_ref) | copy-start | bytes 124420
  34.6 7.7 %collective-permute-start = (s32[1,128]{1,0:T(1,128)S(1)}, s32[1,128]{1,0:T(1,128)S(1)}, u32[]{:S(2)}, u32[]{:S(2)}) collective-permute-start(s32[1,128]{1,0:T(1,128)S(1)} %bitcast.24), channel_id=1, source_target_pairs={{0,16},{16,32},{32,48},{48,64},{64,80},{80,96},{96,112},{112,0},{1... | collective-permute-start | bytes 1544 | tf_op jit(solution)/shard_map/ppermute | solution.py:35
  45.2 16.6 %all-to-all-start.2 = ((bf16[8,3,72,128]{3,2,1,0:T(8,128)(2,1)}), bf16[8,3,72,128]{3,2,1,0:T(8,128)(2,1)S(1)}, u32[]{:S(2)}, u32[]{:S(2)}) async-start(bf16[8,3,72,128]{3,2,1,0:T(8,128)(2,1)} %shard_map.126), calls=%async_computation.2 | async-start | bytes 884736 | tf_op jit(solution)/shard_map/all_to_all | solution.py:410
  61.7 6.8 %collective-permute-start.1 = (bf16[24,72,128]{2,1,0:T(8,128)(2,1)S(1)}, bf16[24,72,128]{2,1,0:T(8,128)(2,1)S(1)}, u32[]{:S(2)}, u32[]{:S(2)}) collective-permute-start(bf16[24,72,128]{2,1,0:T(8,128)(2,1)S(1)} %bitcast.17), channel_id=1, source_target_pairs={{0,8},{8,0},{1,9},{9,1},{2,10},{10,2},{3,11},{11,3},{4,12},{12,4},... | collective-permute-start | bytes 1327112 | tf_op jit(solution)/shard_map/ppermute | solution.py:30
  78.4 4.3 %collective-permute-start.2 = (f32[73,24,128]{2,1,0:T(8,128)S(1)}, f32[73,24,128]{2,1,0:T(8,128)S(1)}, u32[]{:S(2)}, u32[]{:S(2)}) collective-permute-start(f32[73,24,128]{2,1,0:T(8,128)S(1)} %get-tuple-element.34), channel_id=1, source_target_pairs={{0,8},{8,0},{1,9},{9,1},{2,10},{10,2},{3,11},{11,3},{4,12},{12,4},... | collective-permute-start | bytes 2691080 | tf_op jit(solution)/shard_map/ppermute | solution.py:30
  82.7 50.0 %copy-start.1 = (f32[144,160]{1,0:T(8,128)S(1)}, f32[144,160]{1,0:T(8,128)}, u32[]{:S(2)}) copy-start(f32[144,160]{1,0:T(8,128)} %constant.91.clone.table_ref) | copy-start | bytes 276484
  103.8 28.9 %all-to-all-start.4 = ((bf16[64,40,128]{2,1,0:T(8,128)(2,1)}), bf16[64,40,128]{2,1,0:T(8,128)(2,1)S(1)}, u32[]{:S(2)}, u32[]{:S(2)}) async-start(bf16[64,40,128]{2,1,0:T(8,128)(2,1)} %bitcast.9), calls=%async_computation.4 | async-start | bytes 1310720 | tf_op jit(solution)/shard_map/all_to_all | solution.py:462
  111.1 4.6 %collective-permute-start.3 = (f32[2,128]{1,0:T(2,128)S(1)}, f32[2,128]{1,0:T(2,128)S(1)}, u32[]{:S(2)}, u32[]{:S(2)}) collective-permute-start(f32[2,128]{1,0:T(2,128)S(1)} %get-tuple-element.37), channel_id=1, source_target_pairs={{0,2},{1,3},{2,0},{3,1},{4,6},{5,7},{6,4},{7,5},{8,10},{9,11},{10,... | collective-permute-start | bytes 3080 | tf_op jit(solution)/shard_map/ppermute | solution.py:415
  115.7 6.1 %collective-permute-start.4 = (f32[2,128]{1,0:T(2,128)S(1)}, f32[2,128]{1,0:T(2,128)S(1)}, u32[]{:S(2)}, u32[]{:S(2)}) collective-permute-start(f32[2,128]{1,0:T(2,128)S(1)} %pad_maximum_fusion), channel_id=1, source_target_pairs={{0,4},{1,5},{2,6},{3,7},{4,0},{5,1},{6,2},{7,3},{8,12},{9,13},{10,... | collective-permute-start | bytes 3080 | tf_op jit(solution)/shard_map/ppermute | solution.py:415
  121.9 4.7 %collective-permute-start.5 = (f32[2,128]{1,0:T(2,128)S(1)}, f32[2,128]{1,0:T(2,128)S(1)}, u32[]{:S(2)}, u32[]{:S(2)}) collective-permute-start(f32[2,128]{1,0:T(2,128)S(1)} %pad_maximum_fusion.1), channel_id=1, source_target_pairs={{0,1},{1,0},{2,3},{3,2},{4,5},{5,4},{6,7},{7,6},{8,9},{9,8},{10,11... | collective-permute-start | bytes 3080 | tf_op jit(solution)/shard_map/ppermute | solution.py:415

commit v9 on v7

--- a/solution.py
+++ b/solution.py
@@ -33,8 +33,8 @@
 def angle_tables(length):
     counting = np.arange(length)
     products = counting[:, None] * counting[None, :] % length
-    phase_angle = products.astype(np.float64) * (2.0 * math.pi / length)
-    return (np.cos(phase_angle).astype(np.float32), np.sin(phase_angle).astype(np.float32))
+    phase_angle = products.astype(np.float32) * np.float32(2.0 * math.pi / length)
+    return (np.cos(phase_angle), np.sin(phase_angle))
 
 
 def contrast(defocus_rows):
@@ -66,7 +66,7 @@
 
 
 def image_spectra(images, half, contrast_rows, table):
-    particles = contrast_rows.shape[0]
+    particles = contrast_rows.shape[0] // 2
     count = 16
     skipped = half * particles // count
     return pl.pallas_call(
@@ -74,7 +74,7 @@
         grid=(particles // count,),
         in_specs=[
             pl.BlockSpec((2 * ANGLES, ANGLES), lambda i: (0, 0)),
-            pl.BlockSpec((count, CYCLES), lambda i: (i, 0)),
+            pl.BlockSpec((count, CYCLES), lambda i: (i + skipped, 0)),
             pl.BlockSpec((count, ANGLES, 2 * CYCLES), lambda i: (i + skipped, 0, 0)),
         ],
         out_specs=pl.BlockSpec((ANGLES, count, 2 * CYCLES), lambda i: (0, i, 0)),
@@ -89,25 +89,25 @@
     )(table, contrast_rows, images)
 
 
-def pick_kernel(index_ref, source_ref, out_ref):
+def pick_kernel(group_ref, roster_ref, source_ref, out_ref):
+    planes = source_ref.shape[1] == STEPS
     for step in range(STEPS):
-        at = index_ref[step]
-        value = source_ref[at, step if source_ref.shape[1] == STEPS else 0]
+        holder = roster_ref[group_ref[0], step]
+        value = source_ref[holder >> 4, step] if planes else source_ref[holder & 15, 0]
         for copy in range(out_ref.shape[0]):
             out_ref[copy, step] = value
 
 
-def pick(source, index, copies):
+def pick(group, roster, source, copies):
+    smem = pl.BlockSpec(memory_space=pltpu.SMEM)
+    vmem = pl.BlockSpec(memory_space=pltpu.VMEM)
     return pl.pallas_call(
         pick_kernel,
-        in_specs=[
-            pl.BlockSpec(memory_space=pltpu.SMEM),
-            pl.BlockSpec(memory_space=pltpu.VMEM),
-        ],
-        out_specs=pl.BlockSpec(memory_space=pltpu.VMEM),
+        in_specs=[smem, smem, vmem],
+        out_specs=vmem,
         out_shape=jax.ShapeDtypeStruct((copies, STEPS, ANGLES, CYCLES), jnp.bfloat16),
         compiler_params=pltpu.CompilerParams(vmem_limit_bytes=2 * 1024 * 1024),
-    )(index, source)
+    )(group, roster, source)
 
 
 def score_kernel(
@@ -122,8 +122,7 @@
     square_ref,
     prior_ref,
     member_ref,
-    keep_ref,
-    send_ref,
+    sums_ref,
     evidence_ref,
     ref_real,
     ref_imag,
@@ -226,19 +225,18 @@
             [x_real * hr - x_imag * hi, x_real * hi + x_imag * hr], axis=-1
         ).astype(jnp.bfloat16)
         sums = jnp.dot(chosen, aligned, preferred_element_type=jnp.float32)
-        real_sum, imag_sum = sums[:, :CYCLES], sums[:, CYCLES:]
-        keep_ref[m] = jnp.where(first, real_sum, imag_sum)
-        send_ref[m] = jnp.where(first, imag_sum, real_sum)
+        sums_ref[0, m] = sums[:, :CYCLES]
+        sums_ref[1, m] = sums[:, CYCLES:]
     denom = jnp.dot(
         member, square, precision=TOP_PRECISION, preferred_element_type=jnp.float32
     )
-    keep_ref[ANGLES] = denom
-    send_ref[ANGLES] = denom
+    sums_ref[0, ANGLES] = denom
+    sums_ref[1, ANGLES] = denom
 
 
 def score(core, mine, other, early, late, low_table, turn, back, square, prior, member):
     particles = 2 * early.shape[1]
-    sums = jax.ShapeDtypeStruct((ANGLES + 1, CLS_GRP, CYCLES), jnp.float32)
+    sums = jax.ShapeDtypeStruct((2, ANGLES + 1, CLS_GRP, CYCLES), jnp.float32)
     evidence = jax.ShapeDtypeStruct((2, particles), jnp.float32)
     vmem = pl.BlockSpec(memory_space=pltpu.VMEM)
     return pl.pallas_call(
@@ -246,8 +244,8 @@
         in_specs=[pl.BlockSpec(memory_space=pltpu.SMEM), vmem, vmem]
         + [pl.BlockSpec(memory_space=pltpu.HBM)] * 2
         + [vmem] * 6,
-        out_specs=(vmem, vmem, vmem),
-        out_shape=(sums, sums, evidence),
+        out_specs=(vmem, vmem),
+        out_shape=(sums, evidence),
         scratch_shapes=[
             pltpu.VMEM((ANGLES * CLS_GRP, CYCLES), jnp.float32),
             pltpu.VMEM((ANGLES * CLS_GRP, CYCLES), jnp.float32),
@@ -261,25 +259,25 @@
     )(core, mine, other, early, late, low_table, turn, back, square, prior, member)
 
 
-def pack_kernel(keep_ref, got_ref, out_ref):
-    denom = keep_ref[ANGLES] + got_ref[ANGLES]
+def pack_kernel(got_ref, out_ref):
+    denom = got_ref[0, ANGLES] + got_ref[1, ANGLES]
     high = denom.astype(jnp.bfloat16)
     low = (denom - high.astype(jnp.float32)).astype(jnp.bfloat16)
     for z in range(out_ref.shape[0]):
         at = pl.ds(z * ROWS, ROWS)
-        out_ref[z, :ROWS] = (keep_ref[at] + got_ref[at]).astype(jnp.bfloat16)
+        out_ref[z, :ROWS] = (got_ref[0, at] + got_ref[1, at]).astype(jnp.bfloat16)
         out_ref[z, ROWS] = high if z == 0 else low
 
 
-def pack(keep, got):
+def pack(got):
     vmem = pl.BlockSpec(memory_space=pltpu.VMEM)
     return pl.pallas_call(
         pack_kernel,
-        in_specs=[vmem, vmem],
+        in_specs=[vmem],
         out_specs=vmem,
         out_shape=jax.ShapeDtypeStruct((8, ROWS + 1, CLS_GRP, CYCLES), jnp.bfloat16),
         compiler_params=pltpu.CompilerParams(vmem_limit_bytes=4 * 1024 * 1024),
-    )(keep, got)
+    )(got)
 
 
 def rotation_prior(rotation_rows):
@@ -388,17 +386,16 @@
     return np.concatenate([real, imag])
 
 
-def fetch(blocks, holders, images, contrast_rows, table, small):
-    half = contrast_rows.shape[0] // 2
+def fetch(blocks, group, roster, images, contrast_rows, table, small):
     halves = halve(blocks).reshape(BLOCK * 2, ANGLES, CYCLES)
     sliced = lax.all_to_all(halves, ("wide_1", "wide_2"), 0, 0, tiled=True)
-    early = image_spectra(images, 0, contrast_rows[:half], table)
-    sliced, early, later = lax.optimization_barrier((sliced, early, contrast_rows[half:]))
-    picked = pick(sliced[:, None], holders % 16, 4)
+    early = image_spectra(images, 0, contrast_rows, table)
+    sliced, early, later = lax.optimization_barrier((sliced, early, contrast_rows))
+    picked = pick(group, roster, sliced[:, None], 4)
     planes = lax.all_to_all(picked, "wide_0", 0, 0, tiled=True)
     late = image_spectra(images, 1, later, table)
     planes, late, small = lax.optimization_barrier((planes, late, small))
-    picked = pick(planes, holders // 16, 8)
+    picked = pick(group, roster, planes, 8)
     mine = lax.all_to_all(picked, "wide_1", 0, 0, tiled=True).reshape(CLS_GRP, ANGLES, CYCLES)
     return mine, early, late, small
 
@@ -419,7 +416,6 @@
     within = arrival % STEPS * BLOCK + arrival // STEPS
     class_ids = leading_class + within
     mine_group = jnp.arange(8, dtype=jnp.int32)[:, None] == class_group
-    holders = jnp.sum(jnp.where(mine_group, roster, 0), axis=0)
 
     low_table = np.concatenate([cosine_table, sine_table]).astype(jnp.bfloat16)
     turn = np.concatenate([cosine_table, -sine_table], axis=-1)
@@ -440,14 +436,14 @@
     small = (square, prior, member, place)
 
     mine, early, late, small = fetch(
-        ref_store[0, 0], holders, images, contrast_rows, low_table, small
+        ref_store[0, 0], class_group.reshape(1), roster, images, contrast_rows, low_table, small
     )
     square, prior, member, place = small
     other = swapped(mine)
-    keep, send, evidence = score(
+    sums, evidence = score(
         core.reshape(1), mine, other, early, late, low_table, turn, back, square, prior, member
     )
-    share = pack(keep, swapped(send)).reshape(8, (ROWS + 1) * CLS_GRP, CYCLES)
+    share = pack(lax.all_to_all(sums, "wide_2", 0, 0, tiled=True)).reshape(8, (ROWS + 1) * CLS_GRP, CYCLES)
     share = lax.all_to_all(share, "wide_1", 0, 0, tiled=True)
     sent = route(core.reshape(1), place, share).reshape(64, (ROWS + 1) * OWN_MAX, CYCLES)
     sent, evidence = lax.optimization_barrier((sent, evidence))

time: 132 us -> 133 us (level)
  blocking collectives: 34.2 us -> 39.4 us
  starting transfers between devices: 43.2 us -> 40.8 us
  waiting for transfers between devices: 20.7 us -> 18.7 us
    all_to_all x0 -> x1, blocking collectives: none -> 5.16 us  [per_device(): lax.all_to_all(sums, 'wide_2', 0, 0, tiled=True)]
    ppermute x2 -> x1, starting transfers between devices: 8.75 us -> 6.4 us  [swapped(): return lax.ppermute(x, 'wide_2', [(0, 1), (1, 0)])]
    ppermute x2 -> x1, waiting for transfers between devices: 3.44 us -> 1.39 us  [swapped(): return lax.ppermute(x, 'wide_2', [(0, 1), (1, 0)])]
  transfers between devices with their start and end apart: 8 -> 7, of which waited for: 8 -> 7; matrix products, arithmetic and copies ran while one was open for 3% -> 3% of each run, Pallas kernels for 9% -> 9%
where the time goes in v9:
time: 133 us; the launch traced here: 132 us
  starting transfers between devices  40.8 us (31%)
  blocking collectives  39.4 us (30%)
  Pallas kernels  27.3 us (21%)
  waiting for transfers between devices  18.7 us (14%)
  other arithmetic  2.68 us (2%)
  local copies, waits for them, and re-layouts  1.87 us (1%)
    all_to_all x1, blocking collectives, per_device(): share = lax.all_to_all(share, 'wide_1', 0, 0, tiled=True)  19.7 us
    all_to_all x1, blocking collectives, fetch(): lax.all_to_all(picked, 'wide_1', 0, 0, tiled=True)  14.6 us
    all_to_all x1, starting transfers between devices, fetch(): sliced = lax.all_to_all(halves, ('wide_1', 'wide_2'), 0, 0, tiled=True)  11.8 us
    pallas_call x2, Pallas kernels, image_spectra(): pl.pallas_call(spectra_kernel, grid=(particles // count,), in_specs=[pl.B...  11.2 us
    ppermute x3, starting transfers between devices, exchanged_evidence(): got = lax.ppermute(pair, 'narrow', [(k, k ^ bit) for k in range(8)])  10.1 us
    pallas_call x1, Pallas kernels, score(): pl.pallas_call(score_kernel, in_specs=[pl.BlockSpec(memory_space=pltpu.SM...  9.75 us
    all_to_all x1, starting transfers between devices, fetch(): planes = lax.all_to_all(picked, 'wide_0', 0, 0, tiled=True)  6.81 us
    ppermute x1, starting transfers between devices, swapped(): return lax.ppermute(x, 'wide_2', [(0, 1), (1, 0)])  6.4 us
  transfers between devices with their start and end apart: 7, of which 7 were waited for; matrix products, arithmetic and copies ran while one was open for 3% of the time, Pallas kernels for 9%

profile of v9, /device:TPU:1, one launch (start us, length us, event | category | flops | bytes accessed | tf_op | source)
XLA Modules:
  0.0 131.5 jit_solution(853582819893083985)
XLA Ops:
  0.6 1.7 %shard_map.122 = bf16[8,2,72,128]{3,2,1,0:T(8,128)(2,1)} custom-call(bf16[8,72,256]{2,1,0:T(8,128)(2,1)} %bitcast.19), custom_call_target="tpu_custom_call" | custom-call | tf_op jit(solution)/shard_map/pallas_call | solution.py:297
  2.3 11.8 %all-to-all-start = ((bf16[16,72,128]{2,1,0:T(8,128)(2,1)}), bf16[16,72,128]{2,1,0:T(8,128)(2,1)S(1)}, u32[]{:S(2)}, u32[]{:S(2)}) async-start(bf16[16,72,128]{2,1,0:T(8,128)(2,1)} %bitcast.18), calls=%async_computation | async-start | bytes 589824 | tf_op jit(solution)/shard_map/all_to_all | solution.py:391
  14.2 0.7 multiply_multiply_fusion
  14.9 0.8 copy.19.roster_ref
  15.6 0.8 reshape.138
  16.4 0.1 select_reduce_fusion
  16.5 0.1 reshape.139
  16.5 0.1 copy.20
  16.6 0.1 reshape.140
  16.7 0.2 convert_reduce_fusion
  16.9 1.0 fusion.7
  17.9 5.6 %shard_map.123.early_ref = bf16[72,64,256]{2,1,0:T(8,128)(2,1)} custom-call(bf16[144,72]{1,0:T(8,128)(2,1)} %constant.62.clone.table_ref.low_ref, f32[128,128]{1,0:T(8,128)} %get-tuple-element.16.contrast_ref, bf16[128,72,256]{2,1,0:T(8,128)(2,1)} %image_ref.3), custom_call_target="tpu_custom_call" | custom-call | flops 339738624 | bytes 4718592 | tf_op jit(solution)/shard_map/pallas_call | solution.py:72
  23.5 0.0 copy-done.5
  23.5 0.1 compare_convert_fusion.member_ref
  23.6 2.9 %all-to-all-done = bf16[16,72,128]{2,1,0:T(8,128)(2,1)S(1)} async-done(((bf16[16,72,128]{2,1,0:T(8,128)(2,1)}), bf16[16,72,128]{2,1,0:T(8,128)(2,1)S(1)}, u32[]{:S(2)}, u32[]{:S(2)}) %all-to-all-start) | async-done | bytes 294944 | tf_op jit(solution)/shard_map/all_to_all | solution.py:391
  26.5 1.3 %shard_map.124 = bf16[4,3,72,128]{3,2,1,0:T(8,128)(2,1)} custom-call(s32[1]{0:T(128)} %bitcast.1.group_ref, s32[8,3]{1,0:T(8,128)S(1)} %copy.19.roster_ref, bf16[16,1,72,128]{3,2,1,0:T(8,128)(2,1)S(1)} %bitcast.17), custom_call_target="tpu_custom_call" | custom-call | tf_op jit(solution)/shard_map/pallas_call | solution.py:104
  27.9 6.8 %all-to-all-start.1 = ((bf16[4,3,72,128]{3,2,1,0:T(8,128)(2,1)}), bf16[4,3,72,128]{3,2,1,0:T(8,128)(2,1)S(1)}, u32[]{:S(2)}, u32[]{:S(2)}) async-start(bf16[4,3,72,128]{3,2,1,0:T(8,128)(2,1)} %shard_map.124), calls=%async_computation.1 | async-start | bytes 442368 | tf_op jit(solution)/shard_map/all_to_all | solution.py:395
  34.7 0.1 broadcast_add_fusion
  34.7 0.1 add.122.place_ref
  34.8 0.0 copy-done.4
  34.9 0.0 copy-start
  34.9 0.0 copy-start.2
  34.9 0.0 copy-start.3
  34.9 5.6 %shard_map.125.late_ref = bf16[72,64,256]{2,1,0:T(8,128)(2,1)} custom-call(bf16[144,72]{1,0:T(8,128)(2,1)} %constant.62.clone.table_ref.low_ref, f32[128,128]{1,0:T(8,128)} %get-tuple-element.16.contrast_ref, bf16[128,72,256]{2,1,0:T(8,128)(2,1)} %image_ref.3), custom_call_target="tpu_custom_call" | custom-call | flops 339738624 | bytes 4718592 | tf_op jit(solution)/shard_map/pallas_call | solution.py:72
  40.5 3.4 %all-to-all-done.1.source_ref = bf16[4,3,72,128]{3,2,1,0:T(8,128)(2,1)S(1)} async-done(((bf16[4,3,72,128]{3,2,1,0:T(8,128)(2,1)}), bf16[4,3,72,128]{3,2,1,0:T(8,128)(2,1)S(1)}, u32[]{:S(2)}, u32[]{:S(2)}) %all-to-all-start.1) | async-done | bytes 221216 | tf_op jit(solution)/shard_map/all_to_all | solution.py:395
  43.9 0.7 shard_map.126
  44.6 14.6 %all_to_all.30 = bf16[8,3,72,128]{3,2,1,0:T(8,128)(2,1)S(1)} all-to-all(bf16[8,3,72,128]{3,2,1,0:T(8,128)(2,1)S(1)} %shard_map.126), channel_id=1, replica_groups=mesh['wide_0'=4,'wide_1'=8,'wide_2'=2,'narrow'=8] {'wide_1'}, dimensions={0} | all-to-all | bytes 884736 | tf_op jit(solution)/shard_map/all_to_all | solution.py:399
  59.1 6.4 %collective-permute-start = (bf16[24,72,128]{2,1,0:T(8,128)(2,1)S(1)}, bf16[24,72,128]{2,1,0:T(8,128)(2,1)S(1)}, u32[]{:S(2)}, u32[]{:S(2)}) collective-permute-start(bf16[24,72,128]{2,1,0:T(8,128)(2,1)S(1)} %bitcast.15), channel_id=1, source_target_pairs={{0,8},{8,0},{1,9},{9,1},{2,10},{10,2},{3,11},{11,3},{4,12},{12,4},... | collective-permute-start | bytes 1327112 | tf_op jit(solution)/shard_map/ppermute | solution.py:30
  65.5 1.4 %collective-permute-done.other_ref = bf16[24,72,128]{2,1,0:T(8,128)(2,1)S(1)} collective-permute-done((bf16[24,72,128]{2,1,0:T(8,128)(2,1)S(1)}, bf16[24,72,128]{2,1,0:T(8,128)(2,1)S(1)}, u32[]{:S(2)}, u32[]{:S(2)}) %collective-permute-start) | collective-permute-done | bytes 442400 | tf_op jit(solution)/shard_map/ppermute | solution.py:30
  66.9 0.0 copy-done
  66.9 0.0 copy-done.2
  66.9 0.0 copy-done.3
  67.0 9.8 %shard_map.127 = (f32[2,73,24,128]{3,2,1,0:T(8,128)S(1)}, f32[2,128]{1,0:T(2,128)S(1)}) custom-call(s32[1]{0:T(128)} %bitcast.core_ref, bf16[24,72,128]{2,1,0:T(8,128)(2,1)S(1)} %bitcast.16, bf16[24,72,128]{2,1,0:T(8,128)(2,1)S(1)} %collective-permute-done.other_ref, bf16[72,64,256]{2,1,0:T(8,128)(2,1)} %shard_map.123.early_ref, ...), custom_call_target="tpu_custom_call" | custom-call | tf_op jit(solution)/shard_map/pallas_call | solution.py:242
  76.7 5.2 %all_to_all.31.got_ref = f32[2,73,24,128]{3,2,1,0:T(8,128)S(1)} all-to-all(f32[2,73,24,128]{3,2,1,0:T(8,128)S(1)} %get-tuple-element.24), channel_id=1, replica_groups=mesh['wide_0'=4,'wide_1'=8,'wide_2'=2,'narrow'=8] {'wide_2'}, dimensions={0} | all-to-all | bytes 3588096 | tf_op jit(solution)/shard_map/all_to_all | solution.py:446
  81.9 0.1 shard_map.128
  82.0 19.7 %all_to_all.32.got_ref = bf16[8,240,128]{2,1,0:T(8,128)(2,1)S(1)} all-to-all(bf16[8,240,128]{2,1,0:T(8,128)(2,1)S(1)} %bitcast.14), channel_id=1, replica_groups=mesh['wide_0'=4,'wide_1'=8,'wide_2'=2,'narrow'=8] {'wide_1'}, dimensions={0} | all-to-all | bytes 983040 | tf_op jit(solution)/shard_map/all_to_all | solution.py:447
  101.6 1.4 %shard_map.129 = bf16[2560,128]{1,0:T(8,128)(2,1)} custom-call(s32[1]{0:T(128)} %bitcast.core_ref, s32[1,240]{1,0:T(1,128)S(1)} %add.122.place_ref, bf16[8,240,128]{2,1,0:T(8,128)(2,1)S(1)} %all_to_all.32.got_ref), custom_call_target="tpu_custom_call" | custom-call | tf_op jit(solution)/shard_map/pallas_call | solution.py:330
  103.0 5.7 %all-to-all-start.5 = ((bf16[64,40,128]{2,1,0:T(8,128)(2,1)}), bf16[64,40,128]{2,1,0:T(8,128)(2,1)S(1)}, u32[]{:S(2)}, u32[]{:S(2)}) async-start(bf16[64,40,128]{2,1,0:T(8,128)(2,1)} %bitcast.8), calls=%async_computation.5 | async-start | bytes 1310720 | tf_op jit(solution)/shard_map/all_to_all | solution.py:450
  108.7 3.1 %collective-permute-start.1 = (f32[2,128]{1,0:T(2,128)S(1)}, f32[2,128]{1,0:T(2,128)S(1)}, u32[]{:S(2)}, u32[]{:S(2)}) collective-permute-start(f32[2,128]{1,0:T(2,128)S(1)} %get-tuple-element.27), channel_id=1, source_target_pairs={{0,2},{1,3},{2,0},{3,1},{4,6},{5,7},{6,4},{7,5},{8,10},{9,11},{10,... | collective-permute-start | bytes 3080 | tf_op jit(solution)/shard_map/ppermute | solution.py:404
  111.8 1.5 %collective-permute-done.1 = f32[2,128]{1,0:T(2,128)S(1)} collective-permute-done((f32[2,128]{1,0:T(2,128)S(1)}, f32[2,128]{1,0:T(2,128)S(1)}, u32[]{:S(2)}, u32[]{:S(2)}) %collective-permute-start.1) | collective-permute-done | bytes 1056 | tf_op jit(solution)/shard_map/ppermute | solution.py:404
  113.3 4.7 %collective-permute-start.2 = (f32[2,128]{1,0:T(2,128)S(1)}, f32[2,128]{1,0:T(2,128)S(1)}, u32[]{:S(2)}, u32[]{:S(2)}) collective-permute-start(f32[2,128]{1,0:T(2,128)S(1)} %pad_maximum_fusion), channel_id=1, source_target_pairs={{0,4},{1,5},{2,6},{3,7},{4,0},{5,1},{6,2},{7,3},{8,12},{9,13},{10,... | collective-permute-start | bytes 3080 | tf_op jit(solution)/shard_map/ppermute | solution.py:404
  118.0 1.4 %collective-permute-done.2 = f32[2,128]{1,0:T(2,128)S(1)} collective-permute-done((f32[2,128]{1,0:T(2,128)S(1)}, f32[2,128]{1,0:T(2,128)S(1)}, u32[]{:S(2)}, u32[]{:S(2)}) %collective-permute-start.2) | collective-permute-done | bytes 1056 | tf_op jit(solution)/shard_map/ppermute | solution.py:404
  119.5 2.3 %collective-permute-start.3 = (f32[2,128]{1,0:T(2,128)S(1)}, f32[2,128]{1,0:T(2,128)S(1)}, u32[]{:S(2)}, u32[]{:S(2)}) collective-permute-start(f32[2,128]{1,0:T(2,128)S(1)} %pad_maximum_fusion.1), channel_id=1, source_target_pairs={{0,1},{1,0},{2,3},{3,2},{4,5},{5,4},{6,7},{7,6},{8,9},{9,8},{10,11... | collective-permute-start | bytes 3080 | tf_op jit(solution)/shard_map/ppermute | solution.py:404
  121.8 2.4 %collective-permute-done.3 = f32[2,128]{1,0:T(2,128)S(1)} collective-permute-done((f32[2,128]{1,0:T(2,128)S(1)}, f32[2,128]{1,0:T(2,128)S(1)}, u32[]{:S(2)}, u32[]{:S(2)}) %collective-permute-start.3) | collective-permute-done | bytes 1056 | tf_op jit(solution)/shard_map/ppermute | solution.py:404
  124.2 0.5 add_bitcast_fusion
  124.7 5.7 %all-to-all-done.5 = bf16[64,40,128]{2,1,0:T(8,128)(2,1)S(1)} async-done(((bf16[64,40,128]{2,1,0:T(8,128)(2,1)}), bf16[64,40,128]{2,1,0:T(8,128)(2,1)S(1)}, u32[]{:S(2)}, u32[]{:S(2)}) %all-to-all-start.5) | async-done | bytes 655392 | tf_op jit(solution)/shard_map/all_to_all | solution.py:450
  130.4 0.0 copy-done.1
  130.4 1.2 shard_map.130
  (13 shorter events, 0.1 us)
Async XLA Ops:
  2.3 24.2 %all-to-all-start = ((bf16[16,72,128]{2,1,0:T(8,128)(2,1)}), bf16[16,72,128]{2,1,0:T(8,128)(2,1)S(1)}, u32[]{:S(2)}, u32[]{:S(2)}) async-start(bf16[16,72,128]{2,1,0:T(8,128)(2,1)} %bitcast.18), calls=%async_computation | async-start | bytes 589824 | tf_op jit(solution)/shard_map/all_to_all | solution.py:391
  17.9 5.6 %copy-start.5 = (s32[128]{0:T(128)S(1)}, s32[128]{0:T(128)}, u32[]{:S(2)}) copy-start(s32[128]{0:T(128)} %param.13) | copy-start | bytes 1540
  17.9 17.0 %copy-start.4 = (s32[128]{0:T(128)S(1)}, s32[128]{0:T(128)}, u32[]{:S(2)}) copy-start(s32[128]{0:T(128)} %param.14) | copy-start | bytes 1540
  27.9 16.0 %all-to-all-start.1 = ((bf16[4,3,72,128]{3,2,1,0:T(8,128)(2,1)}), bf16[4,3,72,128]{3,2,1,0:T(8,128)(2,1)S(1)}, u32[]{:S(2)}, u32[]{:S(2)}) async-start(bf16[4,3,72,128]{3,2,1,0:T(8,128)(2,1)} %shard_map.124), calls=%async_computation.1 | async-start | bytes 442368 | tf_op jit(solution)/shard_map/all_to_all | solution.py:395
  34.9 32.1 %copy-start = (bf16[144,72]{1,0:T(8,128)(2,1)S(1)}, bf16[144,72]{1,0:T(8,128)(2,1)}, u32[]{:S(2)}) copy-start(bf16[144,72]{1,0:T(8,128)(2,1)} %constant.62.clone.table_ref.low_ref) | copy-start | bytes 62212
  34.9 32.1 %copy-start.2 = (f32[256,72]{1,0:T(8,128)S(1)}, f32[256,72]{1,0:T(8,128)}, u32[]{:S(2)}) copy-start(f32[256,72]{1,0:T(8,128)} %constant.64.clone.back_ref) | copy-start | bytes 221188
  34.9 32.1 %copy-start.3 = (f32[72,144]{1,0:T(8,128)S(1)}, f32[72,144]{1,0:T(8,128)}, u32[]{:S(2)}) copy-start(f32[72,144]{1,0:T(8,128)} %constant.63.clone.turn_ref) | copy-start | bytes 124420
  59.1 7.8 %collective-permute-start = (bf16[24,72,128]{2,1,0:T(8,128)(2,1)S(1)}, bf16[24,72,128]{2,1,0:T(8,128)(2,1)S(1)}, u32[]{:S(2)}, u32[]{:S(2)}) collective-permute-start(bf16[24,72,128]{2,1,0:T(8,128)(2,1)S(1)} %bitcast.15), channel_id=1, source_target_pairs={{0,8},{8,0},{1,9},{9,1},{2,10},{10,2},{3,11},{11,3},{4,12},{12,4},... | collective-permute-start | bytes 1327112 | tf_op jit(solution)/shard_map/ppermute | solution.py:30
  81.9 48.5 %copy-start.1 = (f32[144,160]{1,0:T(8,128)S(1)}, f32[144,160]{1,0:T(8,128)}, u32[]{:S(2)}) copy-start(f32[144,160]{1,0:T(8,128)} %constant.65.clone.table_ref) | copy-start | bytes 276484
  103.0 27.3 %all-to-all-start.5 = ((bf16[64,40,128]{2,1,0:T(8,128)(2,1)}), bf16[64,40,128]{2,1,0:T(8,128)(2,1)S(1)}, u32[]{:S(2)}, u32[]{:S(2)}) async-start(bf16[64,40,128]{2,1,0:T(8,128)(2,1)} %bitcast.8), calls=%async_computation.5 | async-start | bytes 1310720 | tf_op jit(solution)/shard_map/all_to_all | solution.py:450
  108.7 4.6 %collective-permute-start.1 = (f32[2,128]{1,0:T(2,128)S(1)}, f32[2,128]{1,0:T(2,128)S(1)}, u32[]{:S(2)}, u32[]{:S(2)}) collective-permute-start(f32[2,128]{1,0:T(2,128)S(1)} %get-tuple-element.27), channel_id=1, source_target_pairs={{0,2},{1,3},{2,0},{3,1},{4,6},{5,7},{6,4},{7,5},{8,10},{9,11},{10,... | collective-permute-start | bytes 3080 | tf_op jit(solution)/shard_map/ppermute | solution.py:404
  113.3 6.1 %collective-permute-start.2 = (f32[2,128]{1,0:T(2,128)S(1)}, f32[2,128]{1,0:T(2,128)S(1)}, u32[]{:S(2)}, u32[]{:S(2)}) collective-permute-start(f32[2,128]{1,0:T(2,128)S(1)} %pad_maximum_fusion), channel_id=1, source_target_pairs={{0,4},{1,5},{2,6},{3,7},{4,0},{5,1},{6,2},{7,3},{8,12},{9,13},{10,... | collective-permute-start | bytes 3080 | tf_op jit(solution)/shard_map/ppermute | solution.py:404
  119.5 4.7 %collective-permute-start.3 = (f32[2,128]{1,0:T(2,128)S(1)}, f32[2,128]{1,0:T(2,128)S(1)}, u32[]{:S(2)}, u32[]{:S(2)}) collective-permute-start(f32[2,128]{1,0:T(2,128)S(1)} %pad_maximum_fusion.1), channel_id=1, source_target_pairs={{0,1},{1,0},{2,3},{3,2},{4,5},{5,4},{6,7},{7,6},{8,9},{9,8},{10,11... | collective-permute-start | bytes 3080 | tf_op jit(solution)/shard_map/ppermute | solution.py:404

commit v10 on v9

--- a/solution.py
+++ b/solution.py
@@ -16,9 +16,13 @@
 OWN_MAX = 4
 CLS_GRP = 24
 SIGMA_ROT = 8
-ROWS = 9
+SHARES = 16
+ROWS = 5
+SLOT_ROWS = 24
+DENOM_SHARE, DENOM_ROW = divmod(ANGLES, ROWS)
 CHUNKS = 4
-WIDE = ("wide_0", "wide_1", "wide_2")
+HIGH = ("wide_high", "wide_low")
+WIDE = (*HIGH, "wide_1", "wide_2")
 
 
 TAU = 1.0
@@ -263,10 +267,14 @@
     denom = got_ref[0, ANGLES] + got_ref[1, ANGLES]
     high = denom.astype(jnp.bfloat16)
     low = (denom - high.astype(jnp.float32)).astype(jnp.bfloat16)
-    for z in range(out_ref.shape[0]):
-        at = pl.ds(z * ROWS, ROWS)
-        out_ref[z, :ROWS] = (got_ref[0, at] + got_ref[1, at]).astype(jnp.bfloat16)
-        out_ref[z, ROWS] = high if z == 0 else low
+    for m in range(SHARES * ROWS):
+        if m < ANGLES:
+            value = (got_ref[0, m] + got_ref[1, m]).astype(jnp.bfloat16)
+        elif m < ANGLES + 2:
+            value = (high, low)[m - ANGLES]
+        else:
+            value = jnp.zeros_like(high)
+        out_ref[m // ROWS, m % ROWS] = value
 
 
 def pack(got):
@@ -275,7 +283,7 @@
         pack_kernel,
         in_specs=[vmem],
         out_specs=vmem,
-        out_shape=jax.ShapeDtypeStruct((8, ROWS + 1, CLS_GRP, CYCLES), jnp.bfloat16),
+        out_shape=jax.ShapeDtypeStruct((SHARES, ROWS, CLS_GRP, CYCLES), jnp.bfloat16),
         compiler_params=pltpu.CompilerParams(vmem_limit_bytes=4 * 1024 * 1024),
     )(got)
 
@@ -304,51 +312,58 @@
     )(blocks)
 
 
-def route_kernel(core_ref, place_ref, got_ref, out_ref):
+def route_kernel(share_ref, place_ref, got_ref, out_ref):
     total = got_ref[0].astype(jnp.float32)
-    for z in range(1, got_ref.shape[0]):
-        total = total + got_ref[z].astype(jnp.float32)
-    denom = total[ROWS * CLS_GRP :]
+    for peer in range(1, SHARES):
+        total = total + got_ref[peer].astype(jnp.float32)
+    start = DENOM_ROW * CLS_GRP
+    first, second = total[start : start + CLS_GRP], total[start + CLS_GRP : start + 2 * CLS_GRP]
+    denom = first + second
     high = denom.astype(jnp.bfloat16).astype(jnp.float32)
-    denom = jnp.where(core_ref[0] == 0, high, denom - high)
-    share = jnp.concatenate([total[: ROWS * CLS_GRP], denom], axis=0).astype(jnp.bfloat16)
-    rows, columns = (ROWS + 1) * OWN_MAX, (ROWS + 1) * CLS_GRP
+    has_denom = share_ref[0] == DENOM_SHARE
+    empty = jnp.zeros((CYCLES - ROWS * CLS_GRP, CYCLES), jnp.float32)
+    share = jnp.concatenate(
+        [
+            total[:start],
+            jnp.where(has_denom, high, first),
+            jnp.where(has_denom, denom - high, second),
+            total[start + 2 * CLS_GRP :],
+            empty,
+        ],
+        axis=0,
+    ).astype(jnp.bfloat16)
     place = place_ref[...]
-    line = lax.broadcasted_iota(jnp.int32, (rows, columns), 0)
+    line = lax.broadcasted_iota(jnp.int32, (SLOT_ROWS, CYCLES), 0)
     line = (line // OWN_MAX) * 1024 + line % OWN_MAX - place
     for owner in range(0, 64, 8):
         chosen = jnp.concatenate(
             [jnp.where(line == -OWN_MAX * (owner + k), 1.0, 0.0) for k in range(8)], axis=0
         ).astype(jnp.bfloat16)
-        out_ref[owner * rows : (owner + 8) * rows, :] = jnp.dot(
+        out_ref[owner * SLOT_ROWS : (owner + 8) * SLOT_ROWS, :] = jnp.dot(
             chosen, share, preferred_element_type=jnp.float32
         ).astype(jnp.bfloat16)
 
 
-def route(core, place, got):
+def route(share, place, got):
     vmem = pl.BlockSpec(memory_space=pltpu.VMEM)
     return pl.pallas_call(
         route_kernel,
         in_specs=[pl.BlockSpec(memory_space=pltpu.SMEM), vmem, vmem],
         out_specs=vmem,
-        out_shape=jax.ShapeDtypeStruct((64 * (ROWS + 1) * OWN_MAX, CYCLES), jnp.bfloat16),
+        out_shape=jax.ShapeDtypeStruct((64 * SLOT_ROWS, CYCLES), jnp.bfloat16),
         compiler_params=pltpu.CompilerParams(vmem_limit_bytes=6 * 1024 * 1024),
-    )(core, place, got)
+    )(share, place, got)
 
 
 def finish_kernel(table_ref, got_ref, out_ref, held):
-    total = got_ref[0].astype(jnp.float32)
-    for plane in range(1, got_ref.shape[0]):
-        total = total + got_ref[plane].astype(jnp.float32)
+    total = got_ref[0].astype(jnp.float32) + got_ref[1].astype(jnp.float32)
     held[...] = total
-    rows = (ROWS + 1) * OWN_MAX
-    at = ROWS * OWN_MAX
-    denom = total[at : at + OWN_MAX] + total[rows + at : rows + at + OWN_MAX]
-    denom = denom + total[2 * rows + at : 2 * rows + at + OWN_MAX]
+    at = DENOM_SHARE * 2 * SLOT_ROWS + DENOM_ROW * OWN_MAX
+    denom = total[at : at + OWN_MAX] + total[at + OWN_MAX : at + 2 * OWN_MAX]
     scale = (1.0 / ANGLES) / (denom + TAU)
     for slot in range(0, OWN_MAX, 2):
         pair = [
-            held[pl.ds(k, 16 * (ROWS + 1), stride=OWN_MAX), :] * scale[k : k + 1]
+            held[pl.ds(k, held.shape[0] // OWN_MAX, stride=OWN_MAX), :] * scale[k : k + 1]
             for k in (slot, slot + 1)
         ]
         polar = jnp.dot(
@@ -370,19 +385,21 @@
         in_specs=[vmem, vmem],
         out_specs=vmem,
         out_shape=jax.ShapeDtypeStruct((OWN_MAX, ANGLES, 2 * CYCLES), jnp.bfloat16),
-        scratch_shapes=[pltpu.VMEM((16 * (ROWS + 1) * OWN_MAX, CYCLES), jnp.float32)],
+        scratch_shapes=[pltpu.VMEM((2 * SHARES * SLOT_ROWS, CYCLES), jnp.float32)],
         compiler_params=pltpu.CompilerParams(vmem_limit_bytes=6 * 1024 * 1024),
     )(table, got)
 
 
 def finish_table(cosine_table, sine_table):
+    harmonic = np.arange(SHARES)[:, None] * ROWS + np.arange(SLOT_ROWS // OWN_MAX)
+    filled = (np.arange(SLOT_ROWS // OWN_MAX) < ROWS) & (harmonic < ANGLES)
+
     def laid(table):
-        table = table.reshape(ANGLES, 8, 1, ROWS)
-        return np.pad(table, ((0, 0), (0, 0), (0, 0), (0, 1)))
+        return np.where(filled, table[:, harmonic % ANGLES], np.float32(0.0))[:, :, None]
 
     cosine, sine = laid(cosine_table), laid(sine_table)
-    real = np.concatenate([cosine, -sine], axis=2).reshape(ANGLES, 16 * (ROWS + 1))
-    imag = np.concatenate([sine, cosine], axis=2).reshape(ANGLES, 16 * (ROWS + 1))
+    real = np.concatenate([cosine, -sine], axis=2).reshape(ANGLES, -1)
+    imag = np.concatenate([sine, cosine], axis=2).reshape(ANGLES, -1)
     return np.concatenate([real, imag])
 
 
@@ -392,7 +409,7 @@
     early = image_spectra(images, 0, contrast_rows, table)
     sliced, early, later = lax.optimization_barrier((sliced, early, contrast_rows))
     picked = pick(group, roster, sliced[:, None], 4)
-    planes = lax.all_to_all(picked, "wide_0", 0, 0, tiled=True)
+    planes = lax.all_to_all(picked, HIGH, 0, 0, tiled=True)
     late = image_spectra(images, 1, later, table)
     planes, late, small = lax.optimization_barrier((planes, late, small))
     picked = pick(group, roster, planes, 8)
@@ -430,8 +447,12 @@
     same = owners[:, None] == owners[None, :]
     ranking = jnp.sum(same & (within[None, :] < within[:, None]), axis=1)
     place = owners * OWN_MAX + ranking
-    place = jnp.arange(ROWS + 1, dtype=jnp.int32)[:, None] * 1024 + place[None, :]
-    place = place.reshape(1, (ROWS + 1) * CLS_GRP)
+    place = jnp.arange(ROWS, dtype=jnp.int32)[:, None] * 1024 + place[None, :]
+    place = jnp.pad(
+        place.reshape(1, ROWS * CLS_GRP),
+        ((0, 0), (0, CYCLES - ROWS * CLS_GRP)),
+        constant_values=2**20,
+    )
     table = finish_table(cosine_table, sine_table)
     small = (square, prior, member, place)
 
@@ -443,23 +464,25 @@
     sums, evidence = score(
         core.reshape(1), mine, other, early, late, low_table, turn, back, square, prior, member
     )
-    share = pack(lax.all_to_all(sums, "wide_2", 0, 0, tiled=True)).reshape(8, (ROWS + 1) * CLS_GRP, CYCLES)
-    share = lax.all_to_all(share, "wide_1", 0, 0, tiled=True)
-    sent = route(core.reshape(1), place, share).reshape(64, (ROWS + 1) * OWN_MAX, CYCLES)
+    share = pack(lax.all_to_all(sums, "wide_2", 0, 0, tiled=True))
+    share = share.reshape(SHARES, ROWS * CLS_GRP, CYCLES)
+    share = lax.all_to_all(share, ("wide_low", "wide_1"), 0, 0, tiled=True)
+    own_share = lax.axis_index(("wide_low", "wide_1"))
+    sent = route(own_share.reshape(1), place, share).reshape(64, SLOT_ROWS, CYCLES)
     sent, evidence = lax.optimization_barrier((sent, evidence))
     got = lax.all_to_all(sent, WIDE, 0, 0, tiled=True)
     for bit in (2, 4, 1):
         evidence = exchanged_evidence(evidence, bit)
     log_evidence = evidence[0] + jnp.log(evidence[1])
-    got = got.reshape(4, 16 * (ROWS + 1) * OWN_MAX, CYCLES)
+    got = got.reshape(2, 2 * SHARES * SLOT_ROWS, CYCLES)
     new_references = finish(table, got).reshape(1, 1, OWN_MAX, ANGLES, 2 * CYCLES)
     return (new_references, log_evidence)
 
 
 def solution(mesh):
     split = Mesh(
-        mesh.devices.reshape(4, 8, 2, mesh.shape["narrow"]),
-        ("wide_0", "wide_1", "wide_2", "narrow"),
+        mesh.devices.reshape(2, 2, 8, 2, mesh.shape["narrow"]),
+        (*WIDE, "narrow"),
     )
     placed = (
         P(WIDE, None, None),

time: 133 us -> 135 us (1.015)
  blocking collectives: 39.4 us -> 19.7 us
  waiting for transfers between devices: 18.7 us -> 33.4 us
  starting transfers between devices: 40.8 us -> 47.5 us
    all_to_all x2 -> x1, blocking collectives: 24.8 us -> 5.16 us  [per_device(): share = pack(lax.all_to_all(sums, 'wide_2', 0, 0, tiled=True))]
    all_to_all x1 -> x2, waiting for transfers between devices: 3.35 us -> 20.2 us  [the longest x1 16.8 us: per_device(): share = lax.all_to_all(share, ('wide_low', 'wide_1'), 0, 0, tiled=True)]
    all_to_all x1 -> x2, starting transfers between devices: 6.81 us -> 10.9 us  [the longest x1 6.81 us: fetch(): planes = lax.all_to_all(picked, HIGH, 0, 0, tiled=True)]
    all_to_all x1, starting transfers between devices: 5.67 us -> 8.96 us  [per_device(): got = lax.all_to_all(sent, WIDE, 0, 0, tiled=True)]
  transfers between devices with their start and end apart: 7 -> 8, of which waited for: 7 -> 7; matrix products, arithmetic and copies ran while one was open for 3% -> 3% of each run, Pallas kernels for 9% -> 8%
where the time goes in v10:
time: 135 us; the launch traced here: 134 us
  starting transfers between devices  47.5 us (35%)
  waiting for transfers between devices  33.4 us (25%)
  Pallas kernels  27.7 us (21%)
  blocking collectives  19.7 us (15%)
  other arithmetic  2.67 us (2%)
  local copies, waits for them, and re-layouts  1.88 us (1%)
    all_to_all x1, waiting for transfers between devices, per_device(): share = lax.all_to_all(share, ('wide_low', 'wide_1'), 0, 0, tiled=True)  16.8 us
    all_to_all x1, blocking collectives, fetch(): lax.all_to_all(picked, 'wide_1', 0, 0, tiled=True)  14.6 us
    all_to_all x1, starting transfers between devices, fetch(): sliced = lax.all_to_all(halves, ('wide_1', 'wide_2'), 0, 0, tiled=True)  11.8 us
    pallas_call x2, Pallas kernels, image_spectra(): pl.pallas_call(spectra_kernel, grid=(particles // count,), in_specs=[pl.B...  11.2 us
    pallas_call x1, Pallas kernels, score(): pl.pallas_call(score_kernel, in_specs=[pl.BlockSpec(memory_space=pltpu.SM...  9.75 us
    ppermute x3, starting transfers between devices, exchanged_evidence(): got = lax.ppermute(pair, 'narrow', [(k, k ^ bit) for k in range(8)])  9.43 us
    all_to_all x1, starting transfers between devices, per_device(): got = lax.all_to_all(sent, WIDE, 0, 0, tiled=True)  8.96 us
    all_to_all x1, starting transfers between devices, fetch(): planes = lax.all_to_all(picked, HIGH, 0, 0, tiled=True)  6.81 us
  transfers between devices with their start and end apart: 8, of which 7 were waited for; matrix products, arithmetic and copies ran while one was open for 3% of the time, Pallas kernels for 8%

profile of v10, /device:TPU:1, one launch (start us, length us, event | category | flops | bytes accessed | tf_op | source)
XLA Modules:
  0.0 133.7 jit_solution(7792428563484503818)
XLA Ops:
  0.6 1.7 %shard_map.122 = bf16[8,2,72,128]{3,2,1,0:T(8,128)(2,1)} custom-call(bf16[8,72,256]{2,1,0:T(8,128)(2,1)} %bitcast.19), custom_call_target="tpu_custom_call" | custom-call | tf_op jit(solution)/shard_map/pallas_call | solution.py:305
  2.3 11.8 %all-to-all-start = ((bf16[16,72,128]{2,1,0:T(8,128)(2,1)}), bf16[16,72,128]{2,1,0:T(8,128)(2,1)S(1)}, u32[]{:S(2)}, u32[]{:S(2)}) async-start(bf16[16,72,128]{2,1,0:T(8,128)(2,1)} %bitcast.18), calls=%async_computation | async-start | bytes 589824 | tf_op jit(solution)/shard_map/all_to_all | solution.py:408
  14.2 0.7 multiply_multiply_fusion
  14.8 0.8 copy.19.roster_ref
  15.6 0.8 reshape.140
  16.4 0.1 select_reduce_fusion
  16.4 0.1 reshape.141
  16.5 0.1 copy.20
  16.6 0.1 reshape.142
  16.7 0.2 convert_reduce_fusion
  16.9 1.0 fusion.7
  17.8 5.6 %shard_map.123.early_ref = bf16[72,64,256]{2,1,0:T(8,128)(2,1)} custom-call(bf16[144,72]{1,0:T(8,128)(2,1)} %constant.72.clone.table_ref.low_ref, f32[128,128]{1,0:T(8,128)} %get-tuple-element.16.contrast_ref, bf16[128,72,256]{2,1,0:T(8,128)(2,1)} %image_ref.3), custom_call_target="tpu_custom_call" | custom-call | flops 339738624 | bytes 4718592 | tf_op jit(solution)/shard_map/pallas_call | solution.py:76
  23.5 0.0 copy-done.5
  23.5 0.1 compare_convert_fusion.member_ref
  23.6 2.9 %all-to-all-done = bf16[16,72,128]{2,1,0:T(8,128)(2,1)S(1)} async-done(((bf16[16,72,128]{2,1,0:T(8,128)(2,1)}), bf16[16,72,128]{2,1,0:T(8,128)(2,1)S(1)}, u32[]{:S(2)}, u32[]{:S(2)}) %all-to-all-start) | async-done | bytes 294944 | tf_op jit(solution)/shard_map/all_to_all | solution.py:408
  26.5 1.3 shard_map.124
  27.8 6.8 %all-to-all-start.1 = ((bf16[4,3,72,128]{3,2,1,0:T(8,128)(2,1)}), bf16[4,3,72,128]{3,2,1,0:T(8,128)(2,1)S(1)}, u32[]{:S(2)}, u32[]{:S(2)}) async-start(bf16[4,3,72,128]{3,2,1,0:T(8,128)(2,1)} %shard_map.124), calls=%async_computation.1 | async-start | bytes 442368 | tf_op jit(solution)/shard_map/all_to_all | solution.py:412
  34.6 0.1 broadcast_add_fusion
  34.7 0.1 add.128
  34.8 0.0 copy-done.4
  34.8 0.0 copy-start
  34.8 0.0 copy-start.2
  34.9 0.0 copy-start.3
  34.9 5.6 %shard_map.125.late_ref = bf16[72,64,256]{2,1,0:T(8,128)(2,1)} custom-call(bf16[144,72]{1,0:T(8,128)(2,1)} %constant.72.clone.table_ref.low_ref, f32[128,128]{1,0:T(8,128)} %get-tuple-element.16.contrast_ref, bf16[128,72,256]{2,1,0:T(8,128)(2,1)} %image_ref.3), custom_call_target="tpu_custom_call" | custom-call | flops 339738624 | bytes 4718592 | tf_op jit(solution)/shard_map/pallas_call | solution.py:76
  40.5 3.4 %all-to-all-done.1.source_ref = bf16[4,3,72,128]{3,2,1,0:T(8,128)(2,1)S(1)} async-done(((bf16[4,3,72,128]{3,2,1,0:T(8,128)(2,1)}), bf16[4,3,72,128]{3,2,1,0:T(8,128)(2,1)S(1)}, u32[]{:S(2)}, u32[]{:S(2)}) %all-to-all-start.1) | async-done | bytes 221216 | tf_op jit(solution)/shard_map/all_to_all | solution.py:412
  43.9 0.7 shard_map.126
  44.5 14.6 %all_to_all.30 = bf16[8,3,72,128]{3,2,1,0:T(8,128)(2,1)S(1)} all-to-all(bf16[8,3,72,128]{3,2,1,0:T(8,128)(2,1)S(1)} %shard_map.126), channel_id=1, replica_groups=mesh['wide_high'=2,'wide_low'=2,'wide_1'=8,'wide_2'=2,'narrow'=8] {'wide..., dimensions={0} | all-to-all | bytes 884736 | tf_op jit(solution)/shard_map/all_to_all | solution.py:416
  59.1 6.4 %collective-permute-start = (bf16[24,72,128]{2,1,0:T(8,128)(2,1)S(1)}, bf16[24,72,128]{2,1,0:T(8,128)(2,1)S(1)}, u32[]{:S(2)}, u32[]{:S(2)}) collective-permute-start(bf16[24,72,128]{2,1,0:T(8,128)(2,1)S(1)} %bitcast.14), channel_id=1, source_target_pairs={{0,8},{8,0},{1,9},{9,1},{2,10},{10,2},{3,11},{11,3},{4,12},{12,4},... | collective-permute-start | bytes 1327112 | tf_op jit(solution)/shard_map/ppermute | solution.py:34
  65.5 1.4 %collective-permute-done.other_ref = bf16[24,72,128]{2,1,0:T(8,128)(2,1)S(1)} collective-permute-done((bf16[24,72,128]{2,1,0:T(8,128)(2,1)S(1)}, bf16[24,72,128]{2,1,0:T(8,128)(2,1)S(1)}, u32[]{:S(2)}, u32[]{:S(2)}) %collective-permute-start) | collective-permute-done | bytes 442400 | tf_op jit(solution)/shard_map/ppermute | solution.py:34
  66.9 0.0 copy-done
  66.9 0.0 copy-done.2
  66.9 9.8 %shard_map.127 = (f32[2,73,24,128]{3,2,1,0:T(8,128)S(1)}, f32[2,128]{1,0:T(2,128)S(1)}) custom-call(s32[1]{0:T(128)} %bitcast.6.core_ref, bf16[24,72,128]{2,1,0:T(8,128)(2,1)S(1)} %bitcast.15, bf16[24,72,128]{2,1,0:T(8,128)(2,1)S(1)} %collective-permute-done.other_ref, bf16[72,64,256]{2,1,0:T(8,128)(2,1)} %shard_map.123.early_ref, ...), custom_call_target="tpu_custom_call" | custom-call | tf_op jit(solution)/shard_map/pallas_call | solution.py:246
  76.7 5.2 %all_to_all.31.got_ref = f32[2,73,24,128]{3,2,1,0:T(8,128)S(1)} all-to-all(f32[2,73,24,128]{3,2,1,0:T(8,128)S(1)} %get-tuple-element.24), channel_id=1, replica_groups=mesh['wide_high'=2,'wide_low'=2,'wide_1'=8,'wide_2'=2,'narrow'=8] {'wide..., dimensions={0} | all-to-all | bytes 3588096 | tf_op jit(solution)/shard_map/all_to_all | solution.py:467
  81.8 0.9 shard_map.128
  82.7 4.1 %all-to-all-start.4 = ((bf16[16,120,128]{2,1,0:T(8,128)(2,1)}), bf16[16,120,128]{2,1,0:T(8,128)(2,1)S(1)}, u32[]{:S(2)}, u32[]{:S(2)}) async-start(bf16[16,120,128]{2,1,0:T(8,128)(2,1)} %bitcast.8), calls=%async_computation.4 | async-start | bytes 983040 | tf_op jit(solution)/shard_map/all_to_all | solution.py:469
  86.8 16.8 %all-to-all-done.4.got_ref = bf16[16,120,128]{2,1,0:T(8,128)(2,1)S(1)} async-done(((bf16[16,120,128]{2,1,0:T(8,128)(2,1)}), bf16[16,120,128]{2,1,0:T(8,128)(2,1)S(1)}, u32[]{:S(2)}, u32[]{:S(2)}) %all-to-all-start.4) | async-done | bytes 491552 | tf_op jit(solution)/shard_map/all_to_all | solution.py:469
  103.7 1.1 shard_map.129
  104.7 3.1 %collective-permute-start.1 = (f32[2,128]{1,0:T(2,128)S(1)}, f32[2,128]{1,0:T(2,128)S(1)}, u32[]{:S(2)}, u32[]{:S(2)}) collective-permute-start(f32[2,128]{1,0:T(2,128)S(1)} %get-tuple-element.27), channel_id=1, source_target_pairs={{0,2},{1,3},{2,0},{3,1},{4,6},{5,7},{6,4},{7,5},{8,10},{9,11},{10,... | collective-permute-start | bytes 3080 | tf_op jit(solution)/shard_map/ppermute | solution.py:421
  107.9 9.0 %all-to-all-start.5 = ((bf16[64,24,128]{2,1,0:T(8,128)(2,1)}), bf16[64,24,128]{2,1,0:T(8,128)(2,1)S(1)}, u32[]{:S(2)}, u32[]{:S(2)}) async-start(bf16[64,24,128]{2,1,0:T(8,128)(2,1)} %bitcast.9), calls=%async_computation.5 | async-start | bytes 786432 | tf_op jit(solution)/shard_map/all_to_all | solution.py:473
  116.8 0.0 collective-permute-done.1
  116.9 4.4 %collective-permute-start.2 = (f32[2,128]{1,0:T(2,128)S(1)}, f32[2,128]{1,0:T(2,128)S(1)}, u32[]{:S(2)}, u32[]{:S(2)}) collective-permute-start(f32[2,128]{1,0:T(2,128)S(1)} %pad_maximum_fusion), channel_id=1, source_target_pairs={{0,4},{1,5},{2,6},{3,7},{4,0},{5,1},{6,2},{7,3},{8,12},{9,13},{10,... | collective-permute-start | bytes 3080 | tf_op jit(solution)/shard_map/ppermute | solution.py:421
  121.3 1.7 %collective-permute-done.2 = f32[2,128]{1,0:T(2,128)S(1)} collective-permute-done((f32[2,128]{1,0:T(2,128)S(1)}, f32[2,128]{1,0:T(2,128)S(1)}, u32[]{:S(2)}, u32[]{:S(2)}) %collective-permute-start.2) | collective-permute-done | bytes 1056 | tf_op jit(solution)/shard_map/ppermute | solution.py:421
  123.0 1.9 %collective-permute-start.3 = (f32[2,128]{1,0:T(2,128)S(1)}, f32[2,128]{1,0:T(2,128)S(1)}, u32[]{:S(2)}, u32[]{:S(2)}) collective-permute-start(f32[2,128]{1,0:T(2,128)S(1)} %pad_maximum_fusion.1), channel_id=1, source_target_pairs={{0,1},{1,0},{2,3},{3,2},{4,5},{5,4},{6,7},{7,6},{8,9},{9,8},{10,11... | collective-permute-start | bytes 3080 | tf_op jit(solution)/shard_map/ppermute | solution.py:421
  124.9 2.7 %collective-permute-done.3 = f32[2,128]{1,0:T(2,128)S(1)} collective-permute-done((f32[2,128]{1,0:T(2,128)S(1)}, f32[2,128]{1,0:T(2,128)S(1)}, u32[]{:S(2)}, u32[]{:S(2)}) %collective-permute-start.3) | collective-permute-done | bytes 1056 | tf_op jit(solution)/shard_map/ppermute | solution.py:421
  127.6 0.5 add_bitcast_fusion
  128.2 4.4 %all-to-all-done.5 = bf16[64,24,128]{2,1,0:T(8,128)(2,1)S(1)} async-done(((bf16[64,24,128]{2,1,0:T(8,128)(2,1)}), bf16[64,24,128]{2,1,0:T(8,128)(2,1)S(1)}, u32[]{:S(2)}, u32[]{:S(2)}) %all-to-all-start.5) | async-done | bytes 393248 | tf_op jit(solution)/shard_map/all_to_all | solution.py:473
  132.6 0.0 copy-done.1
  132.6 1.2 shard_map.130
  (15 shorter events, 0.1 us)
Async XLA Ops:
  2.3 24.2 %all-to-all-start = ((bf16[16,72,128]{2,1,0:T(8,128)(2,1)}), bf16[16,72,128]{2,1,0:T(8,128)(2,1)S(1)}, u32[]{:S(2)}, u32[]{:S(2)}) async-start(bf16[16,72,128]{2,1,0:T(8,128)(2,1)} %bitcast.18), calls=%async_computation | async-start | bytes 589824 | tf_op jit(solution)/shard_map/all_to_all | solution.py:408
  17.8 5.6 %copy-start.5 = (s32[128]{0:T(128)S(1)}, s32[128]{0:T(128)}, u32[]{:S(2)}) copy-start(s32[128]{0:T(128)} %param.13) | copy-start | bytes 1540
  17.8 17.0 %copy-start.4 = (s32[128]{0:T(128)S(1)}, s32[128]{0:T(128)}, u32[]{:S(2)}) copy-start(s32[128]{0:T(128)} %param.14) | copy-start | bytes 1540
  27.8 16.0 %all-to-all-start.1 = ((bf16[4,3,72,128]{3,2,1,0:T(8,128)(2,1)}), bf16[4,3,72,128]{3,2,1,0:T(8,128)(2,1)S(1)}, u32[]{:S(2)}, u32[]{:S(2)}) async-start(bf16[4,3,72,128]{3,2,1,0:T(8,128)(2,1)} %shard_map.124), calls=%async_computation.1 | async-start | bytes 442368 | tf_op jit(solution)/shard_map/all_to_all | solution.py:412
  34.8 32.1 %copy-start = (bf16[144,72]{1,0:T(8,128)(2,1)S(1)}, bf16[144,72]{1,0:T(8,128)(2,1)}, u32[]{:S(2)}) copy-start(bf16[144,72]{1,0:T(8,128)(2,1)} %constant.72.clone.table_ref.low_ref) | copy-start | bytes 62212
  34.8 32.1 %copy-start.2 = (f32[256,72]{1,0:T(8,128)S(1)}, f32[256,72]{1,0:T(8,128)}, u32[]{:S(2)}) copy-start(f32[256,72]{1,0:T(8,128)} %constant.74.clone.back_ref) | copy-start | bytes 221188
  34.9 32.1 %copy-start.3 = (f32[72,144]{1,0:T(8,128)S(1)}, f32[72,144]{1,0:T(8,128)}, u32[]{:S(2)}) copy-start(f32[72,144]{1,0:T(8,128)} %constant.73.clone.turn_ref) | copy-start | bytes 124420
  59.1 7.8 %collective-permute-start = (bf16[24,72,128]{2,1,0:T(8,128)(2,1)S(1)}, bf16[24,72,128]{2,1,0:T(8,128)(2,1)S(1)}, u32[]{:S(2)}, u32[]{:S(2)}) collective-permute-start(bf16[24,72,128]{2,1,0:T(8,128)(2,1)S(1)} %bitcast.14), channel_id=1, source_target_pairs={{0,8},{8,0},{1,9},{9,1},{2,10},{10,2},{3,11},{11,3},{4,12},{12,4},... | collective-permute-start | bytes 1327112 | tf_op jit(solution)/shard_map/ppermute | solution.py:34
  81.8 50.7 %copy-start.1 = (f32[144,192]{1,0:T(8,128)S(1)}, f32[144,192]{1,0:T(8,128)}, u32[]{:S(2)}) copy-start(f32[144,192]{1,0:T(8,128)} %constant.75.clone.table_ref) | copy-start | bytes 331780
  82.7 21.0 %all-to-all-start.4 = ((bf16[16,120,128]{2,1,0:T(8,128)(2,1)}), bf16[16,120,128]{2,1,0:T(8,128)(2,1)S(1)}, u32[]{:S(2)}, u32[]{:S(2)}) async-start(bf16[16,120,128]{2,1,0:T(8,128)(2,1)} %bitcast.8), calls=%async_computation.4 | async-start | bytes 983040 | tf_op jit(solution)/shard_map/all_to_all | solution.py:469
  104.7 12.1 %collective-permute-start.1 = (f32[2,128]{1,0:T(2,128)S(1)}, f32[2,128]{1,0:T(2,128)S(1)}, u32[]{:S(2)}, u32[]{:S(2)}) collective-permute-start(f32[2,128]{1,0:T(2,128)S(1)} %get-tuple-element.27), channel_id=1, source_target_pairs={{0,2},{1,3},{2,0},{3,1},{4,6},{5,7},{6,4},{7,5},{8,10},{9,11},{10,... | collective-permute-start | bytes 3080 | tf_op jit(solution)/shard_map/ppermute | solution.py:421
  107.9 24.7 %all-to-all-start.5 = ((bf16[64,24,128]{2,1,0:T(8,128)(2,1)}), bf16[64,24,128]{2,1,0:T(8,128)(2,1)S(1)}, u32[]{:S(2)}, u32[]{:S(2)}) async-start(bf16[64,24,128]{2,1,0:T(8,128)(2,1)} %bitcast.9), calls=%async_computation.5 | async-start | bytes 786432 | tf_op jit(solution)/shard_map/all_to_all | solution.py:473
  116.9 6.1 %collective-permute-start.2 = (f32[2,128]{1,0:T(2,128)S(1)}, f32[2,128]{1,0:T(2,128)S(1)}, u32[]{:S(2)}, u32[]{:S(2)}) collective-permute-start(f32[2,128]{1,0:T(2,128)S(1)} %pad_maximum_fusion), channel_id=1, source_target_pairs={{0,4},{1,5},{2,6},{3,7},{4,0},{5,1},{6,2},{7,3},{8,12},{9,13},{10,... | collective-permute-start | bytes 3080 | tf_op jit(solution)/shard_map/ppermute | solution.py:421
  123.0 4.6 %collective-permute-start.3 = (f32[2,128]{1,0:T(2,128)S(1)}, f32[2,128]{1,0:T(2,128)S(1)}, u32[]{:S(2)}, u32[]{:S(2)}) collective-permute-start(f32[2,128]{1,0:T(2,128)S(1)} %pad_maximum_fusion.1), channel_id=1, source_target_pairs={{0,1},{1,0},{2,3},{3,2},{4,5},{5,4},{6,7},{7,6},{8,9},{9,8},{10,11... | collective-permute-start | bytes 3080 | tf_op jit(solution)/shard_map/ppermute | solution.py:421

commit v11 on v10

--- a/solution.py
+++ b/solution.py
@@ -466,13 +466,16 @@
     )
     share = pack(lax.all_to_all(sums, "wide_2", 0, 0, tiled=True))
     share = share.reshape(SHARES, ROWS * CLS_GRP, CYCLES)
+    share, evidence = lax.optimization_barrier((share, evidence))
     share = lax.all_to_all(share, ("wide_low", "wide_1"), 0, 0, tiled=True)
+    for bit in (2, 4):
+        evidence = exchanged_evidence(evidence, bit)
+    share, evidence = lax.optimization_barrier((share, evidence))
     own_share = lax.axis_index(("wide_low", "wide_1"))
     sent = route(own_share.reshape(1), place, share).reshape(64, SLOT_ROWS, CYCLES)
     sent, evidence = lax.optimization_barrier((sent, evidence))
     got = lax.all_to_all(sent, WIDE, 0, 0, tiled=True)
-    for bit in (2, 4, 1):
-        evidence = exchanged_evidence(evidence, bit)
+    evidence = exchanged_evidence(evidence, 1)
     log_evidence = evidence[0] + jnp.log(evidence[1])
     got = got.reshape(2, 2 * SHARES * SLOT_ROWS, CYCLES)
     new_references = finish(table, got).reshape(1, 1, OWN_MAX, ANGLES, 2 * CYCLES)

time: 135 us -> 131 us (0.970)
  waiting for transfers between devices: 33.4 us -> 30 us
    all_to_all x1, waiting for transfers between devices: 16.8 us -> 6.54 us  [per_device(): share = lax.all_to_all(share, ('wide_low', 'wide_1'), 0, 0, tiled=True)]
    ppermute x3, waiting for transfers between devices: 4.4 us -> 8.65 us  [exchanged_evidence(): got = lax.ppermute(pair, 'narrow', [(k, k ^ bit) for k in range(8)])]
    all_to_all x1, waiting for transfers between devices: 4.43 us -> 7.11 us  [per_device(): got = lax.all_to_all(sent, WIDE, 0, 0, tiled=True)]
  transfers between devices with their start and end apart: 8 -> 8, of which waited for: 7 -> 8; matrix products, arithmetic and copies ran while one was open for 3% -> 3% of each run, Pallas kernels for 8% -> 9%
where the time goes in v11:
time: 131 us; the launch traced here: 130 us
  starting transfers between devices  47.5 us (36%)
  waiting for transfers between devices  30 us (23%)
  Pallas kernels  27.7 us (21%)
  blocking collectives  19.7 us (15%)
  other arithmetic  2.67 us (2%)
  local copies, waits for them, and re-layouts  1.88 us (1%)
    all_to_all x1, blocking collectives, fetch(): lax.all_to_all(picked, 'wide_1', 0, 0, tiled=True)  14.6 us
    all_to_all x1, starting transfers between devices, fetch(): sliced = lax.all_to_all(halves, ('wide_1', 'wide_2'), 0, 0, tiled=True)  11.8 us
    pallas_call x2, Pallas kernels, image_spectra(): pl.pallas_call(spectra_kernel, grid=(particles // count,), in_specs=[pl.B...  11.2 us
    pallas_call x1, Pallas kernels, score(): pl.pallas_call(score_kernel, in_specs=[pl.BlockSpec(memory_space=pltpu.SM...  9.75 us
    ppermute x3, starting transfers between devices, exchanged_evidence(): got = lax.ppermute(pair, 'narrow', [(k, k ^ bit) for k in range(8)])  9.68 us
    all_to_all x1, starting transfers between devices, per_device(): got = lax.all_to_all(sent, WIDE, 0, 0, tiled=True)  8.71 us
    ppermute x3, waiting for transfers between devices, exchanged_evidence(): got = lax.ppermute(pair, 'narrow', [(k, k ^ bit) for k in range(8)])  8.65 us
    all_to_all x1, waiting for transfers between devices, per_device(): got = lax.all_to_all(sent, WIDE, 0, 0, tiled=True)  7.11 us
  transfers between devices with their start and end apart: 8, of which 8 were waited for; matrix products, arithmetic and copies ran while one was open for 3% of the time, Pallas kernels for 9%

profile of v11, /device:TPU:1, one launch (start us, length us, event | category | flops | bytes accessed | tf_op | source)
XLA Modules:
  0.0 130.4 jit_solution(6357647673612047916)
XLA Ops:
  0.6 1.7 %shard_map.122 = bf16[8,2,72,128]{3,2,1,0:T(8,128)(2,1)} custom-call(bf16[8,72,256]{2,1,0:T(8,128)(2,1)} %bitcast.19), custom_call_target="tpu_custom_call" | custom-call | tf_op jit(solution)/shard_map/pallas_call | solution.py:305
  2.3 11.8 %all-to-all-start = ((bf16[16,72,128]{2,1,0:T(8,128)(2,1)}), bf16[16,72,128]{2,1,0:T(8,128)(2,1)S(1)}, u32[]{:S(2)}, u32[]{:S(2)}) async-start(bf16[16,72,128]{2,1,0:T(8,128)(2,1)} %bitcast.18), calls=%async_computation | async-start | bytes 589824 | tf_op jit(solution)/shard_map/all_to_all | solution.py:408
  14.2 0.7 multiply_multiply_fusion
  14.8 0.8 copy.19.roster_ref
  15.6 0.8 reshape.140
  16.4 0.1 select_reduce_fusion
  16.4 0.1 reshape.141
  16.5 0.1 copy.20
  16.6 0.1 reshape.142
  16.7 0.2 convert_reduce_fusion
  16.9 1.0 fusion.7
  17.8 5.6 %shard_map.123.early_ref = bf16[72,64,256]{2,1,0:T(8,128)(2,1)} custom-call(bf16[144,72]{1,0:T(8,128)(2,1)} %constant.72.clone.table_ref.low_ref, f32[128,128]{1,0:T(8,128)} %get-tuple-element.20.contrast_ref, bf16[128,72,256]{2,1,0:T(8,128)(2,1)} %image_ref.3), custom_call_target="tpu_custom_call" | custom-call | flops 339738624 | bytes 4718592 | tf_op jit(solution)/shard_map/pallas_call | solution.py:76
  23.5 0.0 copy-done.5
  23.5 0.1 compare_convert_fusion.member_ref
  23.6 2.9 %all-to-all-done = bf16[16,72,128]{2,1,0:T(8,128)(2,1)S(1)} async-done(((bf16[16,72,128]{2,1,0:T(8,128)(2,1)}), bf16[16,72,128]{2,1,0:T(8,128)(2,1)S(1)}, u32[]{:S(2)}, u32[]{:S(2)}) %all-to-all-start) | async-done | bytes 294944 | tf_op jit(solution)/shard_map/all_to_all | solution.py:408
  26.5 1.3 %shard_map.124 = bf16[4,3,72,128]{3,2,1,0:T(8,128)(2,1)} custom-call(s32[1]{0:T(128)} %bitcast.1.group_ref, s32[8,3]{1,0:T(8,128)S(1)} %copy.19.roster_ref, bf16[16,1,72,128]{3,2,1,0:T(8,128)(2,1)S(1)} %bitcast.17), custom_call_target="tpu_custom_call" | custom-call | tf_op jit(solution)/shard_map/pallas_call | solution.py:108
  27.8 6.8 %all-to-all-start.1 = ((bf16[4,3,72,128]{3,2,1,0:T(8,128)(2,1)}), bf16[4,3,72,128]{3,2,1,0:T(8,128)(2,1)S(1)}, u32[]{:S(2)}, u32[]{:S(2)}) async-start(bf16[4,3,72,128]{3,2,1,0:T(8,128)(2,1)} %shard_map.124), calls=%async_computation.1 | async-start | bytes 442368 | tf_op jit(solution)/shard_map/all_to_all | solution.py:412
  34.6 0.1 broadcast_add_fusion
  34.7 0.1 add.128
  34.8 0.0 copy-done.4
  34.8 0.0 copy-start
  34.8 0.0 copy-start.2
  34.9 0.0 copy-start.3
  34.9 5.6 %shard_map.125.late_ref = bf16[72,64,256]{2,1,0:T(8,128)(2,1)} custom-call(bf16[144,72]{1,0:T(8,128)(2,1)} %constant.72.clone.table_ref.low_ref, f32[128,128]{1,0:T(8,128)} %get-tuple-element.20.contrast_ref, bf16[128,72,256]{2,1,0:T(8,128)(2,1)} %image_ref.3), custom_call_target="tpu_custom_call" | custom-call | flops 339738624 | bytes 4718592 | tf_op jit(solution)/shard_map/pallas_call | solution.py:76
  40.5 3.4 %all-to-all-done.1.source_ref = bf16[4,3,72,128]{3,2,1,0:T(8,128)(2,1)S(1)} async-done(((bf16[4,3,72,128]{3,2,1,0:T(8,128)(2,1)}), bf16[4,3,72,128]{3,2,1,0:T(8,128)(2,1)S(1)}, u32[]{:S(2)}, u32[]{:S(2)}) %all-to-all-start.1) | async-done | bytes 221216 | tf_op jit(solution)/shard_map/all_to_all | solution.py:412
  43.9 0.7 shard_map.126
  44.5 14.6 %all_to_all.30 = bf16[8,3,72,128]{3,2,1,0:T(8,128)(2,1)S(1)} all-to-all(bf16[8,3,72,128]{3,2,1,0:T(8,128)(2,1)S(1)} %shard_map.126), channel_id=1, replica_groups=mesh['wide_high'=2,'wide_low'=2,'wide_1'=8,'wide_2'=2,'narrow'=8] {'wide..., dimensions={0} | all-to-all | bytes 884736 | tf_op jit(solution)/shard_map/all_to_all | solution.py:416
  59.1 6.4 %collective-permute-start = (bf16[24,72,128]{2,1,0:T(8,128)(2,1)S(1)}, bf16[24,72,128]{2,1,0:T(8,128)(2,1)S(1)}, u32[]{:S(2)}, u32[]{:S(2)}) collective-permute-start(bf16[24,72,128]{2,1,0:T(8,128)(2,1)S(1)} %bitcast.14), channel_id=1, source_target_pairs={{0,8},{8,0},{1,9},{9,1},{2,10},{10,2},{3,11},{11,3},{4,12},{12,4},... | collective-permute-start | bytes 1327112 | tf_op jit(solution)/shard_map/ppermute | solution.py:34
  65.5 1.4 %collective-permute-done.other_ref = bf16[24,72,128]{2,1,0:T(8,128)(2,1)S(1)} collective-permute-done((bf16[24,72,128]{2,1,0:T(8,128)(2,1)S(1)}, bf16[24,72,128]{2,1,0:T(8,128)(2,1)S(1)}, u32[]{:S(2)}, u32[]{:S(2)}) %collective-permute-start) | collective-permute-done | bytes 442400 | tf_op jit(solution)/shard_map/ppermute | solution.py:34
  66.9 0.0 copy-done
  66.9 0.0 copy-done.2
  66.9 0.0 copy-done.3
  66.9 9.8 %shard_map.127 = (f32[2,73,24,128]{3,2,1,0:T(8,128)S(1)}, f32[2,128]{1,0:T(2,128)S(1)}) custom-call(s32[1]{0:T(128)} %bitcast.6.core_ref, bf16[24,72,128]{2,1,0:T(8,128)(2,1)S(1)} %bitcast.15, bf16[24,72,128]{2,1,0:T(8,128)(2,1)S(1)} %collective-permute-done.other_ref, bf16[72,64,256]{2,1,0:T(8,128)(2,1)} %shard_map.123.early_ref, ...), custom_call_target="tpu_custom_call" | custom-call | tf_op jit(solution)/shard_map/pallas_call | solution.py:246
  76.7 5.2 %all_to_all.31.got_ref = f32[2,73,24,128]{3,2,1,0:T(8,128)S(1)} all-to-all(f32[2,73,24,128]{3,2,1,0:T(8,128)S(1)} %get-tuple-element.28), channel_id=1, replica_groups=mesh['wide_high'=2,'wide_low'=2,'wide_1'=8,'wide_2'=2,'narrow'=8] {'wide..., dimensions={0} | all-to-all | bytes 3588096 | tf_op jit(solution)/shard_map/all_to_all | solution.py:467
  81.8 0.9 shard_map.128
  82.7 4.1 %all-to-all-start.4 = ((bf16[16,120,128]{2,1,0:T(8,128)(2,1)}), bf16[16,120,128]{2,1,0:T(8,128)(2,1)S(1)}, u32[]{:S(2)}, u32[]{:S(2)}) async-start(bf16[16,120,128]{2,1,0:T(8,128)(2,1)} %bitcast.8), calls=%async_computation.4 | async-start | bytes 983040 | tf_op jit(solution)/shard_map/all_to_all | solution.py:470
  86.8 3.1 %collective-permute-start.1 = (f32[2,128]{1,0:T(2,128)S(1)}, f32[2,128]{1,0:T(2,128)S(1)}, u32[]{:S(2)}, u32[]{:S(2)}) collective-permute-start(f32[2,128]{1,0:T(2,128)S(1)} %get-tuple-element.31), channel_id=1, source_target_pairs={{0,2},{1,3},{2,0},{3,1},{4,6},{5,7},{6,4},{7,5},{8,10},{9,11},{10,... | collective-permute-start | bytes 3080 | tf_op jit(solution)/shard_map/ppermute | solution.py:421
  90.0 1.2 collective-permute-done.1
  91.2 4.6 %collective-permute-start.2 = (f32[2,128]{1,0:T(2,128)S(1)}, f32[2,128]{1,0:T(2,128)S(1)}, u32[]{:S(2)}, u32[]{:S(2)}) collective-permute-start(f32[2,128]{1,0:T(2,128)S(1)} %pad_maximum_fusion), channel_id=1, source_target_pairs={{0,4},{1,5},{2,6},{3,7},{4,0},{5,1},{6,2},{7,3},{8,12},{9,13},{10,... | collective-permute-start | bytes 3080 | tf_op jit(solution)/shard_map/ppermute | solution.py:421
  95.8 1.3 collective-permute-done.2
  97.1 6.5 %all-to-all-done.4.got_ref = bf16[16,120,128]{2,1,0:T(8,128)(2,1)S(1)} async-done(((bf16[16,120,128]{2,1,0:T(8,128)(2,1)}), bf16[16,120,128]{2,1,0:T(8,128)(2,1)S(1)}, u32[]{:S(2)}, u32[]{:S(2)}) %all-to-all-start.4) | async-done | bytes 491552 | tf_op jit(solution)/shard_map/all_to_all | solution.py:470
  103.7 1.1 shard_map.129
  104.8 8.7 %all-to-all-start.5 = ((bf16[64,24,128]{2,1,0:T(8,128)(2,1)}), bf16[64,24,128]{2,1,0:T(8,128)(2,1)S(1)}, u32[]{:S(2)}, u32[]{:S(2)}) async-start(bf16[64,24,128]{2,1,0:T(8,128)(2,1)} %bitcast.9), calls=%async_computation.5 | async-start | bytes 786432 | tf_op jit(solution)/shard_map/all_to_all | solution.py:477
  113.5 1.9 %collective-permute-start.3 = (f32[2,128]{1,0:T(2,128)S(1)}, f32[2,128]{1,0:T(2,128)S(1)}, u32[]{:S(2)}, u32[]{:S(2)}) collective-permute-start(f32[2,128]{1,0:T(2,128)S(1)} %pad_maximum_fusion.1), channel_id=1, source_target_pairs={{0,1},{1,0},{2,3},{3,2},{4,5},{5,4},{6,7},{7,6},{8,9},{9,8},{10,11... | collective-permute-start | bytes 3080 | tf_op jit(solution)/shard_map/ppermute | solution.py:421
  115.4 6.2 %collective-permute-done.3 = f32[2,128]{1,0:T(2,128)S(1)} collective-permute-done((f32[2,128]{1,0:T(2,128)S(1)}, f32[2,128]{1,0:T(2,128)S(1)}, u32[]{:S(2)}, u32[]{:S(2)}) %collective-permute-start.3) | collective-permute-done | bytes 1056 | tf_op jit(solution)/shard_map/ppermute | solution.py:421
  121.6 0.5 add_bitcast_fusion
  122.1 7.1 %all-to-all-done.5 = bf16[64,24,128]{2,1,0:T(8,128)(2,1)S(1)} async-done(((bf16[64,24,128]{2,1,0:T(8,128)(2,1)}), bf16[64,24,128]{2,1,0:T(8,128)(2,1)S(1)}, u32[]{:S(2)}, u32[]{:S(2)}) %all-to-all-start.5) | async-done | bytes 393248 | tf_op jit(solution)/shard_map/all_to_all | solution.py:477
  129.2 1.2 shard_map.130
  (15 shorter events, 0.1 us)
Async XLA Ops:
  2.3 24.2 %all-to-all-start = ((bf16[16,72,128]{2,1,0:T(8,128)(2,1)}), bf16[16,72,128]{2,1,0:T(8,128)(2,1)S(1)}, u32[]{:S(2)}, u32[]{:S(2)}) async-start(bf16[16,72,128]{2,1,0:T(8,128)(2,1)} %bitcast.18), calls=%async_computation | async-start | bytes 589824 | tf_op jit(solution)/shard_map/all_to_all | solution.py:408
  17.8 5.6 %copy-start.5 = (s32[128]{0:T(128)S(1)}, s32[128]{0:T(128)}, u32[]{:S(2)}) copy-start(s32[128]{0:T(128)} %param.13) | copy-start | bytes 1540
  17.8 17.0 %copy-start.4 = (s32[128]{0:T(128)S(1)}, s32[128]{0:T(128)}, u32[]{:S(2)}) copy-start(s32[128]{0:T(128)} %param.14) | copy-start | bytes 1540
  27.8 16.0 %all-to-all-start.1 = ((bf16[4,3,72,128]{3,2,1,0:T(8,128)(2,1)}), bf16[4,3,72,128]{3,2,1,0:T(8,128)(2,1)S(1)}, u32[]{:S(2)}, u32[]{:S(2)}) async-start(bf16[4,3,72,128]{3,2,1,0:T(8,128)(2,1)} %shard_map.124), calls=%async_computation.1 | async-start | bytes 442368 | tf_op jit(solution)/shard_map/all_to_all | solution.py:412
  34.8 32.1 %copy-start = (bf16[144,72]{1,0:T(8,128)(2,1)S(1)}, bf16[144,72]{1,0:T(8,128)(2,1)}, u32[]{:S(2)}) copy-start(bf16[144,72]{1,0:T(8,128)(2,1)} %constant.72.clone.table_ref.low_ref) | copy-start | bytes 62212
  34.8 32.1 %copy-start.2 = (f32[256,72]{1,0:T(8,128)S(1)}, f32[256,72]{1,0:T(8,128)}, u32[]{:S(2)}) copy-start(f32[256,72]{1,0:T(8,128)} %constant.74.clone.back_ref) | copy-start | bytes 221188
  34.9 32.1 %copy-start.3 = (f32[72,144]{1,0:T(8,128)S(1)}, f32[72,144]{1,0:T(8,128)}, u32[]{:S(2)}) copy-start(f32[72,144]{1,0:T(8,128)} %constant.73.clone.turn_ref) | copy-start | bytes 124420
  59.1 7.8 %collective-permute-start = (bf16[24,72,128]{2,1,0:T(8,128)(2,1)S(1)}, bf16[24,72,128]{2,1,0:T(8,128)(2,1)S(1)}, u32[]{:S(2)}, u32[]{:S(2)}) collective-permute-start(bf16[24,72,128]{2,1,0:T(8,128)(2,1)S(1)} %bitcast.14), channel_id=1, source_target_pairs={{0,8},{8,0},{1,9},{9,1},{2,10},{10,2},{3,11},{11,3},{4,12},{12,4},... | collective-permute-start | bytes 1327112 | tf_op jit(solution)/shard_map/ppermute | solution.py:34
  81.8 47.4 %copy-start.1 = (f32[144,192]{1,0:T(8,128)S(1)}, f32[144,192]{1,0:T(8,128)}, u32[]{:S(2)}) copy-start(f32[144,192]{1,0:T(8,128)} %constant.75.clone.table_ref) | copy-start | bytes 331780
  82.7 21.0 %all-to-all-start.4 = ((bf16[16,120,128]{2,1,0:T(8,128)(2,1)}), bf16[16,120,128]{2,1,0:T(8,128)(2,1)S(1)}, u32[]{:S(2)}, u32[]{:S(2)}) async-start(bf16[16,120,128]{2,1,0:T(8,128)(2,1)} %bitcast.8), calls=%async_computation.4 | async-start | bytes 983040 | tf_op jit(solution)/shard_map/all_to_all | solution.py:470
  86.8 4.3 %collective-permute-start.1 = (f32[2,128]{1,0:T(2,128)S(1)}, f32[2,128]{1,0:T(2,128)S(1)}, u32[]{:S(2)}, u32[]{:S(2)}) collective-permute-start(f32[2,128]{1,0:T(2,128)S(1)} %get-tuple-element.31), channel_id=1, source_target_pairs={{0,2},{1,3},{2,0},{3,1},{4,6},{5,7},{6,4},{7,5},{8,10},{9,11},{10,... | collective-permute-start | bytes 3080 | tf_op jit(solution)/shard_map/ppermute | solution.py:421
  91.2 5.9 %collective-permute-start.2 = (f32[2,128]{1,0:T(2,128)S(1)}, f32[2,128]{1,0:T(2,128)S(1)}, u32[]{:S(2)}, u32[]{:S(2)}) collective-permute-start(f32[2,128]{1,0:T(2,128)S(1)} %pad_maximum_fusion), channel_id=1, source_target_pairs={{0,4},{1,5},{2,6},{3,7},{4,0},{5,1},{6,2},{7,3},{8,12},{9,13},{10,... | collective-permute-start | bytes 3080 | tf_op jit(solution)/shard_map/ppermute | solution.py:421
  104.8 24.5 %all-to-all-start.5 = ((bf16[64,24,128]{2,1,0:T(8,128)(2,1)}), bf16[64,24,128]{2,1,0:T(8,128)(2,1)S(1)}, u32[]{:S(2)}, u32[]{:S(2)}) async-start(bf16[64,24,128]{2,1,0:T(8,128)(2,1)} %bitcast.9), calls=%async_computation.5 | async-start | bytes 786432 | tf_op jit(solution)/shard_map/all_to_all | solution.py:477
  113.5 8.1 %collective-permute-start.3 = (f32[2,128]{1,0:T(2,128)S(1)}, f32[2,128]{1,0:T(2,128)S(1)}, u32[]{:S(2)}, u32[]{:S(2)}) collective-permute-start(f32[2,128]{1,0:T(2,128)S(1)} %pad_maximum_fusion.1), channel_id=1, source_target_pairs={{0,1},{1,0},{2,3},{3,2},{4,5},{5,4},{6,7},{7,6},{8,9},{9,8},{10,11... | collective-permute-start | bytes 3080 | tf_op jit(solution)/shard_map/ppermute | solution.py:421

commit v12 on v11

--- a/solution.py
+++ b/solution.py
@@ -126,7 +126,8 @@
     square_ref,
     prior_ref,
     member_ref,
-    sums_ref,
+    keep_ref,
+    send_ref,
     evidence_ref,
     ref_real,
     ref_imag,
@@ -229,18 +230,19 @@
             [x_real * hr - x_imag * hi, x_real * hi + x_imag * hr], axis=-1
         ).astype(jnp.bfloat16)
         sums = jnp.dot(chosen, aligned, preferred_element_type=jnp.float32)
-        sums_ref[0, m] = sums[:, :CYCLES]
-        sums_ref[1, m] = sums[:, CYCLES:]
+        real_sum, imag_sum = sums[:, :CYCLES], sums[:, CYCLES:]
+        keep_ref[m] = jnp.where(first, real_sum, imag_sum)
+        send_ref[m] = jnp.where(first, imag_sum, real_sum)
     denom = jnp.dot(
         member, square, precision=TOP_PRECISION, preferred_element_type=jnp.float32
     )
-    sums_ref[0, ANGLES] = denom
-    sums_ref[1, ANGLES] = denom
+    keep_ref[ANGLES] = denom
+    send_ref[ANGLES] = denom
 
 
 def score(core, mine, other, early, late, low_table, turn, back, square, prior, member):
     particles = 2 * early.shape[1]
-    sums = jax.ShapeDtypeStruct((2, ANGLES + 1, CLS_GRP, CYCLES), jnp.float32)
+    sums = jax.ShapeDtypeStruct((ANGLES + 1, CLS_GRP, CYCLES), jnp.float32)
     evidence = jax.ShapeDtypeStruct((2, particles), jnp.float32)
     vmem = pl.BlockSpec(memory_space=pltpu.VMEM)
     return pl.pallas_call(
@@ -248,8 +250,8 @@
         in_specs=[pl.BlockSpec(memory_space=pltpu.SMEM), vmem, vmem]
         + [pl.BlockSpec(memory_space=pltpu.HBM)] * 2
         + [vmem] * 6,
-        out_specs=(vmem, vmem),
-        out_shape=(sums, evidence),
+        out_specs=(vmem, vmem, vmem),
+        out_shape=(sums, sums, evidence),
         scratch_shapes=[
             pltpu.VMEM((ANGLES * CLS_GRP, CYCLES), jnp.float32),
             pltpu.VMEM((ANGLES * CLS_GRP, CYCLES), jnp.float32),
@@ -263,13 +265,13 @@
     )(core, mine, other, early, late, low_table, turn, back, square, prior, member)
 
 
-def pack_kernel(got_ref, out_ref):
-    denom = got_ref[0, ANGLES] + got_ref[1, ANGLES]
+def pack_kernel(keep_ref, got_ref, out_ref):
+    denom = keep_ref[ANGLES] + got_ref[ANGLES]
     high = denom.astype(jnp.bfloat16)
     low = (denom - high.astype(jnp.float32)).astype(jnp.bfloat16)
     for m in range(SHARES * ROWS):
         if m < ANGLES:
-            value = (got_ref[0, m] + got_ref[1, m]).astype(jnp.bfloat16)
+            value = (keep_ref[m] + got_ref[m]).astype(jnp.bfloat16)
         elif m < ANGLES + 2:
             value = (high, low)[m - ANGLES]
         else:
@@ -277,15 +279,15 @@
         out_ref[m // ROWS, m % ROWS] = value
 
 
-def pack(got):
+def pack(keep, got):
     vmem = pl.BlockSpec(memory_space=pltpu.VMEM)
     return pl.pallas_call(
         pack_kernel,
-        in_specs=[vmem],
+        in_specs=[vmem, vmem],
         out_specs=vmem,
         out_shape=jax.ShapeDtypeStruct((SHARES, ROWS, CLS_GRP, CYCLES), jnp.bfloat16),
         compiler_params=pltpu.CompilerParams(vmem_limit_bytes=4 * 1024 * 1024),
-    )(got)
+    )(keep, got)
 
 
 def rotation_prior(rotation_rows):
@@ -442,29 +444,33 @@
     square = contrast_rows * contrast_rows
     prior = rotation_prior(rotation_index).T
     member = (class_index[None, :] == class_ids[:, None]).astype(jnp.float32)
-    owners = jnp.sum(jnp.where(mine_group, owner_map.reshape(8, CLS_GRP), 0), axis=0)
-    owners = owners.reshape(STEPS, BLOCK).T.reshape(CLS_GRP)
-    same = owners[:, None] == owners[None, :]
-    ranking = jnp.sum(same & (within[None, :] < within[:, None]), axis=1)
-    place = owners * OWN_MAX + ranking
-    place = jnp.arange(ROWS, dtype=jnp.int32)[:, None] * 1024 + place[None, :]
-    place = jnp.pad(
-        place.reshape(1, ROWS * CLS_GRP),
-        ((0, 0), (0, CYCLES - ROWS * CLS_GRP)),
-        constant_values=2**20,
-    )
+    def places(owner_map):
+        owners = jnp.sum(jnp.where(mine_group, owner_map.reshape(8, CLS_GRP), 0), axis=0)
+        owners = owners.reshape(STEPS, BLOCK).T.reshape(CLS_GRP)
+        same = owners[:, None] == owners[None, :]
+        ranking = jnp.sum(same & (within[None, :] < within[:, None]), axis=1)
+        place = owners * OWN_MAX + ranking
+        place = jnp.arange(ROWS, dtype=jnp.int32)[:, None] * 1024 + place[None, :]
+        return jnp.pad(
+            place.reshape(1, ROWS * CLS_GRP),
+            ((0, 0), (0, CYCLES - ROWS * CLS_GRP)),
+            constant_values=2**20,
+        )
+
     table = finish_table(cosine_table, sine_table)
-    small = (square, prior, member, place)
+    small = (square, prior, member)
 
     mine, early, late, small = fetch(
         ref_store[0, 0], class_group.reshape(1), roster, images, contrast_rows, low_table, small
     )
-    square, prior, member, place = small
+    square, prior, member = small
     other = swapped(mine)
-    sums, evidence = score(
+    keep, send, evidence = score(
         core.reshape(1), mine, other, early, late, low_table, turn, back, square, prior, member
     )
-    share = pack(lax.all_to_all(sums, "wide_2", 0, 0, tiled=True))
+    send, owner_map = lax.optimization_barrier((send, owner_map))
+    got, place = lax.optimization_barrier((swapped(send), places(owner_map)))
+    share = pack(keep, got)
     share = share.reshape(SHARES, ROWS * CLS_GRP, CYCLES)
     share, evidence = lax.optimization_barrier((share, evidence))
     share = lax.all_to_all(share, ("wide_low", "wide_1"), 0, 0, tiled=True)

time: 131 us -> 130 us (level)
  blocking collectives: 19.7 us -> 16.4 us
  waiting for transfers between devices: 30 us -> 33.1 us
    all_to_all x1 -> x0, blocking collectives: 5.16 us -> none  [per_device(): share = pack(lax.all_to_all(sums, 'wide_2', 0, 0, tiled=True))]
    all_to_all x1, blocking collectives: 14.6 us -> 16.4 us  [fetch(): lax.all_to_all(picked, 'wide_1', 0, 0, tiled=True)]
    all_to_all x1, waiting for transfers between devices: 7.11 us -> 8.78 us  [per_device(): got = lax.all_to_all(sent, WIDE, 0, 0, tiled=True)]
    all_to_all x1, waiting for transfers between devices: 2.94 us -> 4.38 us  [fetch(): sliced = lax.all_to_all(halves, ('wide_1', 'wide_2'), 0, 0, tiled=True)]
    ppermute x1 -> x2, starting transfers between devices: 6.4 us -> 6.83 us  [swapped(): return lax.ppermute(x, 'wide_2', [(0, 1), (1, 0)])]
  transfers between devices with their start and end apart: 8 -> 9, of which waited for: 8 -> 9; matrix products, arithmetic and copies ran while one was open for 3% -> 3% of each run, Pallas kernels for 9% -> 9%
where the time goes in v12:
time: 130 us; the launch traced here: 129 us
  starting transfers between devices  47.1 us (36%)
  waiting for transfers between devices  33.1 us (25%)
  Pallas kernels  27.8 us (21%)
  blocking collectives  16.4 us (13%)
  other arithmetic  2.67 us (2%)
    all_to_all x1, blocking collectives, fetch(): lax.all_to_all(picked, 'wide_1', 0, 0, tiled=True)  16.4 us
    all_to_all x1, starting transfers between devices, fetch(): sliced = lax.all_to_all(halves, ('wide_1', 'wide_2'), 0, 0, tiled=True)  11.8 us
    pallas_call x2, Pallas kernels, image_spectra(): pl.pallas_call(spectra_kernel, grid=(particles // count,), in_specs=[pl.B...  11.2 us
    pallas_call x1, Pallas kernels, score(): pl.pallas_call(score_kernel, in_specs=[pl.BlockSpec(memory_space=pltpu.SM...  9.79 us
    ppermute x3, starting transfers between devices, exchanged_evidence(): got = lax.ppermute(pair, 'narrow', [(k, k ^ bit) for k in range(8)])  9.69 us
    all_to_all x1, waiting for transfers between devices, per_device(): got = lax.all_to_all(sent, WIDE, 0, 0, tiled=True)  8.78 us
    all_to_all x1, starting transfers between devices, per_device(): got = lax.all_to_all(sent, WIDE, 0, 0, tiled=True)  8.41 us
    ppermute x3, waiting for transfers between devices, exchanged_evidence(): got = lax.ppermute(pair, 'narrow', [(k, k ^ bit) for k in range(8)])  8.06 us
  transfers between devices with their start and end apart: 9, of which 9 were waited for; matrix products, arithmetic and copies ran while one was open for 3% of the time, Pallas kernels for 9%

profile of v12, /device:TPU:1, one launch (start us, length us, event | category | flops | bytes accessed | tf_op | source)
XLA Modules:
  0.0 129.1 jit_solution(15942188178796569771)
XLA Ops:
  0.6 1.7 %shard_map.122 = bf16[8,2,72,128]{3,2,1,0:T(8,128)(2,1)} custom-call(bf16[8,72,256]{2,1,0:T(8,128)(2,1)} %bitcast.19), custom_call_target="tpu_custom_call" | custom-call | tf_op jit(solution)/shard_map/pallas_call | solution.py:307
  2.3 11.8 %all-to-all-start = ((bf16[16,72,128]{2,1,0:T(8,128)(2,1)}), bf16[16,72,128]{2,1,0:T(8,128)(2,1)S(1)}, u32[]{:S(2)}, u32[]{:S(2)}) async-start(bf16[16,72,128]{2,1,0:T(8,128)(2,1)} %bitcast.18), calls=%async_computation | async-start | bytes 589824 | tf_op jit(solution)/shard_map/all_to_all | solution.py:410
  14.1 0.8 copy.20.roster_ref
  14.9 0.7 multiply_multiply_fusion
  15.6 1.0 fusion.7
  16.5 5.6 %shard_map.123.early_ref = bf16[72,64,256]{2,1,0:T(8,128)(2,1)} custom-call(bf16[144,72]{1,0:T(8,128)(2,1)} %constant.72.clone.table_ref.low_ref, f32[128,128]{1,0:T(8,128)} %get-tuple-element.24.contrast_ref, bf16[128,72,256]{2,1,0:T(8,128)(2,1)} %image_ref.3), custom_call_target="tpu_custom_call" | custom-call | flops 339738624 | bytes 4718592 | tf_op jit(solution)/shard_map/pallas_call | solution.py:76
  22.1 4.4 %all-to-all-done = bf16[16,72,128]{2,1,0:T(8,128)(2,1)S(1)} async-done(((bf16[16,72,128]{2,1,0:T(8,128)(2,1)}), bf16[16,72,128]{2,1,0:T(8,128)(2,1)S(1)}, u32[]{:S(2)}, u32[]{:S(2)}) %all-to-all-start) | async-done | bytes 294944 | tf_op jit(solution)/shard_map/all_to_all | solution.py:410
  26.5 1.3 %shard_map.124 = bf16[4,3,72,128]{3,2,1,0:T(8,128)(2,1)} custom-call(s32[1]{0:T(128)} %bitcast.2.group_ref, s32[8,3]{1,0:T(8,128)S(1)} %copy.20.roster_ref, bf16[16,1,72,128]{3,2,1,0:T(8,128)(2,1)S(1)} %bitcast.17), custom_call_target="tpu_custom_call" | custom-call | tf_op jit(solution)/shard_map/pallas_call | solution.py:108
  27.8 6.8 %all-to-all-start.1 = ((bf16[4,3,72,128]{3,2,1,0:T(8,128)(2,1)}), bf16[4,3,72,128]{3,2,1,0:T(8,128)(2,1)S(1)}, u32[]{:S(2)}, u32[]{:S(2)}) async-start(bf16[4,3,72,128]{3,2,1,0:T(8,128)(2,1)} %shard_map.124), calls=%async_computation.1 | async-start | bytes 442368 | tf_op jit(solution)/shard_map/all_to_all | solution.py:414
  34.6 0.0 copy-done.6
  34.6 0.1 compare_convert_fusion.member_ref
  34.7 0.0 copy-done.5
  34.7 0.0 copy-start
  34.8 0.0 copy-start.2
  34.8 0.0 copy-start.3
  34.8 5.6 %shard_map.125.late_ref = bf16[72,64,256]{2,1,0:T(8,128)(2,1)} custom-call(bf16[144,72]{1,0:T(8,128)(2,1)} %constant.72.clone.table_ref.low_ref, f32[128,128]{1,0:T(8,128)} %get-tuple-element.24.contrast_ref, bf16[128,72,256]{2,1,0:T(8,128)(2,1)} %image_ref.3), custom_call_target="tpu_custom_call" | custom-call | flops 339738624 | bytes 4718592 | tf_op jit(solution)/shard_map/pallas_call | solution.py:76
  40.4 3.4 %all-to-all-done.1.source_ref = bf16[4,3,72,128]{3,2,1,0:T(8,128)(2,1)S(1)} async-done(((bf16[4,3,72,128]{3,2,1,0:T(8,128)(2,1)}), bf16[4,3,72,128]{3,2,1,0:T(8,128)(2,1)S(1)}, u32[]{:S(2)}, u32[]{:S(2)}) %all-to-all-start.1) | async-done | bytes 221216 | tf_op jit(solution)/shard_map/all_to_all | solution.py:414
  43.9 0.7 shard_map.126
  44.5 16.4 %all_to_all.25 = bf16[8,3,72,128]{3,2,1,0:T(8,128)(2,1)S(1)} all-to-all(bf16[8,3,72,128]{3,2,1,0:T(8,128)(2,1)S(1)} %shard_map.126), channel_id=1, replica_groups=mesh['wide_high'=2,'wide_low'=2,'wide_1'=8,'wide_2'=2,'narrow'=8] {'wide..., dimensions={0} | all-to-all | bytes 884736 | tf_op jit(solution)/shard_map/all_to_all | solution.py:418
  61.0 4.5 %collective-permute-start = (bf16[24,72,128]{2,1,0:T(8,128)(2,1)S(1)}, bf16[24,72,128]{2,1,0:T(8,128)(2,1)S(1)}, u32[]{:S(2)}, u32[]{:S(2)}) collective-permute-start(bf16[24,72,128]{2,1,0:T(8,128)(2,1)S(1)} %bitcast.14), channel_id=1, source_target_pairs={{0,8},{8,0},{1,9},{9,1},{2,10},{10,2},{3,11},{11,3},{4,12},{12,4},... | collective-permute-start | bytes 1327112 | tf_op jit(solution)/shard_map/ppermute | solution.py:34
  65.5 1.4 %collective-permute-done.other_ref = bf16[24,72,128]{2,1,0:T(8,128)(2,1)S(1)} collective-permute-done((bf16[24,72,128]{2,1,0:T(8,128)(2,1)S(1)}, bf16[24,72,128]{2,1,0:T(8,128)(2,1)S(1)}, u32[]{:S(2)}, u32[]{:S(2)}) %collective-permute-start) | collective-permute-done | bytes 442400 | tf_op jit(solution)/shard_map/ppermute | solution.py:34
  66.9 0.0 copy-done
  66.9 0.0 copy-done.2
  66.9 9.8 %shard_map.127 = (f32[73,24,128]{2,1,0:T(8,128)S(1)}, f32[73,24,128]{2,1,0:T(8,128)S(1)}, f32[2,128]{1,0:T(2,128)S(1)}) custom-call(s32[1]{0:T(128)} %bitcast.1.core_ref, bf16[24,72,128]{2,1,0:T(8,128)(2,1)S(1)} %bitcast.15, bf16[24,72,128]{2,1,0:T(8,128)(2,1)S(1)} %collective-permute-done.other_ref, bf16[72,64,256]{2,1,0:T(8,128)(2,1)} %shard_map.123.early_ref, ...), custom_call_target="tpu_custom_call" | custom-call | tf_op jit(solution)/shard_map/pallas_call | solution.py:248
  76.7 2.3 %collective-permute-start.1 = (f32[73,24,128]{2,1,0:T(8,128)S(1)}, f32[73,24,128]{2,1,0:T(8,128)S(1)}, u32[]{:S(2)}, u32[]{:S(2)}) collective-permute-start(f32[73,24,128]{2,1,0:T(8,128)S(1)} %get-tuple-element.32), channel_id=1, source_target_pairs={{0,8},{8,0},{1,9},{9,1},{2,10},{10,2},{3,11},{11,3},{4,12},{12,4},... | collective-permute-start | bytes 2691080 | tf_op jit(solution)/shard_map/ppermute | solution.py:34
  79.1 0.1 reshape.142
  79.1 0.1 select_reduce_fusion
  79.2 0.1 reshape.143
  79.3 0.1 copy.21
  79.4 0.1 reshape.144
  79.5 0.2 convert_reduce_fusion
  79.7 0.1 broadcast_add_fusion
  79.8 0.1 add.128
  79.8 1.2 collective-permute-done.1.got_ref
  81.1 0.9 shard_map.128
  81.9 3.6 %all-to-all-start.3 = ((bf16[16,120,128]{2,1,0:T(8,128)(2,1)}), bf16[16,120,128]{2,1,0:T(8,128)(2,1)S(1)}, u32[]{:S(2)}, u32[]{:S(2)}) async-start(bf16[16,120,128]{2,1,0:T(8,128)(2,1)} %bitcast.8), calls=%async_computation.3 | async-start | bytes 983040 | tf_op jit(solution)/shard_map/all_to_all | solution.py:476
  85.5 3.1 %collective-permute-start.2 = (f32[2,128]{1,0:T(2,128)S(1)}, f32[2,128]{1,0:T(2,128)S(1)}, u32[]{:S(2)}, u32[]{:S(2)}) collective-permute-start(f32[2,128]{1,0:T(2,128)S(1)} %get-tuple-element.39), channel_id=1, source_target_pairs={{0,2},{1,3},{2,0},{3,1},{4,6},{5,7},{6,4},{7,5},{8,10},{9,11},{10,... | collective-permute-start | bytes 3080 | tf_op jit(solution)/shard_map/ppermute | solution.py:423
  88.7 1.5 %collective-permute-done.2 = f32[2,128]{1,0:T(2,128)S(1)} collective-permute-done((f32[2,128]{1,0:T(2,128)S(1)}, f32[2,128]{1,0:T(2,128)S(1)}, u32[]{:S(2)}, u32[]{:S(2)}) %collective-permute-start.2) | collective-permute-done | bytes 1056 | tf_op jit(solution)/shard_map/ppermute | solution.py:423
  90.2 4.6 %collective-permute-start.3 = (f32[2,128]{1,0:T(2,128)S(1)}, f32[2,128]{1,0:T(2,128)S(1)}, u32[]{:S(2)}, u32[]{:S(2)}) collective-permute-start(f32[2,128]{1,0:T(2,128)S(1)} %pad_maximum_fusion), channel_id=1, source_target_pairs={{0,4},{1,5},{2,6},{3,7},{4,0},{5,1},{6,2},{7,3},{8,12},{9,13},{10,... | collective-permute-start | bytes 3080 | tf_op jit(solution)/shard_map/ppermute | solution.py:423
  94.8 1.4 %collective-permute-done.3 = f32[2,128]{1,0:T(2,128)S(1)} collective-permute-done((f32[2,128]{1,0:T(2,128)S(1)}, f32[2,128]{1,0:T(2,128)S(1)}, u32[]{:S(2)}, u32[]{:S(2)}) %collective-permute-start.3) | collective-permute-done | bytes 1056 | tf_op jit(solution)/shard_map/ppermute | solution.py:423
  96.3 5.8 %all-to-all-done.3.got_ref = bf16[16,120,128]{2,1,0:T(8,128)(2,1)S(1)} async-done(((bf16[16,120,128]{2,1,0:T(8,128)(2,1)}), bf16[16,120,128]{2,1,0:T(8,128)(2,1)S(1)}, u32[]{:S(2)}, u32[]{:S(2)}) %all-to-all-start.3) | async-done | bytes 491552 | tf_op jit(solution)/shard_map/all_to_all | solution.py:476
  102.1 1.1 shard_map.129
  103.1 8.4 %all-to-all-start.4 = ((bf16[64,24,128]{2,1,0:T(8,128)(2,1)}), bf16[64,24,128]{2,1,0:T(8,128)(2,1)S(1)}, u32[]{:S(2)}, u32[]{:S(2)}) async-start(bf16[64,24,128]{2,1,0:T(8,128)(2,1)} %bitcast.9), calls=%async_computation.4 | async-start | bytes 786432 | tf_op jit(solution)/shard_map/all_to_all | solution.py:483
  111.6 1.9 %collective-permute-start.4 = (f32[2,128]{1,0:T(2,128)S(1)}, f32[2,128]{1,0:T(2,128)S(1)}, u32[]{:S(2)}, u32[]{:S(2)}) collective-permute-start(f32[2,128]{1,0:T(2,128)S(1)} %pad_maximum_fusion.1), channel_id=1, source_target_pairs={{0,1},{1,0},{2,3},{3,2},{4,5},{5,4},{6,7},{7,6},{8,9},{9,8},{10,11... | collective-permute-start | bytes 3080 | tf_op jit(solution)/shard_map/ppermute | solution.py:423
  113.5 5.1 %collective-permute-done.4 = f32[2,128]{1,0:T(2,128)S(1)} collective-permute-done((f32[2,128]{1,0:T(2,128)S(1)}, f32[2,128]{1,0:T(2,128)S(1)}, u32[]{:S(2)}, u32[]{:S(2)}) %collective-permute-start.4) | collective-permute-done | bytes 1056 | tf_op jit(solution)/shard_map/ppermute | solution.py:423
  118.6 0.5 add_bitcast_fusion
  119.2 8.8 %all-to-all-done.4 = bf16[64,24,128]{2,1,0:T(8,128)(2,1)S(1)} async-done(((bf16[64,24,128]{2,1,0:T(8,128)(2,1)}), bf16[64,24,128]{2,1,0:T(8,128)(2,1)S(1)}, u32[]{:S(2)}, u32[]{:S(2)}) %all-to-all-start.4) | async-done | bytes 393248 | tf_op jit(solution)/shard_map/all_to_all | solution.py:483
  127.9 1.2 shard_map.130
  (18 shorter events, 0.1 us)
Async XLA Ops:
  2.3 24.2 %all-to-all-start = ((bf16[16,72,128]{2,1,0:T(8,128)(2,1)}), bf16[16,72,128]{2,1,0:T(8,128)(2,1)S(1)}, u32[]{:S(2)}, u32[]{:S(2)}) async-start(bf16[16,72,128]{2,1,0:T(8,128)(2,1)} %bitcast.18), calls=%async_computation | async-start | bytes 589824 | tf_op jit(solution)/shard_map/all_to_all | solution.py:410
  16.5 18.1 %copy-start.6 = (s32[128]{0:T(128)S(1)}, s32[128]{0:T(128)}, u32[]{:S(2)}) copy-start(s32[128]{0:T(128)} %param.13) | copy-start | bytes 1540
  16.5 18.2 %copy-start.5 = (s32[128]{0:T(128)S(1)}, s32[128]{0:T(128)}, u32[]{:S(2)}) copy-start(s32[128]{0:T(128)} %param.14) | copy-start | bytes 1540
  27.8 16.0 %all-to-all-start.1 = ((bf16[4,3,72,128]{3,2,1,0:T(8,128)(2,1)}), bf16[4,3,72,128]{3,2,1,0:T(8,128)(2,1)S(1)}, u32[]{:S(2)}, u32[]{:S(2)}) async-start(bf16[4,3,72,128]{3,2,1,0:T(8,128)(2,1)} %shard_map.124), calls=%async_computation.1 | async-start | bytes 442368 | tf_op jit(solution)/shard_map/all_to_all | solution.py:414
  34.7 32.2 %copy-start = (bf16[144,72]{1,0:T(8,128)(2,1)S(1)}, bf16[144,72]{1,0:T(8,128)(2,1)}, u32[]{:S(2)}) copy-start(bf16[144,72]{1,0:T(8,128)(2,1)} %constant.72.clone.table_ref.low_ref) | copy-start | bytes 62212
  34.8 32.2 %copy-start.2 = (f32[256,72]{1,0:T(8,128)S(1)}, f32[256,72]{1,0:T(8,128)}, u32[]{:S(2)}) copy-start(f32[256,72]{1,0:T(8,128)} %constant.74.clone.back_ref) | copy-start | bytes 221188
  34.8 32.2 %copy-start.3 = (f32[72,144]{1,0:T(8,128)S(1)}, f32[72,144]{1,0:T(8,128)}, u32[]{:S(2)}) copy-start(f32[72,144]{1,0:T(8,128)} %constant.73.clone.turn_ref) | copy-start | bytes 124420
  61.0 5.9 %collective-permute-start = (bf16[24,72,128]{2,1,0:T(8,128)(2,1)S(1)}, bf16[24,72,128]{2,1,0:T(8,128)(2,1)S(1)}, u32[]{:S(2)}, u32[]{:S(2)}) collective-permute-start(bf16[24,72,128]{2,1,0:T(8,128)(2,1)S(1)} %bitcast.14), channel_id=1, source_target_pairs={{0,8},{8,0},{1,9},{9,1},{2,10},{10,2},{3,11},{11,3},{4,12},{12,4},... | collective-permute-start | bytes 1327112 | tf_op jit(solution)/shard_map/ppermute | solution.py:34
  66.9 12.1 %copy-start.4 = (s32[192]{0:T(256)S(1)}, s32[192]{0:T(256)}, u32[]{:S(2)}) copy-start(s32[192]{0:T(256)} %param.15) | copy-start | bytes 2308
  76.7 4.3 %collective-permute-start.1 = (f32[73,24,128]{2,1,0:T(8,128)S(1)}, f32[73,24,128]{2,1,0:T(8,128)S(1)}, u32[]{:S(2)}, u32[]{:S(2)}) collective-permute-start(f32[73,24,128]{2,1,0:T(8,128)S(1)} %get-tuple-element.32), channel_id=1, source_target_pairs={{0,8},{8,0},{1,9},{9,1},{2,10},{10,2},{3,11},{11,3},{4,12},{12,4},... | collective-permute-start | bytes 2691080 | tf_op jit(solution)/shard_map/ppermute | solution.py:34
  81.1 46.9 %copy-start.1 = (f32[144,192]{1,0:T(8,128)S(1)}, f32[144,192]{1,0:T(8,128)}, u32[]{:S(2)}) copy-start(f32[144,192]{1,0:T(8,128)} %constant.75.clone.table_ref) | copy-start | bytes 331780
  81.9 20.1 %all-to-all-start.3 = ((bf16[16,120,128]{2,1,0:T(8,128)(2,1)}), bf16[16,120,128]{2,1,0:T(8,128)(2,1)S(1)}, u32[]{:S(2)}, u32[]{:S(2)}) async-start(bf16[16,120,128]{2,1,0:T(8,128)(2,1)} %bitcast.8), calls=%async_computation.3 | async-start | bytes 983040 | tf_op jit(solution)/shard_map/all_to_all | solution.py:476
  85.5 4.6 %collective-permute-start.2 = (f32[2,128]{1,0:T(2,128)S(1)}, f32[2,128]{1,0:T(2,128)S(1)}, u32[]{:S(2)}, u32[]{:S(2)}) collective-permute-start(f32[2,128]{1,0:T(2,128)S(1)} %get-tuple-element.39), channel_id=1, source_target_pairs={{0,2},{1,3},{2,0},{3,1},{4,6},{5,7},{6,4},{7,5},{8,10},{9,11},{10,... | collective-permute-start | bytes 3080 | tf_op jit(solution)/shard_map/ppermute | solution.py:423
  90.2 6.1 %collective-permute-start.3 = (f32[2,128]{1,0:T(2,128)S(1)}, f32[2,128]{1,0:T(2,128)S(1)}, u32[]{:S(2)}, u32[]{:S(2)}) collective-permute-start(f32[2,128]{1,0:T(2,128)S(1)} %pad_maximum_fusion), channel_id=1, source_target_pairs={{0,4},{1,5},{2,6},{3,7},{4,0},{5,1},{6,2},{7,3},{8,12},{9,13},{10,... | collective-permute-start | bytes 3080 | tf_op jit(solution)/shard_map/ppermute | solution.py:423
  103.1 24.8 %all-to-all-start.4 = ((bf16[64,24,128]{2,1,0:T(8,128)(2,1)}), bf16[64,24,128]{2,1,0:T(8,128)(2,1)S(1)}, u32[]{:S(2)}, u32[]{:S(2)}) async-start(bf16[64,24,128]{2,1,0:T(8,128)(2,1)} %bitcast.9), calls=%async_computation.4 | async-start | bytes 786432 | tf_op jit(solution)/shard_map/all_to_all | solution.py:483
  111.6 7.1 %collective-permute-start.4 = (f32[2,128]{1,0:T(2,128)S(1)}, f32[2,128]{1,0:T(2,128)S(1)}, u32[]{:S(2)}, u32[]{:S(2)}) collective-permute-start(f32[2,128]{1,0:T(2,128)S(1)} %pad_maximum_fusion.1), channel_id=1, source_target_pairs={{0,1},{1,0},{2,3},{3,2},{4,5},{5,4},{6,7},{7,6},{8,9},{9,8},{10,11... | collective-permute-start | bytes 3080 | tf_op jit(solution)/shard_map/ppermute | solution.py:423

commit v13 on v12

--- a/solution.py
+++ b/solution.py
@@ -94,12 +94,37 @@
 
 
 def pick_kernel(group_ref, roster_ref, source_ref, out_ref):
-    planes = source_ref.shape[1] == STEPS
     for step in range(STEPS):
         holder = roster_ref[group_ref[0], step]
-        value = source_ref[holder >> 4, step] if planes else source_ref[holder & 15, 0]
+        value = source_ref[holder >> 4, step]
         for copy in range(out_ref.shape[0]):
             out_ref[copy, step] = value
+
+
+def pick_far_kernel(group_ref, roster_ref, source_ref, out_ref, sems):
+    copies = [
+        pltpu.make_async_copy(
+            source_ref.at[roster_ref[group_ref[0], step] & 15], out_ref.at[copy, step], sems.at[copy, step]
+        )
+        for step in range(STEPS)
+        for copy in range(out_ref.shape[0])
+    ]
+    for copy in copies:
+        copy.start()
+    for copy in copies:
+        copy.wait()
+
+
+def pick_far(group, roster, source, copies):
+    smem = pl.BlockSpec(memory_space=pltpu.SMEM)
+    return pl.pallas_call(
+        pick_far_kernel,
+        in_specs=[smem, smem, pl.BlockSpec(memory_space=pltpu.VMEM)],
+        out_specs=pl.BlockSpec(memory_space=pl.ANY),
+        out_shape=jax.ShapeDtypeStruct((copies, STEPS, ANGLES, CYCLES), jnp.bfloat16),
+        scratch_shapes=[pltpu.SemaphoreType.DMA((copies, STEPS))],
+        compiler_params=pltpu.CompilerParams(vmem_limit_bytes=2 * 1024 * 1024),
+    )(group, roster, source)
 
 
 def pick(group, roster, source, copies):
@@ -168,6 +193,12 @@
     energy = 0.5 * lax.dot_general(
         power[...], square, across, precision=TOP_PRECISION, preferred_element_type=jnp.float32
     )
+    member = member_ref[...]
+    denom = jnp.dot(
+        member, square, precision=TOP_PRECISION, preferred_element_type=jnp.float32
+    )
+    keep_ref[ANGLES] = denom
+    send_ref[ANGLES] = denom
     for m in range(ANGLES):
         if m % depth == 0:
             for copy in arriving[m // depth * 2 : m // depth * 2 + 2]:
@@ -207,20 +238,19 @@
             scores[c + k] = value
             best = jnp.maximum(best, value)
             own = own + jnp.where(member_ref[c + k : c + k + 1, :] > 0, value, 0.0)
+    weight = jnp.exp(own - jnp.max(own, axis=0, keepdims=True))
+    weight = weight / jnp.sum(weight, axis=0, keepdims=True)
+    turned_back = jnp.dot(
+        back_ref[...], weight, precision=TOP_PRECISION, preferred_element_type=jnp.float32
+    )
+    h_real = turned_back[:particles].T
+    h_imag = turned_back[particles:].T
     top = jnp.max(best, axis=0, keepdims=True)
     total = jnp.zeros((ANGLES, particles), jnp.float32)
     for c in range(CLS_GRP):
         total = total + jnp.exp(scores[c] - top)
     evidence_ref[0:1, :] = top
     evidence_ref[1:2, :] = jnp.sum(total, axis=0, keepdims=True)
-    weight = jnp.exp(own - jnp.max(own, axis=0, keepdims=True))
-    weight = weight / jnp.sum(weight, axis=0, keepdims=True)
-    turned_back = jnp.dot(
-        back_ref[...], weight, precision=TOP_PRECISION, preferred_element_type=jnp.float32
-    )
-    h_real = turned_back[:particles].T
-    h_imag = turned_back[particles:].T
-    member = member_ref[...]
     chosen = member.astype(jnp.bfloat16)
     for m in range(ANGLES):
         x_real = spectra_ref[m, :, :CYCLES].astype(jnp.float32)
@@ -233,11 +263,6 @@
         real_sum, imag_sum = sums[:, :CYCLES], sums[:, CYCLES:]
         keep_ref[m] = jnp.where(first, real_sum, imag_sum)
         send_ref[m] = jnp.where(first, imag_sum, real_sum)
-    denom = jnp.dot(
-        member, square, precision=TOP_PRECISION, preferred_element_type=jnp.float32
-    )
-    keep_ref[ANGLES] = denom
-    send_ref[ANGLES] = denom
 
 
 def score(core, mine, other, early, late, low_table, turn, back, square, prior, member):
@@ -410,7 +435,7 @@
     sliced = lax.all_to_all(halves, ("wide_1", "wide_2"), 0, 0, tiled=True)
     early = image_spectra(images, 0, contrast_rows, table)
     sliced, early, later = lax.optimization_barrier((sliced, early, contrast_rows))
-    picked = pick(group, roster, sliced[:, None], 4)
+    picked = pick_far(group, roster, sliced, 4)
     planes = lax.all_to_all(picked, HIGH, 0, 0, tiled=True)
     late = image_spectra(images, 1, later, table)
     planes, late, small = lax.optimization_barrier((planes, late, small))

time: 130 us -> 130 us (level)
    pallas_call x0 -> x1, Pallas kernels: none -> 1.42 us  [pick_far(): pl.pallas_call(pick_far_kernel, in_specs=[smem, smem, pl.BlockSpec(memory...]
    pallas_call x2 -> x1, Pallas kernels: 1.99 us -> 0.66 us  [pick(): pl.pallas_call(pick_kernel, in_specs=[smem, smem, vmem], out_specs=vmem,...]
where the time goes in v13:
time: 130 us; the launch traced here: 129 us
  starting transfers between devices  47.1 us (36%)
  waiting for transfers between devices  33 us (25%)
  Pallas kernels  27.7 us (21%)
  blocking collectives  16.4 us (13%)
  other arithmetic  2.67 us (2%)
    all_to_all x1, blocking collectives, fetch(): lax.all_to_all(picked, 'wide_1', 0, 0, tiled=True)  16.4 us
    all_to_all x1, starting transfers between devices, fetch(): sliced = lax.all_to_all(halves, ('wide_1', 'wide_2'), 0, 0, tiled=True)  11.8 us
    pallas_call x2, Pallas kernels, image_spectra(): pl.pallas_call(spectra_kernel, grid=(particles // count,), in_specs=[pl.B...  11.2 us
    ppermute x3, starting transfers between devices, exchanged_evidence(): got = lax.ppermute(pair, 'narrow', [(k, k ^ bit) for k in range(8)])  9.69 us
    pallas_call x1, Pallas kernels, score(): pl.pallas_call(score_kernel, in_specs=[pl.BlockSpec(memory_space=pltpu.SM...  9.66 us
    all_to_all x1, waiting for transfers between devices, per_device(): got = lax.all_to_all(sent, WIDE, 0, 0, tiled=True)  8.75 us
    all_to_all x1, starting transfers between devices, per_device(): got = lax.all_to_all(sent, WIDE, 0, 0, tiled=True)  8.38 us
    ppermute x3, waiting for transfers between devices, exchanged_evidence(): got = lax.ppermute(pair, 'narrow', [(k, k ^ bit) for k in range(8)])  8.07 us
  transfers between devices with their start and end apart: 9, of which 9 were waited for; matrix products, arithmetic and copies ran while one was open for 3% of the time, Pallas kernels for 9%

profile of v13, /device:TPU:1, one launch (start us, length us, event | category | flops | bytes accessed | tf_op | source)
XLA Modules:
  0.0 129.0 jit_solution(17214999775032531541)
XLA Ops:
  0.6 1.7 %shard_map.122 = bf16[8,2,72,128]{3,2,1,0:T(8,128)(2,1)} custom-call(bf16[8,72,256]{2,1,0:T(8,128)(2,1)} %bitcast.17), custom_call_target="tpu_custom_call" | custom-call | tf_op jit(solution)/shard_map/pallas_call | solution.py:332
  2.3 11.8 %all-to-all-start = ((bf16[16,72,128]{2,1,0:T(8,128)(2,1)}), bf16[16,72,128]{2,1,0:T(8,128)(2,1)S(1)}, u32[]{:S(2)}, u32[]{:S(2)}) async-start(bf16[16,72,128]{2,1,0:T(8,128)(2,1)} %bitcast.16), calls=%async_computation | async-start | bytes 589824 | tf_op jit(solution)/shard_map/all_to_all | solution.py:435
  14.1 0.8 copy.20.roster_ref
  14.9 0.7 multiply_multiply_fusion
  15.6 1.0 fusion.7
  16.5 5.6 %shard_map.123.early_ref = bf16[72,64,256]{2,1,0:T(8,128)(2,1)} custom-call(bf16[144,72]{1,0:T(8,128)(2,1)} %constant.72.clone.table_ref.low_ref, f32[128,128]{1,0:T(8,128)} %get-tuple-element.24.contrast_ref, bf16[128,72,256]{2,1,0:T(8,128)(2,1)} %image_ref.3), custom_call_target="tpu_custom_call" | custom-call | flops 339738624 | bytes 4718592 | tf_op jit(solution)/shard_map/pallas_call | solution.py:76
  22.1 4.4 %all-to-all-done.source_ref = bf16[16,72,128]{2,1,0:T(8,128)(2,1)S(1)} async-done(((bf16[16,72,128]{2,1,0:T(8,128)(2,1)}), bf16[16,72,128]{2,1,0:T(8,128)(2,1)S(1)}, u32[]{:S(2)}, u32[]{:S(2)}) %all-to-all-start) | async-done | bytes 294944 | tf_op jit(solution)/shard_map/all_to_all | solution.py:435
  26.5 1.4 %shard_map.124 = bf16[4,3,72,128]{3,2,1,0:T(8,128)(2,1)} custom-call(s32[1]{0:T(128)} %bitcast.2.group_ref, s32[8,3]{1,0:T(8,128)S(1)} %copy.20.roster_ref, bf16[16,72,128]{2,1,0:T(8,128)(2,1)S(1)} %all-to-all-done.source_ref), custom_call_target="tpu_custom_call" | custom-call | tf_op jit(solution)/shard_map/pallas_call | solution.py:120
  27.9 6.8 %all-to-all-start.1 = ((bf16[4,3,72,128]{3,2,1,0:T(8,128)(2,1)}), bf16[4,3,72,128]{3,2,1,0:T(8,128)(2,1)S(1)}, u32[]{:S(2)}, u32[]{:S(2)}) async-start(bf16[4,3,72,128]{3,2,1,0:T(8,128)(2,1)} %shard_map.124), calls=%async_computation.1 | async-start | bytes 442368 | tf_op jit(solution)/shard_map/all_to_all | solution.py:439
  34.8 0.0 copy-done.6
  34.8 0.1 compare_convert_fusion.member_ref
  34.9 0.0 copy-start
  34.9 0.0 copy-start.2
  34.9 0.0 copy-start.3
  34.9 5.6 %shard_map.125.late_ref = bf16[72,64,256]{2,1,0:T(8,128)(2,1)} custom-call(bf16[144,72]{1,0:T(8,128)(2,1)} %constant.72.clone.table_ref.low_ref, f32[128,128]{1,0:T(8,128)} %get-tuple-element.24.contrast_ref, bf16[128,72,256]{2,1,0:T(8,128)(2,1)} %image_ref.3), custom_call_target="tpu_custom_call" | custom-call | flops 339738624 | bytes 4718592 | tf_op jit(solution)/shard_map/pallas_call | solution.py:76
  40.5 3.4 %all-to-all-done.1.source_ref = bf16[4,3,72,128]{3,2,1,0:T(8,128)(2,1)S(1)} async-done(((bf16[4,3,72,128]{3,2,1,0:T(8,128)(2,1)}), bf16[4,3,72,128]{3,2,1,0:T(8,128)(2,1)S(1)}, u32[]{:S(2)}, u32[]{:S(2)}) %all-to-all-start.1) | async-done | bytes 221216 | tf_op jit(solution)/shard_map/all_to_all | solution.py:439
  44.0 0.7 shard_map.126
  44.6 16.4 %all_to_all.25 = bf16[8,3,72,128]{3,2,1,0:T(8,128)(2,1)S(1)} all-to-all(bf16[8,3,72,128]{3,2,1,0:T(8,128)(2,1)S(1)} %shard_map.126), channel_id=1, replica_groups=mesh['wide_high'=2,'wide_low'=2,'wide_1'=8,'wide_2'=2,'narrow'=8] {'wide..., dimensions={0} | all-to-all | bytes 884736 | tf_op jit(solution)/shard_map/all_to_all | solution.py:443
  61.1 4.5 %collective-permute-start = (bf16[24,72,128]{2,1,0:T(8,128)(2,1)S(1)}, bf16[24,72,128]{2,1,0:T(8,128)(2,1)S(1)}, u32[]{:S(2)}, u32[]{:S(2)}) collective-permute-start(bf16[24,72,128]{2,1,0:T(8,128)(2,1)S(1)} %bitcast.13), channel_id=1, source_target_pairs={{0,8},{8,0},{1,9},{9,1},{2,10},{10,2},{3,11},{11,3},{4,12},{12,4},... | collective-permute-start | bytes 1327112 | tf_op jit(solution)/shard_map/ppermute | solution.py:34
  65.6 1.4 %collective-permute-done.other_ref = bf16[24,72,128]{2,1,0:T(8,128)(2,1)S(1)} collective-permute-done((bf16[24,72,128]{2,1,0:T(8,128)(2,1)S(1)}, bf16[24,72,128]{2,1,0:T(8,128)(2,1)S(1)}, u32[]{:S(2)}, u32[]{:S(2)}) %collective-permute-start) | collective-permute-done | bytes 442400 | tf_op jit(solution)/shard_map/ppermute | solution.py:34
  67.0 0.0 copy-done.2
  67.0 9.7 %shard_map.127 = (f32[73,24,128]{2,1,0:T(8,128)S(1)}, f32[73,24,128]{2,1,0:T(8,128)S(1)}, f32[2,128]{1,0:T(2,128)S(1)}) custom-call(s32[1]{0:T(128)} %bitcast.1.core_ref, bf16[24,72,128]{2,1,0:T(8,128)(2,1)S(1)} %bitcast.14, bf16[24,72,128]{2,1,0:T(8,128)(2,1)S(1)} %collective-permute-done.other_ref, bf16[72,64,256]{2,1,0:T(8,128)(2,1)} %shard_map.123.early_ref, ...), custom_call_target="tpu_custom_call" | custom-call | tf_op jit(solution)/shard_map/pallas_call | solution.py:273
  76.7 2.3 %collective-permute-start.1 = (f32[73,24,128]{2,1,0:T(8,128)S(1)}, f32[73,24,128]{2,1,0:T(8,128)S(1)}, u32[]{:S(2)}, u32[]{:S(2)}) collective-permute-start(f32[73,24,128]{2,1,0:T(8,128)S(1)} %get-tuple-element.32), channel_id=1, source_target_pairs={{0,8},{8,0},{1,9},{9,1},{2,10},{10,2},{3,11},{11,3},{4,12},{12,4},... | collective-permute-start | bytes 2691080 | tf_op jit(solution)/shard_map/ppermute | solution.py:34
  79.0 0.0 copy-done.4
  79.0 0.1 reshape.142
  79.1 0.1 select_reduce_fusion
  79.2 0.1 reshape.143
  79.3 0.1 copy.21
  79.4 0.1 reshape.144
  79.5 0.2 convert_reduce_fusion
  79.7 0.1 broadcast_add_fusion
  79.7 0.1 add.128
  79.8 1.2 collective-permute-done.1.got_ref
  81.1 0.9 shard_map.128
  81.9 3.6 %all-to-all-start.3 = ((bf16[16,120,128]{2,1,0:T(8,128)(2,1)}), bf16[16,120,128]{2,1,0:T(8,128)(2,1)S(1)}, u32[]{:S(2)}, u32[]{:S(2)}) async-start(bf16[16,120,128]{2,1,0:T(8,128)(2,1)} %bitcast.7), calls=%async_computation.3 | async-start | bytes 983040 | tf_op jit(solution)/shard_map/all_to_all | solution.py:501
  85.5 3.1 %collective-permute-start.2 = (f32[2,128]{1,0:T(2,128)S(1)}, f32[2,128]{1,0:T(2,128)S(1)}, u32[]{:S(2)}, u32[]{:S(2)}) collective-permute-start(f32[2,128]{1,0:T(2,128)S(1)} %get-tuple-element.39), channel_id=1, source_target_pairs={{0,2},{1,3},{2,0},{3,1},{4,6},{5,7},{6,4},{7,5},{8,10},{9,11},{10,... | collective-permute-start | bytes 3080 | tf_op jit(solution)/shard_map/ppermute | solution.py:448
  88.6 1.5 %collective-permute-done.2 = f32[2,128]{1,0:T(2,128)S(1)} collective-permute-done((f32[2,128]{1,0:T(2,128)S(1)}, f32[2,128]{1,0:T(2,128)S(1)}, u32[]{:S(2)}, u32[]{:S(2)}) %collective-permute-start.2) | collective-permute-done | bytes 1056 | tf_op jit(solution)/shard_map/ppermute | solution.py:448
  90.1 4.6 %collective-permute-start.3 = (f32[2,128]{1,0:T(2,128)S(1)}, f32[2,128]{1,0:T(2,128)S(1)}, u32[]{:S(2)}, u32[]{:S(2)}) collective-permute-start(f32[2,128]{1,0:T(2,128)S(1)} %pad_maximum_fusion), channel_id=1, source_target_pairs={{0,4},{1,5},{2,6},{3,7},{4,0},{5,1},{6,2},{7,3},{8,12},{9,13},{10,... | collective-permute-start | bytes 3080 | tf_op jit(solution)/shard_map/ppermute | solution.py:448
  94.8 1.4 %collective-permute-done.3 = f32[2,128]{1,0:T(2,128)S(1)} collective-permute-done((f32[2,128]{1,0:T(2,128)S(1)}, f32[2,128]{1,0:T(2,128)S(1)}, u32[]{:S(2)}, u32[]{:S(2)}) %collective-permute-start.3) | collective-permute-done | bytes 1056 | tf_op jit(solution)/shard_map/ppermute | solution.py:448
  96.3 5.8 %all-to-all-done.3.got_ref = bf16[16,120,128]{2,1,0:T(8,128)(2,1)S(1)} async-done(((bf16[16,120,128]{2,1,0:T(8,128)(2,1)}), bf16[16,120,128]{2,1,0:T(8,128)(2,1)S(1)}, u32[]{:S(2)}, u32[]{:S(2)}) %all-to-all-start.3) | async-done | bytes 491552 | tf_op jit(solution)/shard_map/all_to_all | solution.py:501
  102.1 1.1 shard_map.129
  103.1 8.4 %all-to-all-start.4 = ((bf16[64,24,128]{2,1,0:T(8,128)(2,1)}), bf16[64,24,128]{2,1,0:T(8,128)(2,1)S(1)}, u32[]{:S(2)}, u32[]{:S(2)}) async-start(bf16[64,24,128]{2,1,0:T(8,128)(2,1)} %bitcast.8), calls=%async_computation.4 | async-start | bytes 786432 | tf_op jit(solution)/shard_map/all_to_all | solution.py:508
  111.5 1.9 %collective-permute-start.4 = (f32[2,128]{1,0:T(2,128)S(1)}, f32[2,128]{1,0:T(2,128)S(1)}, u32[]{:S(2)}, u32[]{:S(2)}) collective-permute-start(f32[2,128]{1,0:T(2,128)S(1)} %pad_maximum_fusion.1), channel_id=1, source_target_pairs={{0,1},{1,0},{2,3},{3,2},{4,5},{5,4},{6,7},{7,6},{8,9},{9,8},{10,11... | collective-permute-start | bytes 3080 | tf_op jit(solution)/shard_map/ppermute | solution.py:448
  113.5 5.1 %collective-permute-done.4 = f32[2,128]{1,0:T(2,128)S(1)} collective-permute-done((f32[2,128]{1,0:T(2,128)S(1)}, f32[2,128]{1,0:T(2,128)S(1)}, u32[]{:S(2)}, u32[]{:S(2)}) %collective-permute-start.4) | collective-permute-done | bytes 1056 | tf_op jit(solution)/shard_map/ppermute | solution.py:448
  118.6 0.5 add_bitcast_fusion
  119.1 8.8 %all-to-all-done.4 = bf16[64,24,128]{2,1,0:T(8,128)(2,1)S(1)} async-done(((bf16[64,24,128]{2,1,0:T(8,128)(2,1)}), bf16[64,24,128]{2,1,0:T(8,128)(2,1)S(1)}, u32[]{:S(2)}, u32[]{:S(2)}) %all-to-all-start.4) | async-done | bytes 393248 | tf_op jit(solution)/shard_map/all_to_all | solution.py:508
  127.9 0.0 copy-done.1
  127.9 1.2 shard_map.130
  (18 shorter events, 0.1 us)
Async XLA Ops:
  2.3 24.2 %all-to-all-start = ((bf16[16,72,128]{2,1,0:T(8,128)(2,1)}), bf16[16,72,128]{2,1,0:T(8,128)(2,1)S(1)}, u32[]{:S(2)}, u32[]{:S(2)}) async-start(bf16[16,72,128]{2,1,0:T(8,128)(2,1)} %bitcast.16), calls=%async_computation | async-start | bytes 589824 | tf_op jit(solution)/shard_map/all_to_all | solution.py:435
  16.5 18.2 %copy-start.6 = (s32[128]{0:T(128)S(1)}, s32[128]{0:T(128)}, u32[]{:S(2)}) copy-start(s32[128]{0:T(128)} %param.13) | copy-start | bytes 1540
  16.5 18.3 %copy-start.5 = (s32[128]{0:T(128)S(1)}, s32[128]{0:T(128)}, u32[]{:S(2)}) copy-start(s32[128]{0:T(128)} %param.14) | copy-start | bytes 1540
  27.9 16.0 %all-to-all-start.1 = ((bf16[4,3,72,128]{3,2,1,0:T(8,128)(2,1)}), bf16[4,3,72,128]{3,2,1,0:T(8,128)(2,1)S(1)}, u32[]{:S(2)}, u32[]{:S(2)}) async-start(bf16[4,3,72,128]{3,2,1,0:T(8,128)(2,1)} %shard_map.124), calls=%async_computation.1 | async-start | bytes 442368 | tf_op jit(solution)/shard_map/all_to_all | solution.py:439
  34.9 32.2 %copy-start = (bf16[144,72]{1,0:T(8,128)(2,1)S(1)}, bf16[144,72]{1,0:T(8,128)(2,1)}, u32[]{:S(2)}) copy-start(bf16[144,72]{1,0:T(8,128)(2,1)} %constant.72.clone.table_ref.low_ref) | copy-start | bytes 62212
  34.9 32.2 %copy-start.2 = (f32[256,72]{1,0:T(8,128)S(1)}, f32[256,72]{1,0:T(8,128)}, u32[]{:S(2)}) copy-start(f32[256,72]{1,0:T(8,128)} %constant.74.clone.back_ref) | copy-start | bytes 221188
  34.9 32.2 %copy-start.3 = (f32[72,144]{1,0:T(8,128)S(1)}, f32[72,144]{1,0:T(8,128)}, u32[]{:S(2)}) copy-start(f32[72,144]{1,0:T(8,128)} %constant.73.clone.turn_ref) | copy-start | bytes 124420
  61.1 5.9 %collective-permute-start = (bf16[24,72,128]{2,1,0:T(8,128)(2,1)S(1)}, bf16[24,72,128]{2,1,0:T(8,128)(2,1)S(1)}, u32[]{:S(2)}, u32[]{:S(2)}) collective-permute-start(bf16[24,72,128]{2,1,0:T(8,128)(2,1)S(1)} %bitcast.13), channel_id=1, source_target_pairs={{0,8},{8,0},{1,9},{9,1},{2,10},{10,2},{3,11},{11,3},{4,12},{12,4},... | collective-permute-start | bytes 1327112 | tf_op jit(solution)/shard_map/ppermute | solution.py:34
  67.0 12.0 %copy-start.4 = (s32[192]{0:T(256)S(1)}, s32[192]{0:T(256)}, u32[]{:S(2)}) copy-start(s32[192]{0:T(256)} %param.15) | copy-start | bytes 2308
  76.7 4.4 %collective-permute-start.1 = (f32[73,24,128]{2,1,0:T(8,128)S(1)}, f32[73,24,128]{2,1,0:T(8,128)S(1)}, u32[]{:S(2)}, u32[]{:S(2)}) collective-permute-start(f32[73,24,128]{2,1,0:T(8,128)S(1)} %get-tuple-element.32), channel_id=1, source_target_pairs={{0,8},{8,0},{1,9},{9,1},{2,10},{10,2},{3,11},{11,3},{4,12},{12,4},... | collective-permute-start | bytes 2691080 | tf_op jit(solution)/shard_map/ppermute | solution.py:34
  81.1 46.8 %copy-start.1 = (f32[144,192]{1,0:T(8,128)S(1)}, f32[144,192]{1,0:T(8,128)}, u32[]{:S(2)}) copy-start(f32[144,192]{1,0:T(8,128)} %constant.75.clone.table_ref) | copy-start | bytes 331780
  81.9 20.1 %all-to-all-start.3 = ((bf16[16,120,128]{2,1,0:T(8,128)(2,1)}), bf16[16,120,128]{2,1,0:T(8,128)(2,1)S(1)}, u32[]{:S(2)}, u32[]{:S(2)}) async-start(bf16[16,120,128]{2,1,0:T(8,128)(2,1)} %bitcast.7), calls=%async_computation.3 | async-start | bytes 983040 | tf_op jit(solution)/shard_map/all_to_all | solution.py:501
  85.5 4.6 %collective-permute-start.2 = (f32[2,128]{1,0:T(2,128)S(1)}, f32[2,128]{1,0:T(2,128)S(1)}, u32[]{:S(2)}, u32[]{:S(2)}) collective-permute-start(f32[2,128]{1,0:T(2,128)S(1)} %get-tuple-element.39), channel_id=1, source_target_pairs={{0,2},{1,3},{2,0},{3,1},{4,6},{5,7},{6,4},{7,5},{8,10},{9,11},{10,... | collective-permute-start | bytes 3080 | tf_op jit(solution)/shard_map/ppermute | solution.py:448
  90.1 6.1 %collective-permute-start.3 = (f32[2,128]{1,0:T(2,128)S(1)}, f32[2,128]{1,0:T(2,128)S(1)}, u32[]{:S(2)}, u32[]{:S(2)}) collective-permute-start(f32[2,128]{1,0:T(2,128)S(1)} %pad_maximum_fusion), channel_id=1, source_target_pairs={{0,4},{1,5},{2,6},{3,7},{4,0},{5,1},{6,2},{7,3},{8,12},{9,13},{10,... | collective-permute-start | bytes 3080 | tf_op jit(solution)/shard_map/ppermute | solution.py:448
  103.1 24.7 %all-to-all-start.4 = ((bf16[64,24,128]{2,1,0:T(8,128)(2,1)}), bf16[64,24,128]{2,1,0:T(8,128)(2,1)S(1)}, u32[]{:S(2)}, u32[]{:S(2)}) async-start(bf16[64,24,128]{2,1,0:T(8,128)(2,1)} %bitcast.8), calls=%async_computation.4 | async-start | bytes 786432 | tf_op jit(solution)/shard_map/all_to_all | solution.py:508
  111.5 7.1 %collective-permute-start.4 = (f32[2,128]{1,0:T(2,128)S(1)}, f32[2,128]{1,0:T(2,128)S(1)}, u32[]{:S(2)}, u32[]{:S(2)}) collective-permute-start(f32[2,128]{1,0:T(2,128)S(1)} %pad_maximum_fusion.1), channel_id=1, source_target_pairs={{0,1},{1,0},{2,3},{3,2},{4,5},{5,4},{6,7},{7,6},{8,9},{9,8},{10,11... | collective-permute-start | bytes 3080 | tf_op jit(solution)/shard_map/ppermute | solution.py:448

commit v14 on v12

--- a/solution.py
+++ b/solution.py
@@ -474,14 +474,14 @@
     share = share.reshape(SHARES, ROWS * CLS_GRP, CYCLES)
     share, evidence = lax.optimization_barrier((share, evidence))
     share = lax.all_to_all(share, ("wide_low", "wide_1"), 0, 0, tiled=True)
-    for bit in (2, 4):
+    for bit in (2,):
         evidence = exchanged_evidence(evidence, bit)
     share, evidence = lax.optimization_barrier((share, evidence))
     own_share = lax.axis_index(("wide_low", "wide_1"))
     sent = route(own_share.reshape(1), place, share).reshape(64, SLOT_ROWS, CYCLES)
     sent, evidence = lax.optimization_barrier((sent, evidence))
     got = lax.all_to_all(sent, WIDE, 0, 0, tiled=True)
-    evidence = exchanged_evidence(evidence, 1)
+    evidence = exchanged_evidence(exchanged_evidence(evidence, 4), 1)
     log_evidence = evidence[0] + jnp.log(evidence[1])
     got = got.reshape(2, 2 * SHARES * SLOT_ROWS, CYCLES)
     new_references = finish(table, got).reshape(1, 1, OWN_MAX, ANGLES, 2 * CYCLES)

time: 130 us -> 130 us (level)
    all_to_all x1, waiting for transfers between devices: 5.79 us -> 11.9 us  [per_device(): share = lax.all_to_all(share, ('wide_low', 'wide_1'), 0, 0, tiled=True)]
    all_to_all x1, waiting for transfers between devices: 8.78 us -> 5.09 us  [per_device(): got = lax.all_to_all(sent, WIDE, 0, 0, tiled=True)]
    ppermute x3, waiting for transfers between devices: 8.06 us -> 5.59 us  [exchanged_evidence(): got = lax.ppermute(pair, 'narrow', [(k, k ^ bit) for k in range(8)])]
where the time goes in v14:
time: 130 us; the launch traced here: 129 us
  starting transfers between devices  47.2 us (36%)
  waiting for transfers between devices  33.1 us (25%)
  Pallas kernels  27.8 us (21%)
  blocking collectives  16.4 us (13%)
  other arithmetic  2.67 us (2%)
    all_to_all x1, blocking collectives, fetch(): lax.all_to_all(picked, 'wide_1', 0, 0, tiled=True)  16.4 us
    all_to_all x1, waiting for transfers between devices, per_device(): share = lax.all_to_all(share, ('wide_low', 'wide_1'), 0, 0, tiled=True)  11.9 us
    all_to_all x1, starting transfers between devices, fetch(): sliced = lax.all_to_all(halves, ('wide_1', 'wide_2'), 0, 0, tiled=True)  11.8 us
    pallas_call x2, Pallas kernels, image_spectra(): pl.pallas_call(spectra_kernel, grid=(particles // count,), in_specs=[pl.B...  11.2 us
    pallas_call x1, Pallas kernels, score(): pl.pallas_call(score_kernel, in_specs=[pl.BlockSpec(memory_space=pltpu.SM...  9.79 us
    ppermute x3, starting transfers between devices, exchanged_evidence(): got = lax.ppermute(pair, 'narrow', [(k, k ^ bit) for k in range(8)])  9.71 us
    all_to_all x1, starting transfers between devices, per_device(): got = lax.all_to_all(sent, WIDE, 0, 0, tiled=True)  8.41 us
    ppermute x2, starting transfers between devices, swapped(): return lax.ppermute(x, 'wide_2', [(0, 1), (1, 0)])  6.83 us
  transfers between devices with their start and end apart: 9, of which 9 were waited for; matrix products, arithmetic and copies ran while one was open for 3% of the time, Pallas kernels for 9%

profile of v14, /device:TPU:1, one launch (start us, length us, event | category | flops | bytes accessed | tf_op | source)
XLA Modules:
  0.0 129.1 jit_solution(4144112491095570637)
XLA Ops:
  0.6 1.7 %shard_map.122 = bf16[8,2,72,128]{3,2,1,0:T(8,128)(2,1)} custom-call(bf16[8,72,256]{2,1,0:T(8,128)(2,1)} %bitcast.19), custom_call_target="tpu_custom_call" | custom-call | tf_op jit(solution)/shard_map/pallas_call | solution.py:307
  2.3 11.8 %all-to-all-start = ((bf16[16,72,128]{2,1,0:T(8,128)(2,1)}), bf16[16,72,128]{2,1,0:T(8,128)(2,1)S(1)}, u32[]{:S(2)}, u32[]{:S(2)}) async-start(bf16[16,72,128]{2,1,0:T(8,128)(2,1)} %bitcast.18), calls=%async_computation | async-start | bytes 589824 | tf_op jit(solution)/shard_map/all_to_all | solution.py:410
  14.1 0.8 copy.20.roster_ref
  14.9 0.7 multiply_multiply_fusion
  15.6 1.0 fusion.7
  16.5 5.6 %shard_map.123.early_ref = bf16[72,64,256]{2,1,0:T(8,128)(2,1)} custom-call(bf16[144,72]{1,0:T(8,128)(2,1)} %constant.72.clone.table_ref.low_ref, f32[128,128]{1,0:T(8,128)} %get-tuple-element.24.contrast_ref, bf16[128,72,256]{2,1,0:T(8,128)(2,1)} %image_ref.3), custom_call_target="tpu_custom_call" | custom-call | flops 339738624 | bytes 4718592 | tf_op jit(solution)/shard_map/pallas_call | solution.py:76
  22.1 4.4 %all-to-all-done = bf16[16,72,128]{2,1,0:T(8,128)(2,1)S(1)} async-done(((bf16[16,72,128]{2,1,0:T(8,128)(2,1)}), bf16[16,72,128]{2,1,0:T(8,128)(2,1)S(1)}, u32[]{:S(2)}, u32[]{:S(2)}) %all-to-all-start) | async-done | bytes 294944 | tf_op jit(solution)/shard_map/all_to_all | solution.py:410
  26.5 1.3 %shard_map.124 = bf16[4,3,72,128]{3,2,1,0:T(8,128)(2,1)} custom-call(s32[1]{0:T(128)} %bitcast.2.group_ref, s32[8,3]{1,0:T(8,128)S(1)} %copy.20.roster_ref, bf16[16,1,72,128]{3,2,1,0:T(8,128)(2,1)S(1)} %bitcast.17), custom_call_target="tpu_custom_call" | custom-call | tf_op jit(solution)/shard_map/pallas_call | solution.py:108
  27.8 6.8 %all-to-all-start.1 = ((bf16[4,3,72,128]{3,2,1,0:T(8,128)(2,1)}), bf16[4,3,72,128]{3,2,1,0:T(8,128)(2,1)S(1)}, u32[]{:S(2)}, u32[]{:S(2)}) async-start(bf16[4,3,72,128]{3,2,1,0:T(8,128)(2,1)} %shard_map.124), calls=%async_computation.1 | async-start | bytes 442368 | tf_op jit(solution)/shard_map/all_to_all | solution.py:414
  34.6 0.0 copy-done.6
  34.6 0.1 compare_convert_fusion.member_ref
  34.7 0.0 copy-done.5
  34.7 0.0 copy-start
  34.8 0.0 copy-start.2
  34.8 0.0 copy-start.3
  34.8 5.6 %shard_map.125.late_ref = bf16[72,64,256]{2,1,0:T(8,128)(2,1)} custom-call(bf16[144,72]{1,0:T(8,128)(2,1)} %constant.72.clone.table_ref.low_ref, f32[128,128]{1,0:T(8,128)} %get-tuple-element.24.contrast_ref, bf16[128,72,256]{2,1,0:T(8,128)(2,1)} %image_ref.3), custom_call_target="tpu_custom_call" | custom-call | flops 339738624 | bytes 4718592 | tf_op jit(solution)/shard_map/pallas_call | solution.py:76
  40.4 3.4 %all-to-all-done.1.source_ref = bf16[4,3,72,128]{3,2,1,0:T(8,128)(2,1)S(1)} async-done(((bf16[4,3,72,128]{3,2,1,0:T(8,128)(2,1)}), bf16[4,3,72,128]{3,2,1,0:T(8,128)(2,1)S(1)}, u32[]{:S(2)}, u32[]{:S(2)}) %all-to-all-start.1) | async-done | bytes 221216 | tf_op jit(solution)/shard_map/all_to_all | solution.py:414
  43.9 0.7 shard_map.126
  44.5 16.4 %all_to_all.25 = bf16[8,3,72,128]{3,2,1,0:T(8,128)(2,1)S(1)} all-to-all(bf16[8,3,72,128]{3,2,1,0:T(8,128)(2,1)S(1)} %shard_map.126), channel_id=1, replica_groups=mesh['wide_high'=2,'wide_low'=2,'wide_1'=8,'wide_2'=2,'narrow'=8] {'wide..., dimensions={0} | all-to-all | bytes 884736 | tf_op jit(solution)/shard_map/all_to_all | solution.py:418
  61.0 4.5 %collective-permute-start = (bf16[24,72,128]{2,1,0:T(8,128)(2,1)S(1)}, bf16[24,72,128]{2,1,0:T(8,128)(2,1)S(1)}, u32[]{:S(2)}, u32[]{:S(2)}) collective-permute-start(bf16[24,72,128]{2,1,0:T(8,128)(2,1)S(1)} %bitcast.14), channel_id=1, source_target_pairs={{0,8},{8,0},{1,9},{9,1},{2,10},{10,2},{3,11},{11,3},{4,12},{12,4},... | collective-permute-start | bytes 1327112 | tf_op jit(solution)/shard_map/ppermute | solution.py:34
  65.5 1.4 %collective-permute-done.other_ref = bf16[24,72,128]{2,1,0:T(8,128)(2,1)S(1)} collective-permute-done((bf16[24,72,128]{2,1,0:T(8,128)(2,1)S(1)}, bf16[24,72,128]{2,1,0:T(8,128)(2,1)S(1)}, u32[]{:S(2)}, u32[]{:S(2)}) %collective-permute-start) | collective-permute-done | bytes 442400 | tf_op jit(solution)/shard_map/ppermute | solution.py:34
  66.9 0.0 copy-done
  66.9 9.8 %shard_map.127 = (f32[73,24,128]{2,1,0:T(8,128)S(1)}, f32[73,24,128]{2,1,0:T(8,128)S(1)}, f32[2,128]{1,0:T(2,128)S(1)}) custom-call(s32[1]{0:T(128)} %bitcast.1.core_ref, bf16[24,72,128]{2,1,0:T(8,128)(2,1)S(1)} %bitcast.15, bf16[24,72,128]{2,1,0:T(8,128)(2,1)S(1)} %collective-permute-done.other_ref, bf16[72,64,256]{2,1,0:T(8,128)(2,1)} %shard_map.123.early_ref, ...), custom_call_target="tpu_custom_call" | custom-call | tf_op jit(solution)/shard_map/pallas_call | solution.py:248
  76.7 2.3 %collective-permute-start.1 = (f32[73,24,128]{2,1,0:T(8,128)S(1)}, f32[73,24,128]{2,1,0:T(8,128)S(1)}, u32[]{:S(2)}, u32[]{:S(2)}) collective-permute-start(f32[73,24,128]{2,1,0:T(8,128)S(1)} %get-tuple-element.32), channel_id=1, source_target_pairs={{0,8},{8,0},{1,9},{9,1},{2,10},{10,2},{3,11},{11,3},{4,12},{12,4},... | collective-permute-start | bytes 2691080 | tf_op jit(solution)/shard_map/ppermute | solution.py:34
  79.1 0.0 copy-done.4
  79.1 0.1 reshape.142
  79.1 0.1 select_reduce_fusion
  79.2 0.1 reshape.143
  79.3 0.1 copy.21
  79.4 0.1 reshape.144
  79.5 0.2 convert_reduce_fusion
  79.7 0.1 broadcast_add_fusion
  79.8 0.1 add.128
  79.8 1.2 collective-permute-done.1.got_ref
  81.1 0.9 shard_map.128
  81.9 3.6 %all-to-all-start.3 = ((bf16[16,120,128]{2,1,0:T(8,128)(2,1)}), bf16[16,120,128]{2,1,0:T(8,128)(2,1)S(1)}, u32[]{:S(2)}, u32[]{:S(2)}) async-start(bf16[16,120,128]{2,1,0:T(8,128)(2,1)} %bitcast.8), calls=%async_computation.3 | async-start | bytes 983040 | tf_op jit(solution)/shard_map/all_to_all | solution.py:476
  85.5 3.1 %collective-permute-start.2 = (f32[2,128]{1,0:T(2,128)S(1)}, f32[2,128]{1,0:T(2,128)S(1)}, u32[]{:S(2)}, u32[]{:S(2)}) collective-permute-start(f32[2,128]{1,0:T(2,128)S(1)} %get-tuple-element.39), channel_id=1, source_target_pairs={{0,2},{1,3},{2,0},{3,1},{4,6},{5,7},{6,4},{7,5},{8,10},{9,11},{10,... | collective-permute-start | bytes 3080 | tf_op jit(solution)/shard_map/ppermute | solution.py:423
  88.7 1.5 %collective-permute-done.2 = f32[2,128]{1,0:T(2,128)S(1)} collective-permute-done((f32[2,128]{1,0:T(2,128)S(1)}, f32[2,128]{1,0:T(2,128)S(1)}, u32[]{:S(2)}, u32[]{:S(2)}) %collective-permute-start.2) | collective-permute-done | bytes 1056 | tf_op jit(solution)/shard_map/ppermute | solution.py:423
  90.2 11.9 %all-to-all-done.3.got_ref = bf16[16,120,128]{2,1,0:T(8,128)(2,1)S(1)} async-done(((bf16[16,120,128]{2,1,0:T(8,128)(2,1)}), bf16[16,120,128]{2,1,0:T(8,128)(2,1)S(1)}, u32[]{:S(2)}, u32[]{:S(2)}) %all-to-all-start.3) | async-done | bytes 491552 | tf_op jit(solution)/shard_map/all_to_all | solution.py:476
  102.1 1.1 shard_map.129
  103.1 8.4 %all-to-all-start.4 = ((bf16[64,24,128]{2,1,0:T(8,128)(2,1)}), bf16[64,24,128]{2,1,0:T(8,128)(2,1)S(1)}, u32[]{:S(2)}, u32[]{:S(2)}) async-start(bf16[64,24,128]{2,1,0:T(8,128)(2,1)} %bitcast.9), calls=%async_computation.4 | async-start | bytes 786432 | tf_op jit(solution)/shard_map/all_to_all | solution.py:483
  111.6 4.7 %collective-permute-start.3 = (f32[2,128]{1,0:T(2,128)S(1)}, f32[2,128]{1,0:T(2,128)S(1)}, u32[]{:S(2)}, u32[]{:S(2)}) collective-permute-start(f32[2,128]{1,0:T(2,128)S(1)} %pad_maximum_fusion), channel_id=1, source_target_pairs={{0,4},{1,5},{2,6},{3,7},{4,0},{5,1},{6,2},{7,3},{8,12},{9,13},{10,... | collective-permute-start | bytes 3080 | tf_op jit(solution)/shard_map/ppermute | solution.py:423
  116.2 1.4 %collective-permute-done.3 = f32[2,128]{1,0:T(2,128)S(1)} collective-permute-done((f32[2,128]{1,0:T(2,128)S(1)}, f32[2,128]{1,0:T(2,128)S(1)}, u32[]{:S(2)}, u32[]{:S(2)}) %collective-permute-start.3) | collective-permute-done | bytes 1056 | tf_op jit(solution)/shard_map/ppermute | solution.py:423
  117.7 1.9 %collective-permute-start.4 = (f32[2,128]{1,0:T(2,128)S(1)}, f32[2,128]{1,0:T(2,128)S(1)}, u32[]{:S(2)}, u32[]{:S(2)}) collective-permute-start(f32[2,128]{1,0:T(2,128)S(1)} %pad_maximum_fusion.1), channel_id=1, source_target_pairs={{0,1},{1,0},{2,3},{3,2},{4,5},{5,4},{6,7},{7,6},{8,9},{9,8},{10,11... | collective-permute-start | bytes 3080 | tf_op jit(solution)/shard_map/ppermute | solution.py:423
  119.6 2.7 %collective-permute-done.4 = f32[2,128]{1,0:T(2,128)S(1)} collective-permute-done((f32[2,128]{1,0:T(2,128)S(1)}, f32[2,128]{1,0:T(2,128)S(1)}, u32[]{:S(2)}, u32[]{:S(2)}) %collective-permute-start.4) | collective-permute-done | bytes 1056 | tf_op jit(solution)/shard_map/ppermute | solution.py:423
  122.3 0.5 add_bitcast_fusion
  122.8 5.1 %all-to-all-done.4 = bf16[64,24,128]{2,1,0:T(8,128)(2,1)S(1)} async-done(((bf16[64,24,128]{2,1,0:T(8,128)(2,1)}), bf16[64,24,128]{2,1,0:T(8,128)(2,1)S(1)}, u32[]{:S(2)}, u32[]{:S(2)}) %all-to-all-start.4) | async-done | bytes 393248 | tf_op jit(solution)/shard_map/all_to_all | solution.py:483
  127.9 1.2 shard_map.130
  (18 shorter events, 0.1 us)
Async XLA Ops:
  2.3 24.2 %all-to-all-start = ((bf16[16,72,128]{2,1,0:T(8,128)(2,1)}), bf16[16,72,128]{2,1,0:T(8,128)(2,1)S(1)}, u32[]{:S(2)}, u32[]{:S(2)}) async-start(bf16[16,72,128]{2,1,0:T(8,128)(2,1)} %bitcast.18), calls=%async_computation | async-start | bytes 589824 | tf_op jit(solution)/shard_map/all_to_all | solution.py:410
  16.5 18.1 %copy-start.6 = (s32[128]{0:T(128)S(1)}, s32[128]{0:T(128)}, u32[]{:S(2)}) copy-start(s32[128]{0:T(128)} %param.13) | copy-start | bytes 1540
  16.5 18.2 %copy-start.5 = (s32[128]{0:T(128)S(1)}, s32[128]{0:T(128)}, u32[]{:S(2)}) copy-start(s32[128]{0:T(128)} %param.14) | copy-start | bytes 1540
  27.8 16.0 %all-to-all-start.1 = ((bf16[4,3,72,128]{3,2,1,0:T(8,128)(2,1)}), bf16[4,3,72,128]{3,2,1,0:T(8,128)(2,1)S(1)}, u32[]{:S(2)}, u32[]{:S(2)}) async-start(bf16[4,3,72,128]{3,2,1,0:T(8,128)(2,1)} %shard_map.124), calls=%async_computation.1 | async-start | bytes 442368 | tf_op jit(solution)/shard_map/all_to_all | solution.py:414
  34.7 32.2 %copy-start = (bf16[144,72]{1,0:T(8,128)(2,1)S(1)}, bf16[144,72]{1,0:T(8,128)(2,1)}, u32[]{:S(2)}) copy-start(bf16[144,72]{1,0:T(8,128)(2,1)} %constant.72.clone.table_ref.low_ref) | copy-start | bytes 62212
  34.8 32.2 %copy-start.2 = (f32[256,72]{1,0:T(8,128)S(1)}, f32[256,72]{1,0:T(8,128)}, u32[]{:S(2)}) copy-start(f32[256,72]{1,0:T(8,128)} %constant.74.clone.back_ref) | copy-start | bytes 221188
  34.8 32.2 %copy-start.3 = (f32[72,144]{1,0:T(8,128)S(1)}, f32[72,144]{1,0:T(8,128)}, u32[]{:S(2)}) copy-start(f32[72,144]{1,0:T(8,128)} %constant.73.clone.turn_ref) | copy-start | bytes 124420
  61.0 5.9 %collective-permute-start = (bf16[24,72,128]{2,1,0:T(8,128)(2,1)S(1)}, bf16[24,72,128]{2,1,0:T(8,128)(2,1)S(1)}, u32[]{:S(2)}, u32[]{:S(2)}) collective-permute-start(bf16[24,72,128]{2,1,0:T(8,128)(2,1)S(1)} %bitcast.14), channel_id=1, source_target_pairs={{0,8},{8,0},{1,9},{9,1},{2,10},{10,2},{3,11},{11,3},{4,12},{12,4},... | collective-permute-start | bytes 1327112 | tf_op jit(solution)/shard_map/ppermute | solution.py:34
  66.9 12.1 %copy-start.4 = (s32[192]{0:T(256)S(1)}, s32[192]{0:T(256)}, u32[]{:S(2)}) copy-start(s32[192]{0:T(256)} %param.15) | copy-start | bytes 2308
  76.7 4.3 %collective-permute-start.1 = (f32[73,24,128]{2,1,0:T(8,128)S(1)}, f32[73,24,128]{2,1,0:T(8,128)S(1)}, u32[]{:S(2)}, u32[]{:S(2)}) collective-permute-start(f32[73,24,128]{2,1,0:T(8,128)S(1)} %get-tuple-element.32), channel_id=1, source_target_pairs={{0,8},{8,0},{1,9},{9,1},{2,10},{10,2},{3,11},{11,3},{4,12},{12,4},... | collective-permute-start | bytes 2691080 | tf_op jit(solution)/shard_map/ppermute | solution.py:34
  81.1 46.9 %copy-start.1 = (f32[144,192]{1,0:T(8,128)S(1)}, f32[144,192]{1,0:T(8,128)}, u32[]{:S(2)}) copy-start(f32[144,192]{1,0:T(8,128)} %constant.75.clone.table_ref) | copy-start | bytes 331780
  81.9 20.1 %all-to-all-start.3 = ((bf16[16,120,128]{2,1,0:T(8,128)(2,1)}), bf16[16,120,128]{2,1,0:T(8,128)(2,1)S(1)}, u32[]{:S(2)}, u32[]{:S(2)}) async-start(bf16[16,120,128]{2,1,0:T(8,128)(2,1)} %bitcast.8), calls=%async_computation.3 | async-start | bytes 983040 | tf_op jit(solution)/shard_map/all_to_all | solution.py:476
  85.5 4.6 %collective-permute-start.2 = (f32[2,128]{1,0:T(2,128)S(1)}, f32[2,128]{1,0:T(2,128)S(1)}, u32[]{:S(2)}, u32[]{:S(2)}) collective-permute-start(f32[2,128]{1,0:T(2,128)S(1)} %get-tuple-element.39), channel_id=1, source_target_pairs={{0,2},{1,3},{2,0},{3,1},{4,6},{5,7},{6,4},{7,5},{8,10},{9,11},{10,... | collective-permute-start | bytes 3080 | tf_op jit(solution)/shard_map/ppermute | solution.py:423
  103.1 24.8 %all-to-all-start.4 = ((bf16[64,24,128]{2,1,0:T(8,128)(2,1)}), bf16[64,24,128]{2,1,0:T(8,128)(2,1)S(1)}, u32[]{:S(2)}, u32[]{:S(2)}) async-start(bf16[64,24,128]{2,1,0:T(8,128)(2,1)} %bitcast.9), calls=%async_computation.4 | async-start | bytes 786432 | tf_op jit(solution)/shard_map/all_to_all | solution.py:483
  111.6 6.1 %collective-permute-start.3 = (f32[2,128]{1,0:T(2,128)S(1)}, f32[2,128]{1,0:T(2,128)S(1)}, u32[]{:S(2)}, u32[]{:S(2)}) collective-permute-start(f32[2,128]{1,0:T(2,128)S(1)} %pad_maximum_fusion), channel_id=1, source_target_pairs={{0,4},{1,5},{2,6},{3,7},{4,0},{5,1},{6,2},{7,3},{8,12},{9,13},{10,... | collective-permute-start | bytes 3080 | tf_op jit(solution)/shard_map/ppermute | solution.py:423
  117.7 4.6 %collective-permute-start.4 = (f32[2,128]{1,0:T(2,128)S(1)}, f32[2,128]{1,0:T(2,128)S(1)}, u32[]{:S(2)}, u32[]{:S(2)}) collective-permute-start(f32[2,128]{1,0:T(2,128)S(1)} %pad_maximum_fusion.1), channel_id=1, source_target_pairs={{0,1},{1,0},{2,3},{3,2},{4,5},{5,4},{6,7},{7,6},{8,9},{9,8},{10,11... | collective-permute-start | bytes 3080 | tf_op jit(solution)/shard_map/ppermute | solution.py:423

commit v15 on v14

--- a/solution.py
+++ b/solution.py
@@ -474,14 +474,14 @@
     share = share.reshape(SHARES, ROWS * CLS_GRP, CYCLES)
     share, evidence = lax.optimization_barrier((share, evidence))
     share = lax.all_to_all(share, ("wide_low", "wide_1"), 0, 0, tiled=True)
-    for bit in (2,):
+    for bit in (1,):
         evidence = exchanged_evidence(evidence, bit)
     share, evidence = lax.optimization_barrier((share, evidence))
     own_share = lax.axis_index(("wide_low", "wide_1"))
     sent = route(own_share.reshape(1), place, share).reshape(64, SLOT_ROWS, CYCLES)
     sent, evidence = lax.optimization_barrier((sent, evidence))
     got = lax.all_to_all(sent, WIDE, 0, 0, tiled=True)
-    evidence = exchanged_evidence(exchanged_evidence(evidence, 4), 1)
+    evidence = exchanged_evidence(exchanged_evidence(evidence, 2), 4)
     log_evidence = evidence[0] + jnp.log(evidence[1])
     got = got.reshape(2, 2 * SHARES * SLOT_ROWS, CYCLES)
     new_references = finish(table, got).reshape(1, 1, OWN_MAX, ANGLES, 2 * CYCLES)

time: 130 us -> 130 us (level)
  no operation moved by 1% of the time
where the time goes in v15:
time: 130 us; the launch traced here: 129 us
  starting transfers between devices  48.3 us (37%)
  waiting for transfers between devices  31.9 us (25%)
  Pallas kernels  27.8 us (21%)
  blocking collectives  16.4 us (13%)
  other arithmetic  2.67 us (2%)
    all_to_all x1, blocking collectives, fetch(): lax.all_to_all(picked, 'wide_1', 0, 0, tiled=True)  16.4 us
    all_to_all x1, starting transfers between devices, fetch(): sliced = lax.all_to_all(halves, ('wide_1', 'wide_2'), 0, 0, tiled=True)  11.8 us
    pallas_call x2, Pallas kernels, image_spectra(): pl.pallas_call(spectra_kernel, grid=(particles // count,), in_specs=[pl.B...  11.2 us
    all_to_all x1, waiting for transfers between devices, per_device(): share = lax.all_to_all(share, ('wide_low', 'wide_1'), 0, 0, tiled=True)  11.1 us
    ppermute x3, starting transfers between devices, exchanged_evidence(): got = lax.ppermute(pair, 'narrow', [(k, k ^ bit) for k in range(8)])  10.9 us
    pallas_call x1, Pallas kernels, score(): pl.pallas_call(score_kernel, in_specs=[pl.BlockSpec(memory_space=pltpu.SM...  9.79 us
    all_to_all x1, starting transfers between devices, per_device(): got = lax.all_to_all(sent, WIDE, 0, 0, tiled=True)  8.41 us
    ppermute x2, starting transfers between devices, swapped(): return lax.ppermute(x, 'wide_2', [(0, 1), (1, 0)])  6.83 us
  transfers between devices with their start and end apart: 9, of which 9 were waited for; matrix products, arithmetic and copies ran while one was open for 3% of the time, Pallas kernels for 9%

profile of v15, /device:TPU:1, one launch (start us, length us, event | category | flops | bytes accessed | tf_op | source)
XLA Modules:
  0.0 129.1 jit_solution(12586714212099746767)
XLA Ops:
  0.6 1.7 %shard_map.122 = bf16[8,2,72,128]{3,2,1,0:T(8,128)(2,1)} custom-call(bf16[8,72,256]{2,1,0:T(8,128)(2,1)} %bitcast.19), custom_call_target="tpu_custom_call" | custom-call | tf_op jit(solution)/shard_map/pallas_call | solution.py:307
  2.3 11.8 %all-to-all-start = ((bf16[16,72,128]{2,1,0:T(8,128)(2,1)}), bf16[16,72,128]{2,1,0:T(8,128)(2,1)S(1)}, u32[]{:S(2)}, u32[]{:S(2)}) async-start(bf16[16,72,128]{2,1,0:T(8,128)(2,1)} %bitcast.18), calls=%async_computation | async-start | bytes 589824 | tf_op jit(solution)/shard_map/all_to_all | solution.py:410
  14.1 0.8 copy.20.roster_ref
  14.9 0.7 multiply_multiply_fusion
  15.6 1.0 fusion.7
  16.5 5.6 %shard_map.123.early_ref = bf16[72,64,256]{2,1,0:T(8,128)(2,1)} custom-call(bf16[144,72]{1,0:T(8,128)(2,1)} %constant.72.clone.table_ref.low_ref, f32[128,128]{1,0:T(8,128)} %get-tuple-element.24.contrast_ref, bf16[128,72,256]{2,1,0:T(8,128)(2,1)} %image_ref.3), custom_call_target="tpu_custom_call" | custom-call | flops 339738624 | bytes 4718592 | tf_op jit(solution)/shard_map/pallas_call | solution.py:76
  22.1 4.4 %all-to-all-done = bf16[16,72,128]{2,1,0:T(8,128)(2,1)S(1)} async-done(((bf16[16,72,128]{2,1,0:T(8,128)(2,1)}), bf16[16,72,128]{2,1,0:T(8,128)(2,1)S(1)}, u32[]{:S(2)}, u32[]{:S(2)}) %all-to-all-start) | async-done | bytes 294944 | tf_op jit(solution)/shard_map/all_to_all | solution.py:410
  26.5 1.3 %shard_map.124 = bf16[4,3,72,128]{3,2,1,0:T(8,128)(2,1)} custom-call(s32[1]{0:T(128)} %bitcast.2.group_ref, s32[8,3]{1,0:T(8,128)S(1)} %copy.20.roster_ref, bf16[16,1,72,128]{3,2,1,0:T(8,128)(2,1)S(1)} %bitcast.17), custom_call_target="tpu_custom_call" | custom-call | tf_op jit(solution)/shard_map/pallas_call | solution.py:108
  27.8 6.8 %all-to-all-start.1 = ((bf16[4,3,72,128]{3,2,1,0:T(8,128)(2,1)}), bf16[4,3,72,128]{3,2,1,0:T(8,128)(2,1)S(1)}, u32[]{:S(2)}, u32[]{:S(2)}) async-start(bf16[4,3,72,128]{3,2,1,0:T(8,128)(2,1)} %shard_map.124), calls=%async_computation.1 | async-start | bytes 442368 | tf_op jit(solution)/shard_map/all_to_all | solution.py:414
  34.6 0.1 compare_convert_fusion.member_ref
  34.7 0.0 copy-done.5
  34.7 0.0 copy-start
  34.8 0.0 copy-start.2
  34.8 0.0 copy-start.3
  34.8 5.6 %shard_map.125.late_ref = bf16[72,64,256]{2,1,0:T(8,128)(2,1)} custom-call(bf16[144,72]{1,0:T(8,128)(2,1)} %constant.72.clone.table_ref.low_ref, f32[128,128]{1,0:T(8,128)} %get-tuple-element.24.contrast_ref, bf16[128,72,256]{2,1,0:T(8,128)(2,1)} %image_ref.3), custom_call_target="tpu_custom_call" | custom-call | flops 339738624 | bytes 4718592 | tf_op jit(solution)/shard_map/pallas_call | solution.py:76
  40.4 3.4 %all-to-all-done.1.source_ref = bf16[4,3,72,128]{3,2,1,0:T(8,128)(2,1)S(1)} async-done(((bf16[4,3,72,128]{3,2,1,0:T(8,128)(2,1)}), bf16[4,3,72,128]{3,2,1,0:T(8,128)(2,1)S(1)}, u32[]{:S(2)}, u32[]{:S(2)}) %all-to-all-start.1) | async-done | bytes 221216 | tf_op jit(solution)/shard_map/all_to_all | solution.py:414
  43.9 0.7 shard_map.126
  44.5 16.4 %all_to_all.25 = bf16[8,3,72,128]{3,2,1,0:T(8,128)(2,1)S(1)} all-to-all(bf16[8,3,72,128]{3,2,1,0:T(8,128)(2,1)S(1)} %shard_map.126), channel_id=1, replica_groups=mesh['wide_high'=2,'wide_low'=2,'wide_1'=8,'wide_2'=2,'narrow'=8] {'wide..., dimensions={0} | all-to-all | bytes 884736 | tf_op jit(solution)/shard_map/all_to_all | solution.py:418
  61.0 4.5 %collective-permute-start = (bf16[24,72,128]{2,1,0:T(8,128)(2,1)S(1)}, bf16[24,72,128]{2,1,0:T(8,128)(2,1)S(1)}, u32[]{:S(2)}, u32[]{:S(2)}) collective-permute-start(bf16[24,72,128]{2,1,0:T(8,128)(2,1)S(1)} %bitcast.14), channel_id=1, source_target_pairs={{0,8},{8,0},{1,9},{9,1},{2,10},{10,2},{3,11},{11,3},{4,12},{12,4},... | collective-permute-start | bytes 1327112 | tf_op jit(solution)/shard_map/ppermute | solution.py:34
  65.5 1.4 %collective-permute-done.other_ref = bf16[24,72,128]{2,1,0:T(8,128)(2,1)S(1)} collective-permute-done((bf16[24,72,128]{2,1,0:T(8,128)(2,1)S(1)}, bf16[24,72,128]{2,1,0:T(8,128)(2,1)S(1)}, u32[]{:S(2)}, u32[]{:S(2)}) %collective-permute-start) | collective-permute-done | bytes 442400 | tf_op jit(solution)/shard_map/ppermute | solution.py:34
  66.9 0.0 copy-done
  66.9 9.8 %shard_map.127 = (f32[73,24,128]{2,1,0:T(8,128)S(1)}, f32[73,24,128]{2,1,0:T(8,128)S(1)}, f32[2,128]{1,0:T(2,128)S(1)}) custom-call(s32[1]{0:T(128)} %bitcast.1.core_ref, bf16[24,72,128]{2,1,0:T(8,128)(2,1)S(1)} %bitcast.15, bf16[24,72,128]{2,1,0:T(8,128)(2,1)S(1)} %collective-permute-done.other_ref, bf16[72,64,256]{2,1,0:T(8,128)(2,1)} %shard_map.123.early_ref, ...), custom_call_target="tpu_custom_call" | custom-call | tf_op jit(solution)/shard_map/pallas_call | solution.py:248
  76.7 2.3 %collective-permute-start.1 = (f32[73,24,128]{2,1,0:T(8,128)S(1)}, f32[73,24,128]{2,1,0:T(8,128)S(1)}, u32[]{:S(2)}, u32[]{:S(2)}) collective-permute-start(f32[73,24,128]{2,1,0:T(8,128)S(1)} %get-tuple-element.32), channel_id=1, source_target_pairs={{0,8},{8,0},{1,9},{9,1},{2,10},{10,2},{3,11},{11,3},{4,12},{12,4},... | collective-permute-start | bytes 2691080 | tf_op jit(solution)/shard_map/ppermute | solution.py:34
  79.1 0.0 copy-done.4
  79.1 0.1 reshape.142
  79.1 0.1 select_reduce_fusion
  79.2 0.1 reshape.143
  79.3 0.1 copy.21
  79.4 0.1 reshape.144
  79.5 0.2 convert_reduce_fusion
  79.7 0.1 broadcast_add_fusion
  79.8 0.1 add.128
  79.8 1.2 collective-permute-done.1.got_ref
  81.1 0.9 shard_map.128
  81.9 3.6 %all-to-all-start.3 = ((bf16[16,120,128]{2,1,0:T(8,128)(2,1)}), bf16[16,120,128]{2,1,0:T(8,128)(2,1)S(1)}, u32[]{:S(2)}, u32[]{:S(2)}) async-start(bf16[16,120,128]{2,1,0:T(8,128)(2,1)} %bitcast.8), calls=%async_computation.3 | async-start | bytes 983040 | tf_op jit(solution)/shard_map/all_to_all | solution.py:476
  85.5 3.1 %collective-permute-start.2 = (f32[2,128]{1,0:T(2,128)S(1)}, f32[2,128]{1,0:T(2,128)S(1)}, u32[]{:S(2)}, u32[]{:S(2)}) collective-permute-start(f32[2,128]{1,0:T(2,128)S(1)} %get-tuple-element.39), channel_id=1, source_target_pairs={{0,1},{1,0},{2,3},{3,2},{4,5},{5,4},{6,7},{7,6},{8,9},{9,8},{10,11... | collective-permute-start | bytes 3080 | tf_op jit(solution)/shard_map/ppermute | solution.py:423
  88.6 2.3 %collective-permute-done.2 = f32[2,128]{1,0:T(2,128)S(1)} collective-permute-done((f32[2,128]{1,0:T(2,128)S(1)}, f32[2,128]{1,0:T(2,128)S(1)}, u32[]{:S(2)}, u32[]{:S(2)}) %collective-permute-start.2) | collective-permute-done | bytes 1056 | tf_op jit(solution)/shard_map/ppermute | solution.py:423
  91.0 11.1 %all-to-all-done.3.got_ref = bf16[16,120,128]{2,1,0:T(8,128)(2,1)S(1)} async-done(((bf16[16,120,128]{2,1,0:T(8,128)(2,1)}), bf16[16,120,128]{2,1,0:T(8,128)(2,1)S(1)}, u32[]{:S(2)}, u32[]{:S(2)}) %all-to-all-start.3) | async-done | bytes 491552 | tf_op jit(solution)/shard_map/all_to_all | solution.py:476
  102.1 1.1 shard_map.129
  103.1 8.4 %all-to-all-start.4 = ((bf16[64,24,128]{2,1,0:T(8,128)(2,1)}), bf16[64,24,128]{2,1,0:T(8,128)(2,1)S(1)}, u32[]{:S(2)}, u32[]{:S(2)}) async-start(bf16[64,24,128]{2,1,0:T(8,128)(2,1)} %bitcast.9), calls=%async_computation.4 | async-start | bytes 786432 | tf_op jit(solution)/shard_map/all_to_all | solution.py:483
  111.6 3.1 %collective-permute-start.3 = (f32[2,128]{1,0:T(2,128)S(1)}, f32[2,128]{1,0:T(2,128)S(1)}, u32[]{:S(2)}, u32[]{:S(2)}) collective-permute-start(f32[2,128]{1,0:T(2,128)S(1)} %pad_maximum_fusion), channel_id=1, source_target_pairs={{0,2},{1,3},{2,0},{3,1},{4,6},{5,7},{6,4},{7,5},{8,10},{9,11},{10,... | collective-permute-start | bytes 3080 | tf_op jit(solution)/shard_map/ppermute | solution.py:423
  114.7 1.5 %collective-permute-done.3 = f32[2,128]{1,0:T(2,128)S(1)} collective-permute-done((f32[2,128]{1,0:T(2,128)S(1)}, f32[2,128]{1,0:T(2,128)S(1)}, u32[]{:S(2)}, u32[]{:S(2)}) %collective-permute-start.3) | collective-permute-done | bytes 1056 | tf_op jit(solution)/shard_map/ppermute | solution.py:423
  116.2 4.7 %collective-permute-start.4 = (f32[2,128]{1,0:T(2,128)S(1)}, f32[2,128]{1,0:T(2,128)S(1)}, u32[]{:S(2)}, u32[]{:S(2)}) collective-permute-start(f32[2,128]{1,0:T(2,128)S(1)} %pad_maximum_fusion.1), channel_id=1, source_target_pairs={{0,4},{1,5},{2,6},{3,7},{4,0},{5,1},{6,2},{7,3},{8,12},{9,13},{10,... | collective-permute-start | bytes 3080 | tf_op jit(solution)/shard_map/ppermute | solution.py:423
  120.9 1.4 %collective-permute-done.4 = f32[2,128]{1,0:T(2,128)S(1)} collective-permute-done((f32[2,128]{1,0:T(2,128)S(1)}, f32[2,128]{1,0:T(2,128)S(1)}, u32[]{:S(2)}, u32[]{:S(2)}) %collective-permute-start.4) | collective-permute-done | bytes 1056 | tf_op jit(solution)/shard_map/ppermute | solution.py:423
  122.3 0.5 add_bitcast_fusion
  122.8 5.1 %all-to-all-done.4 = bf16[64,24,128]{2,1,0:T(8,128)(2,1)S(1)} async-done(((bf16[64,24,128]{2,1,0:T(8,128)(2,1)}), bf16[64,24,128]{2,1,0:T(8,128)(2,1)S(1)}, u32[]{:S(2)}, u32[]{:S(2)}) %all-to-all-start.4) | async-done | bytes 393248 | tf_op jit(solution)/shard_map/all_to_all | solution.py:483
  127.9 0.0 copy-done.1
  127.9 1.2 shard_map.130
  (18 shorter events, 0.1 us)
Async XLA Ops:
  2.3 24.2 %all-to-all-start = ((bf16[16,72,128]{2,1,0:T(8,128)(2,1)}), bf16[16,72,128]{2,1,0:T(8,128)(2,1)S(1)}, u32[]{:S(2)}, u32[]{:S(2)}) async-start(bf16[16,72,128]{2,1,0:T(8,128)(2,1)} %bitcast.18), calls=%async_computation | async-start | bytes 589824 | tf_op jit(solution)/shard_map/all_to_all | solution.py:410
  16.5 18.1 %copy-start.6 = (s32[128]{0:T(128)S(1)}, s32[128]{0:T(128)}, u32[]{:S(2)}) copy-start(s32[128]{0:T(128)} %param.13) | copy-start | bytes 1540
  16.5 18.2 %copy-start.5 = (s32[128]{0:T(128)S(1)}, s32[128]{0:T(128)}, u32[]{:S(2)}) copy-start(s32[128]{0:T(128)} %param.14) | copy-start | bytes 1540
  27.8 16.0 %all-to-all-start.1 = ((bf16[4,3,72,128]{3,2,1,0:T(8,128)(2,1)}), bf16[4,3,72,128]{3,2,1,0:T(8,128)(2,1)S(1)}, u32[]{:S(2)}, u32[]{:S(2)}) async-start(bf16[4,3,72,128]{3,2,1,0:T(8,128)(2,1)} %shard_map.124), calls=%async_computation.1 | async-start | bytes 442368 | tf_op jit(solution)/shard_map/all_to_all | solution.py:414
  34.7 32.2 %copy-start = (bf16[144,72]{1,0:T(8,128)(2,1)S(1)}, bf16[144,72]{1,0:T(8,128)(2,1)}, u32[]{:S(2)}) copy-start(bf16[144,72]{1,0:T(8,128)(2,1)} %constant.72.clone.table_ref.low_ref) | copy-start | bytes 62212
  34.8 32.2 %copy-start.2 = (f32[256,72]{1,0:T(8,128)S(1)}, f32[256,72]{1,0:T(8,128)}, u32[]{:S(2)}) copy-start(f32[256,72]{1,0:T(8,128)} %constant.74.clone.back_ref) | copy-start | bytes 221188
  34.8 32.2 %copy-start.3 = (f32[72,144]{1,0:T(8,128)S(1)}, f32[72,144]{1,0:T(8,128)}, u32[]{:S(2)}) copy-start(f32[72,144]{1,0:T(8,128)} %constant.73.clone.turn_ref) | copy-start | bytes 124420
  61.0 5.9 %collective-permute-start = (bf16[24,72,128]{2,1,0:T(8,128)(2,1)S(1)}, bf16[24,72,128]{2,1,0:T(8,128)(2,1)S(1)}, u32[]{:S(2)}, u32[]{:S(2)}) collective-permute-start(bf16[24,72,128]{2,1,0:T(8,128)(2,1)S(1)} %bitcast.14), channel_id=1, source_target_pairs={{0,8},{8,0},{1,9},{9,1},{2,10},{10,2},{3,11},{11,3},{4,12},{12,4},... | collective-permute-start | bytes 1327112 | tf_op jit(solution)/shard_map/ppermute | solution.py:34
  66.9 12.1 %copy-start.4 = (s32[192]{0:T(256)S(1)}, s32[192]{0:T(256)}, u32[]{:S(2)}) copy-start(s32[192]{0:T(256)} %param.15) | copy-start | bytes 2308
  76.7 4.3 %collective-permute-start.1 = (f32[73,24,128]{2,1,0:T(8,128)S(1)}, f32[73,24,128]{2,1,0:T(8,128)S(1)}, u32[]{:S(2)}, u32[]{:S(2)}) collective-permute-start(f32[73,24,128]{2,1,0:T(8,128)S(1)} %get-tuple-element.32), channel_id=1, source_target_pairs={{0,8},{8,0},{1,9},{9,1},{2,10},{10,2},{3,11},{11,3},{4,12},{12,4},... | collective-permute-start | bytes 2691080 | tf_op jit(solution)/shard_map/ppermute | solution.py:34
  81.1 46.9 %copy-start.1 = (f32[144,192]{1,0:T(8,128)S(1)}, f32[144,192]{1,0:T(8,128)}, u32[]{:S(2)}) copy-start(f32[144,192]{1,0:T(8,128)} %constant.75.clone.table_ref) | copy-start | bytes 331780
  81.9 20.1 %all-to-all-start.3 = ((bf16[16,120,128]{2,1,0:T(8,128)(2,1)}), bf16[16,120,128]{2,1,0:T(8,128)(2,1)S(1)}, u32[]{:S(2)}, u32[]{:S(2)}) async-start(bf16[16,120,128]{2,1,0:T(8,128)(2,1)} %bitcast.8), calls=%async_computation.3 | async-start | bytes 983040 | tf_op jit(solution)/shard_map/all_to_all | solution.py:476
  85.5 5.5 %collective-permute-start.2 = (f32[2,128]{1,0:T(2,128)S(1)}, f32[2,128]{1,0:T(2,128)S(1)}, u32[]{:S(2)}, u32[]{:S(2)}) collective-permute-start(f32[2,128]{1,0:T(2,128)S(1)} %get-tuple-element.39), channel_id=1, source_target_pairs={{0,1},{1,0},{2,3},{3,2},{4,5},{5,4},{6,7},{7,6},{8,9},{9,8},{10,11... | collective-permute-start | bytes 3080 | tf_op jit(solution)/shard_map/ppermute | solution.py:423
  103.1 24.8 %all-to-all-start.4 = ((bf16[64,24,128]{2,1,0:T(8,128)(2,1)}), bf16[64,24,128]{2,1,0:T(8,128)(2,1)S(1)}, u32[]{:S(2)}, u32[]{:S(2)}) async-start(bf16[64,24,128]{2,1,0:T(8,128)(2,1)} %bitcast.9), calls=%async_computation.4 | async-start | bytes 786432 | tf_op jit(solution)/shard_map/all_to_all | solution.py:483
  111.6 4.6 %collective-permute-start.3 = (f32[2,128]{1,0:T(2,128)S(1)}, f32[2,128]{1,0:T(2,128)S(1)}, u32[]{:S(2)}, u32[]{:S(2)}) collective-permute-start(f32[2,128]{1,0:T(2,128)S(1)} %pad_maximum_fusion), channel_id=1, source_target_pairs={{0,2},{1,3},{2,0},{3,1},{4,6},{5,7},{6,4},{7,5},{8,10},{9,11},{10,... | collective-permute-start | bytes 3080 | tf_op jit(solution)/shard_map/ppermute | solution.py:423
  116.2 6.1 %collective-permute-start.4 = (f32[2,128]{1,0:T(2,128)S(1)}, f32[2,128]{1,0:T(2,128)S(1)}, u32[]{:S(2)}, u32[]{:S(2)}) collective-permute-start(f32[2,128]{1,0:T(2,128)S(1)} %pad_maximum_fusion.1), channel_id=1, source_target_pairs={{0,4},{1,5},{2,6},{3,7},{4,0},{5,1},{6,2},{7,3},{8,12},{9,13},{10,... | collective-permute-start | bytes 3080 | tf_op jit(solution)/shard_map/ppermute | solution.py:423
